TPU v7x, 32 devices: a whole 2x2x4 slice. The times are simulated.
32 devices in a mesh: dp: 8 (over y, x, core), mp: 4 (over z).
Axes of the slice: x: 2, y: 2, z: 4, core: 2. Of those that a mesh axis runs over, the one named last changes fastest.
Arguments:
- gen_rows: bfloat16 [1024, 5120], P(('dp', 'mp')), may hold values from -6 to 6
- lengths: int32 [32, 4], P('dp'), may hold values from 1 to 16, 32 in all within a row
- assign: int32 [32, 4], P('dp'), may hold values from 0 to 3, each once within a row
- rewards: float32 [32, 4], P('dp'), may hold values from 0 to 1
- upstream: bfloat16 [2048, 2048], P('dp', 'mp'), may hold values from -6 to 6
- weight: bfloat16 [5120, 2048], P(None, 'mp'), may hold values from -0.078125 to 0.078125
- q_init: float32 [2048, 64], P('mp'), may hold values from -6 to 6
- resid: float32 [32, 128, 2048], P('dp', None, 'mp'), may hold values from -4 to 4
- block_ids: int32 [32], P('dp'), may hold values from 0 to 39, as said below
Outputs:
- p_factor: float32 [5120, 256], P(None, 'mp')
- q_factor: float32 [2048, 64], P('mp')
- resid_out: float32 [32, 128, 2048], P('dp', None, 'mp')
Inputs may be any that keep to these rules, and one draw needn't show every extreme that they name: Each row holds the lengths of one generator's 4 sequences; they sum to 32. `assign`: each row names every learner once. `block_ids`: the 4 ids of one replica are distinct.
All inputs are finite; a program needn't handle non-finite values.
Results may differ from a plain program's by a relative error of at most 0.003.
Values may be sent and summed in bfloat16 or wider, within the bound.
No kernel may reach another device: no remote copies, remote signals or barrier semaphores. Data moves between devices by JAX's collectives and lax.ppermute only.
A program may use at most 64 MiB of HBM per device.

v0:
```python
import jax
import jax.numpy as jnp
from jax import lax
from jax.sharding import PartitionSpec as P

HIGHEST_PRECISION = lax.Precision.HIGHEST


def packed_tables(lengths, assign, rewards, slot_count, capacity):
    groups, sequences = lengths.shape
    offsets = jnp.cumsum(lengths, axis=1) - lengths
    advantage = rewards - jnp.mean(rewards, axis=1, keepdims=True)
    seq_weight = advantage / lengths.astype(rewards.dtype)
    positions = jnp.arange(slot_count)
    seq_index = jnp.arange(sequences)
    inside = (offsets[:, None, :] <= positions[None, :, None]).astype(jnp.int32)
    owner = jnp.sum(inside, axis=2) - 1
    picked = owner[:, :, None] == seq_index[None, None, :]
    seq_start = jnp.sum(jnp.where(picked, offsets[:, None, :], 0), axis=2)
    learner = jnp.sum(jnp.where(picked, assign[:, None, :], 0), axis=2)
    row_weight = jnp.sum(jnp.where(picked, seq_weight[:, None, :], 0.0), axis=2)
    source = jnp.arange(groups)[:, None]
    slot_table = learner * (groups * capacity) + source * capacity + positions[None, :] - seq_start
    return (slot_table, row_weight)


def row_gradient(row_block, upstream_rows, weights_here, weight):
    hidden = jnp.dot(row_block, weight, preferred_element_type=jnp.float32)
    tangent = jnp.tanh(hidden)
    grad_h = (
        weights_here[:, None] * upstream_rows.astype(jnp.float32) * (1.0 - tangent * tangent)
    ).astype(jnp.bfloat16)
    return jnp.einsum("nd,nc->dc", row_block, grad_h, preferred_element_type=jnp.float32)


def shards(gen_rows, lengths, assign, rewards, upstream, weight, q_init, resid, block_ids):
    groups = lax.axis_size("mp")
    slot_count = gen_rows.shape[0]
    capacity = upstream.shape[0] // (groups * groups)
    slot_table, row_weight = packed_tables(lengths, assign, rewards, slot_count, capacity)
    flat_slot = slot_table.reshape(-1)
    flat_weight = row_weight.reshape(-1)
    upstream_rows = jnp.take(upstream, flat_slot, axis=0)
    gradient = row_gradient(
        lax.all_gather(gen_rows, "mp", axis=0, tiled=True), upstream_rows, flat_weight, weight
    )
    block_rows = resid.shape[1]
    for block in range(resid.shape[0]):
        first_row = block_ids[block] * block_rows
        current = lax.dynamic_slice_in_dim(gradient, first_row, block_rows, 0)
        gradient = lax.dynamic_update_slice_in_dim(gradient, current + resid[block], first_row, 0)
    p_local = jnp.dot(gradient, q_init, precision=HIGHEST_PRECISION)
    p_sum = lax.psum(p_local, "dp")
    gram_matrix = jnp.einsum("dr,ds->rs", p_sum, p_sum, precision=HIGHEST_PRECISION)
    factor_low = jnp.linalg.cholesky(gram_matrix)
    p_factor = jax.scipy.linalg.solve_triangular(factor_low, p_sum.T, lower=True).T
    q_local = jnp.einsum("dc,dr->cr", gradient, p_factor, precision=HIGHEST_PRECISION)
    q_factor = lax.psum(q_local, "dp") / lax.axis_size("dp")
    new_blocks = []
    for block in range(resid.shape[0]):
        first_row = block_ids[block] * block_rows
        merged_rows = lax.dynamic_slice_in_dim(gradient, first_row, block_rows, 0)
        p_rows = lax.dynamic_slice_in_dim(p_factor, first_row, block_rows, 0)
        approx = jnp.einsum("br,cr->bc", p_rows, q_factor, precision=HIGHEST_PRECISION)
        new_blocks.append(merged_rows - approx)
    return (p_factor, q_factor, jnp.stack(new_blocks))


def solution(mesh):
    placed = (
        P(("dp", "mp"), None),
        P("dp", None),
        P("dp", None),
        P("dp", None),
        P("dp", "mp"),
        P(None, "mp"),
        P("mp", None),
        P("dp", None, "mp"),
        P("dp"),
    )
    return jax.shard_map(
        shards,
        mesh=mesh,
        in_specs=placed,
        out_specs=(P(None, "mp"), P("mp", None), P("dp", None, "mp")),
        check_vma=False,
    )
```

profile of v0, /device:TPU:0, one launch (start us, length us, event | category | flops | bytes accessed | tf_op | source)
XLA Modules:
  0.0 227.8 jit_solution(15444329244682934595)
XLA Ops:
  7.2 0.0 all-gather.2.cloned.1.call-start
  7.2 0.7 all-gather.2.cloned.1.call-update
  7.9 0.0 all-reduce.3.cloned.1.call-start
  8.0 0.9 reduce_window_sum.11
  8.8 0.7 sub.52
  9.5 0.1 convert_reduce_fusion
  9.6 0.8 select_reduce_fusion.2
  10.4 0.1 add_subtract_fusion
  10.5 0.1 sub.58
  10.5 0.1 sub.57
  10.6 1.5 fusion.36
  14.8 0.8 reduce_sum.46
  15.6 0.8 convert_divide_fusion
  16.3 0.1 select_reduce_fusion.3
  16.4 0.1 mul.70
  16.5 1.3 fusion.35
  17.8 0.1 copy.39
  17.9 0.1 copy.38
  18.0 0.1 copy.37
  18.2 0.1 copy.36
  18.4 0.8 gather_fusion
  19.2 25.8 %all-gather.2.cloned.1.call-done = bf16[128,5120]{1,0:T(8,128)(2,1)} async-done(((bf16[32,5120]{1,0:T(8,128)(2,1)}), bf16[128,5120]{1,0:T(8,128)(2,1)}) %all-gather.2.cloned.1.call-update) | async-done | bytes 1310736 | tf_op jit(solution)/shard_map/all_gather | solution.py:45
  45.0 9.6 %fusion.8 = f32[512,5120]{1,0:T(8,128)} fusion(bf16[128,5120]{1,0:T(8,128)(2,1)} %all-gather.2.cloned.1.call-done, bf16[5120,512]{1,0:T(8,128)(2,1)} %param.14, bf16[128,512]{1,0:T(8,128)(2,1)S(1)} %gather_fusion, f32[128]{0:T(128)S(1)} %mul.70, pred[128]{0:T(512)(128)(4,1)S(1)} %compare_and_fusion), kind=kOutput, calls=%fused_computation.14 | convolution fusion | flops 1342636032 | bytes 17171072 | tf_op jit(solution)/shard_map/nd,nc->dc/dot_general | solution.py:33
  54.6 4.0 %copy.40 = f32[5120,512]{0,1:T(8,128)S(1)} copy(f32[5120,512]{0,1:T(8,128)} %bitcast.57) | data formatting | bytes 20971520
  58.7 1.0 fusion.12
  59.6 0.1 fusion.11
  59.7 0.1 fusion.10
  59.8 0.1 fusion.9
  59.9 4.0 %copy-done.1 = f32[5120,512]{0,1:T(8,128)} copy-done((f32[5120,512]{0,1:T(8,128)}, f32[5120,512]{0,1:T(8,128)S(1)}, u32[]{:S(2)}) %copy-start.1) | copy-done | bytes 10485784
  63.9 8.0 %fusion.37 = f32[5120,64]{0,1:T(8,128)} fusion(f32[5120,512]{0,1:T(8,128)S(1)} %fusion.9, f32[512,64]{0,1:T(8,128)S(1)} %copy-done.4), kind=kOutput, calls=%fused_computation.70 | convolution fusion | flops 2013265920 | bytes 11927552 | tf_op jit(solution)/shard_map/dot_general | solution.py:52
  72.0 0.2 all-reduce.5.cloned.1.call-start
  72.2 56.6 %all-reduce.3.cloned.1.call-done = f32[5120,64]{0,1:T(8,128)} async-done(((f32[5120,64]{0,1:T(8,128)}), f32[5120,64]{0,1:T(8,128)}) %all-reduce.3.cloned.1.call-update) | async-done | bytes 1310736 | tf_op jit(solution)/shard_map/psum | solution.py:53
  128.8 2.9 %fusion.38 = f32[64,64]{1,0:T(8,128)S(1)} fusion(f32[5120,64]{0,1:T(8,128)} %all-reduce.3.cloned.1.call-done), kind=kOutput, calls=%fused_computation.71 | convolution fusion | flops 251658240 | bytes 1327104 | tf_op jit(solution)/shard_map/dr,ds->rs/dot_general | solution.py:54
  131.7 0.1 copy.26
  131.8 5.8 %cholesky.16 = f32[64,64]{1,0:T(8,128)S(1)} custom-call(f32[64,64]{1,0:T(8,128)S(1)} %fusion.23), custom_call_target="Cholesky" | custom-call | tf_op jit(solution)/shard_map/jit(cholesky)/cholesky | solution.py:55
  137.7 0.6 compare_reduce_fusion
  138.3 0.7 fusion.20
  139.0 4.9 %custom-call.7 = f32[1,64,64]{1,2,0:T(8,128)S(1)} custom-call(f32[1,64,64]{2,1,0:T(8,128)S(1)} %fusion.20), custom_call_target="InvertDiagBlocksLowerTriangular" | custom-call | tf_op jit(solution)/shard_map/jit(_solve_triangular)/triangular_solve | solution.py:56
  143.9 2.6 %fusion.21 = f32[64,5120]{1,0:T(8,128)S(1)} fusion(f32[5120,64]{0,1:T(8,128)} %all-reduce.3.cloned.1.call-done, f32[1,64,64]{1,2,0:T(8,128)S(1)} %custom-call.7), kind=kOutput, calls=%fused_computation.34 | convolution fusion | flops 251658240 | bytes 2637824 | tf_op jit(solution)/shard_map/jit(_solve_triangular)/triangular_solve | solution.py:56
  146.5 13.9 %fusion.39 = f32[512,64]{0,1:T(8,128)} fusion(f32[5120,512]{0,1:T(8,128)} %copy-done.1, f32[64,5120]{1,0:T(8,128)S(1)} %fusion.21), kind=kOutput, calls=%fused_computation.72 | convolution fusion | flops 2013265920 | bytes 11927552 | tf_op jit(solution)/shard_map/dc,dr->cr/dot_general | solution.py:57
  160.4 52.3 %all-reduce.5.cloned.1.call-done = f32[512,64]{0,1:T(8,128)} async-done(((f32[512,64]{0,1:T(8,128)}), f32[512,64]{0,1:T(8,128)}) %all-reduce.5.cloned.1.call-update) | async-done | bytes 131088 | tf_op jit(solution)/shard_map/psum | solution.py:58
  212.7 0.9 broadcast_multiply_fusion
  213.6 1.6 fusion
  215.2 1.6 fusion.1
  216.8 1.6 fusion.2
  218.4 1.6 fusion.3
  219.9 0.1 pad_maximum_fusion
  220.0 1.3 copy.31
  (19 shorter events, 0.1 us)
Async XLA Ops:
  7.2 11.2 %copy-start = (bf16[256,512]{1,0:T(8,128)(2,1)S(1)}, bf16[256,512]{1,0:T(8,128)(2,1)}, u32[]{:S(2)}) copy-start(bf16[256,512]{1,0:T(8,128)(2,1)} %param.13) | copy-start | bytes 786436
  7.2 37.8 %all-gather.2.cloned.1.call-start = ((), (), s32[]{:S(2)}) async-start(), calls=%async_computation | async-start | bytes 1638400 | tf_op jit(solution)/shard_map/all_gather | solution.py:45
  7.9 120.9 %all-reduce.3.cloned.1.call-start = ((), (), s32[]{:S(2)}) async-start(), calls=%async_computation.1 | async-start | bytes 2621440 | tf_op jit(solution)/shard_map/psum | solution.py:53
  54.6 9.2 %copy-start.4 = (f32[512,64]{0,1:T(8,128)S(1)}, f32[512,64]{0,1:T(8,128)}, u32[]{:S(2)}) copy-start(f32[512,64]{0,1:T(8,128)} %param.15) | copy-start | bytes 393220
  59.9 4.0 %copy-start.1 = (f32[5120,512]{0,1:T(8,128)}, f32[5120,512]{0,1:T(8,128)S(1)}, u32[]{:S(2)}) copy-start(f32[5120,512]{0,1:T(8,128)S(1)} %fusion.9) | copy-start | bytes 31457284
  72.0 140.7 %all-reduce.5.cloned.1.call-start = ((), (), s32[]{:S(2)}) async-start(), calls=%async_computation.2 | async-start | bytes 262144 | tf_op jit(solution)/shard_map/psum | solution.py:58
  146.5 71.9 %copy-start.2 = (f32[64,5120]{1,0:T(8,128)}, f32[64,5120]{1,0:T(8,128)S(1)}, u32[]{:S(2)}) copy-start(f32[64,5120]{1,0:T(8,128)S(1)} %fusion.21) | copy-start | bytes 3932164
  213.6 7.7 %copy-start.3 = (f32[512,64]{0,1:T(8,128)}, f32[512,64]{0,1:T(8,128)S(1)}, u32[]{:S(2)}) copy-start(f32[512,64]{0,1:T(8,128)S(1)} %broadcast_multiply_fusion) | copy-start | bytes 393220
Sparse Core Ops, SparseCore 0:
  9.6 35.3 all-gather.1
  72.1 56.6 all-reduce.2
  160.5 52.1 all-reduce.4
where the time goes:
time: 228 us
  waiting for transfers between devices  135 us (59%)
  matrix products  43.3 us (19%)
  other arithmetic  18.4 us (8%)
  between operations  16.7 us (7%)
  local copies, waits for them, and re-layouts  13.7 us (6%)
    psum x1, waiting for transfers between devices, shards(): p_sum = lax.psum(p_local, 'dp')  56.6 us
    psum x1, waiting for transfers between devices, shards(): q_factor = lax.psum(q_local, 'dp') / lax.axis_size('dp')  52.3 us
    all_gather x1, waiting for transfers between devices, shards(): lax.all_gather(gen_rows, 'mp', axis=0, tiled=True)  25.8 us
    dot_general x1, matrix products, shards(): jnp.einsum('dc,dr->cr', gradient, p_factor, precision=HIGHEST_PRECISION)  13.9 us
    unnamed x16, local copies, waits for them, and re-layouts  9.83 us
    dot_general x1, matrix products, row_gradient(): jnp.einsum('nd,nc->dc', row_block, grad_h, preferred_element_type=jnp.flo...  9.64 us
    dot_general x1, matrix products, shards(): p_local = jnp.dot(gradient, q_init, precision=HIGHEST_PRECISION)  8.05 us
    another operation x3, other arithmetic, shards(): factor_low = jnp.linalg.cholesky(gram_matrix)  6.52 us
  transfers between devices with their start and end apart: 3, of which 3 were waited for; matrix products, arithmetic and copies ran while one was open for 4% of the time, Pallas kernels for 0%

commit v1 on v0

v1 whole, which is shorter than its diff:
```python
import functools
import jax
import jax.numpy as jnp
from jax import lax
from jax.experimental import pallas as pl
from jax.experimental.pallas import tpu as pltpu
from jax.sharding import PartitionSpec as P

F32 = jnp.float32
BF16 = jnp.bfloat16
HIGHEST = lax.Precision.HIGHEST
VMEM_LIMIT = 48 * 1024 * 1024


def packed_tables(lengths, assign, rewards, slot_count, capacity):
    groups, sequences = lengths.shape
    offsets = jnp.cumsum(lengths, axis=1) - lengths
    advantage = rewards - jnp.mean(rewards, axis=1, keepdims=True)
    seq_weight = advantage / lengths.astype(rewards.dtype)
    positions = jnp.arange(slot_count)
    seq_index = jnp.arange(sequences)
    inside = (offsets[:, None, :] <= positions[None, :, None]).astype(jnp.int32)
    owner = jnp.sum(inside, axis=2) - 1
    picked = owner[:, :, None] == seq_index[None, None, :]
    seq_start = jnp.sum(jnp.where(picked, offsets[:, None, :], 0), axis=2)
    learner = jnp.sum(jnp.where(picked, assign[:, None, :], 0), axis=2)
    row_weight = jnp.sum(jnp.where(picked, seq_weight[:, None, :], 0.0), axis=2)
    source = jnp.arange(groups)[:, None]
    slot_table = learner * (groups * capacity) + source * capacity + positions[None, :] - seq_start
    return (slot_table, row_weight)


def dot(a, b, dims, precision=None):
    return lax.dot_general(a, b, (dims, ((), ())), precision=precision, preferred_element_type=F32)


NN, NT, TN = ((1,), (0,)), ((1,), (1,)), ((0,), (0,))


def split(a, parts):
    out = []
    for _ in range(parts):
        high = a.astype(BF16)
        out.append(high)
        a = a - high.astype(F32)
    return jnp.concatenate(out, axis=0)


def fold(a, parts):
    rows = a.shape[0] // parts
    total = a[:rows]
    for i in range(1, parts):
        total = total + a[i * rows:(i + 1) * rows]
    return total


SMEM = pl.BlockSpec(memory_space=pltpu.SMEM)
VMEM = pl.BlockSpec(memory_space=pltpu.VMEM)


def call(kernel, n_smem, n_vmem, outs, scratch=(), flops=1000000, bytes_accessed=1000000, name=None):
    return pl.pallas_call(
        kernel,
        out_shape=outs,
        in_specs=[SMEM] * n_smem + [VMEM] * n_vmem,
        out_specs=jax.tree.map(lambda _: VMEM, outs),
        scratch_shapes=list(scratch),
        compiler_params=pltpu.CompilerParams(vmem_limit_bytes=VMEM_LIMIT),
        cost_estimate=pl.CostEstimate(flops=flops, bytes_accessed=bytes_accessed, transcendentals=0),
        name=name,
    )


def resid_kernel(q0t, resid, out):
    width = resid.shape[1]
    for k in range(resid.shape[0]):
        out[:, k * width:(k + 1) * width] = dot(q0t[...], resid[k], NT, HIGHEST)


def first_kernel(n_x, sel, ids, place, *refs):
    pieces, refs = refs[:n_x], refs[n_x:]
    w, wups, q0t, ft, xall, g, keep, send, h, pt = refs
    step, last = pl.program_id(0), pl.num_programs(0) - 1
    depth = w.shape[0]

    @pl.when(step == 0)
    def _():
        rows = pieces[0].shape[0]
        for j in range(n_x):
            @pl.when(sel[j] >= 0)
            def _():
                xall[pl.ds(pl.multiple_of(sel[j] * rows, rows), rows), :] = pieces[j][...]
        h[...] = jnp.zeros_like(h)

    h[...] += jnp.dot(xall[:, pl.ds(pl.multiple_of(step * depth, depth), depth)], w[...], preferred_element_type=F32)

    @pl.when(step == last)
    def _():
        tangent = jnp.tanh(h[...])
        grad = (wups[...] * (1.0 - tangent * tangent)).astype(BF16)
        g[...] = grad
        yt = split(dot(q0t[...], grad.astype(F32), NT, HIGHEST), 3)
        wide = 1024
        for i in range(pt.shape[1] // wide):
            at = slice(i * wide, (i + 1) * wide)
            pt[:, at] = fold(dot(yt, xall[:, at], NN), 3)
        block = ft.shape[1] // ids.shape[0]
        for k in range(ids.shape[0]):
            at = pl.ds(pl.multiple_of(ids[k] * block, block), block)
            pt[:, at] += ft[:, k * block:(k + 1) * block]
        write_halves(place, pt, keep, send)


def write_halves(place, pt, keep, send):
    if keep is send:
        keep[...] = pt[...]
        return
    chips, rows = keep.shape[:2]
    for k in range(chips):
        chip = place[0] ^ k
        keep[k] = pt[pl.ds(pl.multiple_of((2 * chip + place[1]) * rows, rows), rows), :]
        send[k] = pt[pl.ds(pl.multiple_of((2 * chip + 1 - place[1]) * rows, rows), rows), :]


def merged_kernel(ids, xall, g, resid, out):
    block = resid.shape[1]
    for k in range(ids.shape[0]):
        at = pl.ds(pl.multiple_of(ids[k] * block, block), block)
        out[k] = dot(xall[:, at], g[...], TN) + resid[k]


def second_kernel(n_p, ids, place, *refs):
    parts, refs = refs[:n_p], refs[n_p:]
    xall, g, resid, pt, gram, ut = refs
    if n_p == 1:
        pt[...] = parts[0][...]
    else:
        rows = parts[0].shape[0]
        for j in range(n_p):
            chip, core = place[0] ^ (j // 2), place[1] ^ (j % 2)
            pt[pl.ds(pl.multiple_of((2 * chip + core) * rows, rows), rows), :] = parts[j][...]
    rank = pt.shape[0]
    ps = split(pt[...], 2)
    both = fold(dot(ps, ps, NT), 2)
    gram[...] = both[:, :rank] + both[:, rank:]
    zt = fold(dot(ps, xall[...], NT), 2)
    total = fold(dot(split(zt, 3), g[...], NN), 3)
    block = resid.shape[1]
    for k in range(ids.shape[0]):
        at = pl.ds(pl.multiple_of(ids[k] * block, block), block)
        total = total + dot(pt[:, at], resid[k], NN, HIGHEST)
    ut[...] = total


def factor_kernel(ids, gram, pt, pft, linv, blocks):
    rank = gram.shape[0]
    row_at = lax.broadcasted_iota(jnp.int32, (rank, rank), 0)
    col_at = lax.broadcasted_iota(jnp.int32, (rank, rank), 1)
    eye = (row_at == col_at).astype(F32)
    aug = jnp.concatenate([gram[...], eye], axis=1)
    below = lax.broadcasted_iota(jnp.int32, (rank, 1), 0)
    scale = jnp.zeros((rank, 1), F32)
    for k in range(rank):
        pivot = aug[k:k + 1, k:k + 1]
        scale = jnp.where(below == k, pivot, scale)
        ratio = jnp.where(below > k, aug[:, k:k + 1] / pivot, 0.0)
        aug = aug - ratio * aug[k:k + 1, :]
    inverse = aug[:, rank:] / jnp.sqrt(scale)
    linv[...] = inverse
    wide = 1024
    for i in range(pt.shape[1] // wide):
        at = slice(i * wide, (i + 1) * wide)
        pft[:, at] = dot(inverse, pt[:, at], NN, HIGHEST)
    block = blocks.shape[1] // ids.shape[0]
    for k in range(ids.shape[0]):
        at = pl.ds(pl.multiple_of(ids[k] * block, block), block)
        blocks[:, k * block:(k + 1) * block] = pft[:, at]


def last_kernel(scale, place, half_own, half_other, linv, blocks, merged, qt, out, ut):
    if half_other is None:
        ut[...] = half_own[...]
    else:
        rows = half_own.shape[0]
        ut[pl.ds(pl.multiple_of(place[1] * rows, rows), rows), :] = half_own[...]
        ut[pl.ds(pl.multiple_of((1 - place[1]) * rows, rows), rows), :] = half_other[...]
    q = dot(linv[...], ut[...], NN, HIGHEST) * scale
    qt[...] = q
    block = merged.shape[1]
    for k in range(merged.shape[0]):
        out[k] = merged[k] - dot(blocks[:, k * block:(k + 1) * block], q, TN, HIGHEST)


def gather_rows(x, groups, at):
    if groups % 2:
        return [lax.all_gather(x, "mp", axis=0, tiled=True)], jnp.zeros((1,), jnp.int32)
    pairs_a = [(i, i ^ 1) for i in range(groups)]
    pairs_b = [(i, i + 1 if i % 2 else i - 1) for i in range(1, groups - 1)]
    even = at % 2 == 0
    pieces, owner = [x], [at]
    from_a, from_b = x, x
    for s in range(1, groups):
        new_a = lax.ppermute(from_b, "mp", pairs_a)
        new_b = lax.ppermute(from_a, "mp", pairs_b) if s < groups - 1 else None
        down, up = at + s, at - s
        pieces.append(new_a)
        owner.append(jnp.where(even, down, up))
        if new_b is not None:
            pieces.append(new_b)
            owner.append(jnp.where(even, up, down))
        from_a, from_b = new_a, new_b
    owner = jnp.stack(owner).astype(jnp.int32)
    return pieces, jnp.where((owner >= 0) & (owner < groups), owner, -1)


def swap(a, bit, size):
    return lax.ppermute(a, "dp", [(i, i ^ bit) for i in range(size)])


def shards(gen_rows, lengths, assign, rewards, upstream, weight, q_init, resid, block_ids):
    groups, replicas = lax.axis_size("mp"), lax.axis_size("dp")
    slot_count, depth = gen_rows.shape
    columns, rank = q_init.shape
    capacity = upstream.shape[0] // (groups * groups)
    kept, block = resid.shape[:2]
    rows = groups * slot_count
    at_dp = lax.axis_index("dp")
    place = jnp.stack([at_dp // 2, at_dp % 2]).astype(jnp.int32)
    direct = replicas == 8

    pieces, owner = gather_rows(gen_rows, groups, lax.axis_index("mp"))
    slot_table, row_weight = packed_tables(lengths, assign, rewards, slot_count, capacity)
    upstream_rows = jnp.take(upstream, slot_table.reshape(-1), axis=0)
    weighted = row_weight.reshape(-1)[:, None] * upstream_rows.astype(F32)
    q0t = q_init.T
    shape = jax.ShapeDtypeStruct
    ft = call(resid_kernel, 0, 2, shape((rank, kept * block), F32), name="resid_term")(q0t, resid)

    steps = 5
    n_x = len(pieces)
    full = lambda *dims: pl.BlockSpec(dims, lambda i: (0,) * len(dims))
    if direct:
        chips = replicas // 2
        part = rank // replicas
        halves = [shape((chips, part, depth), F32)] * 2
        kernel = functools.partial(first_kernel, n_x)
    else:
        halves = [shape((rank, depth), F32)]

        def kernel(*refs):
            first_kernel(n_x, *refs[:-2], refs[-3], *refs[-2:])
    xall, g, *halves = pl.pallas_call(
        kernel,
        out_shape=[shape((rows, depth), BF16), shape((rows, columns), BF16)] + halves,
        grid=(steps,),
        in_specs=[SMEM] * 3
        + [full(*p.shape) for p in pieces]
        + [pl.BlockSpec((depth // steps, columns), lambda i: (i, 0))]
        + [full(rows, columns), full(rank, columns), full(rank, kept * block)],
        out_specs=[full(rows, depth), full(rows, columns)] + [full(*s.shape) for s in halves],
        scratch_shapes=[pltpu.VMEM((rows, columns), F32), pltpu.VMEM((rank, depth), F32)],
        compiler_params=pltpu.CompilerParams(vmem_limit_bytes=VMEM_LIMIT),
        cost_estimate=pl.CostEstimate(flops=2 * rows * depth * columns, bytes_accessed=10000000, transcendentals=0),
        name="first",
    )(owner, block_ids, place, *pieces, weight, weighted, q0t, ft)

    merged = call(merged_kernel, 1, 3, shape((kept, block, columns), F32), name="merged")(block_ids, xall, g, resid)

    if direct:
        keep, send = halves
        back = swap(send, 1, replicas)
        sums = [keep[k] + back[k] for k in range(chips)]
        own = sums[0]
        for k in range(1, chips):
            own = own + swap(sums[k], 2 * k, replicas)
        same = [own] + [swap(own, 2 * k, replicas) for k in range(1, chips)]
        p_parts = []
        for s in same:
            p_parts += [s, swap(s, 1, replicas)]
    else:
        p_parts = [lax.psum(halves[0], "dp")]

    n_p = len(p_parts)
    pt, gram, ut = call(
        functools.partial(second_kernel, n_p), 2, n_p + 3,
        [shape((rank, depth), F32), shape((rank, rank), F32), shape((rank, columns), F32)], name="second",
    )(block_ids, place, *p_parts, xall, g, resid)

    pft, linv, blocks = call(
        factor_kernel, 1, 2,
        [shape((rank, depth), F32), shape((rank, rank), F32), shape((rank, kept * block), F32)], name="factor",
    )(block_ids, gram, pt)

    if direct:
        half = rank // 2
        mine = lax.dynamic_slice_in_dim(ut, place[1] * half, half, 0)
        other = lax.dynamic_slice_in_dim(ut, (1 - place[1]) * half, half, 0)
        chip_sum = mine + swap(other, 1, replicas)
        total = chip_sum
        for k in range(1, chips):
            total = total + swap(chip_sum, 2 * k, replicas)
        u_parts = [total, swap(total, 1, replicas)]
        tail = functools.partial(last_kernel, 1.0 / replicas)
    else:
        u_parts = [lax.psum(ut, "dp")]

        def tail(place, half_own, *refs):
            last_kernel(1.0 / replicas, place, half_own, None, *refs)
    qt, new_resid = call(
        tail, 1, len(u_parts) + 3,
        [shape((rank, columns), F32), shape((kept, block, columns), F32)],
        [pltpu.VMEM((rank, columns), F32)], name="last",
    )(place, *u_parts, linv, blocks, merged)
    return pft.T, qt.T, new_resid


def solution(mesh):
    placed = (
        P(("dp", "mp"), None),
        P("dp", None),
        P("dp", None),
        P("dp", None),
        P("dp", "mp"),
        P(None, "mp"),
        P("mp", None),
        P("dp", None, "mp"),
        P("dp"),
    )
    return jax.shard_map(
        shards,
        mesh=mesh,
        in_specs=placed,
        out_specs=(P(None, "mp"), P("mp", None), P("dp", None, "mp")),
        check_vma=False,
    )
```

time: 228 us -> 93.4 us (0.41)
  waiting for transfers between devices: 135 us -> 32.3 us
  matrix products: 43.3 us -> 0 us
  starting transfers between devices: 0.3 us -> 25.7 us
  Pallas kernels: 0 us -> 22.6 us
  between operations: 16.7 us -> 0.91 us
  other arithmetic: 18.4 us -> 4.5 us
  local copies, waits for them, and re-layouts: 13.7 us -> 6.89 us
    psum x2 -> x0, waiting for transfers between devices: 109 us -> none  [the longest x1 56.6 us: shards(): p_sum = lax.psum(p_local, 'dp')]
    dot_general x8 -> x0, matrix products: 40.8 us -> none  [the longest x1 13.9 us: shards(): jnp.einsum('dc,dr->cr', gradient, p_factor, precision=HIGHEST_PRECISION)]
    ppermute x0 -> x21, waiting for transfers between devices: none -> 32.3 us  [the longest x16 22 us: swap(): return lax.ppermute(a, 'dp', [(i, i ^ bit) for i in range(size)])]
    all_gather x1 -> x0, waiting for transfers between devices: 25.8 us -> none  [shards(): lax.all_gather(gen_rows, 'mp', axis=0, tiled=True)]
    ppermute x0 -> x21, starting transfers between devices: none -> 25.7 us  [the longest x3 12.7 us: gather_rows(): new_a = lax.ppermute(from_b, 'mp', pairs_a)]
    pallas_call x0 -> x6, Pallas kernels: none -> 22.6 us  [the longest x1 8.74 us: shards(): call(factor_kernel, 1, 2, [shape((rank, depth), F32), shape((rank, rank),...]
    another operation x6 -> x1, other arithmetic: 12.1 us -> 0.07 us  [shards(): place = jnp.stack([at_dp // 2, at_dp % 2]).astype(jnp.int32)]
    unnamed x16 -> x30, local copies, waits for them, and re-layouts: 9.83 us -> 5.7 us
  transfers between devices with their start and end apart: 3 -> 21, of which waited for: 3 -> 14; matrix products, arithmetic and copies ran while one was open for 4% -> 6% of each run, Pallas kernels for 0% -> 12%
where the time goes in v1:
time: 93.4 us; the launch traced here: 92.9 us
  waiting for transfers between devices  32.3 us (35%)
  starting transfers between devices  25.7 us (28%)
  Pallas kernels  22.6 us (24%)
  local copies, waits for them, and re-layouts  6.89 us (7%)
  other arithmetic  4.5 us (5%)
    ppermute x16, waiting for transfers between devices, swap(): return lax.ppermute(a, 'dp', [(i, i ^ bit) for i in range(size)])  22 us
    ppermute x3, starting transfers between devices, gather_rows(): new_a = lax.ppermute(from_b, 'mp', pairs_a)  12.7 us
    ppermute x16, starting transfers between devices, swap(): return lax.ppermute(a, 'dp', [(i, i ^ bit) for i in range(size)])  11.6 us
    ppermute x3, waiting for transfers between devices, gather_rows(): new_a = lax.ppermute(from_b, 'mp', pairs_a)  10.3 us
    pallas_call x1, Pallas kernels, shards(): call(factor_kernel, 1, 2, [shape((rank, depth), F32), shape((rank, rank),...  8.74 us
    pallas_call x1, Pallas kernels, shards(): pl.pallas_call(kernel, out_shape=[shape((rows, depth), BF16), shape((rows...  6.39 us
    unnamed x30, local copies, waits for them, and re-layouts  5.7 us
    pallas_call x1, Pallas kernels, shards(): call(tail, 1, len(u_parts) + 3, [shape((rank, columns), F32), shape((kept...  2.76 us
  transfers between devices with their start and end apart: 21, of which 14 were waited for; matrix products, arithmetic and copies ran while one was open for 6% of the time, Pallas kernels for 12%

profile of v1, /device:TPU:0, one launch (start us, length us, event | category | flops | bytes accessed | tf_op | source)
XLA Modules:
  0.0 92.9 jit_solution(13732019192680502276)
XLA Ops:
  0.7 3.1 %collective-permute-start = (bf16[32,5120]{1,0:T(8,128)(2,1)}, bf16[32,5120]{1,0:T(8,128)(2,1)S(1)}, u32[]{:S(2)}, u32[]{:S(2)}) collective-permute-start(bf16[32,5120]{1,0:T(8,128)(2,1)} %refs_0_.1), channel_id=1, source_target_pairs={{0,1},{1,0},{2,3},{3,2},{4,5},{5,4},{6,7},{7,6},{8,9},{9,8},{10,11... | collective-permute-start | bytes 983048 | tf_op jit(solution)/shard_map/ppermute | solution.py:203
  3.8 0.7 collective-permute-start.1
  4.5 0.9 reduce_window_sum.11
  5.3 0.7 sub.54
  6.1 0.8 select_reduce_fusion.1
  7.2 0.8 reduce_sum.46
  8.0 0.8 convert_divide_fusion
  9.0 2.7 %collective-permute-done.refs_1_ = bf16[32,5120]{1,0:T(8,128)(2,1)S(1)} collective-permute-done((bf16[32,5120]{1,0:T(8,128)(2,1)}, bf16[32,5120]{1,0:T(8,128)(2,1)S(1)}, u32[]{:S(2)}, u32[]{:S(2)}) %collective-permute-start) | collective-permute-done | bytes 327712 | tf_op jit(solution)/shard_map/ppermute | solution.py:203
  11.7 0.7 collective-permute-start.3
  12.4 0.8 gather_fusion
  13.3 1.2 %resid_term.1.refs_9_ = f32[64,512]{1,0:T(8,128)S(1)} custom-call(f32[64,512]{1,0:T(8,128)S(1)} %bitcast.27, f32[4,128,512]{2,1,0:T(8,128)S(1)} %copy-done.1), custom_call_target="tpu_custom_call" | custom-call | flops 1000000 | bytes 1000000 | tf_op jit(solution)/shard_map/resid_term/pallas_call | solution.py:237
  14.5 4.6 %collective-permute-start.2 = (bf16[32,5120]{1,0:T(8,128)(2,1)S(1)}, bf16[32,5120]{1,0:T(8,128)(2,1)S(1)}, u32[]{:S(2)}, u32[]{:S(2)}) collective-permute-start(bf16[32,5120]{1,0:T(8,128)(2,1)S(1)} %collective-permute-done.1.refs_2_), channel_id=1, source_target_pairs={{0,1},{1,0},{2,3},{3,2},{4,5},{5,4},{6,7},{7,6},{8,9},{9,8},{10,11... | collective-permute-start | bytes 983048 | tf_op jit(solution)/shard_map/ppermute | solution.py:203
  19.1 5.0 %collective-permute-start.4 = (bf16[32,5120]{1,0:T(8,128)(2,1)S(1)}, bf16[32,5120]{1,0:T(8,128)(2,1)S(1)}, u32[]{:S(2)}, u32[]{:S(2)}) collective-permute-start(bf16[32,5120]{1,0:T(8,128)(2,1)S(1)} %collective-permute-done.3.refs_4_), channel_id=1, source_target_pairs={{0,1},{1,0},{2,3},{3,2},{4,5},{5,4},{6,7},{7,6},{8,9},{9,8},{10,11... | collective-permute-start | bytes 983048 | tf_op jit(solution)/shard_map/ppermute | solution.py:203
  24.2 0.7 copy-done.10
  25.1 2.6 %collective-permute-done.2.refs_3_ = bf16[32,5120]{1,0:T(8,128)(2,1)S(1)} collective-permute-done((bf16[32,5120]{1,0:T(8,128)(2,1)S(1)}, bf16[32,5120]{1,0:T(8,128)(2,1)S(1)}, u32[]{:S(2)}, u32[]{:S(2)}) %collective-permute-start.2) | collective-permute-done | bytes 327712 | tf_op jit(solution)/shard_map/ppermute | solution.py:203
  27.7 5.0 %collective-permute-done.4.refs_5_ = bf16[32,5120]{1,0:T(8,128)(2,1)S(1)} collective-permute-done((bf16[32,5120]{1,0:T(8,128)(2,1)S(1)}, bf16[32,5120]{1,0:T(8,128)(2,1)S(1)}, u32[]{:S(2)}, u32[]{:S(2)}) %collective-permute-start.4) | collective-permute-done | bytes 327712 | tf_op jit(solution)/shard_map/ppermute | solution.py:203
  32.7 1.0 %copy-done.7 = bf16[32,5120]{1,0:T(8,128)(2,1)S(1)} copy-done((bf16[32,5120]{1,0:T(8,128)(2,1)S(1)}, bf16[32,5120]{1,0:T(8,128)(2,1)}, u32[]{:S(2)}) %copy-start.7) | copy-done | bytes 327704
  33.7 1.0 %copy-done.9 = bf16[32,5120]{1,0:T(8,128)(2,1)S(1)} copy-done((bf16[32,5120]{1,0:T(8,128)(2,1)S(1)}, bf16[32,5120]{1,0:T(8,128)(2,1)}, u32[]{:S(2)}) %copy-start.9) | copy-done | bytes 327704
  34.6 1.0 %copy-done.11 = bf16[32,5120]{1,0:T(8,128)(2,1)S(1)} copy-done((bf16[32,5120]{1,0:T(8,128)(2,1)S(1)}, bf16[32,5120]{1,0:T(8,128)(2,1)}, u32[]{:S(2)}) %copy-start.11) | copy-done | bytes 327704
  35.6 6.4 %first.1 = (bf16[128,5120]{1,0:T(8,128)(2,1)S(1)}, bf16[128,512]{1,0:T(8,128)(2,1)S(1)}, f32[4,8,5120]{2,1,0:T(8,128)S(1)}, f32[4,8,5120]{2,1,0:T(8,128)S(1)}) custom-call(s32[6]{0:T(128)S(1)} %and_select_fusion.sel, s32[4]{0:T(128)S(1)} %copy-done.14, s32[2]{0:T(128)S(1)} %pad_add_fusion.place, bf16[32,5120]{1,0:T(8,128)(2,1)S(1)} %copy-done.5, ...), custom_call_target="tpu_custom_call" | custom-call | flops 671088640 | bytes 10000000 | tf_op jit(solution)/shard_map/first/pallas_call | solution.py:252
  42.1 2.1 %collective-permute-done.5 = f32[4,8,5120]{2,1,0:T(8,128)S(1)} collective-permute-done((f32[4,8,5120]{2,1,0:T(8,128)S(1)}, f32[4,8,5120]{2,1,0:T(8,128)S(1)}, u32[]{:S(2)}, u32[]{:S(2)}) %collective-permute-start.5) | collective-permute-done | bytes 655392 | tf_op jit(solution)/shard_map/ppermute | solution.py:217
  44.2 1.6 %collective-permute-start.6 = (f32[8,5120]{1,0:T(8,128)S(1)}, f32[8,5120]{1,0:T(8,128)S(1)}, u32[]{:S(2)}, u32[]{:S(2)}) collective-permute-start(f32[8,5120]{1,0:T(8,128)S(1)} %get-tuple-element.29), channel_id=1, source_target_pairs={{0,8},{4,12},{8,0},{12,4},{16,24},{20,28},{24,16},{28,20},{1,9},{5... | collective-permute-start | bytes 491528 | tf_op jit(solution)/shard_map/ppermute | solution.py:217
  45.8 1.5 %collective-permute-start.7 = (f32[8,5120]{1,0:T(8,128)S(1)}, f32[8,5120]{1,0:T(8,128)S(1)}, u32[]{:S(2)}, u32[]{:S(2)}) collective-permute-start(f32[8,5120]{1,0:T(8,128)S(1)} %get-tuple-element.31), channel_id=1, source_target_pairs={{0,16},{4,20},{8,24},{12,28},{16,0},{20,4},{24,8},{28,12},{1,17},{... | collective-permute-start | bytes 491528 | tf_op jit(solution)/shard_map/ppermute | solution.py:217
  47.3 0.5 collective-permute-start.8
  47.8 3.6 %collective-permute-done.6 = f32[8,5120]{1,0:T(8,128)S(1)} collective-permute-done((f32[8,5120]{1,0:T(8,128)S(1)}, f32[8,5120]{1,0:T(8,128)S(1)}, u32[]{:S(2)}, u32[]{:S(2)}) %collective-permute-start.6) | collective-permute-done | bytes 163872 | tf_op jit(solution)/shard_map/ppermute | solution.py:217
  51.3 3.9 %collective-permute-done.7 = f32[8,5120]{1,0:T(8,128)S(1)} collective-permute-done((f32[8,5120]{1,0:T(8,128)S(1)}, f32[8,5120]{1,0:T(8,128)S(1)}, u32[]{:S(2)}, u32[]{:S(2)}) %collective-permute-start.7) | collective-permute-done | bytes 163872 | tf_op jit(solution)/shard_map/ppermute | solution.py:217
  55.3 1.3 %collective-permute-start.10 = (f32[8,5120]{1,0:T(8,128)S(1)}, f32[8,5120]{1,0:T(8,128)S(1)}, u32[]{:S(2)}, u32[]{:S(2)}) collective-permute-start(f32[8,5120]{1,0:T(8,128)S(1)} %fusion.6.refs_0_), channel_id=1, source_target_pairs={{0,8},{4,12},{8,0},{12,4},{16,24},{20,28},{24,16},{28,20},{1,9},{5... | collective-permute-start | bytes 491528 | tf_op jit(solution)/shard_map/ppermute | solution.py:217
  56.6 0.8 collective-permute-start.12
  57.5 1.4 %collective-permute-start.14 = (f32[8,5120]{1,0:T(8,128)S(1)}, f32[8,5120]{1,0:T(8,128)S(1)}, u32[]{:S(2)}, u32[]{:S(2)}) collective-permute-start(f32[8,5120]{1,0:T(8,128)S(1)} %fusion.6.refs_0_), channel_id=1, source_target_pairs={{0,24},{4,28},{8,16},{12,20},{16,8},{20,12},{24,0},{28,4},{1,25},{... | collective-permute-start | bytes 491528 | tf_op jit(solution)/shard_map/ppermute | solution.py:217
  58.9 3.2 %collective-permute-done.10.refs_2_ = f32[8,5120]{1,0:T(8,128)S(1)} collective-permute-done((f32[8,5120]{1,0:T(8,128)S(1)}, f32[8,5120]{1,0:T(8,128)S(1)}, u32[]{:S(2)}, u32[]{:S(2)}) %collective-permute-start.10) | collective-permute-done | bytes 163872 | tf_op jit(solution)/shard_map/ppermute | solution.py:217
  62.1 3.2 %collective-permute-done.12.refs_4_ = f32[8,5120]{1,0:T(8,128)S(1)} collective-permute-done((f32[8,5120]{1,0:T(8,128)S(1)}, f32[8,5120]{1,0:T(8,128)S(1)}, u32[]{:S(2)}, u32[]{:S(2)}) %collective-permute-start.12) | collective-permute-done | bytes 163872 | tf_op jit(solution)/shard_map/ppermute | solution.py:217
  65.3 0.5 collective-permute-start.15
  65.8 1.0 %collective-permute-done.13.refs_5_ = f32[8,5120]{1,0:T(8,128)} collective-permute-done((f32[8,5120]{1,0:T(8,128)S(1)}, f32[8,5120]{1,0:T(8,128)}, u32[]{:S(2)}, u32[]{:S(2)}) %collective-permute-start.13) | collective-permute-done | bytes 163872 | tf_op jit(solution)/shard_map/ppermute | solution.py:217
  67.0 2.7 %second.1 = (f32[64,5120]{1,0:T(8,128)S(1)}, f32[64,64]{1,0:T(8,128)S(1)}, f32[64,512]{1,0:T(8,128)S(1)}) custom-call(s32[4]{0:T(128)S(1)} %copy-done.14, s32[2]{0:T(128)S(1)} %pad_add_fusion.place, f32[8,5120]{1,0:T(8,128)S(1)} %fusion.6.refs_0_, f32[8,5120]{1,0:T(8,128)} %collective-permute-done.9.refs_1_, f32[8,5120]{1,0:T(8,128)S(1)} %collective-permute-done.10.refs_2_, ...), custom_call_target="tpu_custom_call" | custom-call | flops 1000000 | bytes 1000000 | tf_op jit(solution)/shard_map/second/pallas_call | solution.py:284
  69.7 1.0 %copy-done.2 = f32[64,5120]{1,0:T(8,128)} copy-done((f32[64,5120]{1,0:T(8,128)}, f32[64,5120]{1,0:T(8,128)S(1)}, u32[]{:S(2)}) %copy-start.2) | copy-done | bytes 1310744
  70.8 0.6 copy-done.12
  71.4 0.3 collective-permute-start.16
  71.7 1.0 %collective-permute-done.16 = f32[32,512]{1,0:T(8,128)S(1)} collective-permute-done((f32[32,512]{1,0:T(8,128)S(1)}, f32[32,512]{1,0:T(8,128)S(1)}, u32[]{:S(2)}, u32[]{:S(2)}) %collective-permute-start.16) | collective-permute-done | bytes 65568 | tf_op jit(solution)/shard_map/ppermute | solution.py:217
  72.7 0.9 %collective-permute-start.17 = (f32[32,512]{1,0:T(8,128)S(1)}, f32[32,512]{1,0:T(8,128)S(1)}, u32[]{:S(2)}, u32[]{:S(2)}) collective-permute-start(f32[32,512]{1,0:T(8,128)S(1)} %dynamic-slice_add_fusion), channel_id=1, source_target_pairs={{0,8},{4,12},{8,0},{12,4},{16,24},{20,28},{24,16},{28,20},{1,9},{5... | collective-permute-start | bytes 196616 | tf_op jit(solution)/shard_map/ppermute | solution.py:217
  73.6 1.3 %collective-permute-start.18 = (f32[32,512]{1,0:T(8,128)S(1)}, f32[32,512]{1,0:T(8,128)S(1)}, u32[]{:S(2)}, u32[]{:S(2)}) collective-permute-start(f32[32,512]{1,0:T(8,128)S(1)} %dynamic-slice_add_fusion), channel_id=1, source_target_pairs={{0,16},{4,20},{8,24},{12,28},{16,0},{20,4},{24,8},{28,12},{1,17},{... | collective-permute-start | bytes 196616 | tf_op jit(solution)/shard_map/ppermute | solution.py:217
  74.9 1.4 %collective-permute-start.19 = (f32[32,512]{1,0:T(8,128)S(1)}, f32[32,512]{1,0:T(8,128)S(1)}, u32[]{:S(2)}, u32[]{:S(2)}) collective-permute-start(f32[32,512]{1,0:T(8,128)S(1)} %dynamic-slice_add_fusion), channel_id=1, source_target_pairs={{0,24},{4,28},{8,16},{12,20},{16,8},{20,12},{24,0},{28,4},{1,25},{... | collective-permute-start | bytes 196616 | tf_op jit(solution)/shard_map/ppermute | solution.py:217
  76.2 0.8 collective-permute-done.17
  77.0 0.9 collective-permute-done.18
  77.9 2.2 %collective-permute-done.19 = f32[32,512]{1,0:T(8,128)S(1)} collective-permute-done((f32[32,512]{1,0:T(8,128)S(1)}, f32[32,512]{1,0:T(8,128)S(1)}, u32[]{:S(2)}, u32[]{:S(2)}) %collective-permute-start.19) | collective-permute-done | bytes 65568 | tf_op jit(solution)/shard_map/ppermute | solution.py:217
  80.2 0.9 merged.1
  81.1 0.3 copy-done.3
  81.4 8.7 %factor.1 = (f32[64,5120]{1,0:T(8,128)}, f32[64,64]{1,0:T(8,128)S(1)}, f32[64,512]{1,0:T(8,128)S(1)}) custom-call(s32[4]{0:T(128)S(1)} %copy-done.14, f32[64,64]{1,0:T(8,128)S(1)} %copy-done.13, f32[64,5120]{1,0:T(8,128)S(1)} %copy-done.3), custom_call_target="tpu_custom_call" | custom-call | flops 1000000 | bytes 1000000 | tf_op jit(solution)/shard_map/factor/pallas_call | solution.py:289
  90.1 2.8 %last.1 = (f32[64,512]{1,0:T(8,128)}, f32[4,128,512]{2,1,0:T(8,128)}) custom-call(s32[2]{0:T(128)S(1)} %pad_add_fusion.place, f32[32,512]{1,0:T(8,128)S(1)} %add_add_fusion.half_own, f32[32,512]{1,0:T(8,128)S(1)} %collective-permute-done.20.half_other, f32[64,64]{1,0:T(8,128)S(1)} %get-tuple-element.23.linv, f32[64,512]{1,0:T(8,128)S(1)} %get-tuple-element.24.blocks, ...), custom_call_target="tpu_custom_call" | custom-call | flops 1000000 | bytes 1000000 | tf_op jit(solution)/shard_map/last/pallas_call | solution.py:309
  (57 shorter events, 1.4 us)
Async XLA Ops:
  0.6 11.7 %copy-start = (bf16[256,512]{1,0:T(8,128)(2,1)S(1)}, bf16[256,512]{1,0:T(8,128)(2,1)}, u32[]{:S(2)}) copy-start(bf16[256,512]{1,0:T(8,128)(2,1)} %param.13) | copy-start | bytes 786436
  0.6 12.6 %copy-start.4 = (f32[512,64]{0,1:T(8,128)S(1)}, f32[512,64]{0,1:T(8,128)}, u32[]{:S(2)}) copy-start(f32[512,64]{0,1:T(8,128)} %param.15) | copy-start | bytes 393220
  0.7 12.6 %copy-start.1 = (f32[4,128,512]{2,1,0:T(8,128)S(1)}, f32[4,128,512]{2,1,0:T(8,128)}, u32[]{:S(2)}) copy-start(f32[4,128,512]{2,1,0:T(8,128)} %resid.3) | copy-start | bytes 3145732
  0.7 11.0 %collective-permute-start = (bf16[32,5120]{1,0:T(8,128)(2,1)}, bf16[32,5120]{1,0:T(8,128)(2,1)S(1)}, u32[]{:S(2)}, u32[]{:S(2)}) collective-permute-start(bf16[32,5120]{1,0:T(8,128)(2,1)} %refs_0_.1), channel_id=1, source_target_pairs={{0,1},{1,0},{2,3},{3,2},{4,5},{5,4},{6,7},{7,6},{8,9},{9,8},{10,11... | collective-permute-start | bytes 983048 | tf_op jit(solution)/shard_map/ppermute | solution.py:203
  3.8 10.7 %collective-permute-start.1 = (bf16[32,5120]{1,0:T(8,128)(2,1)}, bf16[32,5120]{1,0:T(8,128)(2,1)S(1)}, u32[]{:S(2)}, u32[]{:S(2)}) collective-permute-start(bf16[32,5120]{1,0:T(8,128)(2,1)} %refs_0_.1), channel_id=1, source_target_pairs={{1,2},{2,1},{5,6},{6,5},{9,10},{10,9},{13,14},{14,13},{17,18},{18,... | collective-permute-start | bytes 983048 | tf_op jit(solution)/shard_map/ppermute | solution.py:204
  11.7 13.4 %copy-start.6 = (bf16[32,5120]{1,0:T(8,128)(2,1)}, bf16[32,5120]{1,0:T(8,128)(2,1)S(1)}, u32[]{:S(2)}) copy-start(bf16[32,5120]{1,0:T(8,128)(2,1)S(1)} %collective-permute-done.refs_1_) | copy-start | bytes 983044
  11.7 7.4 %collective-permute-start.3 = (bf16[32,5120]{1,0:T(8,128)(2,1)S(1)}, bf16[32,5120]{1,0:T(8,128)(2,1)S(1)}, u32[]{:S(2)}, u32[]{:S(2)}) collective-permute-start(bf16[32,5120]{1,0:T(8,128)(2,1)S(1)} %collective-permute-done.refs_1_), channel_id=1, source_target_pairs={{1,2},{2,1},{5,6},{6,5},{9,10},{10,9},{13,14},{14,13},{17,18},{18,... | collective-permute-start | bytes 983048 | tf_op jit(solution)/shard_map/ppermute | solution.py:204
  12.4 20.3 %copy-start.5 = (bf16[32,5120]{1,0:T(8,128)(2,1)S(1)}, bf16[32,5120]{1,0:T(8,128)(2,1)}, u32[]{:S(2)}) copy-start(bf16[32,5120]{1,0:T(8,128)(2,1)} %refs_0_.1) | copy-start | bytes 983044
  12.4 20.3 %copy-start.14 = (s32[4]{0:T(128)S(1)}, s32[4]{0:T(128)}, u32[]{:S(2)}) copy-start(s32[4]{0:T(128)} %ids.7) | copy-start | bytes 52
  14.5 13.2 %copy-start.8 = (bf16[32,5120]{1,0:T(8,128)(2,1)}, bf16[32,5120]{1,0:T(8,128)(2,1)S(1)}, u32[]{:S(2)}) copy-start(bf16[32,5120]{1,0:T(8,128)(2,1)S(1)} %collective-permute-done.1.refs_2_) | copy-start | bytes 983044
  14.5 13.2 %collective-permute-start.2 = (bf16[32,5120]{1,0:T(8,128)(2,1)S(1)}, bf16[32,5120]{1,0:T(8,128)(2,1)S(1)}, u32[]{:S(2)}, u32[]{:S(2)}) collective-permute-start(bf16[32,5120]{1,0:T(8,128)(2,1)S(1)} %collective-permute-done.1.refs_2_), channel_id=1, source_target_pairs={{0,1},{1,0},{2,3},{3,2},{4,5},{5,4},{6,7},{7,6},{8,9},{9,8},{10,11... | collective-permute-start | bytes 983048 | tf_op jit(solution)/shard_map/ppermute | solution.py:203
  19.1 13.6 %collective-permute-start.4 = (bf16[32,5120]{1,0:T(8,128)(2,1)S(1)}, bf16[32,5120]{1,0:T(8,128)(2,1)S(1)}, u32[]{:S(2)}, u32[]{:S(2)}) collective-permute-start(bf16[32,5120]{1,0:T(8,128)(2,1)S(1)} %collective-permute-done.3.refs_4_), channel_id=1, source_target_pairs={{0,1},{1,0},{2,3},{3,2},{4,5},{5,4},{6,7},{7,6},{8,9},{9,8},{10,11... | collective-permute-start | bytes 983048 | tf_op jit(solution)/shard_map/ppermute | solution.py:203
  24.2 0.7 copy-start.10
  32.7 1.0 %copy-start.7 = (bf16[32,5120]{1,0:T(8,128)(2,1)S(1)}, bf16[32,5120]{1,0:T(8,128)(2,1)}, u32[]{:S(2)}) copy-start(bf16[32,5120]{1,0:T(8,128)(2,1)} %copy-done.6) | copy-start | bytes 983044
  33.7 1.0 %copy-start.9 = (bf16[32,5120]{1,0:T(8,128)(2,1)S(1)}, bf16[32,5120]{1,0:T(8,128)(2,1)}, u32[]{:S(2)}) copy-start(bf16[32,5120]{1,0:T(8,128)(2,1)} %copy-done.8) | copy-start | bytes 983044
  34.6 1.0 %copy-start.11 = (bf16[32,5120]{1,0:T(8,128)(2,1)S(1)}, bf16[32,5120]{1,0:T(8,128)(2,1)}, u32[]{:S(2)}) copy-start(bf16[32,5120]{1,0:T(8,128)(2,1)} %copy-done.10) | copy-start | bytes 983044
  42.0 2.2 %collective-permute-start.5 = (f32[4,8,5120]{2,1,0:T(8,128)S(1)}, f32[4,8,5120]{2,1,0:T(8,128)S(1)}, u32[]{:S(2)}, u32[]{:S(2)}) collective-permute-start(f32[4,8,5120]{2,1,0:T(8,128)S(1)} %get-tuple-element.16), channel_id=1, source_target_pairs={{0,4},{4,0},{8,12},{12,8},{16,20},{20,16},{24,28},{28,24},{1,5},{5... | collective-permute-start | bytes 1966088 | tf_op jit(solution)/shard_map/ppermute | solution.py:217
  44.2 7.1 %collective-permute-start.6 = (f32[8,5120]{1,0:T(8,128)S(1)}, f32[8,5120]{1,0:T(8,128)S(1)}, u32[]{:S(2)}, u32[]{:S(2)}) collective-permute-start(f32[8,5120]{1,0:T(8,128)S(1)} %get-tuple-element.29), channel_id=1, source_target_pairs={{0,8},{4,12},{8,0},{12,4},{16,24},{20,28},{24,16},{28,20},{1,9},{5... | collective-permute-start | bytes 491528 | tf_op jit(solution)/shard_map/ppermute | solution.py:217
  45.8 9.5 %collective-permute-start.7 = (f32[8,5120]{1,0:T(8,128)S(1)}, f32[8,5120]{1,0:T(8,128)S(1)}, u32[]{:S(2)}, u32[]{:S(2)}) collective-permute-start(f32[8,5120]{1,0:T(8,128)S(1)} %get-tuple-element.31), channel_id=1, source_target_pairs={{0,16},{4,20},{8,24},{12,28},{16,0},{20,4},{24,8},{28,12},{1,17},{... | collective-permute-start | bytes 491528 | tf_op jit(solution)/shard_map/ppermute | solution.py:217
  47.3 8.0 %collective-permute-start.8 = (f32[8,5120]{1,0:T(8,128)S(1)}, f32[8,5120]{1,0:T(8,128)S(1)}, u32[]{:S(2)}, u32[]{:S(2)}) collective-permute-start(f32[8,5120]{1,0:T(8,128)S(1)} %get-tuple-element.30), channel_id=1, source_target_pairs={{0,24},{4,28},{8,16},{12,20},{16,8},{20,12},{24,0},{28,4},{1,25},{... | collective-permute-start | bytes 491528 | tf_op jit(solution)/shard_map/ppermute | solution.py:217
  55.3 6.7 %collective-permute-start.10 = (f32[8,5120]{1,0:T(8,128)S(1)}, f32[8,5120]{1,0:T(8,128)S(1)}, u32[]{:S(2)}, u32[]{:S(2)}) collective-permute-start(f32[8,5120]{1,0:T(8,128)S(1)} %fusion.6.refs_0_), channel_id=1, source_target_pairs={{0,8},{4,12},{8,0},{12,4},{16,24},{20,28},{24,16},{28,20},{1,9},{5... | collective-permute-start | bytes 491528 | tf_op jit(solution)/shard_map/ppermute | solution.py:217
  56.6 8.6 %collective-permute-start.12 = (f32[8,5120]{1,0:T(8,128)S(1)}, f32[8,5120]{1,0:T(8,128)S(1)}, u32[]{:S(2)}, u32[]{:S(2)}) collective-permute-start(f32[8,5120]{1,0:T(8,128)S(1)} %fusion.6.refs_0_), channel_id=1, source_target_pairs={{0,16},{4,20},{8,24},{12,28},{16,0},{20,4},{24,8},{28,12},{1,17},{... | collective-permute-start | bytes 491528 | tf_op jit(solution)/shard_map/ppermute | solution.py:217
  57.5 7.8 %collective-permute-start.14 = (f32[8,5120]{1,0:T(8,128)S(1)}, f32[8,5120]{1,0:T(8,128)S(1)}, u32[]{:S(2)}, u32[]{:S(2)}) collective-permute-start(f32[8,5120]{1,0:T(8,128)S(1)} %fusion.6.refs_0_), channel_id=1, source_target_pairs={{0,24},{4,28},{8,16},{12,20},{16,8},{20,12},{24,0},{28,4},{1,25},{... | collective-permute-start | bytes 491528 | tf_op jit(solution)/shard_map/ppermute | solution.py:217
  58.9 6.9 %collective-permute-start.9 = (f32[8,5120]{1,0:T(8,128)S(1)}, f32[8,5120]{1,0:T(8,128)}, u32[]{:S(2)}, u32[]{:S(2)}) collective-permute-start(f32[8,5120]{1,0:T(8,128)S(1)} %fusion.6.refs_0_), channel_id=1, source_target_pairs={{0,4},{4,0},{8,12},{12,8},{16,20},{20,16},{24,28},{28,24},{1,5},{5... | collective-permute-start | bytes 491528 | tf_op jit(solution)/shard_map/ppermute | solution.py:217
  62.1 3.7 %collective-permute-start.11 = (f32[8,5120]{1,0:T(8,128)S(1)}, f32[8,5120]{1,0:T(8,128)}, u32[]{:S(2)}, u32[]{:S(2)}) collective-permute-start(f32[8,5120]{1,0:T(8,128)S(1)} %collective-permute-done.10.refs_2_), channel_id=1, source_target_pairs={{0,4},{4,0},{8,12},{12,8},{16,20},{20,16},{24,28},{28,24},{1,5},{5... | collective-permute-start | bytes 491528 | tf_op jit(solution)/shard_map/ppermute | solution.py:217
  65.3 1.5 %collective-permute-start.13 = (f32[8,5120]{1,0:T(8,128)S(1)}, f32[8,5120]{1,0:T(8,128)}, u32[]{:S(2)}, u32[]{:S(2)}) collective-permute-start(f32[8,5120]{1,0:T(8,128)S(1)} %collective-permute-done.12.refs_4_), channel_id=1, source_target_pairs={{0,4},{4,0},{8,12},{12,8},{16,20},{20,16},{24,28},{28,24},{1,5},{5... | collective-permute-start | bytes 491528 | tf_op jit(solution)/shard_map/ppermute | solution.py:217
  65.3 1.8 %collective-permute-start.15 = (f32[8,5120]{1,0:T(8,128)S(1)}, f32[8,5120]{1,0:T(8,128)}, u32[]{:S(2)}, u32[]{:S(2)}) collective-permute-start(f32[8,5120]{1,0:T(8,128)S(1)} %collective-permute-done.14.refs_6_), channel_id=1, source_target_pairs={{0,4},{4,0},{8,12},{12,8},{16,20},{20,16},{24,28},{28,24},{1,5},{5... | collective-permute-start | bytes 491528 | tf_op jit(solution)/shard_map/ppermute | solution.py:217
  69.7 1.1 %copy-start.2 = (f32[64,5120]{1,0:T(8,128)}, f32[64,5120]{1,0:T(8,128)S(1)}, u32[]{:S(2)}) copy-start(f32[64,5120]{1,0:T(8,128)S(1)} %get-tuple-element.20.pt) | copy-start | bytes 3932164
  70.8 0.6 copy-start.12
  71.4 1.3 %collective-permute-start.16 = (f32[32,512]{1,0:T(8,128)S(1)}, f32[32,512]{1,0:T(8,128)S(1)}, u32[]{:S(2)}, u32[]{:S(2)}) collective-permute-start(f32[32,512]{1,0:T(8,128)S(1)} %constant_dynamic-slice_fusion), channel_id=1, source_target_pairs={{0,4},{4,0},{8,12},{12,8},{16,20},{20,16},{24,28},{28,24},{1,5},{5... | collective-permute-start | bytes 196616 | tf_op jit(solution)/shard_map/ppermute | solution.py:217
  72.7 4.3 %collective-permute-start.17 = (f32[32,512]{1,0:T(8,128)S(1)}, f32[32,512]{1,0:T(8,128)S(1)}, u32[]{:S(2)}, u32[]{:S(2)}) collective-permute-start(f32[32,512]{1,0:T(8,128)S(1)} %dynamic-slice_add_fusion), channel_id=1, source_target_pairs={{0,8},{4,12},{8,0},{12,4},{16,24},{20,28},{24,16},{28,20},{1,9},{5... | collective-permute-start | bytes 196616 | tf_op jit(solution)/shard_map/ppermute | solution.py:217
  73.6 4.3 %collective-permute-start.18 = (f32[32,512]{1,0:T(8,128)S(1)}, f32[32,512]{1,0:T(8,128)S(1)}, u32[]{:S(2)}, u32[]{:S(2)}) collective-permute-start(f32[32,512]{1,0:T(8,128)S(1)} %dynamic-slice_add_fusion), channel_id=1, source_target_pairs={{0,16},{4,20},{8,24},{12,28},{16,0},{20,4},{24,8},{28,12},{1,17},{... | collective-permute-start | bytes 196616 | tf_op jit(solution)/shard_map/ppermute | solution.py:217
  74.9 5.2 %collective-permute-start.19 = (f32[32,512]{1,0:T(8,128)S(1)}, f32[32,512]{1,0:T(8,128)S(1)}, u32[]{:S(2)}, u32[]{:S(2)}) collective-permute-start(f32[32,512]{1,0:T(8,128)S(1)} %dynamic-slice_add_fusion), channel_id=1, source_target_pairs={{0,24},{4,28},{8,16},{12,20},{16,8},{20,12},{24,0},{28,4},{1,25},{... | collective-permute-start | bytes 196616 | tf_op jit(solution)/shard_map/ppermute | solution.py:217
  80.1 1.3 %copy-start.3 = (f32[64,5120]{1,0:T(8,128)S(1)}, f32[64,5120]{1,0:T(8,128)}, u32[]{:S(2)}) copy-start(f32[64,5120]{1,0:T(8,128)} %copy-done.2) | copy-start | bytes 3932164
  80.1 1.3 %copy-start.13 = (f32[64,64]{1,0:T(8,128)S(1)}, f32[64,64]{1,0:T(8,128)}, u32[]{:S(2)}) copy-start(f32[64,64]{1,0:T(8,128)} %copy-done.12) | copy-start | bytes 49156
  80.1 10.0 %collective-permute-start.20 = (f32[32,512]{1,0:T(8,128)S(1)}, f32[32,512]{1,0:T(8,128)S(1)}, u32[]{:S(2)}, u32[]{:S(2)}) collective-permute-start(f32[32,512]{1,0:T(8,128)S(1)} %add_add_fusion.half_own), channel_id=1, source_target_pairs={{0,4},{4,0},{8,12},{12,8},{16,20},{20,16},{24,28},{28,24},{1,5},{5... | collective-permute-start | bytes 196616 | tf_op jit(solution)/shard_map/ppermute | solution.py:217

commit v2 on v0

v2 whole, which is shorter than its diff:
```python
import functools
import jax
import jax.numpy as jnp
from jax import lax
from jax.experimental import pallas as pl
from jax.experimental.pallas import tpu as pltpu
from jax.sharding import PartitionSpec as P

F32 = jnp.float32
BF16 = jnp.bfloat16
HIGHEST = lax.Precision.HIGHEST
VMEM_LIMIT = 16 * 1024 * 1024


def packed_tables(lengths, assign, rewards, order, slot_count, capacity):
    groups, sequences = lengths.shape
    lengths, assign, rewards = lengths[order], assign[order], rewards[order]
    offsets = jnp.cumsum(lengths, axis=1) - lengths
    advantage = rewards - jnp.mean(rewards, axis=1, keepdims=True)
    seq_weight = advantage / lengths.astype(rewards.dtype)
    positions = jnp.arange(slot_count)
    seq_index = jnp.arange(sequences)
    inside = (offsets[:, None, :] <= positions[None, :, None]).astype(jnp.int32)
    owner = jnp.sum(inside, axis=2) - 1
    picked = owner[:, :, None] == seq_index[None, None, :]
    seq_start = jnp.sum(jnp.where(picked, offsets[:, None, :], 0), axis=2)
    learner = jnp.sum(jnp.where(picked, assign[:, None, :], 0), axis=2)
    row_weight = jnp.sum(jnp.where(picked, seq_weight[:, None, :], 0.0), axis=2)
    source = order[:, None]
    slot_table = learner * (groups * capacity) + source * capacity + positions[None, :] - seq_start
    return (slot_table, row_weight)


def dot(a, b, dims, precision=None):
    return lax.dot_general(a, b, (dims, ((), ())), precision=precision, preferred_element_type=F32)


NN, NT, TN = ((1,), (0,)), ((1,), (1,)), ((0,), (0,))
SMEM = pl.BlockSpec(memory_space=pltpu.SMEM)
VMEM = pl.BlockSpec(memory_space=pltpu.VMEM)


def split(a, parts):
    out = []
    for _ in range(parts):
        high = a.astype(BF16)
        out.append(high)
        a = a - high.astype(F32)
    return jnp.concatenate(out, axis=0)


def fold(a, parts):
    rows = a.shape[0] // parts
    total = a[:rows]
    for i in range(1, parts):
        total = total + a[i * rows:(i + 1) * rows]
    return total


def lanes(index, width):
    return pl.ds(pl.multiple_of(index * width, width), width)


def call(kernel, n_smem, n_vmem, outs, scratch=(), flops=1000000, name=None):
    return pl.pallas_call(
        kernel,
        out_shape=outs,
        in_specs=[SMEM] * n_smem + [VMEM] * n_vmem,
        out_specs=jax.tree.map(lambda _: VMEM, outs),
        scratch_shapes=list(scratch),
        compiler_params=pltpu.CompilerParams(vmem_limit_bytes=VMEM_LIMIT),
        cost_estimate=pl.CostEstimate(flops=flops, bytes_accessed=1000000, transcendentals=0),
        name=name,
    )


def resid_kernel(q0t, resid, q3, ft, r2):
    q3[...] = split(q0t[...], 3)
    kept, width = resid.shape[:2]
    for k in range(kept):
        ft[:, k * width:(k + 1) * width] = dot(q0t[...], resid[k], NT, HIGHEST)
        high = resid[k].astype(BF16)
        r2[0, k * width:(k + 1) * width, :] = high
        r2[1, k * width:(k + 1) * width, :] = (resid[k] - high.astype(F32)).astype(BF16)


def pick(pieces, flag, choices, at, out):
    rows = out.shape[0] // len(choices)
    for j, (first, second) in enumerate(choices):
        here = slice(j * rows, (j + 1) * rows)
        if second is None:
            out[here, :] = pieces[first][...]
        else:
            @pl.when(flag[0] == 1)
            def _():
                out[here, :] = pieces[first][...]

            @pl.when(flag[0] == 0)
            def _():
                out[here, :] = pieces[second][...]


def row_grad(x, w, weighted, q3, g):
    tangent = jnp.tanh(jnp.dot(x[...], w[...], preferred_element_type=F32))
    grad = (weighted[...] * (1.0 - tangent * tangent)).astype(BF16)
    g[...] = grad
    return split(fold(dot(q3[...], grad, NT), 3), 3)


def stage_kernel(n_x, choices, flag, *refs):
    pieces, (w, weighted, q3, x, g, pt) = refs[:n_x], refs[n_x:]
    pick(pieces, flag, choices, 0, x)
    yt = row_grad(x, w, weighted, q3, g)
    wide = 1024
    for i in range(pt.shape[1] // wide):
        at = slice(i * wide, (i + 1) * wide)
        pt[:, at] = fold(dot(yt, x[:, at], NN), 3)


def tail_kernel(n_x, choices, flag, ids, place, *refs):
    pieces, refs = refs[:n_x], refs[n_x:]
    w, weighted, q3, ft, pt0, x, g = refs[:7]
    outs, pt = refs[7:-1], refs[-1]
    pick(pieces, flag, choices, 0, x)
    yt = row_grad(x, w, weighted, q3, g)
    wide = 1024
    for i in range(pt.shape[1] // wide):
        at = slice(i * wide, (i + 1) * wide)
        pt[:, at] = pt0[:, at] + fold(dot(yt, x[:, at], NN), 3)
    block = ft.shape[1] // ids.shape[0]
    for k in range(ids.shape[0]):
        pt[:, lanes(ids[k], block)] += ft[:, k * block:(k + 1) * block]
    if len(outs) == 1:
        outs[0][...] = pt[...]
        return
    for j, out in enumerate(outs):
        chip, core = place[0] ^ (j // 2), place[1] ^ (j % 2)
        out[...] = pt[lanes(2 * chip + core, out.shape[0]), :]


def merged_kernel(ids, xa, xb, ga, gb, resid, out):
    block = resid.shape[1]
    for k in range(ids.shape[0]):
        at = lanes(ids[k], block)
        out[k] = dot(xa[:, at], ga[...], TN) + dot(xb[:, at], gb[...], TN) + resid[k]


def second_kernel(n_p, ids, place, *refs):
    parts, refs = refs[:n_p], refs[n_p:]
    xa, xb, ga, gb, r2 = refs[:5]
    ps, gram = refs[5:7]
    uts, pt, pk = refs[7:-2], refs[-2], refs[-1]
    if n_p == 1:
        pt[...] = parts[0][...]
    else:
        rows = parts[0].shape[0]
        for j in range(n_p):
            chip, core = place[0] ^ (j // 2), place[1] ^ (j % 2)
            pt[lanes(2 * chip + core, rows), :] = parts[j][...]
    rank = pt.shape[0]
    two = split(pt[...], 2)
    ps[...] = two
    block = pk.shape[1] // ids.shape[0]
    for k in range(ids.shape[0]):
        pk[:, k * block:(k + 1) * block] = ps[:, lanes(ids[k], block)]
    both = fold(dot(two, two, NT), 2)
    gram[...] = both[:, :rank] + both[:, rank:]
    za = split(fold(dot(two, xa[...], NT), 2), 3)
    zb = split(fold(dot(two, xb[...], NT), 2), 3)
    total = fold(dot(za, ga[...], NN) + dot(zb, gb[...], NN), 3)
    total = total + fold(dot(pk[...], r2[0], NN), 2) + dot(pk[:rank, :], r2[1], NN)
    if len(uts) == 1:
        uts[0][...] = total
    else:
        half = rank // 2
        low_is_mine = place[1] == 0
        uts[0][...] = jnp.where(low_is_mine, total[:half], total[half:])
        uts[1][...] = jnp.where(low_is_mine, total[half:], total[:half])


def factor_kernel(ids, gram, ps, pft, linv, blocks):
    rank = gram.shape[0]
    sub = 8
    eye = (lax.broadcasted_iota(jnp.int32, (rank, rank), 0) == lax.broadcasted_iota(jnp.int32, (rank, rank), 1)).astype(F32)
    aug = jnp.concatenate([gram[...], eye], axis=1)
    rows = [aug[b * sub:(b + 1) * sub] for b in range(rank // sub)]
    place = lax.broadcasted_iota(jnp.int32, (sub, 1), 0)
    for k in range(rank):
        b, r = k // sub, k % sub
        row = rows[b][r:r + 1, :]
        pivot = row[:, k:k + 1]
        linv[k:k + 1, :] = (row / jnp.sqrt(pivot))[:, rank:]
        ratio = row / pivot
        if r < sub - 1:
            rows[b] = rows[b] - jnp.where(place > r, rows[b][:, k:k + 1], 0.0) * ratio
        for c in range(b + 1, rank // sub):
            rows[c] = rows[c] - rows[c][:, k:k + 1] * ratio
    inverse = linv[...]
    high = inverse.astype(BF16)
    low = (inverse - high.astype(F32)).astype(BF16)
    lhs = jnp.concatenate([jnp.concatenate([high, high], axis=1), jnp.concatenate([low, jnp.zeros_like(low)], axis=1)], axis=0)
    wide = 1024
    for i in range(pft.shape[1] // wide):
        at = slice(i * wide, (i + 1) * wide)
        pft[:, at] = fold(dot(lhs, ps[:, at], NN), 2)
    block = blocks.shape[1] // ids.shape[0]
    for k in range(ids.shape[0]):
        piece = pft[:, lanes(ids[k], block)]
        two = split(piece, 2)
        at = slice(k * block, (k + 1) * block)
        blocks[:2 * rank, at] = two
        blocks[2 * rank:, at] = two[:rank]


def last_kernel(n_u, scale, place, *refs):
    halves, (linv, blocks, merged, qt, out, ut) = refs[:n_u], refs[n_u:]
    if n_u == 1:
        ut[...] = halves[0][...]
    else:
        rows = halves[0].shape[0]
        ut[lanes(place[1], rows), :] = halves[0][...]
        ut[lanes(1 - place[1], rows), :] = halves[1][...]
    q = dot(linv[...], ut[...], NN, HIGHEST) * scale
    qt[...] = q
    two = split(q, 2)
    rank = q.shape[0]
    rhs = jnp.concatenate([two[:rank], two[:rank], two[rank:]], axis=0)
    block = merged.shape[1]
    for k in range(merged.shape[0]):
        out[k] = merged[k] - dot(blocks[:, k * block:(k + 1) * block], rhs, TN)


def gather_rows(x, groups, at):
    if groups != 4:
        rows = x.shape[0]
        whole = lax.all_gather(x, "mp", axis=0, tiled=True)
        pieces = [whole[j * rows:(j + 1) * rows] for j in range(groups)]
        return pieces, [(j, None) for j in range(groups)], jnp.zeros((1,), jnp.int32), jnp.arange(groups)
    outer = [(0, 1), (1, 0), (2, 3), (3, 2)]
    inner = [(1, 2), (2, 1)]
    a0 = lax.ppermute(x, "mp", outer)
    b0 = lax.ppermute(x, "mp", inner)
    b1 = lax.ppermute(a0, "mp", inner)
    a1 = lax.ppermute(b0, "mp", outer)
    a2 = lax.ppermute(b1, "mp", outer)
    at_end = (at == 0) | (at == 3)
    low = at < 2
    order = jnp.stack([at, at ^ 1, jnp.where(low, 2, 1), jnp.where(low, 3, 0)])
    choices = [(0, None), (1, None), (2, 3), (4, 5)]
    return [x, a0, a1, b0, a2, b1], choices, at_end.astype(jnp.int32).reshape(1), order


def swap(a, bit, size):
    return lax.ppermute(a, "dp", [(i, i ^ bit) for i in range(size)])


def together(*values):
    return lax.optimization_barrier(values)


def shards(gen_rows, lengths, assign, rewards, upstream, weight, q_init, resid, block_ids):
    groups, replicas = lax.axis_size("mp"), lax.axis_size("dp")
    slot_count, depth = gen_rows.shape
    columns, rank = q_init.shape
    capacity = upstream.shape[0] // (groups * groups)
    kept, block = resid.shape[:2]
    at_dp = lax.axis_index("dp")
    place = jnp.stack([at_dp // 2, at_dp % 2]).astype(jnp.int32)
    direct = replicas == 8
    shape = jax.ShapeDtypeStruct

    pieces, choices, flag, order = gather_rows(gen_rows, groups, lax.axis_index("mp"))
    slot_table, row_weight = packed_tables(lengths, assign, rewards, order, slot_count, capacity)
    upstream_rows = jnp.take(upstream, slot_table.reshape(-1), axis=0)
    weighted = row_weight.reshape(-1)[:, None] * upstream_rows.astype(F32)
    q3, ft, r2 = call(
        resid_kernel, 0, 2,
        [shape((3 * rank, columns), BF16), shape((rank, kept * block), F32), shape((2, kept * block, columns), BF16)],
        name="resid_term",
    )(q_init.T, resid)

    early_rows = (groups - 1) * slot_count
    n_early = choices[-2][1] + 1 if choices[-2][1] is not None else choices[-2][0] + 1
    early, late = pieces[:n_early], pieces[n_early:]
    xa, ga, pt0 = call(
        functools.partial(stage_kernel, len(early), choices[:-1]), 1, len(early) + 3,
        [shape((early_rows, depth), BF16), shape((early_rows, columns), BF16), shape((rank, depth), F32)],
        flops=2 * early_rows * depth * columns, name="stage",
    )(flag, *early, weight, weighted[:early_rows], q3)

    late_choices = [(0, 1 if len(late) == 2 else None)]
    if direct:
        outs = [shape((rank // replicas, depth), F32)] * replicas
    else:
        outs = [shape((rank, depth), F32)]
    xb, gb, *parts = call(
        functools.partial(tail_kernel, len(late), late_choices), 3, len(late) + 5,
        [shape((slot_count, depth), BF16), shape((slot_count, columns), BF16)] + outs,
        [pltpu.VMEM((rank, depth), F32)],
        flops=2 * slot_count * depth * columns, name="tail",
    )(flag, block_ids, place, *late, weight, weighted[early_rows:], q3, ft, pt0)

    merged = call(merged_kernel, 1, 5, shape((kept, block, columns), F32), name="merged")(block_ids, xa, xb, ga, gb, resid)

    if direct:
        chips = replicas // 2
        sums = [parts[2 * k] + swap(parts[2 * k + 1], 1, replicas) for k in range(chips)]
        got = [swap(sums[k], 2 * k, replicas) for k in range(1, chips)]
        *got, merged = together(*got, merged)
        own = sums[0] + got[0] + got[1] + got[2]
        same = [own] + [swap(own, 2 * k, replicas) for k in range(1, chips)]
        p_parts = []
        for s in same:
            p_parts += [s, swap(s, 1, replicas)]
        u_shapes = [shape((rank // 2, columns), F32)] * 2
    else:
        p_parts = [lax.psum(parts[0], "dp")]
        u_shapes = [shape((rank, columns), F32)]

    n_p = len(p_parts)
    ps, gram, *us = call(
        functools.partial(second_kernel, n_p), 2, n_p + 5,
        [shape((2 * rank, depth), BF16), shape((rank, rank), F32)] + u_shapes,
        [pltpu.VMEM((rank, depth), F32), pltpu.VMEM((2 * rank, kept * block), BF16)], name="second",
    )(block_ids, place, *p_parts, xa, xb, ga, gb, r2)

    pft, linv, blocks = call(
        factor_kernel, 1, 2,
        [shape((rank, depth), F32), shape((rank, rank), F32), shape((3 * rank, kept * block), BF16)], name="factor",
    )(block_ids, gram, ps)

    if direct:
        chip_sum = us[0] + swap(us[1], 1, replicas)
        got = [swap(chip_sum, 2 * k, replicas) for k in range(1, chips)]
        *got, linv = together(*got, linv)
        total = chip_sum + got[0] + got[1] + got[2]
        u_parts = [total, swap(total, 1, replicas)]
    else:
        u_parts = [lax.psum(us[0], "dp")]
    n_u = len(u_parts)
    qt, new_resid = call(
        functools.partial(last_kernel, n_u, 1.0 / replicas), 1, n_u + 3,
        [shape((rank, columns), F32), shape((kept, block, columns), F32)],
        [pltpu.VMEM((rank, columns), F32)], name="last",
    )(place, *u_parts, linv, blocks, merged)
    return pft.T, qt.T, new_resid


def solution(mesh):
    placed = (
        P(("dp", "mp"), None),
        P("dp", None),
        P("dp", None),
        P("dp", None),
        P("dp", "mp"),
        P(None, "mp"),
        P("mp", None),
        P("dp", None, "mp"),
        P("dp"),
    )
    return jax.shard_map(
        shards,
        mesh=mesh,
        in_specs=placed,
        out_specs=(P(None, "mp"), P("mp", None), P("dp", None, "mp")),
        check_vma=False,
    )
```

time: 228 us -> 77.2 us (0.34)
  waiting for transfers between devices: 135 us -> 18.9 us
  matrix products: 43.3 us -> 0 us
  starting transfers between devices: 0.3 us -> 28 us
  Pallas kernels: 0 us -> 19.1 us
  other arithmetic: 18.4 us -> 1.23 us
  between operations: 16.7 us -> 0.91 us
  local copies, waits for them, and re-layouts: 13.7 us -> 8.81 us
    psum x2 -> x0, waiting for transfers between devices: 109 us -> none  [the longest x1 56.6 us: shards(): p_sum = lax.psum(p_local, 'dp')]
    dot_general x8 -> x0, matrix products: 40.8 us -> none  [the longest x1 13.9 us: shards(): jnp.einsum('dc,dr->cr', gradient, p_factor, precision=HIGHEST_PRECISION)]
    ppermute x0 -> x24, starting transfers between devices: none -> 28 us  [the longest x19 12.3 us: swap(): return lax.ppermute(a, 'dp', [(i, i ^ bit) for i in range(size)])]
    all_gather x1 -> x0, waiting for transfers between devices: 25.8 us -> none  [shards(): lax.all_gather(gen_rows, 'mp', axis=0, tiled=True)]
    pallas_call x0 -> x7, Pallas kernels: none -> 19.1 us  [the longest x1 7.56 us: shards(): call(factor_kernel, 1, 2, [shape((rank, depth), F32), shape((rank, rank),...]
    ppermute x0 -> x24, waiting for transfers between devices: none -> 18.9 us  [the longest x19 16.6 us: swap(): return lax.ppermute(a, 'dp', [(i, i ^ bit) for i in range(size)])]
    another operation x6 -> x1, other arithmetic: 12.1 us -> 0.07 us  [shards(): place = jnp.stack([at_dp // 2, at_dp % 2]).astype(jnp.int32)]
    unnamed x16 -> x14, local copies, waits for them, and re-layouts: 9.83 us -> 3.94 us
  transfers between devices with their start and end apart: 3 -> 24, of which waited for: 3 -> 11; matrix products, arithmetic and copies ran while one was open for 4% -> 8% of each run, Pallas kernels for 0% -> 15%
where the time goes in v2:
time: 77.2 us; the launch traced here: 77 us
  starting transfers between devices  28 us (36%)
  Pallas kernels  19.1 us (25%)
  waiting for transfers between devices  18.9 us (24%)
  local copies, waits for them, and re-layouts  8.81 us (11%)
  other arithmetic  1.23 us (2%)
  between operations  0.91 us (1%)
    ppermute x19, waiting for transfers between devices, swap(): return lax.ppermute(a, 'dp', [(i, i ^ bit) for i in range(size)])  16.6 us
    ppermute x19, starting transfers between devices, swap(): return lax.ppermute(a, 'dp', [(i, i ^ bit) for i in range(size)])  12.3 us
    pallas_call x1, Pallas kernels, shards(): call(factor_kernel, 1, 2, [shape((rank, depth), F32), shape((rank, rank),...  7.56 us
    ppermute x1, starting transfers between devices, gather_rows(): a2 = lax.ppermute(b1, 'mp', outer)  6.67 us
    ppermute x1, starting transfers between devices, gather_rows(): a1 = lax.ppermute(b0, 'mp', outer)  4.61 us
    unnamed x14, local copies, waits for them, and re-layouts  3.94 us
    gather x3, local copies, waits for them, and re-layouts, packed_tables(): lengths, assign, rewards = (lengths[order], assign[order], rewards[order])  3.74 us
    ppermute x1, starting transfers between devices, gather_rows(): a0 = lax.ppermute(x, 'mp', outer)  3.09 us
  transfers between devices with their start and end apart: 24, of which 11 were waited for; matrix products, arithmetic and copies ran while one was open for 8% of the time, Pallas kernels for 15%

profile of v2, /device:TPU:0, one launch (start us, length us, event | category | flops | bytes accessed | tf_op | source)
XLA Modules:
  0.0 77.0 jit_solution(12537686926956362067)
XLA Ops:
  0.7 3.1 %collective-permute-start = (bf16[32,5120]{1,0:T(8,128)(2,1)}, bf16[32,5120]{1,0:T(8,128)(2,1)S(1)}, u32[]{:S(2)}, u32[]{:S(2)}) collective-permute-start(bf16[32,5120]{1,0:T(8,128)(2,1)} %refs_0_.1), channel_id=1, source_target_pairs={{0,1},{1,0},{2,3},{3,2},{4,5},{5,4},{6,7},{7,6},{8,9},{9,8},{10,11... | collective-permute-start | bytes 983048 | tf_op jit(solution)/shard_map/ppermute | solution.py:241
  3.7 0.7 collective-permute-start.3
  4.5 1.2 %gather_fusion = s32[4,4]{1,0:T(4,128)S(1)} fusion(s32[4,4]{1,0:T(4,128)} %param.10, s32[1024]{0:T(1024)S(1)} %pad_clamp_fusion.1), kind=kCustom, calls=%fused_computation | custom fusion | bytes 144 | tf_op jit(solution)/shard_map/gather | solution.py:17
  5.8 1.2 %gather_fusion.2 = s32[4,4]{1,0:T(4,128)S(1)} fusion(s32[4,4]{1,0:T(4,128)} %param.11, s32[1024]{0:T(1024)S(1)} %pad_clamp_fusion.1), kind=kCustom, calls=%fused_computation.2 | custom fusion | bytes 144 | tf_op jit(solution)/shard_map/gather | solution.py:17
  7.0 0.2 reduce_window_sum.11
  7.2 0.1 convert_reduce_fusion
  7.3 0.1 select_reduce_fusion.1
  7.6 0.1 sub.53
  7.7 1.2 %gather_fusion.1 = f32[4,4]{1,0:T(4,128)S(1)} fusion(f32[4,4]{1,0:T(4,128)} %param.12, s32[1024]{0:T(1024)S(1)} %pad_clamp_fusion.1), kind=kCustom, calls=%fused_computation.1 | custom fusion | bytes 144 | tf_op jit(solution)/shard_map/gather | solution.py:17
  9.0 0.1 reduce_sum.46
  9.2 0.1 select_reduce_fusion.2
  9.4 2.3 %collective-permute-done.refs_1_ = bf16[32,5120]{1,0:T(8,128)(2,1)S(1)} collective-permute-done((bf16[32,5120]{1,0:T(8,128)(2,1)}, bf16[32,5120]{1,0:T(8,128)(2,1)S(1)}, u32[]{:S(2)}, u32[]{:S(2)}) %collective-permute-start) | collective-permute-done | bytes 327712 | tf_op jit(solution)/shard_map/ppermute | solution.py:241
  11.7 0.7 collective-permute-start.1
  12.4 0.8 %gather_fusion.3 = bf16[128,512]{1,0:T(8,128)(2,1)S(1)} fusion(bf16[256,512]{1,0:T(8,128)(2,1)S(1)} %copy-done, s32[1024]{0:T(1024)S(1)} %pad_clamp_fusion), kind=kCustom, calls=%fused_computation.3 | custom fusion | bytes 262656 | tf_op jit(solution)/shard_map/jit(_take)/gather | solution.py:274
  13.3 4.6 %collective-permute-start.4 = (bf16[32,5120]{1,0:T(8,128)(2,1)S(1)}, bf16[32,5120]{1,0:T(8,128)(2,1)S(1)}, u32[]{:S(2)}, u32[]{:S(2)}) collective-permute-start(bf16[32,5120]{1,0:T(8,128)(2,1)S(1)} %collective-permute-done.3.refs_3_), channel_id=1, source_target_pairs={{0,1},{1,0},{2,3},{3,2},{4,5},{5,4},{6,7},{7,6},{8,9},{9,8},{10,11... | collective-permute-start | bytes 983048 | tf_op jit(solution)/shard_map/ppermute | solution.py:244
  17.9 6.7 %collective-permute-start.2 = (bf16[32,5120]{1,0:T(8,128)(2,1)S(1)}, bf16[32,5120]{1,0:T(8,128)(2,1)S(1)}, u32[]{:S(2)}, u32[]{:S(2)}) collective-permute-start(bf16[32,5120]{1,0:T(8,128)(2,1)S(1)} %collective-permute-done.1.refs_1_), channel_id=1, source_target_pairs={{0,1},{1,0},{2,3},{3,2},{4,5},{5,4},{6,7},{7,6},{8,9},{9,8},{10,11... | collective-permute-start | bytes 983048 | tf_op jit(solution)/shard_map/ppermute | solution.py:245
  24.5 0.1 convert_multiply_fusion
  24.7 0.9 %copy-done.5 = f32[512,64]{0,1:T(8,128)S(1)} copy-done((f32[512,64]{0,1:T(8,128)S(1)}, f32[512,64]{0,1:T(8,128)}, u32[]{:S(2)}) %copy-start.5) | copy-done | bytes 131096
  25.6 1.3 %resid_term.1 = (bf16[192,512]{1,0:T(8,128)(2,1)S(1)}, f32[64,512]{1,0:T(8,128)S(1)}, bf16[2,512,512]{2,1,0:T(8,128)(2,1)S(1)}) custom-call(f32[64,512]{1,0:T(8,128)S(1)} %bitcast.18, f32[4,128,512]{2,1,0:T(8,128)S(1)} %copy-done.3), custom_call_target="tpu_custom_call" | custom-call | flops 1000000 | bytes 1000000 | tf_op jit(solution)/shard_map/resid_term/pallas_call | solution.py:276
  27.0 2.5 %copy-done.1 = bf16[5120,512]{1,0:T(8,128)(2,1)S(1)} copy-done((bf16[5120,512]{1,0:T(8,128)(2,1)S(1)}, bf16[5120,512]{1,0:T(8,128)(2,1)}, u32[]{:S(2)}) %copy-start.1) | copy-done | bytes 5242904
  29.5 1.9 %stage.1 = (bf16[96,5120]{1,0:T(8,128)(2,1)S(1)}, bf16[96,512]{1,0:T(8,128)(2,1)S(1)}, f32[64,5120]{1,0:T(8,128)S(1)}) custom-call(s32[1]{0:T(128)} %bitcast.2.flag, bf16[32,5120]{1,0:T(8,128)(2,1)S(1)} %copy-done.4, bf16[32,5120]{1,0:T(8,128)(2,1)S(1)} %collective-permute-done.refs_1_, bf16[32,5120]{1,0:T(8,128)(2,1)S(1)} %collective-permute-done.4.refs_2_, ...), custom_call_target="tpu_custom_call" | custom-call | flops 503316480 | bytes 1000000 | tf_op jit(solution)/shard_map/stage/pallas_call | solution.py:285
  31.5 0.5 copy-done.2
  32.0 2.6 %tail.1 = (bf16[32,5120]{1,0:T(8,128)(2,1)S(1)}, bf16[32,512]{1,0:T(8,128)(2,1)S(1)}, f32[8,5120]{1,0:T(8,128)S(1)}, f32[8,5120]{1,0:T(8,128)S(1)}, f32[8,5120]{...) custom-call(s32[1]{0:T(128)} %bitcast.2.flag, ...), custom_call_target="tpu_custom_call" | custom-call | flops 167772160 | bytes 1000000 | tf_op jit(solution)/shard_map/tail/pallas_call | solution.py:296
  34.7 0.5 collective-permute-start.8
  35.2 0.8 %collective-permute-done.6 = f32[8,5120]{1,0:T(8,128)S(1)} collective-permute-done((f32[8,5120]{1,0:T(8,128)S(1)}, f32[8,5120]{1,0:T(8,128)S(1)}, u32[]{:S(2)}, u32[]{:S(2)}) %collective-permute-start.6) | collective-permute-done | bytes 163872 | tf_op jit(solution)/shard_map/ppermute | solution.py:254
  36.1 1.6 %collective-permute-start.7 = (f32[8,5120]{1,0:T(8,128)S(1)}, f32[8,5120]{1,0:T(8,128)S(1)}, u32[]{:S(2)}, u32[]{:S(2)}) collective-permute-start(f32[8,5120]{1,0:T(8,128)S(1)} %add.127), channel_id=1, source_target_pairs={{0,8},{4,12},{8,0},{12,4},{16,24},{20,28},{24,16},{28,20},{1,9},{5... | collective-permute-start | bytes 491528 | tf_op jit(solution)/shard_map/ppermute | solution.py:254
  37.7 1.6 %collective-permute-start.9 = (f32[8,5120]{1,0:T(8,128)S(1)}, f32[8,5120]{1,0:T(8,128)S(1)}, u32[]{:S(2)}, u32[]{:S(2)}) collective-permute-start(f32[8,5120]{1,0:T(8,128)S(1)} %add.128), channel_id=1, source_target_pairs={{0,16},{4,20},{8,24},{12,28},{16,0},{20,4},{24,8},{28,12},{1,17},{... | collective-permute-start | bytes 491528 | tf_op jit(solution)/shard_map/ppermute | solution.py:254
  39.3 0.5 collective-permute-start.11
  39.8 1.0 %merged.1.refs_4_ = f32[4,128,512]{2,1,0:T(8,128)S(1)} custom-call(s32[4]{0:T(128)S(1)} %copy-done.6, bf16[96,5120]{1,0:T(8,128)(2,1)S(1)} %get-tuple-element.47.xa.refs_8_, bf16[32,5120]{1,0:T(8,128)(2,1)S(1)} %get-tuple-element.48.xb.refs_9_, bf16[96,512]{1,0:T(8,128)(2,1)S(1)} %get-tuple-element.49.ga.refs_10_, ...), custom_call_target="tpu_custom_call" | custom-call | flops 1000000 | bytes 1000000 | tf_op jit(solution)/shard_map/merged/pallas_call | solution.py:303
  40.8 2.4 %collective-permute-done.7 = f32[8,5120]{1,0:T(8,128)S(1)} collective-permute-done((f32[8,5120]{1,0:T(8,128)S(1)}, f32[8,5120]{1,0:T(8,128)S(1)}, u32[]{:S(2)}, u32[]{:S(2)}) %collective-permute-start.7) | collective-permute-done | bytes 163872 | tf_op jit(solution)/shard_map/ppermute | solution.py:254
  43.2 4.0 %collective-permute-done.9 = f32[8,5120]{1,0:T(8,128)S(1)} collective-permute-done((f32[8,5120]{1,0:T(8,128)S(1)}, f32[8,5120]{1,0:T(8,128)S(1)}, u32[]{:S(2)}, u32[]{:S(2)}) %collective-permute-start.9) | collective-permute-done | bytes 163872 | tf_op jit(solution)/shard_map/ppermute | solution.py:254
  47.3 1.6 %collective-permute-start.17 = (f32[8,5120]{1,0:T(8,128)S(1)}, f32[8,5120]{1,0:T(8,128)S(1)}, u32[]{:S(2)}, u32[]{:S(2)}) collective-permute-start(f32[8,5120]{1,0:T(8,128)S(1)} %add_add_fusion.refs_0_), channel_id=1, source_target_pairs={{0,24},{4,28},{8,16},{12,20},{16,8},{20,12},{24,0},{28,4},{1,25},{... | collective-permute-start | bytes 491528 | tf_op jit(solution)/shard_map/ppermute | solution.py:254
  48.8 1.1 %collective-permute-start.15 = (f32[8,5120]{1,0:T(8,128)S(1)}, f32[8,5120]{1,0:T(8,128)S(1)}, u32[]{:S(2)}, u32[]{:S(2)}) collective-permute-start(f32[8,5120]{1,0:T(8,128)S(1)} %add_add_fusion.refs_0_), channel_id=1, source_target_pairs={{0,16},{4,20},{8,24},{12,28},{16,0},{20,4},{24,8},{28,12},{1,17},{... | collective-permute-start | bytes 491528 | tf_op jit(solution)/shard_map/ppermute | solution.py:254
  49.9 0.9 %collective-permute-start.13 = (f32[8,5120]{1,0:T(8,128)S(1)}, f32[8,5120]{1,0:T(8,128)S(1)}, u32[]{:S(2)}, u32[]{:S(2)}) collective-permute-start(f32[8,5120]{1,0:T(8,128)S(1)} %add_add_fusion.refs_0_), channel_id=1, source_target_pairs={{0,8},{4,12},{8,0},{12,4},{16,24},{20,28},{24,16},{28,20},{1,9},{5... | collective-permute-start | bytes 491528 | tf_op jit(solution)/shard_map/ppermute | solution.py:254
  50.8 4.3 %collective-permute-done.17.refs_6_ = f32[8,5120]{1,0:T(8,128)S(1)} collective-permute-done((f32[8,5120]{1,0:T(8,128)S(1)}, f32[8,5120]{1,0:T(8,128)S(1)}, u32[]{:S(2)}, u32[]{:S(2)}) %collective-permute-start.17) | collective-permute-done | bytes 163872 | tf_op jit(solution)/shard_map/ppermute | solution.py:254
  55.1 1.7 %collective-permute-done.15.refs_4_ = f32[8,5120]{1,0:T(8,128)S(1)} collective-permute-done((f32[8,5120]{1,0:T(8,128)S(1)}, f32[8,5120]{1,0:T(8,128)S(1)}, u32[]{:S(2)}, u32[]{:S(2)}) %collective-permute-start.15) | collective-permute-done | bytes 163872 | tf_op jit(solution)/shard_map/ppermute | solution.py:254
  56.9 0.5 collective-permute-start.14
  57.4 0.9 %collective-permute-done.16.refs_5_ = f32[8,5120]{1,0:T(8,128)S(1)} collective-permute-done((f32[8,5120]{1,0:T(8,128)S(1)}, f32[8,5120]{1,0:T(8,128)S(1)}, u32[]{:S(2)}, u32[]{:S(2)}) %collective-permute-start.16) | collective-permute-done | bytes 163872 | tf_op jit(solution)/shard_map/ppermute | solution.py:254
  58.2 0.2 collective-permute-done.14.refs_3_
  58.5 2.6 %second.1 = (bf16[128,5120]{1,0:T(8,128)(2,1)S(1)}, f32[64,64]{1,0:T(8,128)S(1)}, f32[32,512]{1,0:T(8,128)S(1)}, f32[32,512]{1,0:T(8,128)S(1)}) custom-call(s32[4]{0:T(128)S(1)} %copy-done.6, s32[2]{0:T(128)S(1)} %pad_add_fusion.place, f32[8,5120]{1,0:T(8,128)S(1)} %add_add_fusion.refs_0_, f32[8,5120]{1,0:T(8,128)S(1)} %collective-permute-done.12.refs_1_, ...), custom_call_target="tpu_custom_call" | custom-call | flops 1000000 | bytes 1000000 | tf_op jit(solution)/shard_map/second/pallas_call | solution.py:321
  61.1 0.3 collective-permute-start.19
  61.4 1.0 %collective-permute-done.19 = f32[32,512]{1,0:T(8,128)S(1)} collective-permute-done((f32[32,512]{1,0:T(8,128)S(1)}, f32[32,512]{1,0:T(8,128)S(1)}, u32[]{:S(2)}, u32[]{:S(2)}) %collective-permute-start.19) | collective-permute-done | bytes 65568 | tf_op jit(solution)/shard_map/ppermute | solution.py:254
  62.4 1.5 %collective-permute-start.22 = (f32[32,512]{1,0:T(8,128)S(1)}, f32[32,512]{1,0:T(8,128)S(1)}, u32[]{:S(2)}, u32[]{:S(2)}) collective-permute-start(f32[32,512]{1,0:T(8,128)S(1)} %add.133), channel_id=1, source_target_pairs={{0,24},{4,28},{8,16},{12,20},{16,8},{20,12},{24,0},{28,4},{1,25},{... | collective-permute-start | bytes 196616 | tf_op jit(solution)/shard_map/ppermute | solution.py:254
  63.9 1.5 %collective-permute-start.21 = (f32[32,512]{1,0:T(8,128)S(1)}, f32[32,512]{1,0:T(8,128)S(1)}, u32[]{:S(2)}, u32[]{:S(2)}) collective-permute-start(f32[32,512]{1,0:T(8,128)S(1)} %add.133), channel_id=1, source_target_pairs={{0,16},{4,20},{8,24},{12,28},{16,0},{20,4},{24,8},{28,12},{1,17},{... | collective-permute-start | bytes 196616 | tf_op jit(solution)/shard_map/ppermute | solution.py:254
  65.4 0.6 collective-permute-start.20
  66.0 7.6 %factor.1 = (f32[64,5120]{1,0:T(8,128)}, f32[64,64]{1,0:T(8,128)S(1)}, bf16[192,512]{1,0:T(8,128)(2,1)S(1)}) custom-call(s32[4]{0:T(128)S(1)} %copy-done.6, f32[64,64]{1,0:T(8,128)S(1)} %get-tuple-element.55.gram, bf16[128,5120]{1,0:T(8,128)(2,1)S(1)} %get-tuple-element.56.ps), custom_call_target="tpu_custom_call" | custom-call | flops 1000000 | bytes 1000000 | tf_op jit(solution)/shard_map/factor/pallas_call | solution.py:327
  73.7 1.2 %collective-permute-done.23.refs_1_ = f32[32,512]{1,0:T(8,128)S(1)} collective-permute-done((f32[32,512]{1,0:T(8,128)S(1)}, f32[32,512]{1,0:T(8,128)S(1)}, u32[]{:S(2)}, u32[]{:S(2)}) %collective-permute-start.23) | collective-permute-done | bytes 65568 | tf_op jit(solution)/shard_map/ppermute | solution.py:254
  74.9 2.1 %last.1 = (f32[64,512]{1,0:T(8,128)}, f32[4,128,512]{2,1,0:T(8,128)}) custom-call(s32[2]{0:T(128)S(1)} %pad_add_fusion.place, f32[32,512]{1,0:T(8,128)S(1)} %add_add_fusion.1.refs_0_, f32[32,512]{1,0:T(8,128)S(1)} %collective-permute-done.23.refs_1_, f32[64,64]{1,0:T(8,128)S(1)} %get-tuple-element.64.refs_2_, ...), custom_call_target="tpu_custom_call" | custom-call | flops 1000000 | bytes 1000000 | tf_op jit(solution)/shard_map/last/pallas_call | solution.py:341
  (54 shorter events, 1.1 us)
Async XLA Ops:
  0.6 11.7 %copy-start = (bf16[256,512]{1,0:T(8,128)(2,1)S(1)}, bf16[256,512]{1,0:T(8,128)(2,1)}, u32[]{:S(2)}) copy-start(bf16[256,512]{1,0:T(8,128)(2,1)} %param.13) | copy-start | bytes 786436
  0.6 24.1 %copy-start.3 = (f32[4,128,512]{2,1,0:T(8,128)S(1)}, f32[4,128,512]{2,1,0:T(8,128)}, u32[]{:S(2)}) copy-start(f32[4,128,512]{2,1,0:T(8,128)} %resid.3) | copy-start | bytes 3145732
  0.7 11.0 %collective-permute-start = (bf16[32,5120]{1,0:T(8,128)(2,1)}, bf16[32,5120]{1,0:T(8,128)(2,1)S(1)}, u32[]{:S(2)}, u32[]{:S(2)}) collective-permute-start(bf16[32,5120]{1,0:T(8,128)(2,1)} %refs_0_.1), channel_id=1, source_target_pairs={{0,1},{1,0},{2,3},{3,2},{4,5},{5,4},{6,7},{7,6},{8,9},{9,8},{10,11... | collective-permute-start | bytes 983048 | tf_op jit(solution)/shard_map/ppermute | solution.py:241
  3.7 9.5 %collective-permute-start.3 = (bf16[32,5120]{1,0:T(8,128)(2,1)}, bf16[32,5120]{1,0:T(8,128)(2,1)S(1)}, u32[]{:S(2)}, u32[]{:S(2)}) collective-permute-start(bf16[32,5120]{1,0:T(8,128)(2,1)} %refs_0_.1), channel_id=1, source_target_pairs={{1,2},{2,1},{5,6},{6,5},{9,10},{10,9},{13,14},{14,13},{17,18},{18,... | collective-permute-start | bytes 983048 | tf_op jit(solution)/shard_map/ppermute | solution.py:242
  11.7 6.2 %collective-permute-start.1 = (bf16[32,5120]{1,0:T(8,128)(2,1)S(1)}, bf16[32,5120]{1,0:T(8,128)(2,1)S(1)}, u32[]{:S(2)}, u32[]{:S(2)}) collective-permute-start(bf16[32,5120]{1,0:T(8,128)(2,1)S(1)} %collective-permute-done.refs_1_), channel_id=1, source_target_pairs={{1,2},{2,1},{5,6},{6,5},{9,10},{10,9},{13,14},{14,13},{17,18},{18,... | collective-permute-start | bytes 983048 | tf_op jit(solution)/shard_map/ppermute | solution.py:243
  13.2 13.8 %copy-start.4 = (bf16[32,5120]{1,0:T(8,128)(2,1)S(1)}, bf16[32,5120]{1,0:T(8,128)(2,1)}, u32[]{:S(2)}) copy-start(bf16[32,5120]{1,0:T(8,128)(2,1)} %refs_0_.1) | copy-start | bytes 983044
  13.3 13.7 %collective-permute-start.4 = (bf16[32,5120]{1,0:T(8,128)(2,1)S(1)}, bf16[32,5120]{1,0:T(8,128)(2,1)S(1)}, u32[]{:S(2)}, u32[]{:S(2)}) collective-permute-start(bf16[32,5120]{1,0:T(8,128)(2,1)S(1)} %collective-permute-done.3.refs_3_), channel_id=1, source_target_pairs={{0,1},{1,0},{2,3},{3,2},{4,5},{5,4},{6,7},{7,6},{8,9},{9,8},{10,11... | collective-permute-start | bytes 983048 | tf_op jit(solution)/shard_map/ppermute | solution.py:244
  17.9 13.6 %collective-permute-start.2 = (bf16[32,5120]{1,0:T(8,128)(2,1)S(1)}, bf16[32,5120]{1,0:T(8,128)(2,1)S(1)}, u32[]{:S(2)}, u32[]{:S(2)}) collective-permute-start(bf16[32,5120]{1,0:T(8,128)(2,1)S(1)} %collective-permute-done.1.refs_1_), channel_id=1, source_target_pairs={{0,1},{1,0},{2,3},{3,2},{4,5},{5,4},{6,7},{7,6},{8,9},{9,8},{10,11... | collective-permute-start | bytes 983048 | tf_op jit(solution)/shard_map/ppermute | solution.py:245
  24.7 0.9 %copy-start.5 = (f32[512,64]{0,1:T(8,128)S(1)}, f32[512,64]{0,1:T(8,128)}, u32[]{:S(2)}) copy-start(f32[512,64]{0,1:T(8,128)} %param.15) | copy-start | bytes 393220
  27.0 2.5 %copy-start.1 = (bf16[5120,512]{1,0:T(8,128)(2,1)S(1)}, bf16[5120,512]{1,0:T(8,128)(2,1)}, u32[]{:S(2)}) copy-start(bf16[5120,512]{1,0:T(8,128)(2,1)} %refs_2_.1) | copy-start | bytes 15728644
  29.5 2.5 %copy-start.2 = (bf16[5120,512]{1,0:T(8,128)(2,1)S(1)}, bf16[5120,512]{1,0:T(8,128)(2,1)}, u32[]{:S(2)}) copy-start(bf16[5120,512]{1,0:T(8,128)(2,1)} %refs_2_.1) | copy-start | bytes 15728644
  29.5 2.5 %copy-start.6 = (s32[4]{0:T(128)S(1)}, s32[4]{0:T(128)}, u32[]{:S(2)}) copy-start(s32[4]{0:T(128)} %ids.7) | copy-start | bytes 52
  34.6 1.5 %collective-permute-start.6 = (f32[8,5120]{1,0:T(8,128)S(1)}, f32[8,5120]{1,0:T(8,128)S(1)}, u32[]{:S(2)}, u32[]{:S(2)}) collective-permute-start(f32[8,5120]{1,0:T(8,128)S(1)} %get-tuple-element.42), channel_id=1, source_target_pairs={{0,4},{4,0},{8,12},{12,8},{16,20},{20,16},{24,28},{28,24},{1,5},{5... | collective-permute-start | bytes 491528 | tf_op jit(solution)/shard_map/ppermute | solution.py:254
  34.7 3.0 %collective-permute-start.8 = (f32[8,5120]{1,0:T(8,128)S(1)}, f32[8,5120]{1,0:T(8,128)S(1)}, u32[]{:S(2)}, u32[]{:S(2)}) collective-permute-start(f32[8,5120]{1,0:T(8,128)S(1)} %get-tuple-element.44), channel_id=1, source_target_pairs={{0,4},{4,0},{8,12},{12,8},{16,20},{20,16},{24,28},{28,24},{1,5},{5... | collective-permute-start | bytes 491528 | tf_op jit(solution)/shard_map/ppermute | solution.py:254
  35.2 4.1 %collective-permute-start.10 = (f32[8,5120]{1,0:T(8,128)S(1)}, f32[8,5120]{1,0:T(8,128)S(1)}, u32[]{:S(2)}, u32[]{:S(2)}) collective-permute-start(f32[8,5120]{1,0:T(8,128)S(1)} %get-tuple-element.46), channel_id=1, source_target_pairs={{0,4},{4,0},{8,12},{12,8},{16,20},{20,16},{24,28},{28,24},{1,5},{5... | collective-permute-start | bytes 491528 | tf_op jit(solution)/shard_map/ppermute | solution.py:254
  36.1 7.1 %collective-permute-start.7 = (f32[8,5120]{1,0:T(8,128)S(1)}, f32[8,5120]{1,0:T(8,128)S(1)}, u32[]{:S(2)}, u32[]{:S(2)}) collective-permute-start(f32[8,5120]{1,0:T(8,128)S(1)} %add.127), channel_id=1, source_target_pairs={{0,8},{4,12},{8,0},{12,4},{16,24},{20,28},{24,16},{28,20},{1,9},{5... | collective-permute-start | bytes 491528 | tf_op jit(solution)/shard_map/ppermute | solution.py:254
  37.7 9.5 %collective-permute-start.9 = (f32[8,5120]{1,0:T(8,128)S(1)}, f32[8,5120]{1,0:T(8,128)S(1)}, u32[]{:S(2)}, u32[]{:S(2)}) collective-permute-start(f32[8,5120]{1,0:T(8,128)S(1)} %add.128), channel_id=1, source_target_pairs={{0,16},{4,20},{8,24},{12,28},{16,0},{20,4},{24,8},{28,12},{1,17},{... | collective-permute-start | bytes 491528 | tf_op jit(solution)/shard_map/ppermute | solution.py:254
  39.3 7.9 %collective-permute-start.11 = (f32[8,5120]{1,0:T(8,128)S(1)}, f32[8,5120]{1,0:T(8,128)S(1)}, u32[]{:S(2)}, u32[]{:S(2)}) collective-permute-start(f32[8,5120]{1,0:T(8,128)S(1)} %add.129), channel_id=1, source_target_pairs={{0,24},{4,28},{8,16},{12,20},{16,8},{20,12},{24,0},{28,4},{1,25},{... | collective-permute-start | bytes 491528 | tf_op jit(solution)/shard_map/ppermute | solution.py:254
  39.8 7.4 %collective-permute-start.5 = (f32[8,5120]{1,0:T(8,128)S(1)}, f32[8,5120]{1,0:T(8,128)S(1)}, u32[]{:S(2)}, u32[]{:S(2)}) collective-permute-start(f32[8,5120]{1,0:T(8,128)S(1)} %get-tuple-element.40), channel_id=1, source_target_pairs={{0,4},{4,0},{8,12},{12,8},{16,20},{20,16},{24,28},{28,24},{1,5},{5... | collective-permute-start | bytes 491528 | tf_op jit(solution)/shard_map/ppermute | solution.py:254
  47.3 7.9 %collective-permute-start.17 = (f32[8,5120]{1,0:T(8,128)S(1)}, f32[8,5120]{1,0:T(8,128)S(1)}, u32[]{:S(2)}, u32[]{:S(2)}) collective-permute-start(f32[8,5120]{1,0:T(8,128)S(1)} %add_add_fusion.refs_0_), channel_id=1, source_target_pairs={{0,24},{4,28},{8,16},{12,20},{16,8},{20,12},{24,0},{28,4},{1,25},{... | collective-permute-start | bytes 491528 | tf_op jit(solution)/shard_map/ppermute | solution.py:254
  48.8 8.0 %collective-permute-start.15 = (f32[8,5120]{1,0:T(8,128)S(1)}, f32[8,5120]{1,0:T(8,128)S(1)}, u32[]{:S(2)}, u32[]{:S(2)}) collective-permute-start(f32[8,5120]{1,0:T(8,128)S(1)} %add_add_fusion.refs_0_), channel_id=1, source_target_pairs={{0,16},{4,20},{8,24},{12,28},{16,0},{20,4},{24,8},{28,12},{1,17},{... | collective-permute-start | bytes 491528 | tf_op jit(solution)/shard_map/ppermute | solution.py:254
  49.9 7.0 %collective-permute-start.13 = (f32[8,5120]{1,0:T(8,128)S(1)}, f32[8,5120]{1,0:T(8,128)S(1)}, u32[]{:S(2)}, u32[]{:S(2)}) collective-permute-start(f32[8,5120]{1,0:T(8,128)S(1)} %add_add_fusion.refs_0_), channel_id=1, source_target_pairs={{0,8},{4,12},{8,0},{12,4},{16,24},{20,28},{24,16},{28,20},{1,9},{5... | collective-permute-start | bytes 491528 | tf_op jit(solution)/shard_map/ppermute | solution.py:254
  50.8 6.5 %collective-permute-start.12 = (f32[8,5120]{1,0:T(8,128)S(1)}, f32[8,5120]{1,0:T(8,128)S(1)}, u32[]{:S(2)}, u32[]{:S(2)}) collective-permute-start(f32[8,5120]{1,0:T(8,128)S(1)} %add_add_fusion.refs_0_), channel_id=1, source_target_pairs={{0,4},{4,0},{8,12},{12,8},{16,20},{20,16},{24,28},{28,24},{1,5},{5... | collective-permute-start | bytes 491528 | tf_op jit(solution)/shard_map/ppermute | solution.py:254
  55.1 2.2 %collective-permute-start.18 = (f32[8,5120]{1,0:T(8,128)S(1)}, f32[8,5120]{1,0:T(8,128)S(1)}, u32[]{:S(2)}, u32[]{:S(2)}) collective-permute-start(f32[8,5120]{1,0:T(8,128)S(1)} %collective-permute-done.17.refs_6_), channel_id=1, source_target_pairs={{0,4},{4,0},{8,12},{12,8},{16,20},{20,16},{24,28},{28,24},{1,5},{5... | collective-permute-start | bytes 491528 | tf_op jit(solution)/shard_map/ppermute | solution.py:254
  56.8 1.4 %collective-permute-start.16 = (f32[8,5120]{1,0:T(8,128)S(1)}, f32[8,5120]{1,0:T(8,128)S(1)}, u32[]{:S(2)}, u32[]{:S(2)}) collective-permute-start(f32[8,5120]{1,0:T(8,128)S(1)} %collective-permute-done.15.refs_4_), channel_id=1, source_target_pairs={{0,4},{4,0},{8,12},{12,8},{16,20},{20,16},{24,28},{28,24},{1,5},{5... | collective-permute-start | bytes 491528 | tf_op jit(solution)/shard_map/ppermute | solution.py:254
  56.9 1.6 %collective-permute-start.14 = (f32[8,5120]{1,0:T(8,128)S(1)}, f32[8,5120]{1,0:T(8,128)S(1)}, u32[]{:S(2)}, u32[]{:S(2)}) collective-permute-start(f32[8,5120]{1,0:T(8,128)S(1)} %collective-permute-done.13.refs_2_), channel_id=1, source_target_pairs={{0,4},{4,0},{8,12},{12,8},{16,20},{20,16},{24,28},{28,24},{1,5},{5... | collective-permute-start | bytes 491528 | tf_op jit(solution)/shard_map/ppermute | solution.py:254
  61.1 1.3 %collective-permute-start.19 = (f32[32,512]{1,0:T(8,128)S(1)}, f32[32,512]{1,0:T(8,128)S(1)}, u32[]{:S(2)}, u32[]{:S(2)}) collective-permute-start(f32[32,512]{1,0:T(8,128)S(1)} %get-tuple-element.59), channel_id=1, source_target_pairs={{0,4},{4,0},{8,12},{12,8},{16,20},{20,16},{24,28},{28,24},{1,5},{5... | collective-permute-start | bytes 196616 | tf_op jit(solution)/shard_map/ppermute | solution.py:254
  62.4 11.1 %collective-permute-start.22 = (f32[32,512]{1,0:T(8,128)S(1)}, f32[32,512]{1,0:T(8,128)S(1)}, u32[]{:S(2)}, u32[]{:S(2)}) collective-permute-start(f32[32,512]{1,0:T(8,128)S(1)} %add.133), channel_id=1, source_target_pairs={{0,24},{4,28},{8,16},{12,20},{16,8},{20,12},{24,0},{28,4},{1,25},{... | collective-permute-start | bytes 196616 | tf_op jit(solution)/shard_map/ppermute | solution.py:254
  63.9 9.6 %collective-permute-start.21 = (f32[32,512]{1,0:T(8,128)S(1)}, f32[32,512]{1,0:T(8,128)S(1)}, u32[]{:S(2)}, u32[]{:S(2)}) collective-permute-start(f32[32,512]{1,0:T(8,128)S(1)} %add.133), channel_id=1, source_target_pairs={{0,16},{4,20},{8,24},{12,28},{16,0},{20,4},{24,8},{28,12},{1,17},{... | collective-permute-start | bytes 196616 | tf_op jit(solution)/shard_map/ppermute | solution.py:254
  65.4 8.1 %collective-permute-start.20 = (f32[32,512]{1,0:T(8,128)S(1)}, f32[32,512]{1,0:T(8,128)S(1)}, u32[]{:S(2)}, u32[]{:S(2)}) collective-permute-start(f32[32,512]{1,0:T(8,128)S(1)} %add.133), channel_id=1, source_target_pairs={{0,8},{4,12},{8,0},{12,4},{16,24},{20,28},{24,16},{28,20},{1,9},{5... | collective-permute-start | bytes 196616 | tf_op jit(solution)/shard_map/ppermute | solution.py:254
  73.6 1.3 %collective-permute-start.23 = (f32[32,512]{1,0:T(8,128)S(1)}, f32[32,512]{1,0:T(8,128)S(1)}, u32[]{:S(2)}, u32[]{:S(2)}) collective-permute-start(f32[32,512]{1,0:T(8,128)S(1)} %add_add_fusion.1.refs_0_), channel_id=1, source_target_pairs={{0,4},{4,0},{8,12},{12,8},{16,20},{20,16},{24,28},{28,24},{1,5},{5... | collective-permute-start | bytes 196616 | tf_op jit(solution)/shard_map/ppermute | solution.py:254

commit v3 on v2

--- a/solution.py
+++ b/solution.py
@@ -61,9 +61,10 @@
     return pl.ds(pl.multiple_of(index * width, width), width)
 
 
-def call(kernel, n_smem, n_vmem, outs, scratch=(), flops=1000000, name=None):
+def call(kernel, n_smem, n_vmem, outs, scratch=(), flops=1000000, name=None, aliases=None):
     return pl.pallas_call(
         kernel,
+        input_output_aliases=aliases or {},
         out_shape=outs,
         in_specs=[SMEM] * n_smem + [VMEM] * n_vmem,
         out_specs=jax.tree.map(lambda _: VMEM, outs),
@@ -84,7 +85,7 @@
         r2[1, k * width:(k + 1) * width, :] = (resid[k] - high.astype(F32)).astype(BF16)
 
 
-def pick(pieces, flag, choices, at, out):
+def pick(pieces, flag, choices, out):
     rows = out.shape[0] // len(choices)
     for j, (first, second) in enumerate(choices):
         here = slice(j * rows, (j + 1) * rows)
@@ -108,8 +109,9 @@
 
 
 def stage_kernel(n_x, choices, flag, *refs):
-    pieces, (w, weighted, q3, x, g, pt) = refs[:n_x], refs[n_x:]
-    pick(pieces, flag, choices, 0, x)
+    pieces, (w, weighted, q3, bx, g, pt) = refs[:n_x], refs[n_x:]
+    x = bx.at[2 * pt.shape[0]:2 * pt.shape[0] + g.shape[0], :]
+    pick(pieces, flag, choices, x)
     yt = row_grad(x, w, weighted, q3, g)
     wide = 1024
     for i in range(pt.shape[1] // wide):
@@ -119,9 +121,10 @@
 
 def tail_kernel(n_x, choices, flag, ids, place, *refs):
     pieces, refs = refs[:n_x], refs[n_x:]
-    w, weighted, q3, ft, pt0, x, g = refs[:7]
-    outs, pt = refs[7:-1], refs[-1]
-    pick(pieces, flag, choices, 0, x)
+    w, weighted, q3, ft, pt0, _, bx, g = refs[:8]
+    outs, pt = refs[8:-1], refs[-1]
+    x = bx.at[bx.shape[0] - g.shape[0]:, :]
+    pick(pieces, flag, choices, x)
     yt = row_grad(x, w, weighted, q3, g)
     wide = 1024
     for i in range(pt.shape[1] // wide):
@@ -138,36 +141,41 @@
         out[...] = pt[lanes(2 * chip + core, out.shape[0]), :]
 
 
-def merged_kernel(ids, xa, xb, ga, gb, resid, out):
+def merged_kernel(ids, bx, ga, gb, resid, out):
     block = resid.shape[1]
+    late = gb.shape[0]
+    early = ga.shape[0]
+    end = bx.shape[0]
     for k in range(ids.shape[0]):
         at = lanes(ids[k], block)
-        out[k] = dot(xa[:, at], ga[...], TN) + dot(xb[:, at], gb[...], TN) + resid[k]
+        out[k] = dot(bx[end - early - late:end - late, at], ga[...], TN) + dot(bx[end - late:, at], gb[...], TN) + resid[k]
 
 
 def second_kernel(n_p, ids, place, *refs):
     parts, refs = refs[:n_p], refs[n_p:]
-    xa, xb, ga, gb, r2 = refs[:5]
-    ps, gram = refs[5:7]
-    uts, pt, pk = refs[7:-2], refs[-2], refs[-1]
+    ga, gb, r2, _, bx, gram = refs[:6]
+    uts, pk = refs[6:-1], refs[-1]
+    rank = pk.shape[0] // 2
     if n_p == 1:
-        pt[...] = parts[0][...]
+        bx[:2 * rank, :] = split(parts[0][...], 2)
     else:
         rows = parts[0].shape[0]
-        for j in range(n_p):
-            chip, core = place[0] ^ (j // 2), place[1] ^ (j % 2)
-            pt[lanes(2 * chip + core, rows), :] = parts[j][...]
-    rank = pt.shape[0]
-    two = split(pt[...], 2)
-    ps[...] = two
+        for j in range(0, n_p, 2):
+            chip = place[0] ^ (j // 2)
+            swapped = place[1] == 1
+            first, second = parts[j][...], parts[j + 1][...]
+            pair = jnp.concatenate([jnp.where(swapped, second, first), jnp.where(swapped, first, second)], axis=0)
+            high = pair.astype(BF16)
+            bx[lanes(chip, 2 * rows), :] = high
+            bx[pl.ds(pl.multiple_of(rank + chip * 2 * rows, 2 * rows), 2 * rows), :] = (pair - high.astype(F32)).astype(BF16)
     block = pk.shape[1] // ids.shape[0]
     for k in range(ids.shape[0]):
-        pk[:, k * block:(k + 1) * block] = ps[:, lanes(ids[k], block)]
-    both = fold(dot(two, two, NT), 2)
-    gram[...] = both[:, :rank] + both[:, rank:]
-    za = split(fold(dot(two, xa[...], NT), 2), 3)
-    zb = split(fold(dot(two, xb[...], NT), 2), 3)
-    total = fold(dot(za, ga[...], NN) + dot(zb, gb[...], NN), 3)
+        pk[:, k * block:(k + 1) * block] = bx[:2 * rank, lanes(ids[k], block)]
+    both = fold(dot(bx[:2 * rank, :], bx[...], NT), 2)
+    gram[...] = both[:, :rank] + both[:, rank:2 * rank]
+    early = ga.shape[0]
+    zt = split(both[:, 2 * rank:], 3)
+    total = fold(dot(zt[:, :early], ga[...], NN) + dot(zt[:, early:], gb[...], NN), 3)
     total = total + fold(dot(pk[...], r2[0], NN), 2) + dot(pk[:rank, :], r2[1], NN)
     if len(uts) == 1:
         uts[0][...] = total
@@ -178,38 +186,60 @@
         uts[1][...] = jnp.where(low_is_mine, total[half:], total[:half])
 
 
-def factor_kernel(ids, gram, ps, pft, linv, blocks):
+def inverse_factor(gram):
+    rank, sub = gram.shape[0], 8
+    blocks = rank // sub
+    eye = (lax.broadcasted_iota(jnp.int32, (rank, rank), 0) == lax.broadcasted_iota(jnp.int32, (rank, rank), 1)).astype(F32)
+    whole = jnp.concatenate([gram, eye], axis=1)
+    rows = [whole[b * sub:(b + 1) * sub] for b in range(blocks)]
+    place = lax.broadcasted_iota(jnp.int32, (sub, 2 * rank), 0)
+
+    def column(a, k):
+        return jnp.take_along_axis(a, jnp.full(a.shape, k, jnp.int32), axis=1)
+
+    out = []
+    for b in range(blocks):
+        panel = rows[b]
+        entry = [column(panel, b * sub + j) for j in range(sub)]
+        pivots = jnp.zeros_like(panel)
+        scale = []
+        for i in range(sub):
+            scale.append(1.0 / entry[i][i:i + 1, :])
+            pivots = jnp.where(place == i, entry[i], pivots)
+            ratio = jnp.where(place > i, entry[i], 0.0) * scale[i]
+            panel = panel - ratio * panel[i:i + 1, :]
+            for j in range(i + 1, sub):
+                entry[j] = entry[j] - ratio * entry[j][i:i + 1, :]
+        out.append((panel / jnp.sqrt(pivots))[:, rank:])
+        solved = [panel[i:i + 1, :] * scale[i] for i in range(sub)]
+        for i in range(sub - 1, -1, -1):
+            for j in range(i + 1, sub):
+                solved[i] = solved[i] - (entry[j][i:i + 1, :] * scale[i]) * solved[j]
+        for c in range(b + 1, blocks):
+            update = column(rows[c], b * sub) * solved[0]
+            for j in range(1, sub):
+                update = update + column(rows[c], b * sub + j) * solved[j]
+            rows[c] = rows[c] - update
+    return jnp.concatenate(out, axis=0)
+
+
+def factor_kernel(ids, gram, bx, pft, linv, blocks):
     rank = gram.shape[0]
-    sub = 8
-    eye = (lax.broadcasted_iota(jnp.int32, (rank, rank), 0) == lax.broadcasted_iota(jnp.int32, (rank, rank), 1)).astype(F32)
-    aug = jnp.concatenate([gram[...], eye], axis=1)
-    rows = [aug[b * sub:(b + 1) * sub] for b in range(rank // sub)]
-    place = lax.broadcasted_iota(jnp.int32, (sub, 1), 0)
-    for k in range(rank):
-        b, r = k // sub, k % sub
-        row = rows[b][r:r + 1, :]
-        pivot = row[:, k:k + 1]
-        linv[k:k + 1, :] = (row / jnp.sqrt(pivot))[:, rank:]
-        ratio = row / pivot
-        if r < sub - 1:
-            rows[b] = rows[b] - jnp.where(place > r, rows[b][:, k:k + 1], 0.0) * ratio
-        for c in range(b + 1, rank // sub):
-            rows[c] = rows[c] - rows[c][:, k:k + 1] * ratio
-    inverse = linv[...]
+    inverse = inverse_factor(gram[...])
+    linv[...] = inverse
     high = inverse.astype(BF16)
     low = (inverse - high.astype(F32)).astype(BF16)
     lhs = jnp.concatenate([jnp.concatenate([high, high], axis=1), jnp.concatenate([low, jnp.zeros_like(low)], axis=1)], axis=0)
     wide = 1024
     for i in range(pft.shape[1] // wide):
         at = slice(i * wide, (i + 1) * wide)
-        pft[:, at] = fold(dot(lhs, ps[:, at], NN), 2)
-    block = blocks.shape[1] // ids.shape[0]
+        pft[:, at] = fold(dot(lhs, bx[:2 * rank, at], NN), 2)
+    block = blocks.shape[0] // ids.shape[0]
     for k in range(ids.shape[0]):
-        piece = pft[:, lanes(ids[k], block)]
-        two = split(piece, 2)
-        at = slice(k * block, (k + 1) * block)
-        blocks[:2 * rank, at] = two
-        blocks[2 * rank:, at] = two[:rank]
+        piece = jnp.transpose(pft[:, lanes(ids[k], block)])
+        high = piece.astype(BF16)
+        low = (piece - high.astype(F32)).astype(BF16)
+        blocks[k * block:(k + 1) * block, :] = jnp.concatenate([high, low, high], axis=1)
 
 
 def last_kernel(n_u, scale, place, *refs):
@@ -227,7 +257,7 @@
     rhs = jnp.concatenate([two[:rank], two[:rank], two[rank:]], axis=0)
     block = merged.shape[1]
     for k in range(merged.shape[0]):
-        out[k] = merged[k] - dot(blocks[:, k * block:(k + 1) * block], rhs, TN)
+        out[k] = merged[k] - dot(blocks[k * block:(k + 1) * block, :], rhs, NN)
 
 
 def gather_rows(x, groups, at):
@@ -282,9 +312,10 @@
     early_rows = (groups - 1) * slot_count
     n_early = choices[-2][1] + 1 if choices[-2][1] is not None else choices[-2][0] + 1
     early, late = pieces[:n_early], pieces[n_early:]
-    xa, ga, pt0 = call(
+    wide_rows = 2 * rank + groups * slot_count
+    bx, ga, pt0 = call(
         functools.partial(stage_kernel, len(early), choices[:-1]), 1, len(early) + 3,
-        [shape((early_rows, depth), BF16), shape((early_rows, columns), BF16), shape((rank, depth), F32)],
+        [shape((wide_rows, depth), BF16), shape((early_rows, columns), BF16), shape((rank, depth), F32)],
         flops=2 * early_rows * depth * columns, name="stage",
     )(flag, *early, weight, weighted[:early_rows], q3)
 
@@ -293,14 +324,14 @@
         outs = [shape((rank // replicas, depth), F32)] * replicas
     else:
         outs = [shape((rank, depth), F32)]
-    xb, gb, *parts = call(
-        functools.partial(tail_kernel, len(late), late_choices), 3, len(late) + 5,
-        [shape((slot_count, depth), BF16), shape((slot_count, columns), BF16)] + outs,
+    bx, gb, *parts = call(
+        functools.partial(tail_kernel, len(late), late_choices), 3, len(late) + 6,
+        [shape((wide_rows, depth), BF16), shape((slot_count, columns), BF16)] + outs,
         [pltpu.VMEM((rank, depth), F32)],
-        flops=2 * slot_count * depth * columns, name="tail",
-    )(flag, block_ids, place, *late, weight, weighted[early_rows:], q3, ft, pt0)
-
-    merged = call(merged_kernel, 1, 5, shape((kept, block, columns), F32), name="merged")(block_ids, xa, xb, ga, gb, resid)
+        flops=2 * slot_count * depth * columns, name="tail", aliases={len(late) + 8: 0},
+    )(flag, block_ids, place, *late, weight, weighted[early_rows:], q3, ft, pt0, bx)
+
+    merged = call(merged_kernel, 1, 4, shape((kept, block, columns), F32), name="merged")(block_ids, bx, ga, gb, resid)
 
     if direct:
         chips = replicas // 2
@@ -318,16 +349,16 @@
         u_shapes = [shape((rank, columns), F32)]
 
     n_p = len(p_parts)
-    ps, gram, *us = call(
-        functools.partial(second_kernel, n_p), 2, n_p + 5,
-        [shape((2 * rank, depth), BF16), shape((rank, rank), F32)] + u_shapes,
-        [pltpu.VMEM((rank, depth), F32), pltpu.VMEM((2 * rank, kept * block), BF16)], name="second",
-    )(block_ids, place, *p_parts, xa, xb, ga, gb, r2)
+    bx, gram, *us = call(
+        functools.partial(second_kernel, n_p), 2, n_p + 4,
+        [shape((wide_rows, depth), BF16), shape((rank, rank), F32)] + u_shapes,
+        [pltpu.VMEM((2 * rank, kept * block), BF16)], name="second", aliases={n_p + 5: 0},
+    )(block_ids, place, *p_parts, ga, gb, r2, bx)
 
     pft, linv, blocks = call(
         factor_kernel, 1, 2,
-        [shape((rank, depth), F32), shape((rank, rank), F32), shape((3 * rank, kept * block), BF16)], name="factor",
-    )(block_ids, gram, ps)
+        [shape((rank, depth), F32), shape((rank, rank), F32), shape((kept * block, 3 * rank), BF16)], name="factor",
+    )(block_ids, gram, bx)
 
     if direct:
         chip_sum = us[0] + swap(us[1], 1, replicas)

time: 77.2 us -> 73.7 us (0.955)
  Pallas kernels: 19.1 us -> 16 us
    pallas_call x1, Pallas kernels: 7.56 us -> 4.41 us  [shards(): call(factor_kernel, 1, 2, [shape((rank, depth), F32), shape((rank, rank),...]
    unnamed x14 -> x12, local copies, waits for them, and re-layouts: 3.94 us -> 3.41 us
  transfers between devices with their start and end apart: 24 -> 24, of which waited for: 11 -> 10; matrix products, arithmetic and copies ran while one was open for 8% -> 8% of each run, Pallas kernels for 15% -> 12%
where the time goes in v3:
time: 73.7 us; the launch traced here: 73.4 us
  starting transfers between devices  28 us (38%)
  waiting for transfers between devices  18.9 us (26%)
  Pallas kernels  16 us (22%)
  local copies, waits for them, and re-layouts  8.28 us (11%)
  other arithmetic  1.24 us (2%)
  between operations  0.92 us (1%)
    ppermute x19, waiting for transfers between devices, swap(): return lax.ppermute(a, 'dp', [(i, i ^ bit) for i in range(size)])  16.6 us
    ppermute x19, starting transfers between devices, swap(): return lax.ppermute(a, 'dp', [(i, i ^ bit) for i in range(size)])  12.3 us
    ppermute x1, starting transfers between devices, gather_rows(): a2 = lax.ppermute(b1, 'mp', outer)  6.67 us
    ppermute x1, starting transfers between devices, gather_rows(): a1 = lax.ppermute(b0, 'mp', outer)  4.61 us
    pallas_call x1, Pallas kernels, shards(): call(factor_kernel, 1, 2, [shape((rank, depth), F32), shape((rank, rank),...  4.41 us
    gather x3, local copies, waits for them, and re-layouts, packed_tables(): lengths, assign, rewards = (lengths[order], assign[order], rewards[order])  3.74 us
    unnamed x12, local copies, waits for them, and re-layouts  3.41 us
    ppermute x1, starting transfers between devices, gather_rows(): a0 = lax.ppermute(x, 'mp', outer)  3.09 us
  transfers between devices with their start and end apart: 24, of which 10 were waited for; matrix products, arithmetic and copies ran while one was open for 8% of the time, Pallas kernels for 12%

profile of v3, /device:TPU:0, one launch (start us, length us, event | category | flops | bytes accessed | tf_op | source)
XLA Modules:
  0.0 73.4 jit_solution(12110112791888496307)
XLA Ops:
  0.7 3.1 %collective-permute-start = (bf16[32,5120]{1,0:T(8,128)(2,1)}, bf16[32,5120]{1,0:T(8,128)(2,1)S(1)}, u32[]{:S(2)}, u32[]{:S(2)}) collective-permute-start(bf16[32,5120]{1,0:T(8,128)(2,1)} %refs_0_.1), channel_id=1, source_target_pairs={{0,1},{1,0},{2,3},{3,2},{4,5},{5,4},{6,7},{7,6},{8,9},{9,8},{10,11... | collective-permute-start | bytes 983048 | tf_op jit(solution)/shard_map/ppermute | solution.py:271
  3.8 0.7 collective-permute-start.3
  4.5 1.2 %gather_fusion = s32[4,4]{1,0:T(4,128)S(1)} fusion(s32[4,4]{1,0:T(4,128)} %param.10, s32[1024]{0:T(1024)S(1)} %pad_clamp_fusion.1), kind=kCustom, calls=%fused_computation | custom fusion | bytes 144 | tf_op jit(solution)/shard_map/gather | solution.py:17
  5.8 1.2 %gather_fusion.2 = s32[4,4]{1,0:T(4,128)S(1)} fusion(s32[4,4]{1,0:T(4,128)} %param.11, s32[1024]{0:T(1024)S(1)} %pad_clamp_fusion.1), kind=kCustom, calls=%fused_computation.2 | custom fusion | bytes 144 | tf_op jit(solution)/shard_map/gather | solution.py:17
  7.0 0.2 reduce_window_sum.11
  7.2 0.1 convert_reduce_fusion
  7.3 0.1 select_reduce_fusion.1
  7.6 0.1 sub.53
  7.7 1.2 %gather_fusion.1 = f32[4,4]{1,0:T(4,128)S(1)} fusion(f32[4,4]{1,0:T(4,128)} %param.12, s32[1024]{0:T(1024)S(1)} %pad_clamp_fusion.1), kind=kCustom, calls=%fused_computation.1 | custom fusion | bytes 144 | tf_op jit(solution)/shard_map/gather | solution.py:17
  9.0 0.1 reduce_sum.46
  9.2 0.1 select_reduce_fusion.2
  9.3 0.1 mul.36
  9.4 2.3 %collective-permute-done.refs_1_ = bf16[32,5120]{1,0:T(8,128)(2,1)S(1)} collective-permute-done((bf16[32,5120]{1,0:T(8,128)(2,1)}, bf16[32,5120]{1,0:T(8,128)(2,1)S(1)}, u32[]{:S(2)}, u32[]{:S(2)}) %collective-permute-start) | collective-permute-done | bytes 327712 | tf_op jit(solution)/shard_map/ppermute | solution.py:271
  11.7 0.7 collective-permute-start.1
  12.4 0.8 %gather_fusion.3 = bf16[128,512]{1,0:T(8,128)(2,1)S(1)} fusion(bf16[256,512]{1,0:T(8,128)(2,1)S(1)} %copy-done, s32[1024]{0:T(1024)S(1)} %pad_clamp_fusion), kind=kCustom, calls=%fused_computation.3 | custom fusion | bytes 262656 | tf_op jit(solution)/shard_map/jit(_take)/gather | solution.py:304
  13.3 4.6 %collective-permute-start.4 = (bf16[32,5120]{1,0:T(8,128)(2,1)S(1)}, bf16[32,5120]{1,0:T(8,128)(2,1)S(1)}, u32[]{:S(2)}, u32[]{:S(2)}) collective-permute-start(bf16[32,5120]{1,0:T(8,128)(2,1)S(1)} %collective-permute-done.3.refs_3_), channel_id=1, source_target_pairs={{0,1},{1,0},{2,3},{3,2},{4,5},{5,4},{6,7},{7,6},{8,9},{9,8},{10,11... | collective-permute-start | bytes 983048 | tf_op jit(solution)/shard_map/ppermute | solution.py:274
  17.9 6.7 %collective-permute-start.2 = (bf16[32,5120]{1,0:T(8,128)(2,1)S(1)}, bf16[32,5120]{1,0:T(8,128)(2,1)S(1)}, u32[]{:S(2)}, u32[]{:S(2)}) collective-permute-start(bf16[32,5120]{1,0:T(8,128)(2,1)S(1)} %collective-permute-done.1.refs_1_), channel_id=1, source_target_pairs={{0,1},{1,0},{2,3},{3,2},{4,5},{5,4},{6,7},{7,6},{8,9},{9,8},{10,11... | collective-permute-start | bytes 983048 | tf_op jit(solution)/shard_map/ppermute | solution.py:275
  24.5 0.1 convert_multiply_fusion
  24.7 0.9 %copy-done.4 = f32[512,64]{0,1:T(8,128)S(1)} copy-done((f32[512,64]{0,1:T(8,128)S(1)}, f32[512,64]{0,1:T(8,128)}, u32[]{:S(2)}) %copy-start.4) | copy-done | bytes 131096
  25.6 1.3 %resid_term.1 = (bf16[192,512]{1,0:T(8,128)(2,1)S(1)}, f32[64,512]{1,0:T(8,128)S(1)}, bf16[2,512,512]{2,1,0:T(8,128)(2,1)S(1)}) custom-call(f32[64,512]{1,0:T(8,128)S(1)} %bitcast.18, f32[4,128,512]{2,1,0:T(8,128)S(1)} %copy-done.2), custom_call_target="tpu_custom_call" | custom-call | flops 1000000 | bytes 1000000 | tf_op jit(solution)/shard_map/resid_term/pallas_call | solution.py:306
  27.0 2.5 %copy-done.1 = bf16[5120,512]{1,0:T(8,128)(2,1)S(1)} copy-done((bf16[5120,512]{1,0:T(8,128)(2,1)S(1)}, bf16[5120,512]{1,0:T(8,128)(2,1)}, u32[]{:S(2)}) %copy-start.1) | copy-done | bytes 5242904
  29.5 1.9 %stage.1 = (bf16[256,5120]{1,0:T(8,128)(2,1)S(1)}, bf16[96,512]{1,0:T(8,128)(2,1)S(1)}, f32[64,5120]{1,0:T(8,128)S(1)}) custom-call(s32[1]{0:T(128)} %bitcast.2.flag, bf16[32,5120]{1,0:T(8,128)(2,1)S(1)} %copy-done.3, bf16[32,5120]{1,0:T(8,128)(2,1)S(1)} %collective-permute-done.refs_1_, bf16[32,5120]{1,0:T(8,128)(2,1)S(1)} %collective-permute-done.4.refs_2_, ...), custom_call_target="tpu_custom_call" | custom-call | flops 503316480 | bytes 1000000 | tf_op jit(solution)/shard_map/stage/pallas_call | solution.py:316
  31.5 2.6 %tail.1 = (bf16[256,5120]{1,0:T(8,128)(2,1)S(1)}, bf16[32,512]{1,0:T(8,128)(2,1)S(1)}, f32[8,5120]{1,0:T(8,128)S(1)}, f32[8,5120]{1,0:T(8,128)S(1)}, f32[8,5120]...) custom-call(s32[1]{0:T(128)} %bitcast.2.flag, ...), custom_call_target="tpu_custom_call", output_to_operand_aliasing={{0}: (10, {})} | custom-call | flops 167772160 | bytes 1000000 | tf_op jit(solution)/shard_map/tail/pallas_call | solution.py:327
  34.2 0.5 collective-permute-start.8
  34.8 0.8 %collective-permute-done.6 = f32[8,5120]{1,0:T(8,128)S(1)} collective-permute-done((f32[8,5120]{1,0:T(8,128)S(1)}, f32[8,5120]{1,0:T(8,128)S(1)}, u32[]{:S(2)}, u32[]{:S(2)}) %collective-permute-start.6) | collective-permute-done | bytes 163872 | tf_op jit(solution)/shard_map/ppermute | solution.py:284
  35.6 1.6 %collective-permute-start.7 = (f32[8,5120]{1,0:T(8,128)S(1)}, f32[8,5120]{1,0:T(8,128)S(1)}, u32[]{:S(2)}, u32[]{:S(2)}) collective-permute-start(f32[8,5120]{1,0:T(8,128)S(1)} %add.127), channel_id=1, source_target_pairs={{0,8},{4,12},{8,0},{12,4},{16,24},{20,28},{24,16},{28,20},{1,9},{5... | collective-permute-start | bytes 491528 | tf_op jit(solution)/shard_map/ppermute | solution.py:284
  37.2 1.6 %collective-permute-start.9 = (f32[8,5120]{1,0:T(8,128)S(1)}, f32[8,5120]{1,0:T(8,128)S(1)}, u32[]{:S(2)}, u32[]{:S(2)}) collective-permute-start(f32[8,5120]{1,0:T(8,128)S(1)} %add.128), channel_id=1, source_target_pairs={{0,16},{4,20},{8,24},{12,28},{16,0},{20,4},{24,8},{28,12},{1,17},{... | collective-permute-start | bytes 491528 | tf_op jit(solution)/shard_map/ppermute | solution.py:284
  38.8 0.5 collective-permute-start.11
  39.3 1.0 %merged.1.refs_4_ = f32[4,128,512]{2,1,0:T(8,128)S(1)} custom-call(s32[4]{0:T(128)S(1)} %copy-done.5, bf16[256,5120]{1,0:T(8,128)(2,1)S(1)} %get-tuple-element.48.bx.refs_11_, bf16[96,512]{1,0:T(8,128)(2,1)S(1)} %get-tuple-element.49.ga.refs_8_, bf16[32,512]{1,0:T(8,128)(2,1)S(1)} %get-tuple-element.50.gb.refs_9_, f32[4,128,512]{2,1,0:T(8,128)S(1)} %copy-done.2), custom_call_target="tpu_custom_call" | custom-call | flops 1000000 | bytes 1000000 | tf_op jit(solution)/shard_map/merged/pallas_call | solution.py:334
  40.3 2.3 %collective-permute-done.7 = f32[8,5120]{1,0:T(8,128)S(1)} collective-permute-done((f32[8,5120]{1,0:T(8,128)S(1)}, f32[8,5120]{1,0:T(8,128)S(1)}, u32[]{:S(2)}, u32[]{:S(2)}) %collective-permute-start.7) | collective-permute-done | bytes 163872 | tf_op jit(solution)/shard_map/ppermute | solution.py:284
  42.7 4.0 %collective-permute-done.9 = f32[8,5120]{1,0:T(8,128)S(1)} collective-permute-done((f32[8,5120]{1,0:T(8,128)S(1)}, f32[8,5120]{1,0:T(8,128)S(1)}, u32[]{:S(2)}, u32[]{:S(2)}) %collective-permute-start.9) | collective-permute-done | bytes 163872 | tf_op jit(solution)/shard_map/ppermute | solution.py:284
  46.8 1.6 %collective-permute-start.17 = (f32[8,5120]{1,0:T(8,128)S(1)}, f32[8,5120]{1,0:T(8,128)S(1)}, u32[]{:S(2)}, u32[]{:S(2)}) collective-permute-start(f32[8,5120]{1,0:T(8,128)S(1)} %add_add_fusion.refs_0_), channel_id=1, source_target_pairs={{0,24},{4,28},{8,16},{12,20},{16,8},{20,12},{24,0},{28,4},{1,25},{... | collective-permute-start | bytes 491528 | tf_op jit(solution)/shard_map/ppermute | solution.py:284
  48.3 1.1 %collective-permute-start.15 = (f32[8,5120]{1,0:T(8,128)S(1)}, f32[8,5120]{1,0:T(8,128)S(1)}, u32[]{:S(2)}, u32[]{:S(2)}) collective-permute-start(f32[8,5120]{1,0:T(8,128)S(1)} %add_add_fusion.refs_0_), channel_id=1, source_target_pairs={{0,16},{4,20},{8,24},{12,28},{16,0},{20,4},{24,8},{28,12},{1,17},{... | collective-permute-start | bytes 491528 | tf_op jit(solution)/shard_map/ppermute | solution.py:284
  49.4 0.9 %collective-permute-start.13 = (f32[8,5120]{1,0:T(8,128)S(1)}, f32[8,5120]{1,0:T(8,128)S(1)}, u32[]{:S(2)}, u32[]{:S(2)}) collective-permute-start(f32[8,5120]{1,0:T(8,128)S(1)} %add_add_fusion.refs_0_), channel_id=1, source_target_pairs={{0,8},{4,12},{8,0},{12,4},{16,24},{20,28},{24,16},{28,20},{1,9},{5... | collective-permute-start | bytes 491528 | tf_op jit(solution)/shard_map/ppermute | solution.py:284
  50.3 4.3 %collective-permute-done.17.refs_6_ = f32[8,5120]{1,0:T(8,128)S(1)} collective-permute-done((f32[8,5120]{1,0:T(8,128)S(1)}, f32[8,5120]{1,0:T(8,128)S(1)}, u32[]{:S(2)}, u32[]{:S(2)}) %collective-permute-start.17) | collective-permute-done | bytes 163872 | tf_op jit(solution)/shard_map/ppermute | solution.py:284
  54.6 1.7 %collective-permute-done.15.refs_4_ = f32[8,5120]{1,0:T(8,128)S(1)} collective-permute-done((f32[8,5120]{1,0:T(8,128)S(1)}, f32[8,5120]{1,0:T(8,128)S(1)}, u32[]{:S(2)}, u32[]{:S(2)}) %collective-permute-start.15) | collective-permute-done | bytes 163872 | tf_op jit(solution)/shard_map/ppermute | solution.py:284
  56.4 0.5 collective-permute-start.14
  56.9 0.9 %collective-permute-done.16.refs_5_ = f32[8,5120]{1,0:T(8,128)S(1)} collective-permute-done((f32[8,5120]{1,0:T(8,128)S(1)}, f32[8,5120]{1,0:T(8,128)S(1)}, u32[]{:S(2)}, u32[]{:S(2)}) %collective-permute-start.16) | collective-permute-done | bytes 163872 | tf_op jit(solution)/shard_map/ppermute | solution.py:284
  57.7 0.2 collective-permute-done.14.refs_3_
  58.0 2.7 %second.1 = (bf16[256,5120]{1,0:T(8,128)(2,1)S(1)}, f32[64,64]{1,0:T(8,128)S(1)}, f32[32,512]{1,0:T(8,128)S(1)}, f32[32,512]{1,0:T(8,128)S(1)}) custom-call(s32[4]{0:T(128)S(1)} %copy-done.5, s32[2]{0:T(128)S(1)} %pad_add_fusion.place, f32[8,5120]{1,0:T(8,128)S(1)} %add_add_fusion.refs_0_, ...), custom_call_target="tpu_custom_call", output_to_operand_aliasing={{0}: (13, {})} | custom-call | flops 1000000 | bytes 1000000 | tf_op jit(solution)/shard_map/second/pallas_call | solution.py:352
  60.7 0.3 collective-permute-start.19
  61.0 1.0 %collective-permute-done.19 = f32[32,512]{1,0:T(8,128)S(1)} collective-permute-done((f32[32,512]{1,0:T(8,128)S(1)}, f32[32,512]{1,0:T(8,128)S(1)}, u32[]{:S(2)}, u32[]{:S(2)}) %collective-permute-start.19) | collective-permute-done | bytes 65568 | tf_op jit(solution)/shard_map/ppermute | solution.py:284
  62.0 1.5 %collective-permute-start.22 = (f32[32,512]{1,0:T(8,128)S(1)}, f32[32,512]{1,0:T(8,128)S(1)}, u32[]{:S(2)}, u32[]{:S(2)}) collective-permute-start(f32[32,512]{1,0:T(8,128)S(1)} %add.133), channel_id=1, source_target_pairs={{0,24},{4,28},{8,16},{12,20},{16,8},{20,12},{24,0},{28,4},{1,25},{... | collective-permute-start | bytes 196616 | tf_op jit(solution)/shard_map/ppermute | solution.py:284
  63.5 1.5 %collective-permute-start.21 = (f32[32,512]{1,0:T(8,128)S(1)}, f32[32,512]{1,0:T(8,128)S(1)}, u32[]{:S(2)}, u32[]{:S(2)}) collective-permute-start(f32[32,512]{1,0:T(8,128)S(1)} %add.133), channel_id=1, source_target_pairs={{0,16},{4,20},{8,24},{12,28},{16,0},{20,4},{24,8},{28,12},{1,17},{... | collective-permute-start | bytes 196616 | tf_op jit(solution)/shard_map/ppermute | solution.py:284
  65.0 0.6 collective-permute-start.20
  65.6 4.4 %factor.1 = (f32[64,5120]{1,0:T(8,128)}, f32[64,64]{1,0:T(8,128)S(1)}, bf16[512,192]{1,0:T(8,128)(2,1)S(1)}) custom-call(s32[4]{0:T(128)S(1)} %copy-done.5, f32[64,64]{1,0:T(8,128)S(1)} %get-tuple-element.55.gram, bf16[256,5120]{1,0:T(8,128)(2,1)S(1)} %get-tuple-element.56.bx), custom_call_target="tpu_custom_call" | custom-call | flops 1000000 | bytes 1000000 | tf_op jit(solution)/shard_map/factor/pallas_call | solution.py:358
  70.1 1.2 %collective-permute-done.23.refs_1_ = f32[32,512]{1,0:T(8,128)S(1)} collective-permute-done((f32[32,512]{1,0:T(8,128)S(1)}, f32[32,512]{1,0:T(8,128)S(1)}, u32[]{:S(2)}, u32[]{:S(2)}) %collective-permute-start.23) | collective-permute-done | bytes 65568 | tf_op jit(solution)/shard_map/ppermute | solution.py:284
  71.3 2.1 %last.1 = (f32[64,512]{1,0:T(8,128)}, f32[4,128,512]{2,1,0:T(8,128)}) custom-call(s32[2]{0:T(128)S(1)} %pad_add_fusion.place, f32[32,512]{1,0:T(8,128)S(1)} %add_add_fusion.1.refs_0_, f32[32,512]{1,0:T(8,128)S(1)} %collective-permute-done.23.refs_1_, f32[64,64]{1,0:T(8,128)S(1)} %get-tuple-element.64.refs_2_, ...), custom_call_target="tpu_custom_call" | custom-call | flops 1000000 | bytes 1000000 | tf_op jit(solution)/shard_map/last/pallas_call | solution.py:372
  (52 shorter events, 1.0 us)
Async XLA Ops:
  0.6 11.7 %copy-start = (bf16[256,512]{1,0:T(8,128)(2,1)S(1)}, bf16[256,512]{1,0:T(8,128)(2,1)}, u32[]{:S(2)}) copy-start(bf16[256,512]{1,0:T(8,128)(2,1)} %param.13) | copy-start | bytes 786436
  0.6 26.4 %copy-start.3 = (bf16[32,5120]{1,0:T(8,128)(2,1)S(1)}, bf16[32,5120]{1,0:T(8,128)(2,1)}, u32[]{:S(2)}) copy-start(bf16[32,5120]{1,0:T(8,128)(2,1)} %refs_0_.1) | copy-start | bytes 983044
  0.7 24.1 %copy-start.2 = (f32[4,128,512]{2,1,0:T(8,128)S(1)}, f32[4,128,512]{2,1,0:T(8,128)}, u32[]{:S(2)}) copy-start(f32[4,128,512]{2,1,0:T(8,128)} %resid.3) | copy-start | bytes 3145732
  0.7 11.0 %collective-permute-start = (bf16[32,5120]{1,0:T(8,128)(2,1)}, bf16[32,5120]{1,0:T(8,128)(2,1)S(1)}, u32[]{:S(2)}, u32[]{:S(2)}) collective-permute-start(bf16[32,5120]{1,0:T(8,128)(2,1)} %refs_0_.1), channel_id=1, source_target_pairs={{0,1},{1,0},{2,3},{3,2},{4,5},{5,4},{6,7},{7,6},{8,9},{9,8},{10,11... | collective-permute-start | bytes 983048 | tf_op jit(solution)/shard_map/ppermute | solution.py:271
  3.8 9.5 %collective-permute-start.3 = (bf16[32,5120]{1,0:T(8,128)(2,1)}, bf16[32,5120]{1,0:T(8,128)(2,1)S(1)}, u32[]{:S(2)}, u32[]{:S(2)}) collective-permute-start(bf16[32,5120]{1,0:T(8,128)(2,1)} %refs_0_.1), channel_id=1, source_target_pairs={{1,2},{2,1},{5,6},{6,5},{9,10},{10,9},{13,14},{14,13},{17,18},{18,... | collective-permute-start | bytes 983048 | tf_op jit(solution)/shard_map/ppermute | solution.py:272
  11.7 6.2 %collective-permute-start.1 = (bf16[32,5120]{1,0:T(8,128)(2,1)S(1)}, bf16[32,5120]{1,0:T(8,128)(2,1)S(1)}, u32[]{:S(2)}, u32[]{:S(2)}) collective-permute-start(bf16[32,5120]{1,0:T(8,128)(2,1)S(1)} %collective-permute-done.refs_1_), channel_id=1, source_target_pairs={{1,2},{2,1},{5,6},{6,5},{9,10},{10,9},{13,14},{14,13},{17,18},{18,... | collective-permute-start | bytes 983048 | tf_op jit(solution)/shard_map/ppermute | solution.py:273
  13.3 13.8 %collective-permute-start.4 = (bf16[32,5120]{1,0:T(8,128)(2,1)S(1)}, bf16[32,5120]{1,0:T(8,128)(2,1)S(1)}, u32[]{:S(2)}, u32[]{:S(2)}) collective-permute-start(bf16[32,5120]{1,0:T(8,128)(2,1)S(1)} %collective-permute-done.3.refs_3_), channel_id=1, source_target_pairs={{0,1},{1,0},{2,3},{3,2},{4,5},{5,4},{6,7},{7,6},{8,9},{9,8},{10,11... | collective-permute-start | bytes 983048 | tf_op jit(solution)/shard_map/ppermute | solution.py:274
  17.9 13.6 %collective-permute-start.2 = (bf16[32,5120]{1,0:T(8,128)(2,1)S(1)}, bf16[32,5120]{1,0:T(8,128)(2,1)S(1)}, u32[]{:S(2)}, u32[]{:S(2)}) collective-permute-start(bf16[32,5120]{1,0:T(8,128)(2,1)S(1)} %collective-permute-done.1.refs_1_), channel_id=1, source_target_pairs={{0,1},{1,0},{2,3},{3,2},{4,5},{5,4},{6,7},{7,6},{8,9},{9,8},{10,11... | collective-permute-start | bytes 983048 | tf_op jit(solution)/shard_map/ppermute | solution.py:275
  24.7 0.9 %copy-start.4 = (f32[512,64]{0,1:T(8,128)S(1)}, f32[512,64]{0,1:T(8,128)}, u32[]{:S(2)}) copy-start(f32[512,64]{0,1:T(8,128)} %param.15) | copy-start | bytes 393220
  27.0 2.5 %copy-start.1 = (bf16[5120,512]{1,0:T(8,128)(2,1)S(1)}, bf16[5120,512]{1,0:T(8,128)(2,1)}, u32[]{:S(2)}) copy-start(bf16[5120,512]{1,0:T(8,128)(2,1)} %refs_2_.1) | copy-start | bytes 15728644
  29.5 2.0 %copy-start.5 = (s32[4]{0:T(128)S(1)}, s32[4]{0:T(128)}, u32[]{:S(2)}) copy-start(s32[4]{0:T(128)} %ids.7) | copy-start | bytes 52
  34.1 1.5 %collective-permute-start.6 = (f32[8,5120]{1,0:T(8,128)S(1)}, f32[8,5120]{1,0:T(8,128)S(1)}, u32[]{:S(2)}, u32[]{:S(2)}) collective-permute-start(f32[8,5120]{1,0:T(8,128)S(1)} %get-tuple-element.43), channel_id=1, source_target_pairs={{0,4},{4,0},{8,12},{12,8},{16,20},{20,16},{24,28},{28,24},{1,5},{5... | collective-permute-start | bytes 491528 | tf_op jit(solution)/shard_map/ppermute | solution.py:284
  34.2 3.0 %collective-permute-start.8 = (f32[8,5120]{1,0:T(8,128)S(1)}, f32[8,5120]{1,0:T(8,128)S(1)}, u32[]{:S(2)}, u32[]{:S(2)}) collective-permute-start(f32[8,5120]{1,0:T(8,128)S(1)} %get-tuple-element.45), channel_id=1, source_target_pairs={{0,4},{4,0},{8,12},{12,8},{16,20},{20,16},{24,28},{28,24},{1,5},{5... | collective-permute-start | bytes 491528 | tf_op jit(solution)/shard_map/ppermute | solution.py:284
  34.7 4.1 %collective-permute-start.10 = (f32[8,5120]{1,0:T(8,128)S(1)}, f32[8,5120]{1,0:T(8,128)S(1)}, u32[]{:S(2)}, u32[]{:S(2)}) collective-permute-start(f32[8,5120]{1,0:T(8,128)S(1)} %get-tuple-element.47), channel_id=1, source_target_pairs={{0,4},{4,0},{8,12},{12,8},{16,20},{20,16},{24,28},{28,24},{1,5},{5... | collective-permute-start | bytes 491528 | tf_op jit(solution)/shard_map/ppermute | solution.py:284
  35.6 7.1 %collective-permute-start.7 = (f32[8,5120]{1,0:T(8,128)S(1)}, f32[8,5120]{1,0:T(8,128)S(1)}, u32[]{:S(2)}, u32[]{:S(2)}) collective-permute-start(f32[8,5120]{1,0:T(8,128)S(1)} %add.127), channel_id=1, source_target_pairs={{0,8},{4,12},{8,0},{12,4},{16,24},{20,28},{24,16},{28,20},{1,9},{5... | collective-permute-start | bytes 491528 | tf_op jit(solution)/shard_map/ppermute | solution.py:284
  37.2 9.5 %collective-permute-start.9 = (f32[8,5120]{1,0:T(8,128)S(1)}, f32[8,5120]{1,0:T(8,128)S(1)}, u32[]{:S(2)}, u32[]{:S(2)}) collective-permute-start(f32[8,5120]{1,0:T(8,128)S(1)} %add.128), channel_id=1, source_target_pairs={{0,16},{4,20},{8,24},{12,28},{16,0},{20,4},{24,8},{28,12},{1,17},{... | collective-permute-start | bytes 491528 | tf_op jit(solution)/shard_map/ppermute | solution.py:284
  38.8 7.9 %collective-permute-start.11 = (f32[8,5120]{1,0:T(8,128)S(1)}, f32[8,5120]{1,0:T(8,128)S(1)}, u32[]{:S(2)}, u32[]{:S(2)}) collective-permute-start(f32[8,5120]{1,0:T(8,128)S(1)} %add.129), channel_id=1, source_target_pairs={{0,24},{4,28},{8,16},{12,20},{16,8},{20,12},{24,0},{28,4},{1,25},{... | collective-permute-start | bytes 491528 | tf_op jit(solution)/shard_map/ppermute | solution.py:284
  39.3 7.4 %collective-permute-start.5 = (f32[8,5120]{1,0:T(8,128)S(1)}, f32[8,5120]{1,0:T(8,128)S(1)}, u32[]{:S(2)}, u32[]{:S(2)}) collective-permute-start(f32[8,5120]{1,0:T(8,128)S(1)} %get-tuple-element.41), channel_id=1, source_target_pairs={{0,4},{4,0},{8,12},{12,8},{16,20},{20,16},{24,28},{28,24},{1,5},{5... | collective-permute-start | bytes 491528 | tf_op jit(solution)/shard_map/ppermute | solution.py:284
  46.8 7.9 %collective-permute-start.17 = (f32[8,5120]{1,0:T(8,128)S(1)}, f32[8,5120]{1,0:T(8,128)S(1)}, u32[]{:S(2)}, u32[]{:S(2)}) collective-permute-start(f32[8,5120]{1,0:T(8,128)S(1)} %add_add_fusion.refs_0_), channel_id=1, source_target_pairs={{0,24},{4,28},{8,16},{12,20},{16,8},{20,12},{24,0},{28,4},{1,25},{... | collective-permute-start | bytes 491528 | tf_op jit(solution)/shard_map/ppermute | solution.py:284
  48.3 8.0 %collective-permute-start.15 = (f32[8,5120]{1,0:T(8,128)S(1)}, f32[8,5120]{1,0:T(8,128)S(1)}, u32[]{:S(2)}, u32[]{:S(2)}) collective-permute-start(f32[8,5120]{1,0:T(8,128)S(1)} %add_add_fusion.refs_0_), channel_id=1, source_target_pairs={{0,16},{4,20},{8,24},{12,28},{16,0},{20,4},{24,8},{28,12},{1,17},{... | collective-permute-start | bytes 491528 | tf_op jit(solution)/shard_map/ppermute | solution.py:284
  49.4 7.0 %collective-permute-start.13 = (f32[8,5120]{1,0:T(8,128)S(1)}, f32[8,5120]{1,0:T(8,128)S(1)}, u32[]{:S(2)}, u32[]{:S(2)}) collective-permute-start(f32[8,5120]{1,0:T(8,128)S(1)} %add_add_fusion.refs_0_), channel_id=1, source_target_pairs={{0,8},{4,12},{8,0},{12,4},{16,24},{20,28},{24,16},{28,20},{1,9},{5... | collective-permute-start | bytes 491528 | tf_op jit(solution)/shard_map/ppermute | solution.py:284
  50.3 6.5 %collective-permute-start.12 = (f32[8,5120]{1,0:T(8,128)S(1)}, f32[8,5120]{1,0:T(8,128)S(1)}, u32[]{:S(2)}, u32[]{:S(2)}) collective-permute-start(f32[8,5120]{1,0:T(8,128)S(1)} %add_add_fusion.refs_0_), channel_id=1, source_target_pairs={{0,4},{4,0},{8,12},{12,8},{16,20},{20,16},{24,28},{28,24},{1,5},{5... | collective-permute-start | bytes 491528 | tf_op jit(solution)/shard_map/ppermute | solution.py:284
  54.6 2.2 %collective-permute-start.18 = (f32[8,5120]{1,0:T(8,128)S(1)}, f32[8,5120]{1,0:T(8,128)S(1)}, u32[]{:S(2)}, u32[]{:S(2)}) collective-permute-start(f32[8,5120]{1,0:T(8,128)S(1)} %collective-permute-done.17.refs_6_), channel_id=1, source_target_pairs={{0,4},{4,0},{8,12},{12,8},{16,20},{20,16},{24,28},{28,24},{1,5},{5... | collective-permute-start | bytes 491528 | tf_op jit(solution)/shard_map/ppermute | solution.py:284
  56.4 1.4 %collective-permute-start.16 = (f32[8,5120]{1,0:T(8,128)S(1)}, f32[8,5120]{1,0:T(8,128)S(1)}, u32[]{:S(2)}, u32[]{:S(2)}) collective-permute-start(f32[8,5120]{1,0:T(8,128)S(1)} %collective-permute-done.15.refs_4_), channel_id=1, source_target_pairs={{0,4},{4,0},{8,12},{12,8},{16,20},{20,16},{24,28},{28,24},{1,5},{5... | collective-permute-start | bytes 491528 | tf_op jit(solution)/shard_map/ppermute | solution.py:284
  56.4 1.6 %collective-permute-start.14 = (f32[8,5120]{1,0:T(8,128)S(1)}, f32[8,5120]{1,0:T(8,128)S(1)}, u32[]{:S(2)}, u32[]{:S(2)}) collective-permute-start(f32[8,5120]{1,0:T(8,128)S(1)} %collective-permute-done.13.refs_2_), channel_id=1, source_target_pairs={{0,4},{4,0},{8,12},{12,8},{16,20},{20,16},{24,28},{28,24},{1,5},{5... | collective-permute-start | bytes 491528 | tf_op jit(solution)/shard_map/ppermute | solution.py:284
  60.7 1.3 %collective-permute-start.19 = (f32[32,512]{1,0:T(8,128)S(1)}, f32[32,512]{1,0:T(8,128)S(1)}, u32[]{:S(2)}, u32[]{:S(2)}) collective-permute-start(f32[32,512]{1,0:T(8,128)S(1)} %get-tuple-element.59), channel_id=1, source_target_pairs={{0,4},{4,0},{8,12},{12,8},{16,20},{20,16},{24,28},{28,24},{1,5},{5... | collective-permute-start | bytes 196616 | tf_op jit(solution)/shard_map/ppermute | solution.py:284
  62.0 8.0 %collective-permute-start.22 = (f32[32,512]{1,0:T(8,128)S(1)}, f32[32,512]{1,0:T(8,128)S(1)}, u32[]{:S(2)}, u32[]{:S(2)}) collective-permute-start(f32[32,512]{1,0:T(8,128)S(1)} %add.133), channel_id=1, source_target_pairs={{0,24},{4,28},{8,16},{12,20},{16,8},{20,12},{24,0},{28,4},{1,25},{... | collective-permute-start | bytes 196616 | tf_op jit(solution)/shard_map/ppermute | solution.py:284
  63.5 6.5 %collective-permute-start.21 = (f32[32,512]{1,0:T(8,128)S(1)}, f32[32,512]{1,0:T(8,128)S(1)}, u32[]{:S(2)}, u32[]{:S(2)}) collective-permute-start(f32[32,512]{1,0:T(8,128)S(1)} %add.133), channel_id=1, source_target_pairs={{0,16},{4,20},{8,24},{12,28},{16,0},{20,4},{24,8},{28,12},{1,17},{... | collective-permute-start | bytes 196616 | tf_op jit(solution)/shard_map/ppermute | solution.py:284
  65.0 5.0 %collective-permute-start.20 = (f32[32,512]{1,0:T(8,128)S(1)}, f32[32,512]{1,0:T(8,128)S(1)}, u32[]{:S(2)}, u32[]{:S(2)}) collective-permute-start(f32[32,512]{1,0:T(8,128)S(1)} %add.133), channel_id=1, source_target_pairs={{0,8},{4,12},{8,0},{12,4},{16,24},{20,28},{24,16},{28,20},{1,9},{5... | collective-permute-start | bytes 196616 | tf_op jit(solution)/shard_map/ppermute | solution.py:284
  70.0 1.3 %collective-permute-start.23 = (f32[32,512]{1,0:T(8,128)S(1)}, f32[32,512]{1,0:T(8,128)S(1)}, u32[]{:S(2)}, u32[]{:S(2)}) collective-permute-start(f32[32,512]{1,0:T(8,128)S(1)} %add_add_fusion.1.refs_0_), channel_id=1, source_target_pairs={{0,4},{4,0},{8,12},{12,8},{16,20},{20,16},{24,28},{28,24},{1,5},{5... | collective-permute-start | bytes 196616 | tf_op jit(solution)/shard_map/ppermute | solution.py:284

commit v4 on v3

v4 whole, which is shorter than its diff:
```python
import functools
import jax
import jax.numpy as jnp
from jax import lax
from jax.experimental import pallas as pl
from jax.experimental.pallas import tpu as pltpu
from jax.sharding import PartitionSpec as P

F32 = jnp.float32
BF16 = jnp.bfloat16
HIGHEST = lax.Precision.HIGHEST
VMEM_LIMIT = 16 * 1024 * 1024
PREPARE_GRANT = 40 * 1024 * 1024


def dot(a, b, dims, precision=None):
    return lax.dot_general(a, b, (dims, ((), ())), precision=precision, preferred_element_type=F32)


NN, NT, TN = ((1,), (0,)), ((1,), (1,)), ((0,), (0,))
VMEM = pl.BlockSpec(memory_space=pltpu.VMEM)
HBM = pl.BlockSpec(memory_space=pltpu.HBM)


def split(a, parts):
    out = []
    for _ in range(parts):
        high = a.astype(BF16)
        out.append(high)
        a = a - high.astype(F32)
    return jnp.concatenate(out, axis=0)


def fold(a, parts):
    rows = a.shape[0] // parts
    total = a[:rows]
    for i in range(1, parts):
        total = total + a[i * rows:(i + 1) * rows]
    return total


def lanes(index, width):
    return pl.ds(pl.multiple_of(index * width, width), width)


def call(kernel, outs, scratch=(), flops=1000000, name=None, aliases=None, out_specs=None, far=0, grant=VMEM_LIMIT):
    def run(*args):
        return pl.pallas_call(
            kernel,
            input_output_aliases=aliases or {},
            out_shape=outs,
            in_specs=[HBM] * far + [VMEM] * (len(args) - far),
            out_specs=out_specs or jax.tree.map(lambda _: VMEM, outs),
            scratch_shapes=list(scratch),
            compiler_params=pltpu.CompilerParams(vmem_limit_bytes=grant),
            cost_estimate=pl.CostEstimate(flops=flops, bytes_accessed=1000000, transcendentals=0),
            name=name,
        )(*args)

    return run


def pick(pieces, choices, out):
    rows = out.shape[0] // len(choices)
    for j, (first, second) in enumerate(choices):
        here = slice(j * rows, (j + 1) * rows)
        if second is None:
            out[here, :] = pieces[first][...]
        else:
            at = lax.axis_index("mp")
            at_end = (at == 0) | (at == lax.axis_size("mp") - 1)

            @pl.when(at_end)
            def _():
                out[here, :] = pieces[first][...]

            @pl.when(jnp.logical_not(at_end))
            def _():
                out[here, :] = pieces[second][...]


def weigh_rows(lengths, assign, rewards, upstream, order, weighted):
    groups, sequences = lengths.shape
    slots = upstream.shape[0]
    capacity = slots // (groups * groups)
    count = weighted.shape[0] // groups
    row = lax.broadcasted_iota(jnp.int32, (count, slots), 0)
    slot = lax.broadcasted_iota(jnp.int32, (count, slots), 1)
    row_only = lax.broadcasted_iota(jnp.int32, (count, 1), 0)
    for j, source in enumerate(order):
        picked = jnp.zeros((count, slots), jnp.bool_)
        gain, size = jnp.zeros((count, 1), F32), jnp.ones((count, 1), F32)
        total = rewards[source, 0]
        for s in range(1, sequences):
            total = total + rewards[source, s]
        mean = total * (1.0 / sequences)
        offset = jnp.int32(0)
        for s in range(sequences):
            length = lengths[source, s]
            base = assign[source, s] * (groups * capacity) + source * capacity - offset
            inside = (row >= offset) & (row < offset + length)
            picked = picked | (inside & (slot == row + base))
            inside = (row_only >= offset) & (row_only < offset + length)
            gain = jnp.where(inside, rewards[source, s] - mean, gain)
            size = jnp.where(inside, length.astype(F32), size)
            offset = offset + length
        rows = jnp.dot(picked.astype(F32).astype(BF16), upstream[...], preferred_element_type=F32)
        weighted[j * count:(j + 1) * count, :] = gain / size * rows


def gather_order(groups):
    if groups != 4:
        return list(range(groups))
    at = lax.axis_index("mp")
    low = at < 2
    return [at, at ^ 1, jnp.where(low, 2, 1), jnp.where(low, 3, 0)]


def prepare_kernel(parts, own, *refs):
    small, (upstream_far, q0t_far, resid_far, w, x), refs = refs[:4], refs[4:9], refs[9:]
    ids, w_near, resid, bx, weighted, q3, r2, total, ordered, upstream, q0t, lengths, assign, rewards, arrived = refs
    pairs = list(zip(small, (lengths, assign, rewards, ids)))
    pairs += [(upstream_far, upstream), (q0t_far, q0t), (resid_far, resid), (w, w_near)]
    if own:
        first = bx.shape[0] - weighted.shape[0]
        pairs.append((x, bx.at[first:first + x.shape[0], :]))
    copies = [pltpu.make_async_copy(a, b, arrived.at[i]) for i, (a, b) in enumerate(pairs)]
    for copy in copies:
        copy.start()
    for copy in copies[:5]:
        copy.wait()
    weigh_rows(lengths, assign, rewards, upstream, gather_order(lengths.shape[0]), weighted)
    copies[5].wait()
    rows, me = ordered.shape[0] // parts, lax.axis_index("dp")
    for j in range(parts):
        ordered[j * rows:(j + 1) * rows, :] = q0t[lanes(me ^ j if parts > 1 else 0, rows), :]
    q3[...] = split(ordered[...], 3)
    total[...] = jnp.zeros_like(total)
    copies[6].wait()
    kept, block = resid.shape[:2]
    for k in range(kept):
        total[:, lanes(ids[0, k], block)] += dot(ordered[...], resid[k], NT, HIGHEST)
        high = resid[k].astype(BF16)
        r2[0, k * block:(k + 1) * block, :] = high
        r2[1, k * block:(k + 1) * block, :] = (resid[k] - high.astype(F32)).astype(BF16)
    for copy in copies[7:]:
        copy.wait()


def next_kernel(n_x, choices, first_row, ready, *refs):
    pieces, (w, weighted, q3, before, _, _, bx, g, *outs) = refs[:n_x], refs[n_x:]
    count = ready + len(choices) * pieces[0].shape[0]
    top = bx.shape[0] - g.shape[0] + first_row
    x = bx.at[top:top + count, :]
    here = slice(first_row, first_row + count)
    pick(pieces, choices, bx.at[top + ready:top + count, :])
    tangent = jnp.tanh(jnp.dot(x[...], w[...], preferred_element_type=F32))
    grad = (weighted[here, :] * (1.0 - tangent * tangent)).astype(BF16)
    g[here, :] = grad
    yt = split(fold(dot(q3[...], grad, NT), 3), 3)
    rows, wide = outs[0].shape[0], 1024
    for i in range(bx.shape[1] // wide):
        at = slice(i * wide, (i + 1) * wide)
        total = before[:, at] + fold(dot(yt, x[:, at], NN), 3)
        for j, out in enumerate(outs):
            out[:, at] = total[j * rows:(j + 1) * rows]


def merged_kernel(ids, bx, g, resid, out):
    block = resid.shape[1]
    for k in range(ids.shape[1]):
        out[k] = dot(bx[bx.shape[0] - g.shape[0]:, lanes(ids[0, k], block)], g[...], TN) + resid[k]


def second_kernel(n_p, ids, *refs):
    parts, refs = refs[:n_p], refs[n_p:]
    g, r2, _, bx, gram = refs[:5]
    uts, pk = refs[5:-1], refs[-1]
    rank, me = pk.shape[0] // 2, lax.axis_index("dp")
    if n_p == 1:
        bx[:2 * rank, :] = split(parts[0][...], 2)
    else:
        rows = parts[0].shape[0]
        for j in range(0, n_p, 2):
            chip = (me ^ j) // 2
            swapped = me % 2 == 1
            first, second = parts[j][...], parts[j + 1][...]
            pair = jnp.concatenate([jnp.where(swapped, second, first), jnp.where(swapped, first, second)], axis=0)
            high = pair.astype(BF16)
            bx[lanes(chip, 2 * rows), :] = high
            bx[pl.ds(pl.multiple_of(rank + chip * 2 * rows, 2 * rows), 2 * rows), :] = (pair - high.astype(F32)).astype(BF16)
    block = pk.shape[1] // ids.shape[1]
    for k in range(ids.shape[1]):
        pk[:, k * block:(k + 1) * block] = bx[:2 * rank, lanes(ids[0, k], block)]
    both = fold(dot(bx[:2 * rank, :], bx[...], NT), 2)
    gram[...] = both[:, :rank] + both[:, rank:2 * rank]
    total = fold(dot(split(both[:, 2 * rank:], 3), g[...], NN), 3)
    total = total + fold(dot(pk[...], r2[0], NN), 2) + dot(pk[:rank, :], r2[1], NN)
    if len(uts) == 1:
        uts[0][...] = total
    else:
        half = rank // 2
        low_is_mine = me % 2 == 0
        uts[0][...] = jnp.where(low_is_mine, total[:half], total[half:])
        uts[1][...] = jnp.where(low_is_mine, total[half:], total[:half])


def inverse_factor(gram):
    rank, sub = gram.shape[0], 8
    blocks = rank // sub
    eye = (lax.broadcasted_iota(jnp.int32, (rank, rank), 0) == lax.broadcasted_iota(jnp.int32, (rank, rank), 1)).astype(F32)
    whole = jnp.concatenate([gram, eye], axis=1)
    rows = [whole[b * sub:(b + 1) * sub] for b in range(blocks)]
    place = lax.broadcasted_iota(jnp.int32, (sub, 2 * rank), 0)

    def column(a, k):
        return jnp.take_along_axis(a, jnp.full(a.shape, k, jnp.int32), axis=1)

    out = []
    for b in range(blocks):
        panel = rows[b]
        entry = [column(panel, b * sub + j) for j in range(sub)]
        pivots = jnp.zeros_like(panel)
        scale = []
        for i in range(sub):
            scale.append(1.0 / entry[i][i:i + 1, :])
            pivots = jnp.where(place == i, entry[i], pivots)
            ratio = jnp.where(place > i, entry[i], 0.0) * scale[i]
            panel = panel - ratio * panel[i:i + 1, :]
            for j in range(i + 1, sub):
                entry[j] = entry[j] - ratio * entry[j][i:i + 1, :]
        out.append((panel / jnp.sqrt(pivots))[:, rank:])
        solved = [panel[i:i + 1, :] * scale[i] for i in range(sub)]
        for i in range(sub - 1, -1, -1):
            for j in range(i + 1, sub):
                solved[i] = solved[i] - (entry[j][i:i + 1, :] * scale[i]) * solved[j]
        for c in range(b + 1, blocks):
            update = column(rows[c], b * sub) * solved[0]
            for j in range(1, sub):
                update = update + column(rows[c], b * sub + j) * solved[j]
            rows[c] = rows[c] - update
    return jnp.concatenate(out, axis=0)


def factor_kernel(ids, gram, bx, pft, linv, blocks):
    rank = gram.shape[0]
    inverse = inverse_factor(gram[...])
    linv[...] = inverse
    high = inverse.astype(BF16)
    low = (inverse - high.astype(F32)).astype(BF16)
    lhs = jnp.concatenate([jnp.concatenate([high, high], axis=1), jnp.concatenate([low, jnp.zeros_like(low)], axis=1)], axis=0)
    wide = 1024
    for i in range(pft.shape[1] // wide):
        at = slice(i * wide, (i + 1) * wide)
        pft[:, at] = fold(dot(lhs, bx[:2 * rank, at], NN), 2)
    block = blocks.shape[0] // ids.shape[1]
    for k in range(ids.shape[1]):
        piece = jnp.transpose(pft[:, lanes(ids[0, k], block)])
        high = piece.astype(BF16)
        low = (piece - high.astype(F32)).astype(BF16)
        blocks[k * block:(k + 1) * block, :] = jnp.concatenate([high, low, high], axis=1)


def last_kernel(n_u, scale, *refs):
    halves, (linv, blocks, merged, qt, out, ut, made, sent) = refs[:n_u], refs[n_u:]
    if n_u == 1:
        ut[...] = halves[0][...]
    else:
        rows, core = halves[0].shape[0], lax.axis_index("dp") % 2
        ut[lanes(core, rows), :] = halves[0][...]
        ut[lanes(1 - core, rows), :] = halves[1][...]
    q = dot(linv[...], ut[...], NN, HIGHEST) * scale
    qt[...] = q
    two = split(q, 2)
    rank = q.shape[0]
    rhs = jnp.concatenate([two[:rank], two[:rank], two[rank:]], axis=0)
    block = merged.shape[1]
    copies = []
    for k in range(merged.shape[0]):
        made[k] = merged[k] - dot(blocks[k * block:(k + 1) * block, :], rhs, NN)
        copies.append(pltpu.make_async_copy(made.at[k], out.at[k], sent.at[k]))
        copies[-1].start()
    for copy in copies:
        copy.wait()


def gather_rows(x, groups, prepared, first_stage):
    if groups != 4:
        rows = x.shape[0]
        whole = lax.all_gather(x, "mp", axis=0, tiled=True)
        pieces = [whole[j * rows:(j + 1) * rows] for j in range(groups)]
        done = first_stage(pieces[:-2], [(j, None) for j in range(groups - 2)], 0)
        return done, [(pieces[j:j + 1], [(0, None)]) for j in (groups - 2, groups - 1)]
    outer = [(0, 1), (1, 0), (2, 3), (3, 2)]
    inner = [(1, 2), (2, 1)]
    a0 = lax.ppermute(x, "mp", outer)
    b0 = lax.ppermute(together(x, lax.axis_index("mp") * 2)[0], "mp", inner)
    a0, _ = together(a0, prepared)
    b1 = lax.ppermute(a0, "mp", inner)
    a1 = lax.ppermute(b0, "mp", outer)
    done = first_stage([a0], [(0, None)], x.shape[0])
    b1, *done = together(b1, *done)
    a2 = lax.ppermute(b1, "mp", outer)
    return done, [([a1, b0], [(0, 1)]), ([a2, b1], [(0, 1)])]


def swap(a, bit, size):
    return lax.ppermute(a, "dp", [(i, i ^ bit) for i in range(size)])


def together(*values):
    return lax.optimization_barrier(values)


def shards(gen_rows, lengths, assign, rewards, upstream, weight, q_init, resid, block_ids):
    groups, replicas = lax.axis_size("mp"), lax.axis_size("dp")
    slot_count, depth = gen_rows.shape
    columns, rank = q_init.shape
    kept, block = resid.shape[:2]
    rows = groups * slot_count
    ids = block_ids.reshape(1, kept)
    direct = replicas == 8
    shape = jax.ShapeDtypeStruct
    wide_rows, grad_rows = shape((2 * rank + rows, depth), BF16), shape((rows, columns), BF16)

    far = (lengths, assign, rewards, ids, upstream, q_init.T, resid, weight, gen_rows)
    far = [pltpu.with_memory_space_constraint(a, pltpu.HBM) for a in far]
    ids, weight, resid, bx, weighted, q3, r2, pt = call(
        functools.partial(prepare_kernel, replicas if direct else 1, groups == 4),
        [shape(ids.shape, jnp.int32), shape(weight.shape, BF16), shape(resid.shape, F32), wide_rows,
         shape((rows, columns), F32), shape((3 * rank, columns), BF16), shape((2, kept * block, columns), BF16),
         shape((rank, depth), F32)],
        [pltpu.VMEM((rank, columns), F32), pltpu.VMEM(upstream.shape, BF16), pltpu.VMEM((rank, columns), F32),
         pltpu.VMEM(lengths.shape, jnp.int32), pltpu.VMEM(assign.shape, jnp.int32), pltpu.VMEM(rewards.shape, F32),
         pltpu.SemaphoreType.DMA((9,))], name="prepare", far=len(far), grant=PREPARE_GRANT,
    )(*far)

    def stage(pieces, choices, first_row, ready, bx, g, pt, outs):
        n = len(pieces)
        return call(
            functools.partial(next_kernel, n, choices, first_row, ready), [wide_rows, grad_rows] + outs,
            flops=2 * slot_count * depth * columns, name="rows", aliases={n + 4: 0, n + 5: 1},
        )(*pieces, weight, weighted, q3, pt, bx, g)

    whole_rank = [shape((rank, depth), F32)]
    (bx, g, pt), stages = gather_rows(
        gen_rows, groups, weighted,
        lambda pieces, choices, ready: stage(pieces, choices, 0, ready, bx, jnp.zeros(grad_rows.shape, BF16), pt, whole_rank),
    )
    for i, (pieces, choices) in enumerate(stages):
        last = i == len(stages) - 1
        outs = [shape((rank // replicas, depth), F32)] * replicas if last and direct else whole_rank
        bx, g, *parts = stage(pieces, choices, rows - (len(stages) - i) * slot_count, 0, bx, g, pt, outs)
        pt = parts[0]

    merged = call(merged_kernel, shape((kept, block, columns), F32), name="merged")(ids, bx, g, resid)

    if direct:
        chips = replicas // 2
        sums = [parts[2 * k] + swap(parts[2 * k + 1], 1, replicas) for k in range(chips)]
        got = [swap(sums[k], 2 * k, replicas) for k in range(1, chips)]
        *got, merged = together(*got, merged)
        own = sums[0] + got[0] + got[1] + got[2]
        same = [own] + [swap(own, 2 * k, replicas) for k in range(1, chips)]
        p_parts = []
        for s in same:
            p_parts += [s, swap(s, 1, replicas)]
        u_shapes = [shape((rank // 2, columns), F32)] * 2
    else:
        p_parts = [lax.psum(parts[0], "dp")]
        u_shapes = [shape((rank, columns), F32)]

    n_p = len(p_parts)
    bx, gram, *us = call(
        functools.partial(second_kernel, n_p),
        [wide_rows, shape((rank, rank), F32)] + u_shapes,
        [pltpu.VMEM((2 * rank, kept * block), BF16)], name="second", aliases={n_p + 3: 0},
    )(ids, *p_parts, g, r2, bx)

    pft, linv, blocks = call(
        factor_kernel,
        [shape((rank, depth), F32), shape((rank, rank), F32), shape((kept * block, 3 * rank), BF16)], name="factor",
    )(ids, gram, bx)

    if direct:
        chip_sum = us[0] + swap(us[1], 1, replicas)
        got = [swap(chip_sum, 2 * k, replicas) for k in range(1, chips)]
        *got, linv = together(*got, linv)
        total = chip_sum + got[0] + got[1] + got[2]
        u_parts = [total, swap(total, 1, replicas)]
    else:
        u_parts = [lax.psum(us[0], "dp")]
    n_u = len(u_parts)
    qt, new_resid = call(
        functools.partial(last_kernel, n_u, 1.0 / replicas),
        [shape((rank, columns), F32), shape((kept, block, columns), F32)],
        [pltpu.VMEM((rank, columns), F32), pltpu.VMEM((kept, block, columns), F32), pltpu.SemaphoreType.DMA((kept,))],
        name="last", out_specs=[VMEM, pl.BlockSpec(memory_space=pl.ANY)],
    )(*u_parts, linv, blocks, merged)
    return pft.T, qt.T, new_resid


def solution(mesh):
    placed = (
        P(("dp", "mp"), None),
        P("dp", None),
        P("dp", None),
        P("dp", None),
        P("dp", "mp"),
        P(None, "mp"),
        P("mp", None),
        P("dp", None, "mp"),
        P("dp"),
    )
    return jax.shard_map(
        shards,
        mesh=mesh,
        in_specs=placed,
        out_specs=(P(None, "mp"), P("mp", None), P("dp", None, "mp")),
        check_vma=False,
    )
```

time: 73.7 us -> 70.8 us (0.961)
  local copies, waits for them, and re-layouts: 8.28 us -> 0.01 us
  waiting for transfers between devices: 18.9 us -> 26.1 us
  starting transfers between devices: 28 us -> 26.3 us
  Pallas kernels: 16 us -> 17.2 us
  other arithmetic: 1.24 us -> 0.17 us
    gather x4 -> x0, local copies, waits for them, and re-layouts: 4.59 us -> none  [the longest x3 3.74 us: packed_tables(): lengths, assign, rewards = (lengths[order], assign[order], rewards[order])]
    ppermute x1, waiting for transfers between devices: 0.01 us -> 4.39 us  [gather_rows(): a2 = lax.ppermute(b1, 'mp', outer)]
    unnamed x12 -> x0, local copies, waits for them, and re-layouts: 3.41 us -> none
    ppermute x1, waiting for transfers between devices: 2.31 us -> 4.12 us  [gather_rows(): a0 = lax.ppermute(x, 'mp', outer)]
    ppermute x1, starting transfers between devices: 6.67 us -> 4.95 us  [gather_rows(): a2 = lax.ppermute(b1, 'mp', outer)]
    pallas_call x7 -> x8, Pallas kernels: 16 us -> 17.2 us  [run(): pl.pallas_call(kernel, input_output_aliases=aliases or {}, out_shape=outs...]
  transfers between devices with their start and end apart: 24 -> 24, of which waited for: 10 -> 13; matrix products, arithmetic and copies ran while one was open for 8% -> 0% of each run, Pallas kernels for 12% -> 16%
where the time goes in v4:
time: 70.8 us; the launch traced here: 70.6 us
  starting transfers between devices  26.3 us (37%)
  waiting for transfers between devices  26.1 us (37%)
  Pallas kernels  17.2 us (24%)
  between operations  0.77 us (1%)
    pallas_call x8, Pallas kernels, run(): pl.pallas_call(kernel, input_output_aliases=aliases or {}, out_shape=outs...  17.2 us
    ppermute x19, waiting for transfers between devices, swap(): return lax.ppermute(a, 'dp', [(i, i ^ bit) for i in range(size)])  17.2 us
    ppermute x19, starting transfers between devices, swap(): return lax.ppermute(a, 'dp', [(i, i ^ bit) for i in range(size)])  12.3 us
    ppermute x1, starting transfers between devices, gather_rows(): a2 = lax.ppermute(b1, 'mp', outer)  4.95 us
    ppermute x1, starting transfers between devices, gather_rows(): a1 = lax.ppermute(b0, 'mp', outer)  4.61 us
    ppermute x1, waiting for transfers between devices, gather_rows(): a2 = lax.ppermute(b1, 'mp', outer)  4.39 us
    ppermute x1, waiting for transfers between devices, gather_rows(): a0 = lax.ppermute(x, 'mp', outer)  4.12 us
    ppermute x1, starting transfers between devices, gather_rows(): a0 = lax.ppermute(x, 'mp', outer)  3.09 us
  transfers between devices with their start and end apart: 24, of which 13 were waited for; matrix products, arithmetic and copies ran while one was open for 0% of the time, Pallas kernels for 16%

profile of v4, /device:TPU:0, one launch (start us, length us, event | category | flops | bytes accessed | tf_op | source)
XLA Modules:
  0.0 70.6 jit_solution(17058985656193202374)
XLA Ops:
  0.6 3.1 %collective-permute-start = (bf16[32,5120]{1,0:T(8,128)(2,1)}, bf16[32,5120]{1,0:T(8,128)(2,1)S(1)}, u32[]{:S(2)}, u32[]{:S(2)}) collective-permute-start(bf16[32,5120]{1,0:T(8,128)(2,1)} %refs_8_.1), channel_id=1, source_target_pairs={{0,1},{1,0},{2,3},{3,2},{4,5},{5,4},{6,7},{7,6},{8,9},{9,8},{10,11... | collective-permute-start | bytes 983048 | tf_op jit(solution)/shard_map/ppermute | solution.py:296
  3.7 0.7 collective-permute-start.3
  4.4 3.1 %prepare.1 = (s32[1,4]{1,0:T(1,128)S(1)}, bf16[5120,512]{1,0:T(8,128)(2,1)S(1)}, f32[4,128,512]{2,1,0:T(8,128)S(1)}, bf16[256,5120]{1,0:T(8,128)(2,1)S(1)}, f32[...) custom-call(s32[4,4]{1,0:T(4,128)} %refs_0_.1, ...), custom_call_target="tpu_custom_call" | custom-call | flops 1000000 | bytes 1000000 | tf_op jit(solution)/shard_map/prepare/pallas_call | solution.py:48
  7.5 4.1 %collective-permute-done.refs_0_ = bf16[32,5120]{1,0:T(8,128)(2,1)S(1)} collective-permute-done((bf16[32,5120]{1,0:T(8,128)(2,1)}, bf16[32,5120]{1,0:T(8,128)(2,1)S(1)}, u32[]{:S(2)}, u32[]{:S(2)}) %collective-permute-start) | collective-permute-done | bytes 327712 | tf_op jit(solution)/shard_map/ppermute | solution.py:296
  11.6 0.7 collective-permute-start.1
  12.3 4.6 %collective-permute-start.4 = (bf16[32,5120]{1,0:T(8,128)(2,1)S(1)}, bf16[32,5120]{1,0:T(8,128)(2,1)S(1)}, u32[]{:S(2)}, u32[]{:S(2)}) collective-permute-start(bf16[32,5120]{1,0:T(8,128)(2,1)S(1)} %collective-permute-done.3.refs_1_), channel_id=1, source_target_pairs={{0,1},{1,0},{2,3},{3,2},{4,5},{5,4},{6,7},{7,6},{8,9},{9,8},{10,11... | collective-permute-start | bytes 983048 | tf_op jit(solution)/shard_map/ppermute | solution.py:300
  17.0 1.9 %rows.3 = (bf16[256,5120]{1,0:T(8,128)(2,1)S(1)}, bf16[128,512]{1,0:T(8,128)(2,1)S(1)}, f32[64,5120]{1,0:T(8,128)S(1)}) custom-call(bf16[32,5120]{1,0:T(8,128)(2,1)S(1)} %collective-permute-done.refs_0_, bf16[5120,512]{1,0:T(8,128)(2,1)S(1)} %get-tuple-element.52.refs_1_.refs_2_, ...), custom_call_target="tpu_custom_call", output_to_operand_aliasing={{0}: (5, {}), {1}: (6, {})} | custom-call | flops 167772160 | bytes 1000000 | tf_op jit(solution)/shard_map/rows/pallas_call | solution.py:48
  18.9 0.0 collective-permute-done.1.refs_1_
  18.9 4.9 %collective-permute-start.2 = (bf16[32,5120]{1,0:T(8,128)(2,1)S(1)}, bf16[32,5120]{1,0:T(8,128)(2,1)S(1)}, u32[]{:S(2)}, u32[]{:S(2)}) collective-permute-start(bf16[32,5120]{1,0:T(8,128)(2,1)S(1)} %collective-permute-done.1.refs_1_), channel_id=1, source_target_pairs={{0,1},{1,0},{2,3},{3,2},{4,5},{5,4},{6,7},{7,6},{8,9},{9,8},{10,11... | collective-permute-start | bytes 983048 | tf_op jit(solution)/shard_map/ppermute | solution.py:303
  23.8 0.3 collective-permute-done.4.refs_0_
  24.2 1.9 %rows.4 = (bf16[256,5120]{1,0:T(8,128)(2,1)S(1)}, bf16[128,512]{1,0:T(8,128)(2,1)S(1)}, f32[64,5120]{1,0:T(8,128)S(1)}) custom-call(bf16[32,5120]{1,0:T(8,128)(2,1)S(1)} %collective-permute-done.4.refs_0_, bf16[32,5120]{1,0:T(8,128)(2,1)S(1)} %collective-permute-done.3.refs_1_, ...), custom_call_target="tpu_custom_call", output_to_operand_aliasing={{0}: (6, {}), {1}: (7, {})} | custom-call | flops 167772160 | bytes 1000000 | tf_op jit(solution)/shard_map/rows/pallas_call | solution.py:48
  26.1 4.4 %collective-permute-done.2.refs_0_ = bf16[32,5120]{1,0:T(8,128)(2,1)S(1)} collective-permute-done((bf16[32,5120]{1,0:T(8,128)(2,1)S(1)}, bf16[32,5120]{1,0:T(8,128)(2,1)S(1)}, u32[]{:S(2)}, u32[]{:S(2)}) %collective-permute-start.2) | collective-permute-done | bytes 327712 | tf_op jit(solution)/shard_map/ppermute | solution.py:303
  30.5 1.9 %rows.5 = (bf16[256,5120]{1,0:T(8,128)(2,1)S(1)}, bf16[128,512]{1,0:T(8,128)(2,1)S(1)}, f32[8,5120]{1,0:T(8,128)S(1)}, f32[8,5120]{1,0:T(8,128)S(1)}, f32[8,5120...) custom-call(bf16[32,5120]{1,0:T(8,128)(2,1)S(1)} %collective-permute, ...), custom_call_target="tpu_custom_call", output_to_operand_aliasing={{0}: (6, {}), {1}: (7, {})} | custom-call | flops 167772160 | bytes 1000000 | tf_op jit(solution)/shard_map/rows/pallas_call | solution.py:48
  32.5 0.1 collective-permute-start.6
  32.5 0.5 collective-permute-start.8
  33.0 0.1 collective-permute-start.10
  33.1 0.8 %collective-permute-done.6 = f32[8,5120]{1,0:T(8,128)S(1)} collective-permute-done((f32[8,5120]{1,0:T(8,128)S(1)}, f32[8,5120]{1,0:T(8,128)S(1)}, u32[]{:S(2)}, u32[]{:S(2)}) %collective-permute-start.6) | collective-permute-done | bytes 163872 | tf_op jit(solution)/shard_map/ppermute | solution.py:308
  33.9 1.6 %collective-permute-start.7 = (f32[8,5120]{1,0:T(8,128)S(1)}, f32[8,5120]{1,0:T(8,128)S(1)}, u32[]{:S(2)}, u32[]{:S(2)}) collective-permute-start(f32[8,5120]{1,0:T(8,128)S(1)} %add.34), channel_id=1, source_target_pairs={{0,8},{4,12},{8,0},{12,4},{16,24},{20,28},{24,16},{28,20},{1,9},{5... | collective-permute-start | bytes 491528 | tf_op jit(solution)/shard_map/ppermute | solution.py:308
  35.5 0.0 collective-permute-done.8
  35.5 1.6 %collective-permute-start.9 = (f32[8,5120]{1,0:T(8,128)S(1)}, f32[8,5120]{1,0:T(8,128)S(1)}, u32[]{:S(2)}, u32[]{:S(2)}) collective-permute-start(f32[8,5120]{1,0:T(8,128)S(1)} %add.35), channel_id=1, source_target_pairs={{0,16},{4,20},{8,24},{12,28},{16,0},{20,4},{24,8},{28,12},{1,17},{... | collective-permute-start | bytes 491528 | tf_op jit(solution)/shard_map/ppermute | solution.py:308
  37.1 0.0 collective-permute-done.10
  37.1 0.5 collective-permute-start.11
  37.7 0.4 merged.1.refs_4_
  38.1 3.0 %collective-permute-done.7 = f32[8,5120]{1,0:T(8,128)S(1)} collective-permute-done((f32[8,5120]{1,0:T(8,128)S(1)}, f32[8,5120]{1,0:T(8,128)S(1)}, u32[]{:S(2)}, u32[]{:S(2)}) %collective-permute-start.7) | collective-permute-done | bytes 163872 | tf_op jit(solution)/shard_map/ppermute | solution.py:308
  41.0 4.0 %collective-permute-done.9 = f32[8,5120]{1,0:T(8,128)S(1)} collective-permute-done((f32[8,5120]{1,0:T(8,128)S(1)}, f32[8,5120]{1,0:T(8,128)S(1)}, u32[]{:S(2)}, u32[]{:S(2)}) %collective-permute-start.9) | collective-permute-done | bytes 163872 | tf_op jit(solution)/shard_map/ppermute | solution.py:308
  45.1 0.0 collective-permute-done.11
  45.1 0.0 collective-permute-done.5
  45.1 0.1 add_add_fusion.refs_0_
  45.1 1.6 %collective-permute-start.17 = (f32[8,5120]{1,0:T(8,128)S(1)}, f32[8,5120]{1,0:T(8,128)S(1)}, u32[]{:S(2)}, u32[]{:S(2)}) collective-permute-start(f32[8,5120]{1,0:T(8,128)S(1)} %add_add_fusion.refs_0_), channel_id=1, source_target_pairs={{0,24},{4,28},{8,16},{12,20},{16,8},{20,12},{24,0},{28,4},{1,25},{... | collective-permute-start | bytes 491528 | tf_op jit(solution)/shard_map/ppermute | solution.py:308
  46.7 1.1 %collective-permute-start.15 = (f32[8,5120]{1,0:T(8,128)S(1)}, f32[8,5120]{1,0:T(8,128)S(1)}, u32[]{:S(2)}, u32[]{:S(2)}) collective-permute-start(f32[8,5120]{1,0:T(8,128)S(1)} %add_add_fusion.refs_0_), channel_id=1, source_target_pairs={{0,16},{4,20},{8,24},{12,28},{16,0},{20,4},{24,8},{28,12},{1,17},{... | collective-permute-start | bytes 491528 | tf_op jit(solution)/shard_map/ppermute | solution.py:308
  47.8 0.9 %collective-permute-start.13 = (f32[8,5120]{1,0:T(8,128)S(1)}, f32[8,5120]{1,0:T(8,128)S(1)}, u32[]{:S(2)}, u32[]{:S(2)}) collective-permute-start(f32[8,5120]{1,0:T(8,128)S(1)} %add_add_fusion.refs_0_), channel_id=1, source_target_pairs={{0,8},{4,12},{8,0},{12,4},{16,24},{20,28},{24,16},{28,20},{1,9},{5... | collective-permute-start | bytes 491528 | tf_op jit(solution)/shard_map/ppermute | solution.py:308
  48.7 0.0 collective-permute-start.12
  48.7 4.3 %collective-permute-done.17.refs_6_ = f32[8,5120]{1,0:T(8,128)S(1)} collective-permute-done((f32[8,5120]{1,0:T(8,128)S(1)}, f32[8,5120]{1,0:T(8,128)S(1)}, u32[]{:S(2)}, u32[]{:S(2)}) %collective-permute-start.17) | collective-permute-done | bytes 163872 | tf_op jit(solution)/shard_map/ppermute | solution.py:308
  53.0 1.7 %collective-permute-done.15.refs_4_ = f32[8,5120]{1,0:T(8,128)S(1)} collective-permute-done((f32[8,5120]{1,0:T(8,128)S(1)}, f32[8,5120]{1,0:T(8,128)S(1)}, u32[]{:S(2)}, u32[]{:S(2)}) %collective-permute-start.15) | collective-permute-done | bytes 163872 | tf_op jit(solution)/shard_map/ppermute | solution.py:308
  54.7 0.1 collective-permute-done.13.refs_2_
  54.8 0.5 collective-permute-start.14
  55.2 0.9 %collective-permute-done.16.refs_5_ = f32[8,5120]{1,0:T(8,128)S(1)} collective-permute-done((f32[8,5120]{1,0:T(8,128)S(1)}, f32[8,5120]{1,0:T(8,128)S(1)}, u32[]{:S(2)}, u32[]{:S(2)}) %collective-permute-start.16) | collective-permute-done | bytes 163872 | tf_op jit(solution)/shard_map/ppermute | solution.py:308
  56.1 0.2 collective-permute-done.14.refs_3_
  56.3 2.0 %second.1 = (bf16[256,5120]{1,0:T(8,128)(2,1)S(1)}, f32[64,64]{1,0:T(8,128)S(1)}, f32[32,512]{1,0:T(8,128)S(1)}, f32[32,512]{1,0:T(8,128)S(1)}) custom-call(s32[1,4]{1,0:T(1,128)S(1)} %get-tuple-element.49.ids, f32[8,5120]{1,0:T(8,128)S(1)} %add_add_fusion.refs_0_, f32[8,5120]{1,0:T(8,128)S(1)} %collective-permute-done.12.refs_1_, ...), custom_call_target="tpu_custom_call", output_to_operand_aliasing={{0}: (11, {})} | custom-call | flops 1000000 | bytes 1000000 | tf_op jit(solution)/shard_map/second/pallas_call | solution.py:48
  58.3 0.3 collective-permute-start.19
  58.7 1.0 %collective-permute-done.19 = f32[32,512]{1,0:T(8,128)S(1)} collective-permute-done((f32[32,512]{1,0:T(8,128)S(1)}, f32[32,512]{1,0:T(8,128)S(1)}, u32[]{:S(2)}, u32[]{:S(2)}) %collective-permute-start.19) | collective-permute-done | bytes 65568 | tf_op jit(solution)/shard_map/ppermute | solution.py:308
  59.7 1.5 %collective-permute-start.22 = (f32[32,512]{1,0:T(8,128)S(1)}, f32[32,512]{1,0:T(8,128)S(1)}, u32[]{:S(2)}, u32[]{:S(2)}) collective-permute-start(f32[32,512]{1,0:T(8,128)S(1)} %add.40), channel_id=1, source_target_pairs={{0,24},{4,28},{8,16},{12,20},{16,8},{20,12},{24,0},{28,4},{1,25},{... | collective-permute-start | bytes 196616 | tf_op jit(solution)/shard_map/ppermute | solution.py:308
  61.2 1.5 %collective-permute-start.21 = (f32[32,512]{1,0:T(8,128)S(1)}, f32[32,512]{1,0:T(8,128)S(1)}, u32[]{:S(2)}, u32[]{:S(2)}) collective-permute-start(f32[32,512]{1,0:T(8,128)S(1)} %add.40), channel_id=1, source_target_pairs={{0,16},{4,20},{8,24},{12,28},{16,0},{20,4},{24,8},{28,12},{1,17},{... | collective-permute-start | bytes 196616 | tf_op jit(solution)/shard_map/ppermute | solution.py:308
  62.7 0.6 collective-permute-start.20
  63.2 3.9 %factor.1 = (f32[64,5120]{1,0:T(8,128)}, f32[64,64]{1,0:T(8,128)S(1)}, bf16[512,192]{1,0:T(8,128)(2,1)S(1)}) custom-call(s32[1,4]{1,0:T(1,128)S(1)} %get-tuple-element.49.ids, f32[64,64]{1,0:T(8,128)S(1)} %get-tuple-element.81.gram, bf16[256,5120]{1,0:T(8,128)(2,1)S(1)} %get-tuple-element.82.bx), custom_call_target="tpu_custom_call" | custom-call | flops 1000000 | bytes 1000000 | tf_op jit(solution)/shard_map/factor/pallas_call | solution.py:48
  67.1 0.1 collective-permute-start.23
  67.2 1.2 %collective-permute-done.23.refs_1_ = f32[32,512]{1,0:T(8,128)S(1)} collective-permute-done((f32[32,512]{1,0:T(8,128)S(1)}, f32[32,512]{1,0:T(8,128)S(1)}, u32[]{:S(2)}, u32[]{:S(2)}) %collective-permute-start.23) | collective-permute-done | bytes 65568 | tf_op jit(solution)/shard_map/ppermute | solution.py:308
  68.5 2.1 %last.1 = (f32[64,512]{1,0:T(8,128)}, f32[4,128,512]{2,1,0:T(8,128)}) custom-call(f32[32,512]{1,0:T(8,128)S(1)} %add_add_fusion.1.refs_0_, f32[32,512]{1,0:T(8,128)S(1)} %collective-permute-done.23.refs_1_, f32[64,64]{1,0:T(8,128)S(1)} %get-tuple-element.90.refs_2_, bf16[512,192]{1,0:T(8,128)(2,1)S(1)} %get-tuple-element.91.refs_3_, ...), custom_call_target="tpu_custom_call" | custom-call | flops 1000000 | bytes 1000000 | tf_op jit(solution)/shard_map/last/pallas_call | solution.py:48
  (15 shorter events, 0.1 us)
Async XLA Ops:
  0.6 11.0 %collective-permute-start = (bf16[32,5120]{1,0:T(8,128)(2,1)}, bf16[32,5120]{1,0:T(8,128)(2,1)S(1)}, u32[]{:S(2)}, u32[]{:S(2)}) collective-permute-start(bf16[32,5120]{1,0:T(8,128)(2,1)} %refs_8_.1), channel_id=1, source_target_pairs={{0,1},{1,0},{2,3},{3,2},{4,5},{5,4},{6,7},{7,6},{8,9},{9,8},{10,11... | collective-permute-start | bytes 983048 | tf_op jit(solution)/shard_map/ppermute | solution.py:296
  3.7 8.6 %collective-permute-start.3 = (bf16[32,5120]{1,0:T(8,128)(2,1)}, bf16[32,5120]{1,0:T(8,128)(2,1)S(1)}, u32[]{:S(2)}, u32[]{:S(2)}) collective-permute-start(bf16[32,5120]{1,0:T(8,128)(2,1)} %refs_8_.1), channel_id=1, source_target_pairs={{1,2},{2,1},{5,6},{6,5},{9,10},{10,9},{13,14},{14,13},{17,18},{18,... | collective-permute-start | bytes 983048 | tf_op jit(solution)/shard_map/ppermute | solution.py:297
  11.6 7.2 %collective-permute-start.1 = (bf16[32,5120]{1,0:T(8,128)(2,1)S(1)}, bf16[32,5120]{1,0:T(8,128)(2,1)S(1)}, u32[]{:S(2)}, u32[]{:S(2)}) collective-permute-start(bf16[32,5120]{1,0:T(8,128)(2,1)S(1)} %collective-permute-done.refs_0_), channel_id=1, source_target_pairs={{1,2},{2,1},{5,6},{6,5},{9,10},{10,9},{13,14},{14,13},{17,18},{18,... | collective-permute-start | bytes 983048 | tf_op jit(solution)/shard_map/ppermute | solution.py:299
  12.3 11.9 %collective-permute-start.4 = (bf16[32,5120]{1,0:T(8,128)(2,1)S(1)}, bf16[32,5120]{1,0:T(8,128)(2,1)S(1)}, u32[]{:S(2)}, u32[]{:S(2)}) collective-permute-start(bf16[32,5120]{1,0:T(8,128)(2,1)S(1)} %collective-permute-done.3.refs_1_), channel_id=1, source_target_pairs={{0,1},{1,0},{2,3},{3,2},{4,5},{5,4},{6,7},{7,6},{8,9},{9,8},{10,11... | collective-permute-start | bytes 983048 | tf_op jit(solution)/shard_map/ppermute | solution.py:300
  18.9 11.6 %collective-permute-start.2 = (bf16[32,5120]{1,0:T(8,128)(2,1)S(1)}, bf16[32,5120]{1,0:T(8,128)(2,1)S(1)}, u32[]{:S(2)}, u32[]{:S(2)}) collective-permute-start(bf16[32,5120]{1,0:T(8,128)(2,1)S(1)} %collective-permute-done.1.refs_1_), channel_id=1, source_target_pairs={{0,1},{1,0},{2,3},{3,2},{4,5},{5,4},{6,7},{7,6},{8,9},{9,8},{10,11... | collective-permute-start | bytes 983048 | tf_op jit(solution)/shard_map/ppermute | solution.py:303
  32.5 1.5 %collective-permute-start.6 = (f32[8,5120]{1,0:T(8,128)S(1)}, f32[8,5120]{1,0:T(8,128)S(1)}, u32[]{:S(2)}, u32[]{:S(2)}) collective-permute-start(f32[8,5120]{1,0:T(8,128)S(1)} %get-tuple-element.69), channel_id=1, source_target_pairs={{0,4},{4,0},{8,12},{12,8},{16,20},{20,16},{24,28},{28,24},{1,5},{5... | collective-permute-start | bytes 491528 | tf_op jit(solution)/shard_map/ppermute | solution.py:308
  32.5 3.0 %collective-permute-start.8 = (f32[8,5120]{1,0:T(8,128)S(1)}, f32[8,5120]{1,0:T(8,128)S(1)}, u32[]{:S(2)}, u32[]{:S(2)}) collective-permute-start(f32[8,5120]{1,0:T(8,128)S(1)} %get-tuple-element.71), channel_id=1, source_target_pairs={{0,4},{4,0},{8,12},{12,8},{16,20},{20,16},{24,28},{28,24},{1,5},{5... | collective-permute-start | bytes 491528 | tf_op jit(solution)/shard_map/ppermute | solution.py:308
  33.0 4.1 %collective-permute-start.10 = (f32[8,5120]{1,0:T(8,128)S(1)}, f32[8,5120]{1,0:T(8,128)S(1)}, u32[]{:S(2)}, u32[]{:S(2)}) collective-permute-start(f32[8,5120]{1,0:T(8,128)S(1)} %get-tuple-element.73), channel_id=1, source_target_pairs={{0,4},{4,0},{8,12},{12,8},{16,20},{20,16},{24,28},{28,24},{1,5},{5... | collective-permute-start | bytes 491528 | tf_op jit(solution)/shard_map/ppermute | solution.py:308
  33.9 7.1 %collective-permute-start.7 = (f32[8,5120]{1,0:T(8,128)S(1)}, f32[8,5120]{1,0:T(8,128)S(1)}, u32[]{:S(2)}, u32[]{:S(2)}) collective-permute-start(f32[8,5120]{1,0:T(8,128)S(1)} %add.34), channel_id=1, source_target_pairs={{0,8},{4,12},{8,0},{12,4},{16,24},{20,28},{24,16},{28,20},{1,9},{5... | collective-permute-start | bytes 491528 | tf_op jit(solution)/shard_map/ppermute | solution.py:308
  35.5 9.5 %collective-permute-start.9 = (f32[8,5120]{1,0:T(8,128)S(1)}, f32[8,5120]{1,0:T(8,128)S(1)}, u32[]{:S(2)}, u32[]{:S(2)}) collective-permute-start(f32[8,5120]{1,0:T(8,128)S(1)} %add.35), channel_id=1, source_target_pairs={{0,16},{4,20},{8,24},{12,28},{16,0},{20,4},{24,8},{28,12},{1,17},{... | collective-permute-start | bytes 491528 | tf_op jit(solution)/shard_map/ppermute | solution.py:308
  37.1 7.9 %collective-permute-start.11 = (f32[8,5120]{1,0:T(8,128)S(1)}, f32[8,5120]{1,0:T(8,128)S(1)}, u32[]{:S(2)}, u32[]{:S(2)}) collective-permute-start(f32[8,5120]{1,0:T(8,128)S(1)} %add.36), channel_id=1, source_target_pairs={{0,24},{4,28},{8,16},{12,20},{16,8},{20,12},{24,0},{28,4},{1,25},{... | collective-permute-start | bytes 491528 | tf_op jit(solution)/shard_map/ppermute | solution.py:308
  37.7 7.4 %collective-permute-start.5 = (f32[8,5120]{1,0:T(8,128)S(1)}, f32[8,5120]{1,0:T(8,128)S(1)}, u32[]{:S(2)}, u32[]{:S(2)}) collective-permute-start(f32[8,5120]{1,0:T(8,128)S(1)} %get-tuple-element.67), channel_id=1, source_target_pairs={{0,4},{4,0},{8,12},{12,8},{16,20},{20,16},{24,28},{28,24},{1,5},{5... | collective-permute-start | bytes 491528 | tf_op jit(solution)/shard_map/ppermute | solution.py:308
  45.1 7.8 %collective-permute-start.17 = (f32[8,5120]{1,0:T(8,128)S(1)}, f32[8,5120]{1,0:T(8,128)S(1)}, u32[]{:S(2)}, u32[]{:S(2)}) collective-permute-start(f32[8,5120]{1,0:T(8,128)S(1)} %add_add_fusion.refs_0_), channel_id=1, source_target_pairs={{0,24},{4,28},{8,16},{12,20},{16,8},{20,12},{24,0},{28,4},{1,25},{... | collective-permute-start | bytes 491528 | tf_op jit(solution)/shard_map/ppermute | solution.py:308
  46.7 8.0 %collective-permute-start.15 = (f32[8,5120]{1,0:T(8,128)S(1)}, f32[8,5120]{1,0:T(8,128)S(1)}, u32[]{:S(2)}, u32[]{:S(2)}) collective-permute-start(f32[8,5120]{1,0:T(8,128)S(1)} %add_add_fusion.refs_0_), channel_id=1, source_target_pairs={{0,16},{4,20},{8,24},{12,28},{16,0},{20,4},{24,8},{28,12},{1,17},{... | collective-permute-start | bytes 491528 | tf_op jit(solution)/shard_map/ppermute | solution.py:308
  47.8 7.0 %collective-permute-start.13 = (f32[8,5120]{1,0:T(8,128)S(1)}, f32[8,5120]{1,0:T(8,128)S(1)}, u32[]{:S(2)}, u32[]{:S(2)}) collective-permute-start(f32[8,5120]{1,0:T(8,128)S(1)} %add_add_fusion.refs_0_), channel_id=1, source_target_pairs={{0,8},{4,12},{8,0},{12,4},{16,24},{20,28},{24,16},{28,20},{1,9},{5... | collective-permute-start | bytes 491528 | tf_op jit(solution)/shard_map/ppermute | solution.py:308
  48.7 6.5 %collective-permute-start.12 = (f32[8,5120]{1,0:T(8,128)S(1)}, f32[8,5120]{1,0:T(8,128)S(1)}, u32[]{:S(2)}, u32[]{:S(2)}) collective-permute-start(f32[8,5120]{1,0:T(8,128)S(1)} %add_add_fusion.refs_0_), channel_id=1, source_target_pairs={{0,4},{4,0},{8,12},{12,8},{16,20},{20,16},{24,28},{28,24},{1,5},{5... | collective-permute-start | bytes 491528 | tf_op jit(solution)/shard_map/ppermute | solution.py:308
  53.0 2.2 %collective-permute-start.18 = (f32[8,5120]{1,0:T(8,128)S(1)}, f32[8,5120]{1,0:T(8,128)S(1)}, u32[]{:S(2)}, u32[]{:S(2)}) collective-permute-start(f32[8,5120]{1,0:T(8,128)S(1)} %collective-permute-done.17.refs_6_), channel_id=1, source_target_pairs={{0,4},{4,0},{8,12},{12,8},{16,20},{20,16},{24,28},{28,24},{1,5},{5... | collective-permute-start | bytes 491528 | tf_op jit(solution)/shard_map/ppermute | solution.py:308
  54.7 1.4 %collective-permute-start.16 = (f32[8,5120]{1,0:T(8,128)S(1)}, f32[8,5120]{1,0:T(8,128)S(1)}, u32[]{:S(2)}, u32[]{:S(2)}) collective-permute-start(f32[8,5120]{1,0:T(8,128)S(1)} %collective-permute-done.15.refs_4_), channel_id=1, source_target_pairs={{0,4},{4,0},{8,12},{12,8},{16,20},{20,16},{24,28},{28,24},{1,5},{5... | collective-permute-start | bytes 491528 | tf_op jit(solution)/shard_map/ppermute | solution.py:308
  54.8 1.6 %collective-permute-start.14 = (f32[8,5120]{1,0:T(8,128)S(1)}, f32[8,5120]{1,0:T(8,128)S(1)}, u32[]{:S(2)}, u32[]{:S(2)}) collective-permute-start(f32[8,5120]{1,0:T(8,128)S(1)} %collective-permute-done.13.refs_2_), channel_id=1, source_target_pairs={{0,4},{4,0},{8,12},{12,8},{16,20},{20,16},{24,28},{28,24},{1,5},{5... | collective-permute-start | bytes 491528 | tf_op jit(solution)/shard_map/ppermute | solution.py:308
  58.3 1.3 %collective-permute-start.19 = (f32[32,512]{1,0:T(8,128)S(1)}, f32[32,512]{1,0:T(8,128)S(1)}, u32[]{:S(2)}, u32[]{:S(2)}) collective-permute-start(f32[32,512]{1,0:T(8,128)S(1)} %get-tuple-element.85), channel_id=1, source_target_pairs={{0,4},{4,0},{8,12},{12,8},{16,20},{20,16},{24,28},{28,24},{1,5},{5... | collective-permute-start | bytes 196616 | tf_op jit(solution)/shard_map/ppermute | solution.py:308
  59.7 7.4 %collective-permute-start.22 = (f32[32,512]{1,0:T(8,128)S(1)}, f32[32,512]{1,0:T(8,128)S(1)}, u32[]{:S(2)}, u32[]{:S(2)}) collective-permute-start(f32[32,512]{1,0:T(8,128)S(1)} %add.40), channel_id=1, source_target_pairs={{0,24},{4,28},{8,16},{12,20},{16,8},{20,12},{24,0},{28,4},{1,25},{... | collective-permute-start | bytes 196616 | tf_op jit(solution)/shard_map/ppermute | solution.py:308
  61.2 5.9 %collective-permute-start.21 = (f32[32,512]{1,0:T(8,128)S(1)}, f32[32,512]{1,0:T(8,128)S(1)}, u32[]{:S(2)}, u32[]{:S(2)}) collective-permute-start(f32[32,512]{1,0:T(8,128)S(1)} %add.40), channel_id=1, source_target_pairs={{0,16},{4,20},{8,24},{12,28},{16,0},{20,4},{24,8},{28,12},{1,17},{... | collective-permute-start | bytes 196616 | tf_op jit(solution)/shard_map/ppermute | solution.py:308
  62.7 4.5 %collective-permute-start.20 = (f32[32,512]{1,0:T(8,128)S(1)}, f32[32,512]{1,0:T(8,128)S(1)}, u32[]{:S(2)}, u32[]{:S(2)}) collective-permute-start(f32[32,512]{1,0:T(8,128)S(1)} %add.40), channel_id=1, source_target_pairs={{0,8},{4,12},{8,0},{12,4},{16,24},{20,28},{24,16},{28,20},{1,9},{5... | collective-permute-start | bytes 196616 | tf_op jit(solution)/shard_map/ppermute | solution.py:308
  67.1 1.3 %collective-permute-start.23 = (f32[32,512]{1,0:T(8,128)S(1)}, f32[32,512]{1,0:T(8,128)S(1)}, u32[]{:S(2)}, u32[]{:S(2)}) collective-permute-start(f32[32,512]{1,0:T(8,128)S(1)} %add_add_fusion.1.refs_0_), channel_id=1, source_target_pairs={{0,4},{4,0},{8,12},{12,8},{16,20},{20,16},{24,28},{28,24},{1,5},{5... | collective-permute-start | bytes 196616 | tf_op jit(solution)/shard_map/ppermute | solution.py:308

commit v5 on v4

--- a/solution.py
+++ b/solution.py
@@ -77,6 +77,13 @@
             @pl.when(jnp.logical_not(at_end))
             def _():
                 out[here, :] = pieces[second][...]
+
+
+def begin_kernel(w, end, between, _, bx, hidden):
+    cut = end.shape[1]
+    x = bx.at[bx.shape[0] - end.shape[0]:, :cut]
+    pick([end, between.at[:, :cut]], [(0, 1)], x)
+    hidden[...] = jnp.dot(x[...], w[:cut, :], preferred_element_type=F32)
 
 
 def weigh_rows(lengths, assign, rewards, upstream, order, weighted):
@@ -147,14 +154,22 @@
         copy.wait()
 
 
-def next_kernel(n_x, choices, first_row, ready, *refs):
-    pieces, (w, weighted, q3, before, _, _, bx, g, *outs) = refs[:n_x], refs[n_x:]
+def next_kernel(n_x, choices, first_row, ready, cut, *refs):
+    pieces, (w, weighted, q3, before, *refs) = refs[:n_x], refs[n_x:]
+    (begun,), refs = (refs[:1], refs[1:]) if cut else ((None,), refs)
+    _, _, bx, g, *outs = refs
     count = ready + len(choices) * pieces[0].shape[0]
     top = bx.shape[0] - g.shape[0] + first_row
     x = bx.at[top:top + count, :]
     here = slice(first_row, first_row + count)
-    pick(pieces, choices, bx.at[top + ready:top + count, :])
-    tangent = jnp.tanh(jnp.dot(x[...], w[...], preferred_element_type=F32))
+    if cut:
+        pick([pieces[0], pieces[1].at[:, cut:]], choices, bx.at[top + ready:top + count, cut:])
+    else:
+        pick(pieces, choices, bx.at[top + ready:top + count, :])
+    hidden = jnp.dot(x[:, cut:], w[cut:, :], preferred_element_type=F32)
+    if cut:
+        hidden = begun[...] + hidden
+    tangent = jnp.tanh(hidden)
     grad = (weighted[here, :] * (1.0 - tangent * tangent)).astype(BF16)
     g[here, :] = grad
     yt = split(fold(dot(q3[...], grad, NT), 3), 3)
@@ -192,9 +207,10 @@
     block = pk.shape[1] // ids.shape[1]
     for k in range(ids.shape[1]):
         pk[:, k * block:(k + 1) * block] = bx[:2 * rank, lanes(ids[0, k], block)]
-    both = fold(dot(bx[:2 * rank, :], bx[...], NT), 2)
-    gram[...] = both[:, :rank] + both[:, rank:2 * rank]
-    total = fold(dot(split(both[:, 2 * rank:], 3), g[...], NN), 3)
+    both = dot(bx[...], bx[:2 * rank, :], NT)
+    both = both[:, :rank] + both[:, rank:]
+    gram[...] = fold(both[:2 * rank], 2)
+    total = fold(dot(split(jnp.transpose(both[2 * rank:]), 3), g[...], NN), 3)
     total = total + fold(dot(pk[...], r2[0], NN), 2) + dot(pk[:rank, :], r2[1], NN)
     if len(uts) == 1:
         uts[0][...] = total
@@ -242,12 +258,14 @@
     return jnp.concatenate(out, axis=0)
 
 
-def factor_kernel(ids, gram, bx, pft, linv, blocks):
-    rank = gram.shape[0]
-    inverse = inverse_factor(gram[...])
-    linv[...] = inverse
-    high = inverse.astype(BF16)
-    low = (inverse - high.astype(F32)).astype(BF16)
+def factor_kernel(gram, linv):
+    linv[...] = inverse_factor(gram[...])
+
+
+def left_kernel(ids, linv, bx, pft, blocks):
+    rank = linv.shape[0]
+    high = linv[...].astype(BF16)
+    low = (linv[...] - high.astype(F32)).astype(BF16)
     lhs = jnp.concatenate([jnp.concatenate([high, high], axis=1), jnp.concatenate([low, jnp.zeros_like(low)], axis=1)], axis=0)
     wide = 1024
     for i in range(pft.shape[1] // wide):
@@ -262,7 +280,7 @@
 
 
 def last_kernel(n_u, scale, *refs):
-    halves, (linv, blocks, merged, qt, out, ut, made, sent) = refs[:n_u], refs[n_u:]
+    halves, (linv, blocks, merged, qt, out, ut, right, made, sent) = refs[:n_u], refs[n_u:]
     if n_u == 1:
         ut[...] = halves[0][...]
     else:
@@ -270,12 +288,13 @@
         ut[lanes(core, rows), :] = halves[0][...]
         ut[lanes(1 - core, rows), :] = halves[1][...]
     q = dot(linv[...], ut[...], NN, HIGHEST) * scale
-    qt[...] = q
+    right[...] = q
+    copies = [pltpu.make_async_copy(right, qt, sent.at[merged.shape[0]])]
+    copies[0].start()
     two = split(q, 2)
     rank = q.shape[0]
     rhs = jnp.concatenate([two[:rank], two[:rank], two[rank:]], axis=0)
     block = merged.shape[1]
-    copies = []
     for k in range(merged.shape[0]):
         made[k] = merged[k] - dot(blocks[k * block:(k + 1) * block, :], rhs, NN)
         copies.append(pltpu.make_async_copy(made.at[k], out.at[k], sent.at[k]))
@@ -300,8 +319,9 @@
     a1 = lax.ppermute(b0, "mp", outer)
     done = first_stage([a0], [(0, None)], x.shape[0])
     b1, *done = together(b1, *done)
-    a2 = lax.ppermute(b1, "mp", outer)
-    return done, [([a1, b0], [(0, 1)]), ([a2, b1], [(0, 1)])]
+    cut = x.shape[1] * 3 // 4
+    a2 = [lax.ppermute(part, "mp", outer) for part in (b1[:, :cut], b1[:, cut:])]
+    return done, [([a1, b0], [(0, 1)]), ([a2[0], b1], [(0, 1)]), ([a2[1], b1], [(0, 1)])]
 
 
 def swap(a, bit, size):
@@ -335,23 +355,27 @@
          pltpu.SemaphoreType.DMA((9,))], name="prepare", far=len(far), grant=PREPARE_GRANT,
     )(*far)
 
-    def stage(pieces, choices, first_row, ready, bx, g, pt, outs):
+    def stage(pieces, choices, first_row, ready, bx, g, pt, outs, begun=()):
         n = len(pieces)
+        cut = depth - pieces[0].shape[1]
         return call(
-            functools.partial(next_kernel, n, choices, first_row, ready), [wide_rows, grad_rows] + outs,
-            flops=2 * slot_count * depth * columns, name="rows", aliases={n + 4: 0, n + 5: 1},
-        )(*pieces, weight, weighted, q3, pt, bx, g)
+            functools.partial(next_kernel, n, choices, first_row, ready, cut), [wide_rows, grad_rows] + outs,
+            flops=2 * slot_count * depth * columns, name="rows", aliases={n + 4 + len(begun): 0, n + 5 + len(begun): 1},
+        )(*pieces, weight, weighted, q3, pt, *begun, bx, g)
 
     whole_rank = [shape((rank, depth), F32)]
     (bx, g, pt), stages = gather_rows(
         gen_rows, groups, weighted,
         lambda pieces, choices, ready: stage(pieces, choices, 0, ready, bx, jnp.zeros(grad_rows.shape, BF16), pt, whole_rank),
     )
-    for i, (pieces, choices) in enumerate(stages):
-        last = i == len(stages) - 1
-        outs = [shape((rank // replicas, depth), F32)] * replicas if last and direct else whole_rank
-        bx, g, *parts = stage(pieces, choices, rows - (len(stages) - i) * slot_count, 0, bx, g, pt, outs)
-        pt = parts[0]
+    final = [shape((rank // replicas, depth), F32)] * replicas if direct else whole_rank
+    bx, g, pt = stage(*stages[0], rows - 2 * slot_count, 0, bx, g, pt, whole_rank)
+    begun = ()
+    if len(stages) == 3:
+        bx, *begun = call(
+            begin_kernel, [wide_rows, shape((slot_count, columns), F32)], name="begin", aliases={3: 0},
+        )(weight, *stages[1][0], bx)
+    bx, g, *parts = stage(*stages[-1], rows - slot_count, 0, bx, g, pt, final, begun)
 
     merged = call(merged_kernel, shape((kept, block, columns), F32), name="merged")(ids, bx, g, resid)
 
@@ -377,25 +401,30 @@
         [pltpu.VMEM((2 * rank, kept * block), BF16)], name="second", aliases={n_p + 3: 0},
     )(ids, *p_parts, g, r2, bx)
 
-    pft, linv, blocks = call(
-        factor_kernel,
-        [shape((rank, depth), F32), shape((rank, rank), F32), shape((kept * block, 3 * rank), BF16)], name="factor",
-    )(ids, gram, bx)
+    linv = call(factor_kernel, shape((rank, rank), F32), name="factor")(gram)
 
     if direct:
         chip_sum = us[0] + swap(us[1], 1, replicas)
         got = [swap(chip_sum, 2 * k, replicas) for k in range(1, chips)]
         *got, linv = together(*got, linv)
         total = chip_sum + got[0] + got[1] + got[2]
+        bx, total = together(bx, total)
         u_parts = [total, swap(total, 1, replicas)]
     else:
         u_parts = [lax.psum(us[0], "dp")]
+    pft, blocks = call(
+        left_kernel, [shape((rank, depth), F32), shape((kept * block, 3 * rank), BF16)], name="left",
+    )(ids, linv, bx)
+    if direct:
+        other, blocks = together(u_parts[1], blocks)
+        u_parts = [u_parts[0], other]
     n_u = len(u_parts)
     qt, new_resid = call(
         functools.partial(last_kernel, n_u, 1.0 / replicas),
         [shape((rank, columns), F32), shape((kept, block, columns), F32)],
-        [pltpu.VMEM((rank, columns), F32), pltpu.VMEM((kept, block, columns), F32), pltpu.SemaphoreType.DMA((kept,))],
-        name="last", out_specs=[VMEM, pl.BlockSpec(memory_space=pl.ANY)],
+        [pltpu.VMEM((rank, columns), F32), pltpu.VMEM((rank, columns), F32),
+         pltpu.VMEM((kept, block, columns), F32), pltpu.SemaphoreType.DMA((kept + 1,))],
+        name="last", out_specs=[pl.BlockSpec(memory_space=pl.ANY)] * 2,
     )(*u_parts, linv, blocks, merged)
     return pft.T, qt.T, new_resid
 

time: 70.8 us -> 69.6 us (0.983)
  waiting for transfers between devices: 26.1 us -> 25.2 us
    ppermute x1 -> x2, waiting for transfers between devices: 4.39 us -> 3.71 us  [gather_rows(): lax.ppermute(part, 'mp', outer)]
    pallas_call x8 -> x10, Pallas kernels: 17.2 us -> 16.7 us  [run(): pl.pallas_call(kernel, input_output_aliases=aliases or {}, out_shape=outs...]
    ppermute x1 -> x2, starting transfers between devices: 4.95 us -> 5.1 us  [gather_rows(): lax.ppermute(part, 'mp', outer)]
  transfers between devices with their start and end apart: 24 -> 25, of which waited for: 13 -> 14; matrix products, arithmetic and copies ran while one was open for 0% -> 0% of each run, Pallas kernels for 16% -> 17%
where the time goes in v5:
time: 69.6 us; the launch traced here: 69.4 us
  starting transfers between devices  26.5 us (38%)
  waiting for transfers between devices  25.2 us (36%)
  Pallas kernels  16.7 us (24%)
  between operations  0.77 us (1%)
    ppermute x19, waiting for transfers between devices, swap(): return lax.ppermute(a, 'dp', [(i, i ^ bit) for i in range(size)])  17.3 us
    pallas_call x10, Pallas kernels, run(): pl.pallas_call(kernel, input_output_aliases=aliases or {}, out_shape=outs...  16.7 us
    ppermute x19, starting transfers between devices, swap(): return lax.ppermute(a, 'dp', [(i, i ^ bit) for i in range(size)])  12.3 us
    ppermute x2, starting transfers between devices, gather_rows(): lax.ppermute(part, 'mp', outer)  5.1 us
    ppermute x1, starting transfers between devices, gather_rows(): a1 = lax.ppermute(b0, 'mp', outer)  4.61 us
    ppermute x1, waiting for transfers between devices, gather_rows(): a0 = lax.ppermute(x, 'mp', outer)  4.12 us
    ppermute x2, waiting for transfers between devices, gather_rows(): lax.ppermute(part, 'mp', outer)  3.71 us
    ppermute x1, starting transfers between devices, gather_rows(): a0 = lax.ppermute(x, 'mp', outer)  3.09 us
  transfers between devices with their start and end apart: 25, of which 14 were waited for; matrix products, arithmetic and copies ran while one was open for 0% of the time, Pallas kernels for 17%

profile of v5, /device:TPU:0, one launch (start us, length us, event | category | flops | bytes accessed | tf_op | source)
XLA Modules:
  0.0 69.4 jit_solution(17316209866720398402)
XLA Ops:
  0.6 3.1 %collective-permute-start = (bf16[32,5120]{1,0:T(8,128)(2,1)}, bf16[32,5120]{1,0:T(8,128)(2,1)S(1)}, u32[]{:S(2)}, u32[]{:S(2)}) collective-permute-start(bf16[32,5120]{1,0:T(8,128)(2,1)} %refs_8_.1), channel_id=1, source_target_pairs={{0,1},{1,0},{2,3},{3,2},{4,5},{5,4},{6,7},{7,6},{8,9},{9,8},{10,11... | collective-permute-start | bytes 983048 | tf_op jit(solution)/shard_map/ppermute | solution.py:315
  3.7 0.7 collective-permute-start.3
  4.4 3.1 %prepare.1 = (s32[1,4]{1,0:T(1,128)S(1)}, bf16[5120,512]{1,0:T(8,128)(2,1)S(1)}, f32[4,128,512]{2,1,0:T(8,128)S(1)}, bf16[256,5120]{1,0:T(8,128)(2,1)S(1)}, f32[...) custom-call(s32[4,4]{1,0:T(4,128)} %refs_0_.1, ...), custom_call_target="tpu_custom_call" | custom-call | flops 1000000 | bytes 1000000 | tf_op jit(solution)/shard_map/prepare/pallas_call | solution.py:48
  7.5 4.1 %collective-permute-done.refs_0_ = bf16[32,5120]{1,0:T(8,128)(2,1)S(1)} collective-permute-done((bf16[32,5120]{1,0:T(8,128)(2,1)}, bf16[32,5120]{1,0:T(8,128)(2,1)S(1)}, u32[]{:S(2)}, u32[]{:S(2)}) %collective-permute-start) | collective-permute-done | bytes 327712 | tf_op jit(solution)/shard_map/ppermute | solution.py:315
  11.6 0.7 collective-permute-start.1
  12.3 0.0 collective-permute-done.3.refs_1_
  12.3 4.6 %collective-permute-start.4 = (bf16[32,5120]{1,0:T(8,128)(2,1)S(1)}, bf16[32,5120]{1,0:T(8,128)(2,1)S(1)}, u32[]{:S(2)}, u32[]{:S(2)}) collective-permute-start(bf16[32,5120]{1,0:T(8,128)(2,1)S(1)} %collective-permute-done.3.refs_1_), channel_id=1, source_target_pairs={{0,1},{1,0},{2,3},{3,2},{4,5},{5,4},{6,7},{7,6},{8,9},{9,8},{10,11... | collective-permute-start | bytes 983048 | tf_op jit(solution)/shard_map/ppermute | solution.py:319
  17.0 1.9 %rows.3 = (bf16[256,5120]{1,0:T(8,128)(2,1)S(1)}, bf16[128,512]{1,0:T(8,128)(2,1)S(1)}, f32[64,5120]{1,0:T(8,128)S(1)}) custom-call(bf16[32,5120]{1,0:T(8,128)(2,1)S(1)} %collective-permute-done.refs_0_, bf16[5120,512]{1,0:T(8,128)(2,1)S(1)} %get-tuple-element.57.refs_1_.refs_2_.w, ...), custom_call_target="tpu_custom_call", output_to_operand_aliasing={{0}: (5, {}), {1}: (6, {})} | custom-call | flops 167772160 | bytes 1000000 | tf_op jit(solution)/shard_map/rows/pallas_call | solution.py:48
  18.9 5.0 %collective-permute-start.5 = (bf16[32,3840]{1,0:T(8,128)(2,1)S(1)}, bf16[32,3840]{1,0:T(8,128)(2,1)S(1)}, u32[]{:S(2)}, u32[]{:S(2)}) collective-permute-start(bf16[32,3840]{1,0:T(8,128)(2,1)S(1)} %slice.7), channel_id=1, source_target_pairs={{0,1},{1,0},{2,3},{3,2},{4,5},{5,4},{6,7},{7,6},{8,9},{9,8},{10,11... | collective-permute-start | bytes 737288 | tf_op jit(solution)/shard_map/ppermute | solution.py:323
  23.9 0.1 collective-permute-start.2
  24.0 0.1 collective-permute-done.4.refs_0_
  24.1 1.9 %rows.4 = (bf16[256,5120]{1,0:T(8,128)(2,1)S(1)}, bf16[128,512]{1,0:T(8,128)(2,1)S(1)}, f32[64,5120]{1,0:T(8,128)S(1)}) custom-call(bf16[32,5120]{1,0:T(8,128)(2,1)S(1)} %collective-permute-done.4.refs_0_, bf16[32,5120]{1,0:T(8,128)(2,1)S(1)} %collective-permute-done.3.refs_1_, ...), custom_call_target="tpu_custom_call", output_to_operand_aliasing={{0}: (6, {}), {1}: (7, {})} | custom-call | flops 167772160 | bytes 1000000 | tf_op jit(solution)/shard_map/rows/pallas_call | solution.py:48
  26.0 3.6 %collective-permute-done.5.end = bf16[32,3840]{1,0:T(8,128)(2,1)S(1)} collective-permute-done((bf16[32,3840]{1,0:T(8,128)(2,1)S(1)}, bf16[32,3840]{1,0:T(8,128)(2,1)S(1)}, u32[]{:S(2)}, u32[]{:S(2)}) %collective-permute-start.5) | collective-permute-done | bytes 245792 | tf_op jit(solution)/shard_map/ppermute | solution.py:323
  29.6 0.8 %begin.1 = (bf16[256,5120]{1,0:T(8,128)(2,1)S(1)}, f32[32,512]{1,0:T(8,128)S(1)}) custom-call(bf16[5120,512]{1,0:T(8,128)(2,1)S(1)} %get-tuple-element.57.refs_1_.refs_2_.w, bf16[32,3840]{1,0:T(8,128)(2,1)S(1)} %collective-permute-done.5.end, bf16[32,5120]{1,0:T(8,128)(2,1)S(1)} %collective-permute-done.1.between.refs_1_, ...), custom_call_target="tpu_custom_call", output_to_operand_aliasing={{0}: (3, {})} | custom-call | flops 1000000 | bytes 1000000 | tf_op jit(solution)/shard_map/begin/pallas_call | solution.py:48
  30.4 0.1 collective-permute-done.2.refs_0_
  30.5 1.2 %rows.5 = (bf16[256,5120]{1,0:T(8,128)(2,1)S(1)}, bf16[128,512]{1,0:T(8,128)(2,1)S(1)}, f32[8,5120]{1,0:T(8,128)S(1)}, f32[8,5120]{1,0:T(8,128)S(1)}, f32[8,5120...) custom-call(bf16[32,1280]{1,0:T(8,128)(2,1)S(1)} %collective-permute, ...), custom_call_target="tpu_custom_call", output_to_operand_aliasing={{0}: (7, {}), {1}: (8, {})} | custom-call | flops 167772160 | bytes 1000000 | tf_op jit(solution)/shard_map/rows/pallas_call | solution.py:48
  31.8 0.1 collective-permute-start.7
  31.8 0.5 collective-permute-start.9
  32.3 0.1 collective-permute-start.11
  32.4 0.8 %collective-permute-done.7 = f32[8,5120]{1,0:T(8,128)S(1)} collective-permute-done((f32[8,5120]{1,0:T(8,128)S(1)}, f32[8,5120]{1,0:T(8,128)S(1)}, u32[]{:S(2)}, u32[]{:S(2)}) %collective-permute-start.7) | collective-permute-done | bytes 163872 | tf_op jit(solution)/shard_map/ppermute | solution.py:328
  33.3 1.6 %collective-permute-start.8 = (f32[8,5120]{1,0:T(8,128)S(1)}, f32[8,5120]{1,0:T(8,128)S(1)}, u32[]{:S(2)}, u32[]{:S(2)}) collective-permute-start(f32[8,5120]{1,0:T(8,128)S(1)} %add.34), channel_id=1, source_target_pairs={{0,8},{4,12},{8,0},{12,4},{16,24},{20,28},{24,16},{28,20},{1,9},{5... | collective-permute-start | bytes 491528 | tf_op jit(solution)/shard_map/ppermute | solution.py:328
  34.8 1.6 %collective-permute-start.10 = (f32[8,5120]{1,0:T(8,128)S(1)}, f32[8,5120]{1,0:T(8,128)S(1)}, u32[]{:S(2)}, u32[]{:S(2)}) collective-permute-start(f32[8,5120]{1,0:T(8,128)S(1)} %add.35), channel_id=1, source_target_pairs={{0,16},{4,20},{8,24},{12,28},{16,0},{20,4},{24,8},{28,12},{1,17},{... | collective-permute-start | bytes 491528 | tf_op jit(solution)/shard_map/ppermute | solution.py:328
  36.5 0.5 collective-permute-start.12
  37.0 0.4 merged.1.refs_4_
  37.4 3.0 %collective-permute-done.8 = f32[8,5120]{1,0:T(8,128)S(1)} collective-permute-done((f32[8,5120]{1,0:T(8,128)S(1)}, f32[8,5120]{1,0:T(8,128)S(1)}, u32[]{:S(2)}, u32[]{:S(2)}) %collective-permute-start.8) | collective-permute-done | bytes 163872 | tf_op jit(solution)/shard_map/ppermute | solution.py:328
  40.4 4.0 %collective-permute-done.10 = f32[8,5120]{1,0:T(8,128)S(1)} collective-permute-done((f32[8,5120]{1,0:T(8,128)S(1)}, f32[8,5120]{1,0:T(8,128)S(1)}, u32[]{:S(2)}, u32[]{:S(2)}) %collective-permute-start.10) | collective-permute-done | bytes 163872 | tf_op jit(solution)/shard_map/ppermute | solution.py:328
  44.4 0.1 add_add_fusion.refs_0_
  44.5 1.6 %collective-permute-start.18 = (f32[8,5120]{1,0:T(8,128)S(1)}, f32[8,5120]{1,0:T(8,128)S(1)}, u32[]{:S(2)}, u32[]{:S(2)}) collective-permute-start(f32[8,5120]{1,0:T(8,128)S(1)} %add_add_fusion.refs_0_), channel_id=1, source_target_pairs={{0,24},{4,28},{8,16},{12,20},{16,8},{20,12},{24,0},{28,4},{1,25},{... | collective-permute-start | bytes 491528 | tf_op jit(solution)/shard_map/ppermute | solution.py:328
  46.0 1.1 %collective-permute-start.16 = (f32[8,5120]{1,0:T(8,128)S(1)}, f32[8,5120]{1,0:T(8,128)S(1)}, u32[]{:S(2)}, u32[]{:S(2)}) collective-permute-start(f32[8,5120]{1,0:T(8,128)S(1)} %add_add_fusion.refs_0_), channel_id=1, source_target_pairs={{0,16},{4,20},{8,24},{12,28},{16,0},{20,4},{24,8},{28,12},{1,17},{... | collective-permute-start | bytes 491528 | tf_op jit(solution)/shard_map/ppermute | solution.py:328
  47.1 0.9 %collective-permute-start.14 = (f32[8,5120]{1,0:T(8,128)S(1)}, f32[8,5120]{1,0:T(8,128)S(1)}, u32[]{:S(2)}, u32[]{:S(2)}) collective-permute-start(f32[8,5120]{1,0:T(8,128)S(1)} %add_add_fusion.refs_0_), channel_id=1, source_target_pairs={{0,8},{4,12},{8,0},{12,4},{16,24},{20,28},{24,16},{28,20},{1,9},{5... | collective-permute-start | bytes 491528 | tf_op jit(solution)/shard_map/ppermute | solution.py:328
  48.0 4.3 %collective-permute-done.18.refs_6_ = f32[8,5120]{1,0:T(8,128)S(1)} collective-permute-done((f32[8,5120]{1,0:T(8,128)S(1)}, f32[8,5120]{1,0:T(8,128)S(1)}, u32[]{:S(2)}, u32[]{:S(2)}) %collective-permute-start.18) | collective-permute-done | bytes 163872 | tf_op jit(solution)/shard_map/ppermute | solution.py:328
  52.3 1.7 %collective-permute-done.16.refs_4_ = f32[8,5120]{1,0:T(8,128)S(1)} collective-permute-done((f32[8,5120]{1,0:T(8,128)S(1)}, f32[8,5120]{1,0:T(8,128)S(1)}, u32[]{:S(2)}, u32[]{:S(2)}) %collective-permute-start.16) | collective-permute-done | bytes 163872 | tf_op jit(solution)/shard_map/ppermute | solution.py:328
  54.1 0.0 collective-permute-done.14.refs_2_
  54.1 0.5 collective-permute-start.15
  54.6 0.9 %collective-permute-done.17.refs_5_ = f32[8,5120]{1,0:T(8,128)S(1)} collective-permute-done((f32[8,5120]{1,0:T(8,128)S(1)}, f32[8,5120]{1,0:T(8,128)S(1)}, u32[]{:S(2)}, u32[]{:S(2)}) %collective-permute-start.17) | collective-permute-done | bytes 163872 | tf_op jit(solution)/shard_map/ppermute | solution.py:328
  55.4 0.2 collective-permute-done.15.refs_3_
  55.7 2.0 %second.1 = (bf16[256,5120]{1,0:T(8,128)(2,1)S(1)}, f32[64,64]{1,0:T(8,128)S(1)}, f32[32,512]{1,0:T(8,128)S(1)}, f32[32,512]{1,0:T(8,128)S(1)}) custom-call(s32[1,4]{1,0:T(1,128)S(1)} %get-tuple-element.54.ids, f32[8,5120]{1,0:T(8,128)S(1)} %add_add_fusion.refs_0_, f32[8,5120]{1,0:T(8,128)S(1)} %collective-permute-done.13.refs_1_, ...), custom_call_target="tpu_custom_call", output_to_operand_aliasing={{0}: (11, {})} | custom-call | flops 1000000 | bytes 1000000 | tf_op jit(solution)/shard_map/second/pallas_call | solution.py:48
  57.6 0.3 collective-permute-start.20
  58.0 1.0 %collective-permute-done.20 = f32[32,512]{1,0:T(8,128)S(1)} collective-permute-done((f32[32,512]{1,0:T(8,128)S(1)}, f32[32,512]{1,0:T(8,128)S(1)}, u32[]{:S(2)}, u32[]{:S(2)}) %collective-permute-start.20) | collective-permute-done | bytes 65568 | tf_op jit(solution)/shard_map/ppermute | solution.py:328
  59.0 1.5 %collective-permute-start.23 = (f32[32,512]{1,0:T(8,128)S(1)}, f32[32,512]{1,0:T(8,128)S(1)}, u32[]{:S(2)}, u32[]{:S(2)}) collective-permute-start(f32[32,512]{1,0:T(8,128)S(1)} %add.40), channel_id=1, source_target_pairs={{0,24},{4,28},{8,16},{12,20},{16,8},{20,12},{24,0},{28,4},{1,25},{... | collective-permute-start | bytes 196616 | tf_op jit(solution)/shard_map/ppermute | solution.py:328
  60.5 1.5 %collective-permute-start.22 = (f32[32,512]{1,0:T(8,128)S(1)}, f32[32,512]{1,0:T(8,128)S(1)}, u32[]{:S(2)}, u32[]{:S(2)}) collective-permute-start(f32[32,512]{1,0:T(8,128)S(1)} %add.40), channel_id=1, source_target_pairs={{0,16},{4,20},{8,24},{12,28},{16,0},{20,4},{24,8},{28,12},{1,17},{... | collective-permute-start | bytes 196616 | tf_op jit(solution)/shard_map/ppermute | solution.py:328
  62.0 0.6 collective-permute-start.21
  62.5 2.3 %factor.1.linv.refs_2_ = f32[64,64]{1,0:T(8,128)S(1)} custom-call(f32[64,64]{1,0:T(8,128)S(1)} %get-tuple-element.90.gram), custom_call_target="tpu_custom_call" | custom-call | flops 1000000 | bytes 1000000 | tf_op jit(solution)/shard_map/factor/pallas_call | solution.py:48
  64.9 0.8 %collective-permute-done.22 = f32[32,512]{1,0:T(8,128)S(1)} collective-permute-done((f32[32,512]{1,0:T(8,128)S(1)}, f32[32,512]{1,0:T(8,128)S(1)}, u32[]{:S(2)}, u32[]{:S(2)}) %collective-permute-start.22) | collective-permute-done | bytes 65568 | tf_op jit(solution)/shard_map/ppermute | solution.py:328
  65.6 0.6 collective-permute-done.21
  66.2 0.1 collective-permute-start.24
  66.3 1.6 %left.1 = (f32[64,5120]{1,0:T(8,128)}, bf16[512,192]{1,0:T(8,128)(2,1)S(1)}) custom-call(s32[1,4]{1,0:T(1,128)S(1)} %get-tuple-element.54.ids, f32[64,64]{1,0:T(8,128)S(1)} %factor.1.linv.refs_2_, bf16[256,5120]{1,0:T(8,128)(2,1)S(1)} %get-tuple-element.96.bx), custom_call_target="tpu_custom_call" | custom-call | flops 1000000 | bytes 1000000 | tf_op jit(solution)/shard_map/left/pallas_call | solution.py:48
  67.9 1.5 %last.1 = (f32[64,512]{1,0:T(8,128)}, f32[4,128,512]{2,1,0:T(8,128)}) custom-call(f32[32,512]{1,0:T(8,128)S(1)} %add_add_fusion.1.refs_0_, f32[32,512]{1,0:T(8,128)S(1)} %collective-permute-done.24.refs_1_, f32[64,64]{1,0:T(8,128)S(1)} %factor.1.linv.refs_2_, bf16[512,192]{1,0:T(8,128)(2,1)S(1)} %get-tuple-element.101.refs_3_, f32[4,128,512]{2,1,0:T(8,128)S(1)} %merged.1.refs_4_), custom_call_target="tpu_custom_call" | custom-call | flops 1000000 | bytes 1000000 | tf_op jit(solution)/shard_map/last/pallas_call | solution.py:48
  (21 shorter events, 0.2 us)
Async XLA Ops:
  0.6 11.0 %collective-permute-start = (bf16[32,5120]{1,0:T(8,128)(2,1)}, bf16[32,5120]{1,0:T(8,128)(2,1)S(1)}, u32[]{:S(2)}, u32[]{:S(2)}) collective-permute-start(bf16[32,5120]{1,0:T(8,128)(2,1)} %refs_8_.1), channel_id=1, source_target_pairs={{0,1},{1,0},{2,3},{3,2},{4,5},{5,4},{6,7},{7,6},{8,9},{9,8},{10,11... | collective-permute-start | bytes 983048 | tf_op jit(solution)/shard_map/ppermute | solution.py:315
  3.7 8.6 %collective-permute-start.3 = (bf16[32,5120]{1,0:T(8,128)(2,1)}, bf16[32,5120]{1,0:T(8,128)(2,1)S(1)}, u32[]{:S(2)}, u32[]{:S(2)}) collective-permute-start(bf16[32,5120]{1,0:T(8,128)(2,1)} %refs_8_.1), channel_id=1, source_target_pairs={{1,2},{2,1},{5,6},{6,5},{9,10},{10,9},{13,14},{14,13},{17,18},{18,... | collective-permute-start | bytes 983048 | tf_op jit(solution)/shard_map/ppermute | solution.py:316
  11.6 7.2 %collective-permute-start.1 = (bf16[32,5120]{1,0:T(8,128)(2,1)S(1)}, bf16[32,5120]{1,0:T(8,128)(2,1)S(1)}, u32[]{:S(2)}, u32[]{:S(2)}) collective-permute-start(bf16[32,5120]{1,0:T(8,128)(2,1)S(1)} %collective-permute-done.refs_0_), channel_id=1, source_target_pairs={{1,2},{2,1},{5,6},{6,5},{9,10},{10,9},{13,14},{14,13},{17,18},{18,... | collective-permute-start | bytes 983048 | tf_op jit(solution)/shard_map/ppermute | solution.py:318
  12.3 11.8 %collective-permute-start.4 = (bf16[32,5120]{1,0:T(8,128)(2,1)S(1)}, bf16[32,5120]{1,0:T(8,128)(2,1)S(1)}, u32[]{:S(2)}, u32[]{:S(2)}) collective-permute-start(bf16[32,5120]{1,0:T(8,128)(2,1)S(1)} %collective-permute-done.3.refs_1_), channel_id=1, source_target_pairs={{0,1},{1,0},{2,3},{3,2},{4,5},{5,4},{6,7},{7,6},{8,9},{9,8},{10,11... | collective-permute-start | bytes 983048 | tf_op jit(solution)/shard_map/ppermute | solution.py:319
  18.9 10.7 %collective-permute-start.5 = (bf16[32,3840]{1,0:T(8,128)(2,1)S(1)}, bf16[32,3840]{1,0:T(8,128)(2,1)S(1)}, u32[]{:S(2)}, u32[]{:S(2)}) collective-permute-start(bf16[32,3840]{1,0:T(8,128)(2,1)S(1)} %slice.7), channel_id=1, source_target_pairs={{0,1},{1,0},{2,3},{3,2},{4,5},{5,4},{6,7},{7,6},{8,9},{9,8},{10,11... | collective-permute-start | bytes 737288 | tf_op jit(solution)/shard_map/ppermute | solution.py:323
  23.9 6.6 %collective-permute-start.2 = (bf16[32,1280]{1,0:T(8,128)(2,1)S(1)}, bf16[32,1280]{1,0:T(8,128)(2,1)S(1)}, u32[]{:S(2)}, u32[]{:S(2)}) collective-permute-start(bf16[32,1280]{1,0:T(8,128)(2,1)S(1)} %slice.6), channel_id=1, source_target_pairs={{0,1},{1,0},{2,3},{3,2},{4,5},{5,4},{6,7},{7,6},{8,9},{9,8},{10,11... | collective-permute-start | bytes 245768 | tf_op jit(solution)/shard_map/ppermute | solution.py:323
  31.8 1.5 %collective-permute-start.7 = (f32[8,5120]{1,0:T(8,128)S(1)}, f32[8,5120]{1,0:T(8,128)S(1)}, u32[]{:S(2)}, u32[]{:S(2)}) collective-permute-start(f32[8,5120]{1,0:T(8,128)S(1)} %get-tuple-element.76), channel_id=1, source_target_pairs={{0,4},{4,0},{8,12},{12,8},{16,20},{20,16},{24,28},{28,24},{1,5},{5... | collective-permute-start | bytes 491528 | tf_op jit(solution)/shard_map/ppermute | solution.py:328
  31.8 3.0 %collective-permute-start.9 = (f32[8,5120]{1,0:T(8,128)S(1)}, f32[8,5120]{1,0:T(8,128)S(1)}, u32[]{:S(2)}, u32[]{:S(2)}) collective-permute-start(f32[8,5120]{1,0:T(8,128)S(1)} %get-tuple-element.78), channel_id=1, source_target_pairs={{0,4},{4,0},{8,12},{12,8},{16,20},{20,16},{24,28},{28,24},{1,5},{5... | collective-permute-start | bytes 491528 | tf_op jit(solution)/shard_map/ppermute | solution.py:328
  32.3 4.1 %collective-permute-start.11 = (f32[8,5120]{1,0:T(8,128)S(1)}, f32[8,5120]{1,0:T(8,128)S(1)}, u32[]{:S(2)}, u32[]{:S(2)}) collective-permute-start(f32[8,5120]{1,0:T(8,128)S(1)} %get-tuple-element.80), channel_id=1, source_target_pairs={{0,4},{4,0},{8,12},{12,8},{16,20},{20,16},{24,28},{28,24},{1,5},{5... | collective-permute-start | bytes 491528 | tf_op jit(solution)/shard_map/ppermute | solution.py:328
  33.3 7.1 %collective-permute-start.8 = (f32[8,5120]{1,0:T(8,128)S(1)}, f32[8,5120]{1,0:T(8,128)S(1)}, u32[]{:S(2)}, u32[]{:S(2)}) collective-permute-start(f32[8,5120]{1,0:T(8,128)S(1)} %add.34), channel_id=1, source_target_pairs={{0,8},{4,12},{8,0},{12,4},{16,24},{20,28},{24,16},{28,20},{1,9},{5... | collective-permute-start | bytes 491528 | tf_op jit(solution)/shard_map/ppermute | solution.py:328
  34.8 9.5 %collective-permute-start.10 = (f32[8,5120]{1,0:T(8,128)S(1)}, f32[8,5120]{1,0:T(8,128)S(1)}, u32[]{:S(2)}, u32[]{:S(2)}) collective-permute-start(f32[8,5120]{1,0:T(8,128)S(1)} %add.35), channel_id=1, source_target_pairs={{0,16},{4,20},{8,24},{12,28},{16,0},{20,4},{24,8},{28,12},{1,17},{... | collective-permute-start | bytes 491528 | tf_op jit(solution)/shard_map/ppermute | solution.py:328
  36.5 7.9 %collective-permute-start.12 = (f32[8,5120]{1,0:T(8,128)S(1)}, f32[8,5120]{1,0:T(8,128)S(1)}, u32[]{:S(2)}, u32[]{:S(2)}) collective-permute-start(f32[8,5120]{1,0:T(8,128)S(1)} %add.36), channel_id=1, source_target_pairs={{0,24},{4,28},{8,16},{12,20},{16,8},{20,12},{24,0},{28,4},{1,25},{... | collective-permute-start | bytes 491528 | tf_op jit(solution)/shard_map/ppermute | solution.py:328
  37.0 7.4 %collective-permute-start.6 = (f32[8,5120]{1,0:T(8,128)S(1)}, f32[8,5120]{1,0:T(8,128)S(1)}, u32[]{:S(2)}, u32[]{:S(2)}) collective-permute-start(f32[8,5120]{1,0:T(8,128)S(1)} %get-tuple-element.74), channel_id=1, source_target_pairs={{0,4},{4,0},{8,12},{12,8},{16,20},{20,16},{24,28},{28,24},{1,5},{5... | collective-permute-start | bytes 491528 | tf_op jit(solution)/shard_map/ppermute | solution.py:328
  44.5 7.9 %collective-permute-start.18 = (f32[8,5120]{1,0:T(8,128)S(1)}, f32[8,5120]{1,0:T(8,128)S(1)}, u32[]{:S(2)}, u32[]{:S(2)}) collective-permute-start(f32[8,5120]{1,0:T(8,128)S(1)} %add_add_fusion.refs_0_), channel_id=1, source_target_pairs={{0,24},{4,28},{8,16},{12,20},{16,8},{20,12},{24,0},{28,4},{1,25},{... | collective-permute-start | bytes 491528 | tf_op jit(solution)/shard_map/ppermute | solution.py:328
  46.0 8.0 %collective-permute-start.16 = (f32[8,5120]{1,0:T(8,128)S(1)}, f32[8,5120]{1,0:T(8,128)S(1)}, u32[]{:S(2)}, u32[]{:S(2)}) collective-permute-start(f32[8,5120]{1,0:T(8,128)S(1)} %add_add_fusion.refs_0_), channel_id=1, source_target_pairs={{0,16},{4,20},{8,24},{12,28},{16,0},{20,4},{24,8},{28,12},{1,17},{... | collective-permute-start | bytes 491528 | tf_op jit(solution)/shard_map/ppermute | solution.py:328
  47.1 7.0 %collective-permute-start.14 = (f32[8,5120]{1,0:T(8,128)S(1)}, f32[8,5120]{1,0:T(8,128)S(1)}, u32[]{:S(2)}, u32[]{:S(2)}) collective-permute-start(f32[8,5120]{1,0:T(8,128)S(1)} %add_add_fusion.refs_0_), channel_id=1, source_target_pairs={{0,8},{4,12},{8,0},{12,4},{16,24},{20,28},{24,16},{28,20},{1,9},{5... | collective-permute-start | bytes 491528 | tf_op jit(solution)/shard_map/ppermute | solution.py:328
  48.0 6.5 %collective-permute-start.13 = (f32[8,5120]{1,0:T(8,128)S(1)}, f32[8,5120]{1,0:T(8,128)S(1)}, u32[]{:S(2)}, u32[]{:S(2)}) collective-permute-start(f32[8,5120]{1,0:T(8,128)S(1)} %add_add_fusion.refs_0_), channel_id=1, source_target_pairs={{0,4},{4,0},{8,12},{12,8},{16,20},{20,16},{24,28},{28,24},{1,5},{5... | collective-permute-start | bytes 491528 | tf_op jit(solution)/shard_map/ppermute | solution.py:328
  52.3 2.2 %collective-permute-start.19 = (f32[8,5120]{1,0:T(8,128)S(1)}, f32[8,5120]{1,0:T(8,128)S(1)}, u32[]{:S(2)}, u32[]{:S(2)}) collective-permute-start(f32[8,5120]{1,0:T(8,128)S(1)} %collective-permute-done.18.refs_6_), channel_id=1, source_target_pairs={{0,4},{4,0},{8,12},{12,8},{16,20},{20,16},{24,28},{28,24},{1,5},{5... | collective-permute-start | bytes 491528 | tf_op jit(solution)/shard_map/ppermute | solution.py:328
  54.1 1.4 %collective-permute-start.17 = (f32[8,5120]{1,0:T(8,128)S(1)}, f32[8,5120]{1,0:T(8,128)S(1)}, u32[]{:S(2)}, u32[]{:S(2)}) collective-permute-start(f32[8,5120]{1,0:T(8,128)S(1)} %collective-permute-done.16.refs_4_), channel_id=1, source_target_pairs={{0,4},{4,0},{8,12},{12,8},{16,20},{20,16},{24,28},{28,24},{1,5},{5... | collective-permute-start | bytes 491528 | tf_op jit(solution)/shard_map/ppermute | solution.py:328
  54.1 1.6 %collective-permute-start.15 = (f32[8,5120]{1,0:T(8,128)S(1)}, f32[8,5120]{1,0:T(8,128)S(1)}, u32[]{:S(2)}, u32[]{:S(2)}) collective-permute-start(f32[8,5120]{1,0:T(8,128)S(1)} %collective-permute-done.14.refs_2_), channel_id=1, source_target_pairs={{0,4},{4,0},{8,12},{12,8},{16,20},{20,16},{24,28},{28,24},{1,5},{5... | collective-permute-start | bytes 491528 | tf_op jit(solution)/shard_map/ppermute | solution.py:328
  57.6 1.3 %collective-permute-start.20 = (f32[32,512]{1,0:T(8,128)S(1)}, f32[32,512]{1,0:T(8,128)S(1)}, u32[]{:S(2)}, u32[]{:S(2)}) collective-permute-start(f32[32,512]{1,0:T(8,128)S(1)} %get-tuple-element.89), channel_id=1, source_target_pairs={{0,4},{4,0},{8,12},{12,8},{16,20},{20,16},{24,28},{28,24},{1,5},{5... | collective-permute-start | bytes 196616 | tf_op jit(solution)/shard_map/ppermute | solution.py:328
  59.0 5.9 %collective-permute-start.23 = (f32[32,512]{1,0:T(8,128)S(1)}, f32[32,512]{1,0:T(8,128)S(1)}, u32[]{:S(2)}, u32[]{:S(2)}) collective-permute-start(f32[32,512]{1,0:T(8,128)S(1)} %add.40), channel_id=1, source_target_pairs={{0,24},{4,28},{8,16},{12,20},{16,8},{20,12},{24,0},{28,4},{1,25},{... | collective-permute-start | bytes 196616 | tf_op jit(solution)/shard_map/ppermute | solution.py:328
  60.5 5.1 %collective-permute-start.22 = (f32[32,512]{1,0:T(8,128)S(1)}, f32[32,512]{1,0:T(8,128)S(1)}, u32[]{:S(2)}, u32[]{:S(2)}) collective-permute-start(f32[32,512]{1,0:T(8,128)S(1)} %add.40), channel_id=1, source_target_pairs={{0,16},{4,20},{8,24},{12,28},{16,0},{20,4},{24,8},{28,12},{1,17},{... | collective-permute-start | bytes 196616 | tf_op jit(solution)/shard_map/ppermute | solution.py:328
  62.0 4.3 %collective-permute-start.21 = (f32[32,512]{1,0:T(8,128)S(1)}, f32[32,512]{1,0:T(8,128)S(1)}, u32[]{:S(2)}, u32[]{:S(2)}) collective-permute-start(f32[32,512]{1,0:T(8,128)S(1)} %add.40), channel_id=1, source_target_pairs={{0,8},{4,12},{8,0},{12,4},{16,24},{20,28},{24,16},{28,20},{1,9},{5... | collective-permute-start | bytes 196616 | tf_op jit(solution)/shard_map/ppermute | solution.py:328
  66.2 1.7 %collective-permute-start.24 = (f32[32,512]{1,0:T(8,128)S(1)}, f32[32,512]{1,0:T(8,128)S(1)}, u32[]{:S(2)}, u32[]{:S(2)}) collective-permute-start(f32[32,512]{1,0:T(8,128)S(1)} %add_add_fusion.1.refs_0_), channel_id=1, source_target_pairs={{0,4},{4,0},{8,12},{12,8},{16,20},{20,16},{24,28},{28,24},{1,5},{5... | collective-permute-start | bytes 196616 | tf_op jit(solution)/shard_map/ppermute | solution.py:328

commit v6 on v5

--- a/solution.py
+++ b/solution.py
@@ -22,13 +22,13 @@
 HBM = pl.BlockSpec(memory_space=pltpu.HBM)
 
 
-def split(a, parts):
+def split(a, parts, axis=0):
     out = []
     for _ in range(parts):
         high = a.astype(BF16)
         out.append(high)
         a = a - high.astype(F32)
-    return jnp.concatenate(out, axis=0)
+    return jnp.concatenate(out, axis=axis)
 
 
 def fold(a, parts):
@@ -172,11 +172,11 @@
     tangent = jnp.tanh(hidden)
     grad = (weighted[here, :] * (1.0 - tangent * tangent)).astype(BF16)
     g[here, :] = grad
-    yt = split(fold(dot(q3[...], grad, NT), 3), 3)
+    yt = split(fold(dot(q3[...], grad, NT), 3), 3, axis=1)
     rows, wide = outs[0].shape[0], 1024
     for i in range(bx.shape[1] // wide):
         at = slice(i * wide, (i + 1) * wide)
-        total = before[:, at] + fold(dot(yt, x[:, at], NN), 3)
+        total = before[:, at] + dot(yt, jnp.concatenate([x[:, at]] * 3, axis=0), NN)
         for j, out in enumerate(outs):
             out[:, at] = total[j * rows:(j + 1) * rows]
 
@@ -266,11 +266,11 @@
     rank = linv.shape[0]
     high = linv[...].astype(BF16)
     low = (linv[...] - high.astype(F32)).astype(BF16)
-    lhs = jnp.concatenate([jnp.concatenate([high, high], axis=1), jnp.concatenate([low, jnp.zeros_like(low)], axis=1)], axis=0)
+    lhs = jnp.concatenate([high, high, low], axis=1)
     wide = 1024
     for i in range(pft.shape[1] // wide):
         at = slice(i * wide, (i + 1) * wide)
-        pft[:, at] = fold(dot(lhs, bx[:2 * rank, at], NN), 2)
+        pft[:, at] = dot(lhs, jnp.concatenate([bx[:2 * rank, at], bx[:rank, at]], axis=0), NN)
     block = blocks.shape[0] // ids.shape[1]
     for k in range(ids.shape[1]):
         piece = jnp.transpose(pft[:, lanes(ids[0, k], block)])

time: 69.6 us -> 69.3 us (level)
  no operation moved by 1% of the time
where the time goes in v6:
time: 69.3 us; the launch traced here: 69.1 us
  starting transfers between devices  26.6 us (38%)
  waiting for transfers between devices  25.5 us (37%)
  Pallas kernels  16.1 us (23%)
  between operations  0.76 us (1%)
    ppermute x19, waiting for transfers between devices, swap(): return lax.ppermute(a, 'dp', [(i, i ^ bit) for i in range(size)])  17.3 us
    pallas_call x10, Pallas kernels, run(): pl.pallas_call(kernel, input_output_aliases=aliases or {}, out_shape=outs...  16.1 us
    ppermute x19, starting transfers between devices, swap(): return lax.ppermute(a, 'dp', [(i, i ^ bit) for i in range(size)])  12.3 us
    ppermute x2, starting transfers between devices, gather_rows(): lax.ppermute(part, 'mp', outer)  5.22 us
    ppermute x1, starting transfers between devices, gather_rows(): a1 = lax.ppermute(b0, 'mp', outer)  4.61 us
    ppermute x1, waiting for transfers between devices, gather_rows(): a0 = lax.ppermute(x, 'mp', outer)  4.12 us
    ppermute x2, waiting for transfers between devices, gather_rows(): lax.ppermute(part, 'mp', outer)  3.97 us
    ppermute x1, starting transfers between devices, gather_rows(): a0 = lax.ppermute(x, 'mp', outer)  3.09 us
  transfers between devices with their start and end apart: 25, of which 14 were waited for; matrix products, arithmetic and copies ran while one was open for 0% of the time, Pallas kernels for 17%

profile of v6, /device:TPU:0, one launch (start us, length us, event | category | flops | bytes accessed | tf_op | source)
XLA Modules:
  0.0 69.1 jit_solution(4717905981482519767)
XLA Ops:
  0.6 3.1 %collective-permute-start = (bf16[32,5120]{1,0:T(8,128)(2,1)}, bf16[32,5120]{1,0:T(8,128)(2,1)S(1)}, u32[]{:S(2)}, u32[]{:S(2)}) collective-permute-start(bf16[32,5120]{1,0:T(8,128)(2,1)} %refs_8_.1), channel_id=1, source_target_pairs={{0,1},{1,0},{2,3},{3,2},{4,5},{5,4},{6,7},{7,6},{8,9},{9,8},{10,11... | collective-permute-start | bytes 983048 | tf_op jit(solution)/shard_map/ppermute | solution.py:315
  3.7 0.7 collective-permute-start.3
  4.4 3.1 %prepare.1 = (s32[1,4]{1,0:T(1,128)S(1)}, bf16[5120,512]{1,0:T(8,128)(2,1)S(1)}, f32[4,128,512]{2,1,0:T(8,128)S(1)}, bf16[256,5120]{1,0:T(8,128)(2,1)S(1)}, f32[...) custom-call(s32[4,4]{1,0:T(4,128)} %refs_0_.1, ...), custom_call_target="tpu_custom_call" | custom-call | flops 1000000 | bytes 1000000 | tf_op jit(solution)/shard_map/prepare/pallas_call | solution.py:48
  7.5 4.1 %collective-permute-done.refs_0_ = bf16[32,5120]{1,0:T(8,128)(2,1)S(1)} collective-permute-done((bf16[32,5120]{1,0:T(8,128)(2,1)}, bf16[32,5120]{1,0:T(8,128)(2,1)S(1)}, u32[]{:S(2)}, u32[]{:S(2)}) %collective-permute-start) | collective-permute-done | bytes 327712 | tf_op jit(solution)/shard_map/ppermute | solution.py:315
  11.6 0.7 collective-permute-start.1
  12.3 0.0 collective-permute-done.3.refs_1_
  12.3 4.6 %collective-permute-start.4 = (bf16[32,5120]{1,0:T(8,128)(2,1)S(1)}, bf16[32,5120]{1,0:T(8,128)(2,1)S(1)}, u32[]{:S(2)}, u32[]{:S(2)}) collective-permute-start(bf16[32,5120]{1,0:T(8,128)(2,1)S(1)} %collective-permute-done.3.refs_1_), channel_id=1, source_target_pairs={{0,1},{1,0},{2,3},{3,2},{4,5},{5,4},{6,7},{7,6},{8,9},{9,8},{10,11... | collective-permute-start | bytes 983048 | tf_op jit(solution)/shard_map/ppermute | solution.py:319
  17.0 1.8 %rows.3 = (bf16[256,5120]{1,0:T(8,128)(2,1)S(1)}, bf16[128,512]{1,0:T(8,128)(2,1)S(1)}, f32[64,5120]{1,0:T(8,128)S(1)}) custom-call(bf16[32,5120]{1,0:T(8,128)(2,1)S(1)} %collective-permute-done.refs_0_, bf16[5120,512]{1,0:T(8,128)(2,1)S(1)} %get-tuple-element.57.refs_1_.refs_2_.w, ...), custom_call_target="tpu_custom_call", output_to_operand_aliasing={{0}: (5, {}), {1}: (6, {})} | custom-call | flops 167772160 | bytes 1000000 | tf_op jit(solution)/shard_map/rows/pallas_call | solution.py:48
  18.8 5.1 %collective-permute-start.5 = (bf16[32,3840]{1,0:T(8,128)(2,1)S(1)}, bf16[32,3840]{1,0:T(8,128)(2,1)S(1)}, u32[]{:S(2)}, u32[]{:S(2)}) collective-permute-start(bf16[32,3840]{1,0:T(8,128)(2,1)S(1)} %slice.7), channel_id=1, source_target_pairs={{0,1},{1,0},{2,3},{3,2},{4,5},{5,4},{6,7},{7,6},{8,9},{9,8},{10,11... | collective-permute-start | bytes 737288 | tf_op jit(solution)/shard_map/ppermute | solution.py:323
  23.9 0.1 collective-permute-start.2
  24.0 0.1 collective-permute-done.4.refs_0_
  24.1 1.7 %rows.4 = (bf16[256,5120]{1,0:T(8,128)(2,1)S(1)}, bf16[128,512]{1,0:T(8,128)(2,1)S(1)}, f32[64,5120]{1,0:T(8,128)S(1)}) custom-call(bf16[32,5120]{1,0:T(8,128)(2,1)S(1)} %collective-permute-done.4.refs_0_, bf16[32,5120]{1,0:T(8,128)(2,1)S(1)} %collective-permute-done.3.refs_1_, ...), custom_call_target="tpu_custom_call", output_to_operand_aliasing={{0}: (6, {}), {1}: (7, {})} | custom-call | flops 167772160 | bytes 1000000 | tf_op jit(solution)/shard_map/rows/pallas_call | solution.py:48
  25.8 3.9 %collective-permute-done.5.end = bf16[32,3840]{1,0:T(8,128)(2,1)S(1)} collective-permute-done((bf16[32,3840]{1,0:T(8,128)(2,1)S(1)}, bf16[32,3840]{1,0:T(8,128)(2,1)S(1)}, u32[]{:S(2)}, u32[]{:S(2)}) %collective-permute-start.5) | collective-permute-done | bytes 245792 | tf_op jit(solution)/shard_map/ppermute | solution.py:323
  29.6 0.8 %begin.1 = (bf16[256,5120]{1,0:T(8,128)(2,1)S(1)}, f32[32,512]{1,0:T(8,128)S(1)}) custom-call(bf16[5120,512]{1,0:T(8,128)(2,1)S(1)} %get-tuple-element.57.refs_1_.refs_2_.w, bf16[32,3840]{1,0:T(8,128)(2,1)S(1)} %collective-permute-done.5.end, bf16[32,5120]{1,0:T(8,128)(2,1)S(1)} %collective-permute-done.1.between.refs_1_, ...), custom_call_target="tpu_custom_call", output_to_operand_aliasing={{0}: (3, {})} | custom-call | flops 1000000 | bytes 1000000 | tf_op jit(solution)/shard_map/begin/pallas_call | solution.py:48
  30.4 0.1 collective-permute-done.2.refs_0_
  30.5 1.0 %rows.5 = (bf16[256,5120]{1,0:T(8,128)(2,1)S(1)}, bf16[128,512]{1,0:T(8,128)(2,1)S(1)}, f32[8,5120]{1,0:T(8,128)S(1)}, f32[8,5120]{1,0:T(8,128)S(1)}, f32[8,5120...) custom-call(bf16[32,1280]{1,0:T(8,128)(2,1)S(1)} %collective-permute, ...), custom_call_target="tpu_custom_call", output_to_operand_aliasing={{0}: (7, {}), {1}: (8, {})} | custom-call | flops 167772160 | bytes 1000000 | tf_op jit(solution)/shard_map/rows/pallas_call | solution.py:48
  31.5 0.1 collective-permute-start.7
  31.6 0.5 collective-permute-start.9
  32.1 0.1 collective-permute-start.11
  32.2 0.8 %collective-permute-done.7 = f32[8,5120]{1,0:T(8,128)S(1)} collective-permute-done((f32[8,5120]{1,0:T(8,128)S(1)}, f32[8,5120]{1,0:T(8,128)S(1)}, u32[]{:S(2)}, u32[]{:S(2)}) %collective-permute-start.7) | collective-permute-done | bytes 163872 | tf_op jit(solution)/shard_map/ppermute | solution.py:328
  33.0 1.6 %collective-permute-start.8 = (f32[8,5120]{1,0:T(8,128)S(1)}, f32[8,5120]{1,0:T(8,128)S(1)}, u32[]{:S(2)}, u32[]{:S(2)}) collective-permute-start(f32[8,5120]{1,0:T(8,128)S(1)} %add.34), channel_id=1, source_target_pairs={{0,8},{4,12},{8,0},{12,4},{16,24},{20,28},{24,16},{28,20},{1,9},{5... | collective-permute-start | bytes 491528 | tf_op jit(solution)/shard_map/ppermute | solution.py:328
  34.6 1.6 %collective-permute-start.10 = (f32[8,5120]{1,0:T(8,128)S(1)}, f32[8,5120]{1,0:T(8,128)S(1)}, u32[]{:S(2)}, u32[]{:S(2)}) collective-permute-start(f32[8,5120]{1,0:T(8,128)S(1)} %add.35), channel_id=1, source_target_pairs={{0,16},{4,20},{8,24},{12,28},{16,0},{20,4},{24,8},{28,12},{1,17},{... | collective-permute-start | bytes 491528 | tf_op jit(solution)/shard_map/ppermute | solution.py:328
  36.2 0.5 collective-permute-start.12
  36.7 0.4 merged.1.refs_4_
  37.1 3.0 %collective-permute-done.8 = f32[8,5120]{1,0:T(8,128)S(1)} collective-permute-done((f32[8,5120]{1,0:T(8,128)S(1)}, f32[8,5120]{1,0:T(8,128)S(1)}, u32[]{:S(2)}, u32[]{:S(2)}) %collective-permute-start.8) | collective-permute-done | bytes 163872 | tf_op jit(solution)/shard_map/ppermute | solution.py:328
  40.1 4.0 %collective-permute-done.10 = f32[8,5120]{1,0:T(8,128)S(1)} collective-permute-done((f32[8,5120]{1,0:T(8,128)S(1)}, f32[8,5120]{1,0:T(8,128)S(1)}, u32[]{:S(2)}, u32[]{:S(2)}) %collective-permute-start.10) | collective-permute-done | bytes 163872 | tf_op jit(solution)/shard_map/ppermute | solution.py:328
  44.1 0.1 add_add_fusion.refs_0_
  44.2 1.6 %collective-permute-start.18 = (f32[8,5120]{1,0:T(8,128)S(1)}, f32[8,5120]{1,0:T(8,128)S(1)}, u32[]{:S(2)}, u32[]{:S(2)}) collective-permute-start(f32[8,5120]{1,0:T(8,128)S(1)} %add_add_fusion.refs_0_), channel_id=1, source_target_pairs={{0,24},{4,28},{8,16},{12,20},{16,8},{20,12},{24,0},{28,4},{1,25},{... | collective-permute-start | bytes 491528 | tf_op jit(solution)/shard_map/ppermute | solution.py:328
  45.8 1.1 %collective-permute-start.16 = (f32[8,5120]{1,0:T(8,128)S(1)}, f32[8,5120]{1,0:T(8,128)S(1)}, u32[]{:S(2)}, u32[]{:S(2)}) collective-permute-start(f32[8,5120]{1,0:T(8,128)S(1)} %add_add_fusion.refs_0_), channel_id=1, source_target_pairs={{0,16},{4,20},{8,24},{12,28},{16,0},{20,4},{24,8},{28,12},{1,17},{... | collective-permute-start | bytes 491528 | tf_op jit(solution)/shard_map/ppermute | solution.py:328
  46.9 0.9 %collective-permute-start.14 = (f32[8,5120]{1,0:T(8,128)S(1)}, f32[8,5120]{1,0:T(8,128)S(1)}, u32[]{:S(2)}, u32[]{:S(2)}) collective-permute-start(f32[8,5120]{1,0:T(8,128)S(1)} %add_add_fusion.refs_0_), channel_id=1, source_target_pairs={{0,8},{4,12},{8,0},{12,4},{16,24},{20,28},{24,16},{28,20},{1,9},{5... | collective-permute-start | bytes 491528 | tf_op jit(solution)/shard_map/ppermute | solution.py:328
  47.8 4.3 %collective-permute-done.18.refs_6_ = f32[8,5120]{1,0:T(8,128)S(1)} collective-permute-done((f32[8,5120]{1,0:T(8,128)S(1)}, f32[8,5120]{1,0:T(8,128)S(1)}, u32[]{:S(2)}, u32[]{:S(2)}) %collective-permute-start.18) | collective-permute-done | bytes 163872 | tf_op jit(solution)/shard_map/ppermute | solution.py:328
  52.1 1.7 %collective-permute-done.16.refs_4_ = f32[8,5120]{1,0:T(8,128)S(1)} collective-permute-done((f32[8,5120]{1,0:T(8,128)S(1)}, f32[8,5120]{1,0:T(8,128)S(1)}, u32[]{:S(2)}, u32[]{:S(2)}) %collective-permute-start.16) | collective-permute-done | bytes 163872 | tf_op jit(solution)/shard_map/ppermute | solution.py:328
  53.8 0.0 collective-permute-done.14.refs_2_
  53.8 0.5 collective-permute-start.15
  54.3 0.9 %collective-permute-done.17.refs_5_ = f32[8,5120]{1,0:T(8,128)S(1)} collective-permute-done((f32[8,5120]{1,0:T(8,128)S(1)}, f32[8,5120]{1,0:T(8,128)S(1)}, u32[]{:S(2)}, u32[]{:S(2)}) %collective-permute-start.17) | collective-permute-done | bytes 163872 | tf_op jit(solution)/shard_map/ppermute | solution.py:328
  55.2 0.2 collective-permute-done.15.refs_3_
  55.4 2.0 %second.1 = (bf16[256,5120]{1,0:T(8,128)(2,1)S(1)}, f32[64,64]{1,0:T(8,128)S(1)}, f32[32,512]{1,0:T(8,128)S(1)}, f32[32,512]{1,0:T(8,128)S(1)}) custom-call(s32[1,4]{1,0:T(1,128)S(1)} %get-tuple-element.54.ids, f32[8,5120]{1,0:T(8,128)S(1)} %add_add_fusion.refs_0_, f32[8,5120]{1,0:T(8,128)S(1)} %collective-permute-done.13.refs_1_, ...), custom_call_target="tpu_custom_call", output_to_operand_aliasing={{0}: (11, {})} | custom-call | flops 1000000 | bytes 1000000 | tf_op jit(solution)/shard_map/second/pallas_call | solution.py:48
  57.4 0.3 collective-permute-start.20
  57.7 1.0 %collective-permute-done.20 = f32[32,512]{1,0:T(8,128)S(1)} collective-permute-done((f32[32,512]{1,0:T(8,128)S(1)}, f32[32,512]{1,0:T(8,128)S(1)}, u32[]{:S(2)}, u32[]{:S(2)}) %collective-permute-start.20) | collective-permute-done | bytes 65568 | tf_op jit(solution)/shard_map/ppermute | solution.py:328
  58.7 1.5 %collective-permute-start.23 = (f32[32,512]{1,0:T(8,128)S(1)}, f32[32,512]{1,0:T(8,128)S(1)}, u32[]{:S(2)}, u32[]{:S(2)}) collective-permute-start(f32[32,512]{1,0:T(8,128)S(1)} %add.40), channel_id=1, source_target_pairs={{0,24},{4,28},{8,16},{12,20},{16,8},{20,12},{24,0},{28,4},{1,25},{... | collective-permute-start | bytes 196616 | tf_op jit(solution)/shard_map/ppermute | solution.py:328
  60.2 1.5 %collective-permute-start.22 = (f32[32,512]{1,0:T(8,128)S(1)}, f32[32,512]{1,0:T(8,128)S(1)}, u32[]{:S(2)}, u32[]{:S(2)}) collective-permute-start(f32[32,512]{1,0:T(8,128)S(1)} %add.40), channel_id=1, source_target_pairs={{0,16},{4,20},{8,24},{12,28},{16,0},{20,4},{24,8},{28,12},{1,17},{... | collective-permute-start | bytes 196616 | tf_op jit(solution)/shard_map/ppermute | solution.py:328
  61.7 0.6 collective-permute-start.21
  62.3 2.3 %factor.1.linv.refs_2_ = f32[64,64]{1,0:T(8,128)S(1)} custom-call(f32[64,64]{1,0:T(8,128)S(1)} %get-tuple-element.90.gram), custom_call_target="tpu_custom_call" | custom-call | flops 1000000 | bytes 1000000 | tf_op jit(solution)/shard_map/factor/pallas_call | solution.py:48
  64.6 0.8 %collective-permute-done.22 = f32[32,512]{1,0:T(8,128)S(1)} collective-permute-done((f32[32,512]{1,0:T(8,128)S(1)}, f32[32,512]{1,0:T(8,128)S(1)}, u32[]{:S(2)}, u32[]{:S(2)}) %collective-permute-start.22) | collective-permute-done | bytes 65568 | tf_op jit(solution)/shard_map/ppermute | solution.py:328
  65.4 0.6 collective-permute-done.21
  66.0 0.1 collective-permute-start.24
  66.1 1.6 %left.1 = (f32[64,5120]{1,0:T(8,128)}, bf16[512,192]{1,0:T(8,128)(2,1)S(1)}) custom-call(s32[1,4]{1,0:T(1,128)S(1)} %get-tuple-element.54.ids, f32[64,64]{1,0:T(8,128)S(1)} %factor.1.linv.refs_2_, bf16[256,5120]{1,0:T(8,128)(2,1)S(1)} %get-tuple-element.96.bx), custom_call_target="tpu_custom_call" | custom-call | flops 1000000 | bytes 1000000 | tf_op jit(solution)/shard_map/left/pallas_call | solution.py:48
  67.6 1.5 %last.1 = (f32[64,512]{1,0:T(8,128)}, f32[4,128,512]{2,1,0:T(8,128)}) custom-call(f32[32,512]{1,0:T(8,128)S(1)} %add_add_fusion.1.refs_0_, f32[32,512]{1,0:T(8,128)S(1)} %collective-permute-done.24.refs_1_, f32[64,64]{1,0:T(8,128)S(1)} %factor.1.linv.refs_2_, bf16[512,192]{1,0:T(8,128)(2,1)S(1)} %get-tuple-element.101.refs_3_, f32[4,128,512]{2,1,0:T(8,128)S(1)} %merged.1.refs_4_), custom_call_target="tpu_custom_call" | custom-call | flops 1000000 | bytes 1000000 | tf_op jit(solution)/shard_map/last/pallas_call | solution.py:48
  (21 shorter events, 0.2 us)
Async XLA Ops:
  0.6 11.0 %collective-permute-start = (bf16[32,5120]{1,0:T(8,128)(2,1)}, bf16[32,5120]{1,0:T(8,128)(2,1)S(1)}, u32[]{:S(2)}, u32[]{:S(2)}) collective-permute-start(bf16[32,5120]{1,0:T(8,128)(2,1)} %refs_8_.1), channel_id=1, source_target_pairs={{0,1},{1,0},{2,3},{3,2},{4,5},{5,4},{6,7},{7,6},{8,9},{9,8},{10,11... | collective-permute-start | bytes 983048 | tf_op jit(solution)/shard_map/ppermute | solution.py:315
  3.7 8.6 %collective-permute-start.3 = (bf16[32,5120]{1,0:T(8,128)(2,1)}, bf16[32,5120]{1,0:T(8,128)(2,1)S(1)}, u32[]{:S(2)}, u32[]{:S(2)}) collective-permute-start(bf16[32,5120]{1,0:T(8,128)(2,1)} %refs_8_.1), channel_id=1, source_target_pairs={{1,2},{2,1},{5,6},{6,5},{9,10},{10,9},{13,14},{14,13},{17,18},{18,... | collective-permute-start | bytes 983048 | tf_op jit(solution)/shard_map/ppermute | solution.py:316
  11.6 7.1 %collective-permute-start.1 = (bf16[32,5120]{1,0:T(8,128)(2,1)S(1)}, bf16[32,5120]{1,0:T(8,128)(2,1)S(1)}, u32[]{:S(2)}, u32[]{:S(2)}) collective-permute-start(bf16[32,5120]{1,0:T(8,128)(2,1)S(1)} %collective-permute-done.refs_0_), channel_id=1, source_target_pairs={{1,2},{2,1},{5,6},{6,5},{9,10},{10,9},{13,14},{14,13},{17,18},{18,... | collective-permute-start | bytes 983048 | tf_op jit(solution)/shard_map/ppermute | solution.py:318
  12.3 11.8 %collective-permute-start.4 = (bf16[32,5120]{1,0:T(8,128)(2,1)S(1)}, bf16[32,5120]{1,0:T(8,128)(2,1)S(1)}, u32[]{:S(2)}, u32[]{:S(2)}) collective-permute-start(bf16[32,5120]{1,0:T(8,128)(2,1)S(1)} %collective-permute-done.3.refs_1_), channel_id=1, source_target_pairs={{0,1},{1,0},{2,3},{3,2},{4,5},{5,4},{6,7},{7,6},{8,9},{9,8},{10,11... | collective-permute-start | bytes 983048 | tf_op jit(solution)/shard_map/ppermute | solution.py:319
  18.8 10.8 %collective-permute-start.5 = (bf16[32,3840]{1,0:T(8,128)(2,1)S(1)}, bf16[32,3840]{1,0:T(8,128)(2,1)S(1)}, u32[]{:S(2)}, u32[]{:S(2)}) collective-permute-start(bf16[32,3840]{1,0:T(8,128)(2,1)S(1)} %slice.7), channel_id=1, source_target_pairs={{0,1},{1,0},{2,3},{3,2},{4,5},{5,4},{6,7},{7,6},{8,9},{9,8},{10,11... | collective-permute-start | bytes 737288 | tf_op jit(solution)/shard_map/ppermute | solution.py:323
  23.9 6.6 %collective-permute-start.2 = (bf16[32,1280]{1,0:T(8,128)(2,1)S(1)}, bf16[32,1280]{1,0:T(8,128)(2,1)S(1)}, u32[]{:S(2)}, u32[]{:S(2)}) collective-permute-start(bf16[32,1280]{1,0:T(8,128)(2,1)S(1)} %slice.6), channel_id=1, source_target_pairs={{0,1},{1,0},{2,3},{3,2},{4,5},{5,4},{6,7},{7,6},{8,9},{9,8},{10,11... | collective-permute-start | bytes 245768 | tf_op jit(solution)/shard_map/ppermute | solution.py:323
  31.5 1.5 %collective-permute-start.7 = (f32[8,5120]{1,0:T(8,128)S(1)}, f32[8,5120]{1,0:T(8,128)S(1)}, u32[]{:S(2)}, u32[]{:S(2)}) collective-permute-start(f32[8,5120]{1,0:T(8,128)S(1)} %get-tuple-element.76), channel_id=1, source_target_pairs={{0,4},{4,0},{8,12},{12,8},{16,20},{20,16},{24,28},{28,24},{1,5},{5... | collective-permute-start | bytes 491528 | tf_op jit(solution)/shard_map/ppermute | solution.py:328
  31.6 3.0 %collective-permute-start.9 = (f32[8,5120]{1,0:T(8,128)S(1)}, f32[8,5120]{1,0:T(8,128)S(1)}, u32[]{:S(2)}, u32[]{:S(2)}) collective-permute-start(f32[8,5120]{1,0:T(8,128)S(1)} %get-tuple-element.78), channel_id=1, source_target_pairs={{0,4},{4,0},{8,12},{12,8},{16,20},{20,16},{24,28},{28,24},{1,5},{5... | collective-permute-start | bytes 491528 | tf_op jit(solution)/shard_map/ppermute | solution.py:328
  32.1 4.1 %collective-permute-start.11 = (f32[8,5120]{1,0:T(8,128)S(1)}, f32[8,5120]{1,0:T(8,128)S(1)}, u32[]{:S(2)}, u32[]{:S(2)}) collective-permute-start(f32[8,5120]{1,0:T(8,128)S(1)} %get-tuple-element.80), channel_id=1, source_target_pairs={{0,4},{4,0},{8,12},{12,8},{16,20},{20,16},{24,28},{28,24},{1,5},{5... | collective-permute-start | bytes 491528 | tf_op jit(solution)/shard_map/ppermute | solution.py:328
  33.0 7.1 %collective-permute-start.8 = (f32[8,5120]{1,0:T(8,128)S(1)}, f32[8,5120]{1,0:T(8,128)S(1)}, u32[]{:S(2)}, u32[]{:S(2)}) collective-permute-start(f32[8,5120]{1,0:T(8,128)S(1)} %add.34), channel_id=1, source_target_pairs={{0,8},{4,12},{8,0},{12,4},{16,24},{20,28},{24,16},{28,20},{1,9},{5... | collective-permute-start | bytes 491528 | tf_op jit(solution)/shard_map/ppermute | solution.py:328
  34.6 9.5 %collective-permute-start.10 = (f32[8,5120]{1,0:T(8,128)S(1)}, f32[8,5120]{1,0:T(8,128)S(1)}, u32[]{:S(2)}, u32[]{:S(2)}) collective-permute-start(f32[8,5120]{1,0:T(8,128)S(1)} %add.35), channel_id=1, source_target_pairs={{0,16},{4,20},{8,24},{12,28},{16,0},{20,4},{24,8},{28,12},{1,17},{... | collective-permute-start | bytes 491528 | tf_op jit(solution)/shard_map/ppermute | solution.py:328
  36.2 7.9 %collective-permute-start.12 = (f32[8,5120]{1,0:T(8,128)S(1)}, f32[8,5120]{1,0:T(8,128)S(1)}, u32[]{:S(2)}, u32[]{:S(2)}) collective-permute-start(f32[8,5120]{1,0:T(8,128)S(1)} %add.36), channel_id=1, source_target_pairs={{0,24},{4,28},{8,16},{12,20},{16,8},{20,12},{24,0},{28,4},{1,25},{... | collective-permute-start | bytes 491528 | tf_op jit(solution)/shard_map/ppermute | solution.py:328
  36.7 7.4 %collective-permute-start.6 = (f32[8,5120]{1,0:T(8,128)S(1)}, f32[8,5120]{1,0:T(8,128)S(1)}, u32[]{:S(2)}, u32[]{:S(2)}) collective-permute-start(f32[8,5120]{1,0:T(8,128)S(1)} %get-tuple-element.74), channel_id=1, source_target_pairs={{0,4},{4,0},{8,12},{12,8},{16,20},{20,16},{24,28},{28,24},{1,5},{5... | collective-permute-start | bytes 491528 | tf_op jit(solution)/shard_map/ppermute | solution.py:328
  44.2 7.9 %collective-permute-start.18 = (f32[8,5120]{1,0:T(8,128)S(1)}, f32[8,5120]{1,0:T(8,128)S(1)}, u32[]{:S(2)}, u32[]{:S(2)}) collective-permute-start(f32[8,5120]{1,0:T(8,128)S(1)} %add_add_fusion.refs_0_), channel_id=1, source_target_pairs={{0,24},{4,28},{8,16},{12,20},{16,8},{20,12},{24,0},{28,4},{1,25},{... | collective-permute-start | bytes 491528 | tf_op jit(solution)/shard_map/ppermute | solution.py:328
  45.8 8.0 %collective-permute-start.16 = (f32[8,5120]{1,0:T(8,128)S(1)}, f32[8,5120]{1,0:T(8,128)S(1)}, u32[]{:S(2)}, u32[]{:S(2)}) collective-permute-start(f32[8,5120]{1,0:T(8,128)S(1)} %add_add_fusion.refs_0_), channel_id=1, source_target_pairs={{0,16},{4,20},{8,24},{12,28},{16,0},{20,4},{24,8},{28,12},{1,17},{... | collective-permute-start | bytes 491528 | tf_op jit(solution)/shard_map/ppermute | solution.py:328
  46.9 7.0 %collective-permute-start.14 = (f32[8,5120]{1,0:T(8,128)S(1)}, f32[8,5120]{1,0:T(8,128)S(1)}, u32[]{:S(2)}, u32[]{:S(2)}) collective-permute-start(f32[8,5120]{1,0:T(8,128)S(1)} %add_add_fusion.refs_0_), channel_id=1, source_target_pairs={{0,8},{4,12},{8,0},{12,4},{16,24},{20,28},{24,16},{28,20},{1,9},{5... | collective-permute-start | bytes 491528 | tf_op jit(solution)/shard_map/ppermute | solution.py:328
  47.8 6.5 %collective-permute-start.13 = (f32[8,5120]{1,0:T(8,128)S(1)}, f32[8,5120]{1,0:T(8,128)S(1)}, u32[]{:S(2)}, u32[]{:S(2)}) collective-permute-start(f32[8,5120]{1,0:T(8,128)S(1)} %add_add_fusion.refs_0_), channel_id=1, source_target_pairs={{0,4},{4,0},{8,12},{12,8},{16,20},{20,16},{24,28},{28,24},{1,5},{5... | collective-permute-start | bytes 491528 | tf_op jit(solution)/shard_map/ppermute | solution.py:328
  52.1 2.2 %collective-permute-start.19 = (f32[8,5120]{1,0:T(8,128)S(1)}, f32[8,5120]{1,0:T(8,128)S(1)}, u32[]{:S(2)}, u32[]{:S(2)}) collective-permute-start(f32[8,5120]{1,0:T(8,128)S(1)} %collective-permute-done.18.refs_6_), channel_id=1, source_target_pairs={{0,4},{4,0},{8,12},{12,8},{16,20},{20,16},{24,28},{28,24},{1,5},{5... | collective-permute-start | bytes 491528 | tf_op jit(solution)/shard_map/ppermute | solution.py:328
  53.8 1.4 %collective-permute-start.17 = (f32[8,5120]{1,0:T(8,128)S(1)}, f32[8,5120]{1,0:T(8,128)S(1)}, u32[]{:S(2)}, u32[]{:S(2)}) collective-permute-start(f32[8,5120]{1,0:T(8,128)S(1)} %collective-permute-done.16.refs_4_), channel_id=1, source_target_pairs={{0,4},{4,0},{8,12},{12,8},{16,20},{20,16},{24,28},{28,24},{1,5},{5... | collective-permute-start | bytes 491528 | tf_op jit(solution)/shard_map/ppermute | solution.py:328
  53.8 1.6 %collective-permute-start.15 = (f32[8,5120]{1,0:T(8,128)S(1)}, f32[8,5120]{1,0:T(8,128)S(1)}, u32[]{:S(2)}, u32[]{:S(2)}) collective-permute-start(f32[8,5120]{1,0:T(8,128)S(1)} %collective-permute-done.14.refs_2_), channel_id=1, source_target_pairs={{0,4},{4,0},{8,12},{12,8},{16,20},{20,16},{24,28},{28,24},{1,5},{5... | collective-permute-start | bytes 491528 | tf_op jit(solution)/shard_map/ppermute | solution.py:328
  57.4 1.3 %collective-permute-start.20 = (f32[32,512]{1,0:T(8,128)S(1)}, f32[32,512]{1,0:T(8,128)S(1)}, u32[]{:S(2)}, u32[]{:S(2)}) collective-permute-start(f32[32,512]{1,0:T(8,128)S(1)} %get-tuple-element.89), channel_id=1, source_target_pairs={{0,4},{4,0},{8,12},{12,8},{16,20},{20,16},{24,28},{28,24},{1,5},{5... | collective-permute-start | bytes 196616 | tf_op jit(solution)/shard_map/ppermute | solution.py:328
  58.7 5.9 %collective-permute-start.23 = (f32[32,512]{1,0:T(8,128)S(1)}, f32[32,512]{1,0:T(8,128)S(1)}, u32[]{:S(2)}, u32[]{:S(2)}) collective-permute-start(f32[32,512]{1,0:T(8,128)S(1)} %add.40), channel_id=1, source_target_pairs={{0,24},{4,28},{8,16},{12,20},{16,8},{20,12},{24,0},{28,4},{1,25},{... | collective-permute-start | bytes 196616 | tf_op jit(solution)/shard_map/ppermute | solution.py:328
  60.2 5.2 %collective-permute-start.22 = (f32[32,512]{1,0:T(8,128)S(1)}, f32[32,512]{1,0:T(8,128)S(1)}, u32[]{:S(2)}, u32[]{:S(2)}) collective-permute-start(f32[32,512]{1,0:T(8,128)S(1)} %add.40), channel_id=1, source_target_pairs={{0,16},{4,20},{8,24},{12,28},{16,0},{20,4},{24,8},{28,12},{1,17},{... | collective-permute-start | bytes 196616 | tf_op jit(solution)/shard_map/ppermute | solution.py:328
  61.7 4.3 %collective-permute-start.21 = (f32[32,512]{1,0:T(8,128)S(1)}, f32[32,512]{1,0:T(8,128)S(1)}, u32[]{:S(2)}, u32[]{:S(2)}) collective-permute-start(f32[32,512]{1,0:T(8,128)S(1)} %add.40), channel_id=1, source_target_pairs={{0,8},{4,12},{8,0},{12,4},{16,24},{20,28},{24,16},{28,20},{1,9},{5... | collective-permute-start | bytes 196616 | tf_op jit(solution)/shard_map/ppermute | solution.py:328
  66.0 1.7 %collective-permute-start.24 = (f32[32,512]{1,0:T(8,128)S(1)}, f32[32,512]{1,0:T(8,128)S(1)}, u32[]{:S(2)}, u32[]{:S(2)}) collective-permute-start(f32[32,512]{1,0:T(8,128)S(1)} %add_add_fusion.1.refs_0_), channel_id=1, source_target_pairs={{0,4},{4,0},{8,12},{12,8},{16,20},{20,16},{24,28},{28,24},{1,5},{5... | collective-permute-start | bytes 196616 | tf_op jit(solution)/shard_map/ppermute | solution.py:328

commit v7 on v6

--- a/solution.py
+++ b/solution.py
@@ -173,7 +173,7 @@
     grad = (weighted[here, :] * (1.0 - tangent * tangent)).astype(BF16)
     g[here, :] = grad
     yt = split(fold(dot(q3[...], grad, NT), 3), 3, axis=1)
-    rows, wide = outs[0].shape[0], 1024
+    rows, wide = outs[0].shape[0], 512
     for i in range(bx.shape[1] // wide):
         at = slice(i * wide, (i + 1) * wide)
         total = before[:, at] + dot(yt, jnp.concatenate([x[:, at]] * 3, axis=0), NN)
@@ -267,7 +267,7 @@
     high = linv[...].astype(BF16)
     low = (linv[...] - high.astype(F32)).astype(BF16)
     lhs = jnp.concatenate([high, high, low], axis=1)
-    wide = 1024
+    wide = 512
     for i in range(pft.shape[1] // wide):
         at = slice(i * wide, (i + 1) * wide)
         pft[:, at] = dot(lhs, jnp.concatenate([bx[:2 * rank, at], bx[:rank, at]], axis=0), NN)

time: 69.3 us -> 69.3 us (level)
  no operation moved by 1% of the time
where the time goes in v7:
time: 69.3 us; the launch traced here: 69.1 us
  starting transfers between devices  26.6 us (38%)
  waiting for transfers between devices  25.5 us (37%)
  Pallas kernels  16.1 us (23%)
  between operations  0.76 us (1%)
    ppermute x19, waiting for transfers between devices, swap(): return lax.ppermute(a, 'dp', [(i, i ^ bit) for i in range(size)])  17.3 us
    pallas_call x10, Pallas kernels, run(): pl.pallas_call(kernel, input_output_aliases=aliases or {}, out_shape=outs...  16.1 us
    ppermute x19, starting transfers between devices, swap(): return lax.ppermute(a, 'dp', [(i, i ^ bit) for i in range(size)])  12.3 us
    ppermute x2, starting transfers between devices, gather_rows(): lax.ppermute(part, 'mp', outer)  5.22 us
    ppermute x1, starting transfers between devices, gather_rows(): a1 = lax.ppermute(b0, 'mp', outer)  4.61 us
    ppermute x1, waiting for transfers between devices, gather_rows(): a0 = lax.ppermute(x, 'mp', outer)  4.12 us
    ppermute x2, waiting for transfers between devices, gather_rows(): lax.ppermute(part, 'mp', outer)  3.97 us
    ppermute x1, starting transfers between devices, gather_rows(): a0 = lax.ppermute(x, 'mp', outer)  3.09 us
  transfers between devices with their start and end apart: 25, of which 14 were waited for; matrix products, arithmetic and copies ran while one was open for 0% of the time, Pallas kernels for 17%

profile of v7, /device:TPU:0, one launch (start us, length us, event | category | flops | bytes accessed | tf_op | source)
XLA Modules:
  0.0 69.1 jit_solution(4717905981482519767)
XLA Ops:
  0.6 3.1 %collective-permute-start = (bf16[32,5120]{1,0:T(8,128)(2,1)}, bf16[32,5120]{1,0:T(8,128)(2,1)S(1)}, u32[]{:S(2)}, u32[]{:S(2)}) collective-permute-start(bf16[32,5120]{1,0:T(8,128)(2,1)} %refs_8_.1), channel_id=1, source_target_pairs={{0,1},{1,0},{2,3},{3,2},{4,5},{5,4},{6,7},{7,6},{8,9},{9,8},{10,11... | collective-permute-start | bytes 983048 | tf_op jit(solution)/shard_map/ppermute | solution.py:315
  3.7 0.7 collective-permute-start.3
  4.4 3.1 %prepare.1 = (s32[1,4]{1,0:T(1,128)S(1)}, bf16[5120,512]{1,0:T(8,128)(2,1)S(1)}, f32[4,128,512]{2,1,0:T(8,128)S(1)}, bf16[256,5120]{1,0:T(8,128)(2,1)S(1)}, f32[...) custom-call(s32[4,4]{1,0:T(4,128)} %refs_0_.1, ...), custom_call_target="tpu_custom_call" | custom-call | flops 1000000 | bytes 1000000 | tf_op jit(solution)/shard_map/prepare/pallas_call | solution.py:48
  7.5 4.1 %collective-permute-done.refs_0_ = bf16[32,5120]{1,0:T(8,128)(2,1)S(1)} collective-permute-done((bf16[32,5120]{1,0:T(8,128)(2,1)}, bf16[32,5120]{1,0:T(8,128)(2,1)S(1)}, u32[]{:S(2)}, u32[]{:S(2)}) %collective-permute-start) | collective-permute-done | bytes 327712 | tf_op jit(solution)/shard_map/ppermute | solution.py:315
  11.6 0.7 collective-permute-start.1
  12.3 4.6 %collective-permute-start.4 = (bf16[32,5120]{1,0:T(8,128)(2,1)S(1)}, bf16[32,5120]{1,0:T(8,128)(2,1)S(1)}, u32[]{:S(2)}, u32[]{:S(2)}) collective-permute-start(bf16[32,5120]{1,0:T(8,128)(2,1)S(1)} %collective-permute-done.3.refs_1_), channel_id=1, source_target_pairs={{0,1},{1,0},{2,3},{3,2},{4,5},{5,4},{6,7},{7,6},{8,9},{9,8},{10,11... | collective-permute-start | bytes 983048 | tf_op jit(solution)/shard_map/ppermute | solution.py:319
  17.0 1.8 %rows.3 = (bf16[256,5120]{1,0:T(8,128)(2,1)S(1)}, bf16[128,512]{1,0:T(8,128)(2,1)S(1)}, f32[64,5120]{1,0:T(8,128)S(1)}) custom-call(bf16[32,5120]{1,0:T(8,128)(2,1)S(1)} %collective-permute-done.refs_0_, bf16[5120,512]{1,0:T(8,128)(2,1)S(1)} %get-tuple-element.57.refs_1_.refs_2_.w, ...), custom_call_target="tpu_custom_call", output_to_operand_aliasing={{0}: (5, {}), {1}: (6, {})} | custom-call | flops 167772160 | bytes 1000000 | tf_op jit(solution)/shard_map/rows/pallas_call | solution.py:48
  18.8 5.1 %collective-permute-start.5 = (bf16[32,3840]{1,0:T(8,128)(2,1)S(1)}, bf16[32,3840]{1,0:T(8,128)(2,1)S(1)}, u32[]{:S(2)}, u32[]{:S(2)}) collective-permute-start(bf16[32,3840]{1,0:T(8,128)(2,1)S(1)} %slice.7), channel_id=1, source_target_pairs={{0,1},{1,0},{2,3},{3,2},{4,5},{5,4},{6,7},{7,6},{8,9},{9,8},{10,11... | collective-permute-start | bytes 737288 | tf_op jit(solution)/shard_map/ppermute | solution.py:323
  23.9 0.1 collective-permute-start.2
  24.0 0.1 collective-permute-done.4.refs_0_
  24.1 1.7 %rows.4 = (bf16[256,5120]{1,0:T(8,128)(2,1)S(1)}, bf16[128,512]{1,0:T(8,128)(2,1)S(1)}, f32[64,5120]{1,0:T(8,128)S(1)}) custom-call(bf16[32,5120]{1,0:T(8,128)(2,1)S(1)} %collective-permute-done.4.refs_0_, bf16[32,5120]{1,0:T(8,128)(2,1)S(1)} %collective-permute-done.3.refs_1_, ...), custom_call_target="tpu_custom_call", output_to_operand_aliasing={{0}: (6, {}), {1}: (7, {})} | custom-call | flops 167772160 | bytes 1000000 | tf_op jit(solution)/shard_map/rows/pallas_call | solution.py:48
  25.8 3.9 %collective-permute-done.5.end = bf16[32,3840]{1,0:T(8,128)(2,1)S(1)} collective-permute-done((bf16[32,3840]{1,0:T(8,128)(2,1)S(1)}, bf16[32,3840]{1,0:T(8,128)(2,1)S(1)}, u32[]{:S(2)}, u32[]{:S(2)}) %collective-permute-start.5) | collective-permute-done | bytes 245792 | tf_op jit(solution)/shard_map/ppermute | solution.py:323
  29.6 0.8 %begin.1 = (bf16[256,5120]{1,0:T(8,128)(2,1)S(1)}, f32[32,512]{1,0:T(8,128)S(1)}) custom-call(bf16[5120,512]{1,0:T(8,128)(2,1)S(1)} %get-tuple-element.57.refs_1_.refs_2_.w, bf16[32,3840]{1,0:T(8,128)(2,1)S(1)} %collective-permute-done.5.end, bf16[32,5120]{1,0:T(8,128)(2,1)S(1)} %collective-permute-done.1.between.refs_1_, ...), custom_call_target="tpu_custom_call", output_to_operand_aliasing={{0}: (3, {})} | custom-call | flops 1000000 | bytes 1000000 | tf_op jit(solution)/shard_map/begin/pallas_call | solution.py:48
  30.4 0.1 collective-permute-done.2.refs_0_
  30.5 1.0 %rows.5 = (bf16[256,5120]{1,0:T(8,128)(2,1)S(1)}, bf16[128,512]{1,0:T(8,128)(2,1)S(1)}, f32[8,5120]{1,0:T(8,128)S(1)}, f32[8,5120]{1,0:T(8,128)S(1)}, f32[8,5120...) custom-call(bf16[32,1280]{1,0:T(8,128)(2,1)S(1)} %collective-permute, ...), custom_call_target="tpu_custom_call", output_to_operand_aliasing={{0}: (7, {}), {1}: (8, {})} | custom-call | flops 167772160 | bytes 1000000 | tf_op jit(solution)/shard_map/rows/pallas_call | solution.py:48
  31.5 0.1 collective-permute-start.7
  31.6 0.5 collective-permute-start.9
  32.1 0.1 collective-permute-start.11
  32.2 0.8 %collective-permute-done.7 = f32[8,5120]{1,0:T(8,128)S(1)} collective-permute-done((f32[8,5120]{1,0:T(8,128)S(1)}, f32[8,5120]{1,0:T(8,128)S(1)}, u32[]{:S(2)}, u32[]{:S(2)}) %collective-permute-start.7) | collective-permute-done | bytes 163872 | tf_op jit(solution)/shard_map/ppermute | solution.py:328
  33.0 1.6 %collective-permute-start.8 = (f32[8,5120]{1,0:T(8,128)S(1)}, f32[8,5120]{1,0:T(8,128)S(1)}, u32[]{:S(2)}, u32[]{:S(2)}) collective-permute-start(f32[8,5120]{1,0:T(8,128)S(1)} %add.34), channel_id=1, source_target_pairs={{0,8},{4,12},{8,0},{12,4},{16,24},{20,28},{24,16},{28,20},{1,9},{5... | collective-permute-start | bytes 491528 | tf_op jit(solution)/shard_map/ppermute | solution.py:328
  34.6 0.0 collective-permute-done.9
  34.6 1.6 %collective-permute-start.10 = (f32[8,5120]{1,0:T(8,128)S(1)}, f32[8,5120]{1,0:T(8,128)S(1)}, u32[]{:S(2)}, u32[]{:S(2)}) collective-permute-start(f32[8,5120]{1,0:T(8,128)S(1)} %add.35), channel_id=1, source_target_pairs={{0,16},{4,20},{8,24},{12,28},{16,0},{20,4},{24,8},{28,12},{1,17},{... | collective-permute-start | bytes 491528 | tf_op jit(solution)/shard_map/ppermute | solution.py:328
  36.2 0.5 collective-permute-start.12
  36.7 0.4 merged.1.refs_4_
  37.1 3.0 %collective-permute-done.8 = f32[8,5120]{1,0:T(8,128)S(1)} collective-permute-done((f32[8,5120]{1,0:T(8,128)S(1)}, f32[8,5120]{1,0:T(8,128)S(1)}, u32[]{:S(2)}, u32[]{:S(2)}) %collective-permute-start.8) | collective-permute-done | bytes 163872 | tf_op jit(solution)/shard_map/ppermute | solution.py:328
  40.1 4.0 %collective-permute-done.10 = f32[8,5120]{1,0:T(8,128)S(1)} collective-permute-done((f32[8,5120]{1,0:T(8,128)S(1)}, f32[8,5120]{1,0:T(8,128)S(1)}, u32[]{:S(2)}, u32[]{:S(2)}) %collective-permute-start.10) | collective-permute-done | bytes 163872 | tf_op jit(solution)/shard_map/ppermute | solution.py:328
  44.1 0.1 add_add_fusion.refs_0_
  44.2 1.6 %collective-permute-start.18 = (f32[8,5120]{1,0:T(8,128)S(1)}, f32[8,5120]{1,0:T(8,128)S(1)}, u32[]{:S(2)}, u32[]{:S(2)}) collective-permute-start(f32[8,5120]{1,0:T(8,128)S(1)} %add_add_fusion.refs_0_), channel_id=1, source_target_pairs={{0,24},{4,28},{8,16},{12,20},{16,8},{20,12},{24,0},{28,4},{1,25},{... | collective-permute-start | bytes 491528 | tf_op jit(solution)/shard_map/ppermute | solution.py:328
  45.8 1.1 %collective-permute-start.16 = (f32[8,5120]{1,0:T(8,128)S(1)}, f32[8,5120]{1,0:T(8,128)S(1)}, u32[]{:S(2)}, u32[]{:S(2)}) collective-permute-start(f32[8,5120]{1,0:T(8,128)S(1)} %add_add_fusion.refs_0_), channel_id=1, source_target_pairs={{0,16},{4,20},{8,24},{12,28},{16,0},{20,4},{24,8},{28,12},{1,17},{... | collective-permute-start | bytes 491528 | tf_op jit(solution)/shard_map/ppermute | solution.py:328
  46.9 0.9 %collective-permute-start.14 = (f32[8,5120]{1,0:T(8,128)S(1)}, f32[8,5120]{1,0:T(8,128)S(1)}, u32[]{:S(2)}, u32[]{:S(2)}) collective-permute-start(f32[8,5120]{1,0:T(8,128)S(1)} %add_add_fusion.refs_0_), channel_id=1, source_target_pairs={{0,8},{4,12},{8,0},{12,4},{16,24},{20,28},{24,16},{28,20},{1,9},{5... | collective-permute-start | bytes 491528 | tf_op jit(solution)/shard_map/ppermute | solution.py:328
  47.8 4.3 %collective-permute-done.18.refs_6_ = f32[8,5120]{1,0:T(8,128)S(1)} collective-permute-done((f32[8,5120]{1,0:T(8,128)S(1)}, f32[8,5120]{1,0:T(8,128)S(1)}, u32[]{:S(2)}, u32[]{:S(2)}) %collective-permute-start.18) | collective-permute-done | bytes 163872 | tf_op jit(solution)/shard_map/ppermute | solution.py:328
  52.1 1.7 %collective-permute-done.16.refs_4_ = f32[8,5120]{1,0:T(8,128)S(1)} collective-permute-done((f32[8,5120]{1,0:T(8,128)S(1)}, f32[8,5120]{1,0:T(8,128)S(1)}, u32[]{:S(2)}, u32[]{:S(2)}) %collective-permute-start.16) | collective-permute-done | bytes 163872 | tf_op jit(solution)/shard_map/ppermute | solution.py:328
  53.8 0.0 collective-permute-done.14.refs_2_
  53.8 0.5 collective-permute-start.15
  54.3 0.9 %collective-permute-done.17.refs_5_ = f32[8,5120]{1,0:T(8,128)S(1)} collective-permute-done((f32[8,5120]{1,0:T(8,128)S(1)}, f32[8,5120]{1,0:T(8,128)S(1)}, u32[]{:S(2)}, u32[]{:S(2)}) %collective-permute-start.17) | collective-permute-done | bytes 163872 | tf_op jit(solution)/shard_map/ppermute | solution.py:328
  55.2 0.2 collective-permute-done.15.refs_3_
  55.4 2.0 %second.1 = (bf16[256,5120]{1,0:T(8,128)(2,1)S(1)}, f32[64,64]{1,0:T(8,128)S(1)}, f32[32,512]{1,0:T(8,128)S(1)}, f32[32,512]{1,0:T(8,128)S(1)}) custom-call(s32[1,4]{1,0:T(1,128)S(1)} %get-tuple-element.54.ids, f32[8,5120]{1,0:T(8,128)S(1)} %add_add_fusion.refs_0_, f32[8,5120]{1,0:T(8,128)S(1)} %collective-permute-done.13.refs_1_, ...), custom_call_target="tpu_custom_call", output_to_operand_aliasing={{0}: (11, {})} | custom-call | flops 1000000 | bytes 1000000 | tf_op jit(solution)/shard_map/second/pallas_call | solution.py:48
  57.4 0.3 collective-permute-start.20
  57.7 1.0 %collective-permute-done.20 = f32[32,512]{1,0:T(8,128)S(1)} collective-permute-done((f32[32,512]{1,0:T(8,128)S(1)}, f32[32,512]{1,0:T(8,128)S(1)}, u32[]{:S(2)}, u32[]{:S(2)}) %collective-permute-start.20) | collective-permute-done | bytes 65568 | tf_op jit(solution)/shard_map/ppermute | solution.py:328
  58.7 1.5 %collective-permute-start.23 = (f32[32,512]{1,0:T(8,128)S(1)}, f32[32,512]{1,0:T(8,128)S(1)}, u32[]{:S(2)}, u32[]{:S(2)}) collective-permute-start(f32[32,512]{1,0:T(8,128)S(1)} %add.40), channel_id=1, source_target_pairs={{0,24},{4,28},{8,16},{12,20},{16,8},{20,12},{24,0},{28,4},{1,25},{... | collective-permute-start | bytes 196616 | tf_op jit(solution)/shard_map/ppermute | solution.py:328
  60.2 1.5 %collective-permute-start.22 = (f32[32,512]{1,0:T(8,128)S(1)}, f32[32,512]{1,0:T(8,128)S(1)}, u32[]{:S(2)}, u32[]{:S(2)}) collective-permute-start(f32[32,512]{1,0:T(8,128)S(1)} %add.40), channel_id=1, source_target_pairs={{0,16},{4,20},{8,24},{12,28},{16,0},{20,4},{24,8},{28,12},{1,17},{... | collective-permute-start | bytes 196616 | tf_op jit(solution)/shard_map/ppermute | solution.py:328
  61.7 0.6 collective-permute-start.21
  62.3 2.3 %factor.1.linv.refs_2_ = f32[64,64]{1,0:T(8,128)S(1)} custom-call(f32[64,64]{1,0:T(8,128)S(1)} %get-tuple-element.90.gram), custom_call_target="tpu_custom_call" | custom-call | flops 1000000 | bytes 1000000 | tf_op jit(solution)/shard_map/factor/pallas_call | solution.py:48
  64.6 0.8 %collective-permute-done.22 = f32[32,512]{1,0:T(8,128)S(1)} collective-permute-done((f32[32,512]{1,0:T(8,128)S(1)}, f32[32,512]{1,0:T(8,128)S(1)}, u32[]{:S(2)}, u32[]{:S(2)}) %collective-permute-start.22) | collective-permute-done | bytes 65568 | tf_op jit(solution)/shard_map/ppermute | solution.py:328
  65.4 0.6 collective-permute-done.21
  66.0 0.1 collective-permute-start.24
  66.1 1.6 %left.1 = (f32[64,5120]{1,0:T(8,128)}, bf16[512,192]{1,0:T(8,128)(2,1)S(1)}) custom-call(s32[1,4]{1,0:T(1,128)S(1)} %get-tuple-element.54.ids, f32[64,64]{1,0:T(8,128)S(1)} %factor.1.linv.refs_2_, bf16[256,5120]{1,0:T(8,128)(2,1)S(1)} %get-tuple-element.96.bx), custom_call_target="tpu_custom_call" | custom-call | flops 1000000 | bytes 1000000 | tf_op jit(solution)/shard_map/left/pallas_call | solution.py:48
  67.6 1.5 %last.1 = (f32[64,512]{1,0:T(8,128)}, f32[4,128,512]{2,1,0:T(8,128)}) custom-call(f32[32,512]{1,0:T(8,128)S(1)} %add_add_fusion.1.refs_0_, f32[32,512]{1,0:T(8,128)S(1)} %collective-permute-done.24.refs_1_, f32[64,64]{1,0:T(8,128)S(1)} %factor.1.linv.refs_2_, bf16[512,192]{1,0:T(8,128)(2,1)S(1)} %get-tuple-element.101.refs_3_, f32[4,128,512]{2,1,0:T(8,128)S(1)} %merged.1.refs_4_), custom_call_target="tpu_custom_call" | custom-call | flops 1000000 | bytes 1000000 | tf_op jit(solution)/shard_map/last/pallas_call | solution.py:48
  (21 shorter events, 0.2 us)
Async XLA Ops:
  0.6 11.0 %collective-permute-start = (bf16[32,5120]{1,0:T(8,128)(2,1)}, bf16[32,5120]{1,0:T(8,128)(2,1)S(1)}, u32[]{:S(2)}, u32[]{:S(2)}) collective-permute-start(bf16[32,5120]{1,0:T(8,128)(2,1)} %refs_8_.1), channel_id=1, source_target_pairs={{0,1},{1,0},{2,3},{3,2},{4,5},{5,4},{6,7},{7,6},{8,9},{9,8},{10,11... | collective-permute-start | bytes 983048 | tf_op jit(solution)/shard_map/ppermute | solution.py:315
  3.7 8.6 %collective-permute-start.3 = (bf16[32,5120]{1,0:T(8,128)(2,1)}, bf16[32,5120]{1,0:T(8,128)(2,1)S(1)}, u32[]{:S(2)}, u32[]{:S(2)}) collective-permute-start(bf16[32,5120]{1,0:T(8,128)(2,1)} %refs_8_.1), channel_id=1, source_target_pairs={{1,2},{2,1},{5,6},{6,5},{9,10},{10,9},{13,14},{14,13},{17,18},{18,... | collective-permute-start | bytes 983048 | tf_op jit(solution)/shard_map/ppermute | solution.py:316
  11.6 7.1 %collective-permute-start.1 = (bf16[32,5120]{1,0:T(8,128)(2,1)S(1)}, bf16[32,5120]{1,0:T(8,128)(2,1)S(1)}, u32[]{:S(2)}, u32[]{:S(2)}) collective-permute-start(bf16[32,5120]{1,0:T(8,128)(2,1)S(1)} %collective-permute-done.refs_0_), channel_id=1, source_target_pairs={{1,2},{2,1},{5,6},{6,5},{9,10},{10,9},{13,14},{14,13},{17,18},{18,... | collective-permute-start | bytes 983048 | tf_op jit(solution)/shard_map/ppermute | solution.py:318
  12.3 11.8 %collective-permute-start.4 = (bf16[32,5120]{1,0:T(8,128)(2,1)S(1)}, bf16[32,5120]{1,0:T(8,128)(2,1)S(1)}, u32[]{:S(2)}, u32[]{:S(2)}) collective-permute-start(bf16[32,5120]{1,0:T(8,128)(2,1)S(1)} %collective-permute-done.3.refs_1_), channel_id=1, source_target_pairs={{0,1},{1,0},{2,3},{3,2},{4,5},{5,4},{6,7},{7,6},{8,9},{9,8},{10,11... | collective-permute-start | bytes 983048 | tf_op jit(solution)/shard_map/ppermute | solution.py:319
  18.8 10.8 %collective-permute-start.5 = (bf16[32,3840]{1,0:T(8,128)(2,1)S(1)}, bf16[32,3840]{1,0:T(8,128)(2,1)S(1)}, u32[]{:S(2)}, u32[]{:S(2)}) collective-permute-start(bf16[32,3840]{1,0:T(8,128)(2,1)S(1)} %slice.7), channel_id=1, source_target_pairs={{0,1},{1,0},{2,3},{3,2},{4,5},{5,4},{6,7},{7,6},{8,9},{9,8},{10,11... | collective-permute-start | bytes 737288 | tf_op jit(solution)/shard_map/ppermute | solution.py:323
  23.9 6.6 %collective-permute-start.2 = (bf16[32,1280]{1,0:T(8,128)(2,1)S(1)}, bf16[32,1280]{1,0:T(8,128)(2,1)S(1)}, u32[]{:S(2)}, u32[]{:S(2)}) collective-permute-start(bf16[32,1280]{1,0:T(8,128)(2,1)S(1)} %slice.6), channel_id=1, source_target_pairs={{0,1},{1,0},{2,3},{3,2},{4,5},{5,4},{6,7},{7,6},{8,9},{9,8},{10,11... | collective-permute-start | bytes 245768 | tf_op jit(solution)/shard_map/ppermute | solution.py:323
  31.5 1.5 %collective-permute-start.7 = (f32[8,5120]{1,0:T(8,128)S(1)}, f32[8,5120]{1,0:T(8,128)S(1)}, u32[]{:S(2)}, u32[]{:S(2)}) collective-permute-start(f32[8,5120]{1,0:T(8,128)S(1)} %get-tuple-element.76), channel_id=1, source_target_pairs={{0,4},{4,0},{8,12},{12,8},{16,20},{20,16},{24,28},{28,24},{1,5},{5... | collective-permute-start | bytes 491528 | tf_op jit(solution)/shard_map/ppermute | solution.py:328
  31.6 3.0 %collective-permute-start.9 = (f32[8,5120]{1,0:T(8,128)S(1)}, f32[8,5120]{1,0:T(8,128)S(1)}, u32[]{:S(2)}, u32[]{:S(2)}) collective-permute-start(f32[8,5120]{1,0:T(8,128)S(1)} %get-tuple-element.78), channel_id=1, source_target_pairs={{0,4},{4,0},{8,12},{12,8},{16,20},{20,16},{24,28},{28,24},{1,5},{5... | collective-permute-start | bytes 491528 | tf_op jit(solution)/shard_map/ppermute | solution.py:328
  32.1 4.1 %collective-permute-start.11 = (f32[8,5120]{1,0:T(8,128)S(1)}, f32[8,5120]{1,0:T(8,128)S(1)}, u32[]{:S(2)}, u32[]{:S(2)}) collective-permute-start(f32[8,5120]{1,0:T(8,128)S(1)} %get-tuple-element.80), channel_id=1, source_target_pairs={{0,4},{4,0},{8,12},{12,8},{16,20},{20,16},{24,28},{28,24},{1,5},{5... | collective-permute-start | bytes 491528 | tf_op jit(solution)/shard_map/ppermute | solution.py:328
  33.0 7.1 %collective-permute-start.8 = (f32[8,5120]{1,0:T(8,128)S(1)}, f32[8,5120]{1,0:T(8,128)S(1)}, u32[]{:S(2)}, u32[]{:S(2)}) collective-permute-start(f32[8,5120]{1,0:T(8,128)S(1)} %add.34), channel_id=1, source_target_pairs={{0,8},{4,12},{8,0},{12,4},{16,24},{20,28},{24,16},{28,20},{1,9},{5... | collective-permute-start | bytes 491528 | tf_op jit(solution)/shard_map/ppermute | solution.py:328
  34.6 9.5 %collective-permute-start.10 = (f32[8,5120]{1,0:T(8,128)S(1)}, f32[8,5120]{1,0:T(8,128)S(1)}, u32[]{:S(2)}, u32[]{:S(2)}) collective-permute-start(f32[8,5120]{1,0:T(8,128)S(1)} %add.35), channel_id=1, source_target_pairs={{0,16},{4,20},{8,24},{12,28},{16,0},{20,4},{24,8},{28,12},{1,17},{... | collective-permute-start | bytes 491528 | tf_op jit(solution)/shard_map/ppermute | solution.py:328
  36.2 7.9 %collective-permute-start.12 = (f32[8,5120]{1,0:T(8,128)S(1)}, f32[8,5120]{1,0:T(8,128)S(1)}, u32[]{:S(2)}, u32[]{:S(2)}) collective-permute-start(f32[8,5120]{1,0:T(8,128)S(1)} %add.36), channel_id=1, source_target_pairs={{0,24},{4,28},{8,16},{12,20},{16,8},{20,12},{24,0},{28,4},{1,25},{... | collective-permute-start | bytes 491528 | tf_op jit(solution)/shard_map/ppermute | solution.py:328
  36.7 7.4 %collective-permute-start.6 = (f32[8,5120]{1,0:T(8,128)S(1)}, f32[8,5120]{1,0:T(8,128)S(1)}, u32[]{:S(2)}, u32[]{:S(2)}) collective-permute-start(f32[8,5120]{1,0:T(8,128)S(1)} %get-tuple-element.74), channel_id=1, source_target_pairs={{0,4},{4,0},{8,12},{12,8},{16,20},{20,16},{24,28},{28,24},{1,5},{5... | collective-permute-start | bytes 491528 | tf_op jit(solution)/shard_map/ppermute | solution.py:328
  44.2 7.9 %collective-permute-start.18 = (f32[8,5120]{1,0:T(8,128)S(1)}, f32[8,5120]{1,0:T(8,128)S(1)}, u32[]{:S(2)}, u32[]{:S(2)}) collective-permute-start(f32[8,5120]{1,0:T(8,128)S(1)} %add_add_fusion.refs_0_), channel_id=1, source_target_pairs={{0,24},{4,28},{8,16},{12,20},{16,8},{20,12},{24,0},{28,4},{1,25},{... | collective-permute-start | bytes 491528 | tf_op jit(solution)/shard_map/ppermute | solution.py:328
  45.8 8.0 %collective-permute-start.16 = (f32[8,5120]{1,0:T(8,128)S(1)}, f32[8,5120]{1,0:T(8,128)S(1)}, u32[]{:S(2)}, u32[]{:S(2)}) collective-permute-start(f32[8,5120]{1,0:T(8,128)S(1)} %add_add_fusion.refs_0_), channel_id=1, source_target_pairs={{0,16},{4,20},{8,24},{12,28},{16,0},{20,4},{24,8},{28,12},{1,17},{... | collective-permute-start | bytes 491528 | tf_op jit(solution)/shard_map/ppermute | solution.py:328
  46.9 7.0 %collective-permute-start.14 = (f32[8,5120]{1,0:T(8,128)S(1)}, f32[8,5120]{1,0:T(8,128)S(1)}, u32[]{:S(2)}, u32[]{:S(2)}) collective-permute-start(f32[8,5120]{1,0:T(8,128)S(1)} %add_add_fusion.refs_0_), channel_id=1, source_target_pairs={{0,8},{4,12},{8,0},{12,4},{16,24},{20,28},{24,16},{28,20},{1,9},{5... | collective-permute-start | bytes 491528 | tf_op jit(solution)/shard_map/ppermute | solution.py:328
  47.8 6.5 %collective-permute-start.13 = (f32[8,5120]{1,0:T(8,128)S(1)}, f32[8,5120]{1,0:T(8,128)S(1)}, u32[]{:S(2)}, u32[]{:S(2)}) collective-permute-start(f32[8,5120]{1,0:T(8,128)S(1)} %add_add_fusion.refs_0_), channel_id=1, source_target_pairs={{0,4},{4,0},{8,12},{12,8},{16,20},{20,16},{24,28},{28,24},{1,5},{5... | collective-permute-start | bytes 491528 | tf_op jit(solution)/shard_map/ppermute | solution.py:328
  52.1 2.2 %collective-permute-start.19 = (f32[8,5120]{1,0:T(8,128)S(1)}, f32[8,5120]{1,0:T(8,128)S(1)}, u32[]{:S(2)}, u32[]{:S(2)}) collective-permute-start(f32[8,5120]{1,0:T(8,128)S(1)} %collective-permute-done.18.refs_6_), channel_id=1, source_target_pairs={{0,4},{4,0},{8,12},{12,8},{16,20},{20,16},{24,28},{28,24},{1,5},{5... | collective-permute-start | bytes 491528 | tf_op jit(solution)/shard_map/ppermute | solution.py:328
  53.8 1.4 %collective-permute-start.17 = (f32[8,5120]{1,0:T(8,128)S(1)}, f32[8,5120]{1,0:T(8,128)S(1)}, u32[]{:S(2)}, u32[]{:S(2)}) collective-permute-start(f32[8,5120]{1,0:T(8,128)S(1)} %collective-permute-done.16.refs_4_), channel_id=1, source_target_pairs={{0,4},{4,0},{8,12},{12,8},{16,20},{20,16},{24,28},{28,24},{1,5},{5... | collective-permute-start | bytes 491528 | tf_op jit(solution)/shard_map/ppermute | solution.py:328
  53.8 1.6 %collective-permute-start.15 = (f32[8,5120]{1,0:T(8,128)S(1)}, f32[8,5120]{1,0:T(8,128)S(1)}, u32[]{:S(2)}, u32[]{:S(2)}) collective-permute-start(f32[8,5120]{1,0:T(8,128)S(1)} %collective-permute-done.14.refs_2_), channel_id=1, source_target_pairs={{0,4},{4,0},{8,12},{12,8},{16,20},{20,16},{24,28},{28,24},{1,5},{5... | collective-permute-start | bytes 491528 | tf_op jit(solution)/shard_map/ppermute | solution.py:328
  57.4 1.3 %collective-permute-start.20 = (f32[32,512]{1,0:T(8,128)S(1)}, f32[32,512]{1,0:T(8,128)S(1)}, u32[]{:S(2)}, u32[]{:S(2)}) collective-permute-start(f32[32,512]{1,0:T(8,128)S(1)} %get-tuple-element.89), channel_id=1, source_target_pairs={{0,4},{4,0},{8,12},{12,8},{16,20},{20,16},{24,28},{28,24},{1,5},{5... | collective-permute-start | bytes 196616 | tf_op jit(solution)/shard_map/ppermute | solution.py:328
  58.7 5.9 %collective-permute-start.23 = (f32[32,512]{1,0:T(8,128)S(1)}, f32[32,512]{1,0:T(8,128)S(1)}, u32[]{:S(2)}, u32[]{:S(2)}) collective-permute-start(f32[32,512]{1,0:T(8,128)S(1)} %add.40), channel_id=1, source_target_pairs={{0,24},{4,28},{8,16},{12,20},{16,8},{20,12},{24,0},{28,4},{1,25},{... | collective-permute-start | bytes 196616 | tf_op jit(solution)/shard_map/ppermute | solution.py:328
  60.2 5.1 %collective-permute-start.22 = (f32[32,512]{1,0:T(8,128)S(1)}, f32[32,512]{1,0:T(8,128)S(1)}, u32[]{:S(2)}, u32[]{:S(2)}) collective-permute-start(f32[32,512]{1,0:T(8,128)S(1)} %add.40), channel_id=1, source_target_pairs={{0,16},{4,20},{8,24},{12,28},{16,0},{20,4},{24,8},{28,12},{1,17},{... | collective-permute-start | bytes 196616 | tf_op jit(solution)/shard_map/ppermute | solution.py:328
  61.7 4.3 %collective-permute-start.21 = (f32[32,512]{1,0:T(8,128)S(1)}, f32[32,512]{1,0:T(8,128)S(1)}, u32[]{:S(2)}, u32[]{:S(2)}) collective-permute-start(f32[32,512]{1,0:T(8,128)S(1)} %add.40), channel_id=1, source_target_pairs={{0,8},{4,12},{8,0},{12,4},{16,24},{20,28},{24,16},{28,20},{1,9},{5... | collective-permute-start | bytes 196616 | tf_op jit(solution)/shard_map/ppermute | solution.py:328
  66.0 1.7 %collective-permute-start.24 = (f32[32,512]{1,0:T(8,128)S(1)}, f32[32,512]{1,0:T(8,128)S(1)}, u32[]{:S(2)}, u32[]{:S(2)}) collective-permute-start(f32[32,512]{1,0:T(8,128)S(1)} %add_add_fusion.1.refs_0_), channel_id=1, source_target_pairs={{0,4},{4,0},{8,12},{12,8},{16,20},{20,16},{24,28},{28,24},{1,5},{5... | collective-permute-start | bytes 196616 | tf_op jit(solution)/shard_map/ppermute | solution.py:328

commit v8 on v6

--- a/solution.py
+++ b/solution.py
@@ -10,6 +10,7 @@
 BF16 = jnp.bfloat16
 HIGHEST = lax.Precision.HIGHEST
 VMEM_LIMIT = 16 * 1024 * 1024
+LEFT_TILE = 1024
 PREPARE_GRANT = 40 * 1024 * 1024
 
 
@@ -262,21 +263,25 @@
     linv[...] = inverse_factor(gram[...])
 
 
-def left_kernel(ids, linv, bx, pft, blocks):
+def left_kernel(ids, linv, bx, out, blocks, pft, sent):
     rank = linv.shape[0]
     high = linv[...].astype(BF16)
     low = (linv[...] - high.astype(F32)).astype(BF16)
     lhs = jnp.concatenate([high, high, low], axis=1)
-    wide = 1024
+    copies, wide = [], LEFT_TILE
     for i in range(pft.shape[1] // wide):
         at = slice(i * wide, (i + 1) * wide)
         pft[:, at] = dot(lhs, jnp.concatenate([bx[:2 * rank, at], bx[:rank, at]], axis=0), NN)
+        copies.append(pltpu.make_async_copy(pft.at[:, at], out.at[:, at], sent.at[i]))
+        copies[-1].start()
     block = blocks.shape[0] // ids.shape[1]
     for k in range(ids.shape[1]):
         piece = jnp.transpose(pft[:, lanes(ids[0, k], block)])
         high = piece.astype(BF16)
         low = (piece - high.astype(F32)).astype(BF16)
         blocks[k * block:(k + 1) * block, :] = jnp.concatenate([high, low, high], axis=1)
+    for copy in copies:
+        copy.wait()
 
 
 def last_kernel(n_u, scale, *refs):
@@ -413,7 +418,9 @@
     else:
         u_parts = [lax.psum(us[0], "dp")]
     pft, blocks = call(
-        left_kernel, [shape((rank, depth), F32), shape((kept * block, 3 * rank), BF16)], name="left",
+        left_kernel, [shape((rank, depth), F32), shape((kept * block, 3 * rank), BF16)],
+        [pltpu.VMEM((rank, depth), F32), pltpu.SemaphoreType.DMA((depth // LEFT_TILE,))], name="left",
+        out_specs=[pl.BlockSpec(memory_space=pl.ANY), VMEM],
     )(ids, linv, bx)
     if direct:
         other, blocks = together(u_parts[1], blocks)

time: 69.3 us -> 69.2 us (level)
  no operation moved by 1% of the time
where the time goes in v8:
time: 69.2 us; the launch traced here: 68.9 us
  starting transfers between devices  26.6 us (38%)
  waiting for transfers between devices  25.5 us (37%)
  Pallas kernels  15.9 us (23%)
  between operations  0.78 us (1%)
    ppermute x19, waiting for transfers between devices, swap(): return lax.ppermute(a, 'dp', [(i, i ^ bit) for i in range(size)])  17.3 us
    pallas_call x10, Pallas kernels, run(): pl.pallas_call(kernel, input_output_aliases=aliases or {}, out_shape=outs...  15.9 us
    ppermute x19, starting transfers between devices, swap(): return lax.ppermute(a, 'dp', [(i, i ^ bit) for i in range(size)])  12.3 us
    ppermute x2, starting transfers between devices, gather_rows(): lax.ppermute(part, 'mp', outer)  5.22 us
    ppermute x1, starting transfers between devices, gather_rows(): a1 = lax.ppermute(b0, 'mp', outer)  4.61 us
    ppermute x1, waiting for transfers between devices, gather_rows(): a0 = lax.ppermute(x, 'mp', outer)  4.12 us
    ppermute x2, waiting for transfers between devices, gather_rows(): lax.ppermute(part, 'mp', outer)  3.97 us
    ppermute x1, starting transfers between devices, gather_rows(): a0 = lax.ppermute(x, 'mp', outer)  3.09 us
  transfers between devices with their start and end apart: 25, of which 14 were waited for; matrix products, arithmetic and copies ran while one was open for 0% of the time, Pallas kernels for 17%

profile of v8, /device:TPU:0, one launch (start us, length us, event | category | flops | bytes accessed | tf_op | source)
XLA Modules:
  0.0 68.9 jit_solution(10178293256592978260)
XLA Ops:
  0.6 3.1 %collective-permute-start = (bf16[32,5120]{1,0:T(8,128)(2,1)}, bf16[32,5120]{1,0:T(8,128)(2,1)S(1)}, u32[]{:S(2)}, u32[]{:S(2)}) collective-permute-start(bf16[32,5120]{1,0:T(8,128)(2,1)} %refs_8_.1), channel_id=1, source_target_pairs={{0,1},{1,0},{2,3},{3,2},{4,5},{5,4},{6,7},{7,6},{8,9},{9,8},{10,11... | collective-permute-start | bytes 983048 | tf_op jit(solution)/shard_map/ppermute | solution.py:320
  3.7 0.7 collective-permute-start.3
  4.4 3.1 %prepare.1 = (s32[1,4]{1,0:T(1,128)S(1)}, bf16[5120,512]{1,0:T(8,128)(2,1)S(1)}, f32[4,128,512]{2,1,0:T(8,128)S(1)}, bf16[256,5120]{1,0:T(8,128)(2,1)S(1)}, f32[...) custom-call(s32[4,4]{1,0:T(4,128)} %refs_0_.1, ...), custom_call_target="tpu_custom_call" | custom-call | flops 1000000 | bytes 1000000 | tf_op jit(solution)/shard_map/prepare/pallas_call | solution.py:49
  7.5 4.1 %collective-permute-done.refs_0_ = bf16[32,5120]{1,0:T(8,128)(2,1)S(1)} collective-permute-done((bf16[32,5120]{1,0:T(8,128)(2,1)}, bf16[32,5120]{1,0:T(8,128)(2,1)S(1)}, u32[]{:S(2)}, u32[]{:S(2)}) %collective-permute-start) | collective-permute-done | bytes 327712 | tf_op jit(solution)/shard_map/ppermute | solution.py:320
  11.6 0.7 collective-permute-start.1
  12.3 0.0 collective-permute-done.3.refs_1_
  12.3 4.6 %collective-permute-start.4 = (bf16[32,5120]{1,0:T(8,128)(2,1)S(1)}, bf16[32,5120]{1,0:T(8,128)(2,1)S(1)}, u32[]{:S(2)}, u32[]{:S(2)}) collective-permute-start(bf16[32,5120]{1,0:T(8,128)(2,1)S(1)} %collective-permute-done.3.refs_1_), channel_id=1, source_target_pairs={{0,1},{1,0},{2,3},{3,2},{4,5},{5,4},{6,7},{7,6},{8,9},{9,8},{10,11... | collective-permute-start | bytes 983048 | tf_op jit(solution)/shard_map/ppermute | solution.py:324
  17.0 1.8 %rows.3 = (bf16[256,5120]{1,0:T(8,128)(2,1)S(1)}, bf16[128,512]{1,0:T(8,128)(2,1)S(1)}, f32[64,5120]{1,0:T(8,128)S(1)}) custom-call(bf16[32,5120]{1,0:T(8,128)(2,1)S(1)} %collective-permute-done.refs_0_, bf16[5120,512]{1,0:T(8,128)(2,1)S(1)} %get-tuple-element.57.refs_1_.refs_2_.w, ...), custom_call_target="tpu_custom_call", output_to_operand_aliasing={{0}: (5, {}), {1}: (6, {})} | custom-call | flops 167772160 | bytes 1000000 | tf_op jit(solution)/shard_map/rows/pallas_call | solution.py:49
  18.8 5.1 %collective-permute-start.5 = (bf16[32,3840]{1,0:T(8,128)(2,1)S(1)}, bf16[32,3840]{1,0:T(8,128)(2,1)S(1)}, u32[]{:S(2)}, u32[]{:S(2)}) collective-permute-start(bf16[32,3840]{1,0:T(8,128)(2,1)S(1)} %slice.7), channel_id=1, source_target_pairs={{0,1},{1,0},{2,3},{3,2},{4,5},{5,4},{6,7},{7,6},{8,9},{9,8},{10,11... | collective-permute-start | bytes 737288 | tf_op jit(solution)/shard_map/ppermute | solution.py:328
  23.9 0.1 collective-permute-start.2
  24.0 0.1 collective-permute-done.4.refs_0_
  24.1 1.7 %rows.4 = (bf16[256,5120]{1,0:T(8,128)(2,1)S(1)}, bf16[128,512]{1,0:T(8,128)(2,1)S(1)}, f32[64,5120]{1,0:T(8,128)S(1)}) custom-call(bf16[32,5120]{1,0:T(8,128)(2,1)S(1)} %collective-permute-done.4.refs_0_, bf16[32,5120]{1,0:T(8,128)(2,1)S(1)} %collective-permute-done.3.refs_1_, ...), custom_call_target="tpu_custom_call", output_to_operand_aliasing={{0}: (6, {}), {1}: (7, {})} | custom-call | flops 167772160 | bytes 1000000 | tf_op jit(solution)/shard_map/rows/pallas_call | solution.py:49
  25.8 3.9 %collective-permute-done.5.end = bf16[32,3840]{1,0:T(8,128)(2,1)S(1)} collective-permute-done((bf16[32,3840]{1,0:T(8,128)(2,1)S(1)}, bf16[32,3840]{1,0:T(8,128)(2,1)S(1)}, u32[]{:S(2)}, u32[]{:S(2)}) %collective-permute-start.5) | collective-permute-done | bytes 245792 | tf_op jit(solution)/shard_map/ppermute | solution.py:328
  29.6 0.8 %begin.1 = (bf16[256,5120]{1,0:T(8,128)(2,1)S(1)}, f32[32,512]{1,0:T(8,128)S(1)}) custom-call(bf16[5120,512]{1,0:T(8,128)(2,1)S(1)} %get-tuple-element.57.refs_1_.refs_2_.w, bf16[32,3840]{1,0:T(8,128)(2,1)S(1)} %collective-permute-done.5.end, bf16[32,5120]{1,0:T(8,128)(2,1)S(1)} %collective-permute-done.1.between.refs_1_, ...), custom_call_target="tpu_custom_call", output_to_operand_aliasing={{0}: (3, {})} | custom-call | flops 1000000 | bytes 1000000 | tf_op jit(solution)/shard_map/begin/pallas_call | solution.py:49
  30.4 0.1 collective-permute-done.2.refs_0_
  30.5 1.0 %rows.5 = (bf16[256,5120]{1,0:T(8,128)(2,1)S(1)}, bf16[128,512]{1,0:T(8,128)(2,1)S(1)}, f32[8,5120]{1,0:T(8,128)S(1)}, f32[8,5120]{1,0:T(8,128)S(1)}, f32[8,5120...) custom-call(bf16[32,1280]{1,0:T(8,128)(2,1)S(1)} %collective-permute, ...), custom_call_target="tpu_custom_call", output_to_operand_aliasing={{0}: (7, {}), {1}: (8, {})} | custom-call | flops 167772160 | bytes 1000000 | tf_op jit(solution)/shard_map/rows/pallas_call | solution.py:49
  31.5 0.1 collective-permute-start.7
  31.6 0.5 collective-permute-start.9
  32.1 0.1 collective-permute-start.11
  32.2 0.8 %collective-permute-done.7 = f32[8,5120]{1,0:T(8,128)S(1)} collective-permute-done((f32[8,5120]{1,0:T(8,128)S(1)}, f32[8,5120]{1,0:T(8,128)S(1)}, u32[]{:S(2)}, u32[]{:S(2)}) %collective-permute-start.7) | collective-permute-done | bytes 163872 | tf_op jit(solution)/shard_map/ppermute | solution.py:333
  33.0 1.6 %collective-permute-start.8 = (f32[8,5120]{1,0:T(8,128)S(1)}, f32[8,5120]{1,0:T(8,128)S(1)}, u32[]{:S(2)}, u32[]{:S(2)}) collective-permute-start(f32[8,5120]{1,0:T(8,128)S(1)} %add.34), channel_id=1, source_target_pairs={{0,8},{4,12},{8,0},{12,4},{16,24},{20,28},{24,16},{28,20},{1,9},{5... | collective-permute-start | bytes 491528 | tf_op jit(solution)/shard_map/ppermute | solution.py:333
  34.6 1.6 %collective-permute-start.10 = (f32[8,5120]{1,0:T(8,128)S(1)}, f32[8,5120]{1,0:T(8,128)S(1)}, u32[]{:S(2)}, u32[]{:S(2)}) collective-permute-start(f32[8,5120]{1,0:T(8,128)S(1)} %add.35), channel_id=1, source_target_pairs={{0,16},{4,20},{8,24},{12,28},{16,0},{20,4},{24,8},{28,12},{1,17},{... | collective-permute-start | bytes 491528 | tf_op jit(solution)/shard_map/ppermute | solution.py:333
  36.2 0.5 collective-permute-start.12
  36.7 0.4 merged.1.refs_4_
  37.1 3.0 %collective-permute-done.8 = f32[8,5120]{1,0:T(8,128)S(1)} collective-permute-done((f32[8,5120]{1,0:T(8,128)S(1)}, f32[8,5120]{1,0:T(8,128)S(1)}, u32[]{:S(2)}, u32[]{:S(2)}) %collective-permute-start.8) | collective-permute-done | bytes 163872 | tf_op jit(solution)/shard_map/ppermute | solution.py:333
  40.1 4.0 %collective-permute-done.10 = f32[8,5120]{1,0:T(8,128)S(1)} collective-permute-done((f32[8,5120]{1,0:T(8,128)S(1)}, f32[8,5120]{1,0:T(8,128)S(1)}, u32[]{:S(2)}, u32[]{:S(2)}) %collective-permute-start.10) | collective-permute-done | bytes 163872 | tf_op jit(solution)/shard_map/ppermute | solution.py:333
  44.1 0.1 add_add_fusion.refs_0_
  44.2 1.6 %collective-permute-start.18 = (f32[8,5120]{1,0:T(8,128)S(1)}, f32[8,5120]{1,0:T(8,128)S(1)}, u32[]{:S(2)}, u32[]{:S(2)}) collective-permute-start(f32[8,5120]{1,0:T(8,128)S(1)} %add_add_fusion.refs_0_), channel_id=1, source_target_pairs={{0,24},{4,28},{8,16},{12,20},{16,8},{20,12},{24,0},{28,4},{1,25},{... | collective-permute-start | bytes 491528 | tf_op jit(solution)/shard_map/ppermute | solution.py:333
  45.8 1.1 %collective-permute-start.16 = (f32[8,5120]{1,0:T(8,128)S(1)}, f32[8,5120]{1,0:T(8,128)S(1)}, u32[]{:S(2)}, u32[]{:S(2)}) collective-permute-start(f32[8,5120]{1,0:T(8,128)S(1)} %add_add_fusion.refs_0_), channel_id=1, source_target_pairs={{0,16},{4,20},{8,24},{12,28},{16,0},{20,4},{24,8},{28,12},{1,17},{... | collective-permute-start | bytes 491528 | tf_op jit(solution)/shard_map/ppermute | solution.py:333
  46.9 0.9 %collective-permute-start.14 = (f32[8,5120]{1,0:T(8,128)S(1)}, f32[8,5120]{1,0:T(8,128)S(1)}, u32[]{:S(2)}, u32[]{:S(2)}) collective-permute-start(f32[8,5120]{1,0:T(8,128)S(1)} %add_add_fusion.refs_0_), channel_id=1, source_target_pairs={{0,8},{4,12},{8,0},{12,4},{16,24},{20,28},{24,16},{28,20},{1,9},{5... | collective-permute-start | bytes 491528 | tf_op jit(solution)/shard_map/ppermute | solution.py:333
  47.8 4.3 %collective-permute-done.18.refs_6_ = f32[8,5120]{1,0:T(8,128)S(1)} collective-permute-done((f32[8,5120]{1,0:T(8,128)S(1)}, f32[8,5120]{1,0:T(8,128)S(1)}, u32[]{:S(2)}, u32[]{:S(2)}) %collective-permute-start.18) | collective-permute-done | bytes 163872 | tf_op jit(solution)/shard_map/ppermute | solution.py:333
  52.1 1.7 %collective-permute-done.16.refs_4_ = f32[8,5120]{1,0:T(8,128)S(1)} collective-permute-done((f32[8,5120]{1,0:T(8,128)S(1)}, f32[8,5120]{1,0:T(8,128)S(1)}, u32[]{:S(2)}, u32[]{:S(2)}) %collective-permute-start.16) | collective-permute-done | bytes 163872 | tf_op jit(solution)/shard_map/ppermute | solution.py:333
  53.8 0.0 collective-permute-done.14.refs_2_
  53.8 0.5 collective-permute-start.15
  54.3 0.9 %collective-permute-done.17.refs_5_ = f32[8,5120]{1,0:T(8,128)S(1)} collective-permute-done((f32[8,5120]{1,0:T(8,128)S(1)}, f32[8,5120]{1,0:T(8,128)S(1)}, u32[]{:S(2)}, u32[]{:S(2)}) %collective-permute-start.17) | collective-permute-done | bytes 163872 | tf_op jit(solution)/shard_map/ppermute | solution.py:333
  55.2 0.2 collective-permute-done.15.refs_3_
  55.4 2.0 %second.1 = (bf16[256,5120]{1,0:T(8,128)(2,1)S(1)}, f32[64,64]{1,0:T(8,128)S(1)}, f32[32,512]{1,0:T(8,128)S(1)}, f32[32,512]{1,0:T(8,128)S(1)}) custom-call(s32[1,4]{1,0:T(1,128)S(1)} %get-tuple-element.54.ids, f32[8,5120]{1,0:T(8,128)S(1)} %add_add_fusion.refs_0_, f32[8,5120]{1,0:T(8,128)S(1)} %collective-permute-done.13.refs_1_, ...), custom_call_target="tpu_custom_call", output_to_operand_aliasing={{0}: (11, {})} | custom-call | flops 1000000 | bytes 1000000 | tf_op jit(solution)/shard_map/second/pallas_call | solution.py:49
  57.4 0.3 collective-permute-start.20
  57.7 1.0 %collective-permute-done.20 = f32[32,512]{1,0:T(8,128)S(1)} collective-permute-done((f32[32,512]{1,0:T(8,128)S(1)}, f32[32,512]{1,0:T(8,128)S(1)}, u32[]{:S(2)}, u32[]{:S(2)}) %collective-permute-start.20) | collective-permute-done | bytes 65568 | tf_op jit(solution)/shard_map/ppermute | solution.py:333
  58.7 1.5 %collective-permute-start.23 = (f32[32,512]{1,0:T(8,128)S(1)}, f32[32,512]{1,0:T(8,128)S(1)}, u32[]{:S(2)}, u32[]{:S(2)}) collective-permute-start(f32[32,512]{1,0:T(8,128)S(1)} %add.40), channel_id=1, source_target_pairs={{0,24},{4,28},{8,16},{12,20},{16,8},{20,12},{24,0},{28,4},{1,25},{... | collective-permute-start | bytes 196616 | tf_op jit(solution)/shard_map/ppermute | solution.py:333
  60.2 1.5 %collective-permute-start.22 = (f32[32,512]{1,0:T(8,128)S(1)}, f32[32,512]{1,0:T(8,128)S(1)}, u32[]{:S(2)}, u32[]{:S(2)}) collective-permute-start(f32[32,512]{1,0:T(8,128)S(1)} %add.40), channel_id=1, source_target_pairs={{0,16},{4,20},{8,24},{12,28},{16,0},{20,4},{24,8},{28,12},{1,17},{... | collective-permute-start | bytes 196616 | tf_op jit(solution)/shard_map/ppermute | solution.py:333
  61.7 0.6 collective-permute-start.21
  62.3 2.3 %factor.1.linv.refs_2_ = f32[64,64]{1,0:T(8,128)S(1)} custom-call(f32[64,64]{1,0:T(8,128)S(1)} %get-tuple-element.90.gram), custom_call_target="tpu_custom_call" | custom-call | flops 1000000 | bytes 1000000 | tf_op jit(solution)/shard_map/factor/pallas_call | solution.py:49
  64.6 0.8 %collective-permute-done.22 = f32[32,512]{1,0:T(8,128)S(1)} collective-permute-done((f32[32,512]{1,0:T(8,128)S(1)}, f32[32,512]{1,0:T(8,128)S(1)}, u32[]{:S(2)}, u32[]{:S(2)}) %collective-permute-start.22) | collective-permute-done | bytes 65568 | tf_op jit(solution)/shard_map/ppermute | solution.py:333
  65.4 0.6 collective-permute-done.21
  66.0 0.1 collective-permute-start.24
  66.1 1.4 %left.1 = (f32[64,5120]{1,0:T(8,128)}, bf16[512,192]{1,0:T(8,128)(2,1)S(1)}) custom-call(s32[1,4]{1,0:T(1,128)S(1)} %get-tuple-element.54.ids, f32[64,64]{1,0:T(8,128)S(1)} %factor.1.linv.refs_2_, bf16[256,5120]{1,0:T(8,128)(2,1)S(1)} %get-tuple-element.96.bx), custom_call_target="tpu_custom_call" | custom-call | flops 1000000 | bytes 1000000 | tf_op jit(solution)/shard_map/left/pallas_call | solution.py:49
  67.5 1.5 %last.1 = (f32[64,512]{1,0:T(8,128)}, f32[4,128,512]{2,1,0:T(8,128)}) custom-call(f32[32,512]{1,0:T(8,128)S(1)} %add_add_fusion.1.refs_0_, f32[32,512]{1,0:T(8,128)S(1)} %collective-permute-done.24.refs_1_, f32[64,64]{1,0:T(8,128)S(1)} %factor.1.linv.refs_2_, bf16[512,192]{1,0:T(8,128)(2,1)S(1)} %get-tuple-element.101.refs_3_, f32[4,128,512]{2,1,0:T(8,128)S(1)} %merged.1.refs_4_), custom_call_target="tpu_custom_call" | custom-call | flops 1000000 | bytes 1000000 | tf_op jit(solution)/shard_map/last/pallas_call | solution.py:49
  (21 shorter events, 0.2 us)
Async XLA Ops:
  0.6 11.0 %collective-permute-start = (bf16[32,5120]{1,0:T(8,128)(2,1)}, bf16[32,5120]{1,0:T(8,128)(2,1)S(1)}, u32[]{:S(2)}, u32[]{:S(2)}) collective-permute-start(bf16[32,5120]{1,0:T(8,128)(2,1)} %refs_8_.1), channel_id=1, source_target_pairs={{0,1},{1,0},{2,3},{3,2},{4,5},{5,4},{6,7},{7,6},{8,9},{9,8},{10,11... | collective-permute-start | bytes 983048 | tf_op jit(solution)/shard_map/ppermute | solution.py:320
  3.7 8.6 %collective-permute-start.3 = (bf16[32,5120]{1,0:T(8,128)(2,1)}, bf16[32,5120]{1,0:T(8,128)(2,1)S(1)}, u32[]{:S(2)}, u32[]{:S(2)}) collective-permute-start(bf16[32,5120]{1,0:T(8,128)(2,1)} %refs_8_.1), channel_id=1, source_target_pairs={{1,2},{2,1},{5,6},{6,5},{9,10},{10,9},{13,14},{14,13},{17,18},{18,... | collective-permute-start | bytes 983048 | tf_op jit(solution)/shard_map/ppermute | solution.py:321
  11.6 7.1 %collective-permute-start.1 = (bf16[32,5120]{1,0:T(8,128)(2,1)S(1)}, bf16[32,5120]{1,0:T(8,128)(2,1)S(1)}, u32[]{:S(2)}, u32[]{:S(2)}) collective-permute-start(bf16[32,5120]{1,0:T(8,128)(2,1)S(1)} %collective-permute-done.refs_0_), channel_id=1, source_target_pairs={{1,2},{2,1},{5,6},{6,5},{9,10},{10,9},{13,14},{14,13},{17,18},{18,... | collective-permute-start | bytes 983048 | tf_op jit(solution)/shard_map/ppermute | solution.py:323
  12.3 11.8 %collective-permute-start.4 = (bf16[32,5120]{1,0:T(8,128)(2,1)S(1)}, bf16[32,5120]{1,0:T(8,128)(2,1)S(1)}, u32[]{:S(2)}, u32[]{:S(2)}) collective-permute-start(bf16[32,5120]{1,0:T(8,128)(2,1)S(1)} %collective-permute-done.3.refs_1_), channel_id=1, source_target_pairs={{0,1},{1,0},{2,3},{3,2},{4,5},{5,4},{6,7},{7,6},{8,9},{9,8},{10,11... | collective-permute-start | bytes 983048 | tf_op jit(solution)/shard_map/ppermute | solution.py:324
  18.8 10.8 %collective-permute-start.5 = (bf16[32,3840]{1,0:T(8,128)(2,1)S(1)}, bf16[32,3840]{1,0:T(8,128)(2,1)S(1)}, u32[]{:S(2)}, u32[]{:S(2)}) collective-permute-start(bf16[32,3840]{1,0:T(8,128)(2,1)S(1)} %slice.7), channel_id=1, source_target_pairs={{0,1},{1,0},{2,3},{3,2},{4,5},{5,4},{6,7},{7,6},{8,9},{9,8},{10,11... | collective-permute-start | bytes 737288 | tf_op jit(solution)/shard_map/ppermute | solution.py:328
  23.9 6.6 %collective-permute-start.2 = (bf16[32,1280]{1,0:T(8,128)(2,1)S(1)}, bf16[32,1280]{1,0:T(8,128)(2,1)S(1)}, u32[]{:S(2)}, u32[]{:S(2)}) collective-permute-start(bf16[32,1280]{1,0:T(8,128)(2,1)S(1)} %slice.6), channel_id=1, source_target_pairs={{0,1},{1,0},{2,3},{3,2},{4,5},{5,4},{6,7},{7,6},{8,9},{9,8},{10,11... | collective-permute-start | bytes 245768 | tf_op jit(solution)/shard_map/ppermute | solution.py:328
  31.5 1.5 %collective-permute-start.7 = (f32[8,5120]{1,0:T(8,128)S(1)}, f32[8,5120]{1,0:T(8,128)S(1)}, u32[]{:S(2)}, u32[]{:S(2)}) collective-permute-start(f32[8,5120]{1,0:T(8,128)S(1)} %get-tuple-element.76), channel_id=1, source_target_pairs={{0,4},{4,0},{8,12},{12,8},{16,20},{20,16},{24,28},{28,24},{1,5},{5... | collective-permute-start | bytes 491528 | tf_op jit(solution)/shard_map/ppermute | solution.py:333
  31.6 3.0 %collective-permute-start.9 = (f32[8,5120]{1,0:T(8,128)S(1)}, f32[8,5120]{1,0:T(8,128)S(1)}, u32[]{:S(2)}, u32[]{:S(2)}) collective-permute-start(f32[8,5120]{1,0:T(8,128)S(1)} %get-tuple-element.78), channel_id=1, source_target_pairs={{0,4},{4,0},{8,12},{12,8},{16,20},{20,16},{24,28},{28,24},{1,5},{5... | collective-permute-start | bytes 491528 | tf_op jit(solution)/shard_map/ppermute | solution.py:333
  32.1 4.1 %collective-permute-start.11 = (f32[8,5120]{1,0:T(8,128)S(1)}, f32[8,5120]{1,0:T(8,128)S(1)}, u32[]{:S(2)}, u32[]{:S(2)}) collective-permute-start(f32[8,5120]{1,0:T(8,128)S(1)} %get-tuple-element.80), channel_id=1, source_target_pairs={{0,4},{4,0},{8,12},{12,8},{16,20},{20,16},{24,28},{28,24},{1,5},{5... | collective-permute-start | bytes 491528 | tf_op jit(solution)/shard_map/ppermute | solution.py:333
  33.0 7.1 %collective-permute-start.8 = (f32[8,5120]{1,0:T(8,128)S(1)}, f32[8,5120]{1,0:T(8,128)S(1)}, u32[]{:S(2)}, u32[]{:S(2)}) collective-permute-start(f32[8,5120]{1,0:T(8,128)S(1)} %add.34), channel_id=1, source_target_pairs={{0,8},{4,12},{8,0},{12,4},{16,24},{20,28},{24,16},{28,20},{1,9},{5... | collective-permute-start | bytes 491528 | tf_op jit(solution)/shard_map/ppermute | solution.py:333
  34.6 9.5 %collective-permute-start.10 = (f32[8,5120]{1,0:T(8,128)S(1)}, f32[8,5120]{1,0:T(8,128)S(1)}, u32[]{:S(2)}, u32[]{:S(2)}) collective-permute-start(f32[8,5120]{1,0:T(8,128)S(1)} %add.35), channel_id=1, source_target_pairs={{0,16},{4,20},{8,24},{12,28},{16,0},{20,4},{24,8},{28,12},{1,17},{... | collective-permute-start | bytes 491528 | tf_op jit(solution)/shard_map/ppermute | solution.py:333
  36.2 7.9 %collective-permute-start.12 = (f32[8,5120]{1,0:T(8,128)S(1)}, f32[8,5120]{1,0:T(8,128)S(1)}, u32[]{:S(2)}, u32[]{:S(2)}) collective-permute-start(f32[8,5120]{1,0:T(8,128)S(1)} %add.36), channel_id=1, source_target_pairs={{0,24},{4,28},{8,16},{12,20},{16,8},{20,12},{24,0},{28,4},{1,25},{... | collective-permute-start | bytes 491528 | tf_op jit(solution)/shard_map/ppermute | solution.py:333
  36.7 7.4 %collective-permute-start.6 = (f32[8,5120]{1,0:T(8,128)S(1)}, f32[8,5120]{1,0:T(8,128)S(1)}, u32[]{:S(2)}, u32[]{:S(2)}) collective-permute-start(f32[8,5120]{1,0:T(8,128)S(1)} %get-tuple-element.74), channel_id=1, source_target_pairs={{0,4},{4,0},{8,12},{12,8},{16,20},{20,16},{24,28},{28,24},{1,5},{5... | collective-permute-start | bytes 491528 | tf_op jit(solution)/shard_map/ppermute | solution.py:333
  44.2 7.9 %collective-permute-start.18 = (f32[8,5120]{1,0:T(8,128)S(1)}, f32[8,5120]{1,0:T(8,128)S(1)}, u32[]{:S(2)}, u32[]{:S(2)}) collective-permute-start(f32[8,5120]{1,0:T(8,128)S(1)} %add_add_fusion.refs_0_), channel_id=1, source_target_pairs={{0,24},{4,28},{8,16},{12,20},{16,8},{20,12},{24,0},{28,4},{1,25},{... | collective-permute-start | bytes 491528 | tf_op jit(solution)/shard_map/ppermute | solution.py:333
  45.8 8.0 %collective-permute-start.16 = (f32[8,5120]{1,0:T(8,128)S(1)}, f32[8,5120]{1,0:T(8,128)S(1)}, u32[]{:S(2)}, u32[]{:S(2)}) collective-permute-start(f32[8,5120]{1,0:T(8,128)S(1)} %add_add_fusion.refs_0_), channel_id=1, source_target_pairs={{0,16},{4,20},{8,24},{12,28},{16,0},{20,4},{24,8},{28,12},{1,17},{... | collective-permute-start | bytes 491528 | tf_op jit(solution)/shard_map/ppermute | solution.py:333
  46.9 7.0 %collective-permute-start.14 = (f32[8,5120]{1,0:T(8,128)S(1)}, f32[8,5120]{1,0:T(8,128)S(1)}, u32[]{:S(2)}, u32[]{:S(2)}) collective-permute-start(f32[8,5120]{1,0:T(8,128)S(1)} %add_add_fusion.refs_0_), channel_id=1, source_target_pairs={{0,8},{4,12},{8,0},{12,4},{16,24},{20,28},{24,16},{28,20},{1,9},{5... | collective-permute-start | bytes 491528 | tf_op jit(solution)/shard_map/ppermute | solution.py:333
  47.8 6.5 %collective-permute-start.13 = (f32[8,5120]{1,0:T(8,128)S(1)}, f32[8,5120]{1,0:T(8,128)S(1)}, u32[]{:S(2)}, u32[]{:S(2)}) collective-permute-start(f32[8,5120]{1,0:T(8,128)S(1)} %add_add_fusion.refs_0_), channel_id=1, source_target_pairs={{0,4},{4,0},{8,12},{12,8},{16,20},{20,16},{24,28},{28,24},{1,5},{5... | collective-permute-start | bytes 491528 | tf_op jit(solution)/shard_map/ppermute | solution.py:333
  52.1 2.2 %collective-permute-start.19 = (f32[8,5120]{1,0:T(8,128)S(1)}, f32[8,5120]{1,0:T(8,128)S(1)}, u32[]{:S(2)}, u32[]{:S(2)}) collective-permute-start(f32[8,5120]{1,0:T(8,128)S(1)} %collective-permute-done.18.refs_6_), channel_id=1, source_target_pairs={{0,4},{4,0},{8,12},{12,8},{16,20},{20,16},{24,28},{28,24},{1,5},{5... | collective-permute-start | bytes 491528 | tf_op jit(solution)/shard_map/ppermute | solution.py:333
  53.8 1.4 %collective-permute-start.17 = (f32[8,5120]{1,0:T(8,128)S(1)}, f32[8,5120]{1,0:T(8,128)S(1)}, u32[]{:S(2)}, u32[]{:S(2)}) collective-permute-start(f32[8,5120]{1,0:T(8,128)S(1)} %collective-permute-done.16.refs_4_), channel_id=1, source_target_pairs={{0,4},{4,0},{8,12},{12,8},{16,20},{20,16},{24,28},{28,24},{1,5},{5... | collective-permute-start | bytes 491528 | tf_op jit(solution)/shard_map/ppermute | solution.py:333
  53.8 1.6 %collective-permute-start.15 = (f32[8,5120]{1,0:T(8,128)S(1)}, f32[8,5120]{1,0:T(8,128)S(1)}, u32[]{:S(2)}, u32[]{:S(2)}) collective-permute-start(f32[8,5120]{1,0:T(8,128)S(1)} %collective-permute-done.14.refs_2_), channel_id=1, source_target_pairs={{0,4},{4,0},{8,12},{12,8},{16,20},{20,16},{24,28},{28,24},{1,5},{5... | collective-permute-start | bytes 491528 | tf_op jit(solution)/shard_map/ppermute | solution.py:333
  57.4 1.3 %collective-permute-start.20 = (f32[32,512]{1,0:T(8,128)S(1)}, f32[32,512]{1,0:T(8,128)S(1)}, u32[]{:S(2)}, u32[]{:S(2)}) collective-permute-start(f32[32,512]{1,0:T(8,128)S(1)} %get-tuple-element.89), channel_id=1, source_target_pairs={{0,4},{4,0},{8,12},{12,8},{16,20},{20,16},{24,28},{28,24},{1,5},{5... | collective-permute-start | bytes 196616 | tf_op jit(solution)/shard_map/ppermute | solution.py:333
  58.7 5.9 %collective-permute-start.23 = (f32[32,512]{1,0:T(8,128)S(1)}, f32[32,512]{1,0:T(8,128)S(1)}, u32[]{:S(2)}, u32[]{:S(2)}) collective-permute-start(f32[32,512]{1,0:T(8,128)S(1)} %add.40), channel_id=1, source_target_pairs={{0,24},{4,28},{8,16},{12,20},{16,8},{20,12},{24,0},{28,4},{1,25},{... | collective-permute-start | bytes 196616 | tf_op jit(solution)/shard_map/ppermute | solution.py:333
  60.2 5.2 %collective-permute-start.22 = (f32[32,512]{1,0:T(8,128)S(1)}, f32[32,512]{1,0:T(8,128)S(1)}, u32[]{:S(2)}, u32[]{:S(2)}) collective-permute-start(f32[32,512]{1,0:T(8,128)S(1)} %add.40), channel_id=1, source_target_pairs={{0,16},{4,20},{8,24},{12,28},{16,0},{20,4},{24,8},{28,12},{1,17},{... | collective-permute-start | bytes 196616 | tf_op jit(solution)/shard_map/ppermute | solution.py:333
  61.7 4.3 %collective-permute-start.21 = (f32[32,512]{1,0:T(8,128)S(1)}, f32[32,512]{1,0:T(8,128)S(1)}, u32[]{:S(2)}, u32[]{:S(2)}) collective-permute-start(f32[32,512]{1,0:T(8,128)S(1)} %add.40), channel_id=1, source_target_pairs={{0,8},{4,12},{8,0},{12,4},{16,24},{20,28},{24,16},{28,20},{1,9},{5... | collective-permute-start | bytes 196616 | tf_op jit(solution)/shard_map/ppermute | solution.py:333
  66.0 1.5 %collective-permute-start.24 = (f32[32,512]{1,0:T(8,128)S(1)}, f32[32,512]{1,0:T(8,128)S(1)}, u32[]{:S(2)}, u32[]{:S(2)}) collective-permute-start(f32[32,512]{1,0:T(8,128)S(1)} %add_add_fusion.1.refs_0_), channel_id=1, source_target_pairs={{0,4},{4,0},{8,12},{12,8},{16,20},{20,16},{24,28},{28,24},{1,5},{5... | collective-permute-start | bytes 196616 | tf_op jit(solution)/shard_map/ppermute | solution.py:333

commit v9 on v8

--- a/solution.py
+++ b/solution.py
@@ -10,7 +10,7 @@
 BF16 = jnp.bfloat16
 HIGHEST = lax.Precision.HIGHEST
 VMEM_LIMIT = 16 * 1024 * 1024
-LEFT_TILE = 1024
+LEFT_TILE = 512
 PREPARE_GRANT = 40 * 1024 * 1024
 
 

time: 69.2 us -> 69.2 us (level)
  no operation moved by 1% of the time
where the time goes in v9:
time: 69.2 us; the launch traced here: 68.9 us
  starting transfers between devices  26.6 us (38%)
  waiting for transfers between devices  25.5 us (37%)
  Pallas kernels  15.9 us (23%)
  between operations  0.78 us (1%)
    ppermute x19, waiting for transfers between devices, swap(): return lax.ppermute(a, 'dp', [(i, i ^ bit) for i in range(size)])  17.3 us
    pallas_call x10, Pallas kernels, run(): pl.pallas_call(kernel, input_output_aliases=aliases or {}, out_shape=outs...  15.9 us
    ppermute x19, starting transfers between devices, swap(): return lax.ppermute(a, 'dp', [(i, i ^ bit) for i in range(size)])  12.3 us
    ppermute x2, starting transfers between devices, gather_rows(): lax.ppermute(part, 'mp', outer)  5.22 us
    ppermute x1, starting transfers between devices, gather_rows(): a1 = lax.ppermute(b0, 'mp', outer)  4.61 us
    ppermute x1, waiting for transfers between devices, gather_rows(): a0 = lax.ppermute(x, 'mp', outer)  4.12 us
    ppermute x2, waiting for transfers between devices, gather_rows(): lax.ppermute(part, 'mp', outer)  3.97 us
    ppermute x1, starting transfers between devices, gather_rows(): a0 = lax.ppermute(x, 'mp', outer)  3.09 us
  transfers between devices with their start and end apart: 25, of which 14 were waited for; matrix products, arithmetic and copies ran while one was open for 0% of the time, Pallas kernels for 17%

profile of v9, /device:TPU:0, one launch (start us, length us, event | category | flops | bytes accessed | tf_op | source)
XLA Modules:
  0.0 68.9 jit_solution(13842588072718546727)
XLA Ops:
  0.6 3.1 %collective-permute-start = (bf16[32,5120]{1,0:T(8,128)(2,1)}, bf16[32,5120]{1,0:T(8,128)(2,1)S(1)}, u32[]{:S(2)}, u32[]{:S(2)}) collective-permute-start(bf16[32,5120]{1,0:T(8,128)(2,1)} %refs_8_.1), channel_id=1, source_target_pairs={{0,1},{1,0},{2,3},{3,2},{4,5},{5,4},{6,7},{7,6},{8,9},{9,8},{10,11... | collective-permute-start | bytes 983048 | tf_op jit(solution)/shard_map/ppermute | solution.py:320
  3.7 0.7 collective-permute-start.3
  4.4 3.1 %prepare.1 = (s32[1,4]{1,0:T(1,128)S(1)}, bf16[5120,512]{1,0:T(8,128)(2,1)S(1)}, f32[4,128,512]{2,1,0:T(8,128)S(1)}, bf16[256,5120]{1,0:T(8,128)(2,1)S(1)}, f32[...) custom-call(s32[4,4]{1,0:T(4,128)} %refs_0_.1, ...), custom_call_target="tpu_custom_call" | custom-call | flops 1000000 | bytes 1000000 | tf_op jit(solution)/shard_map/prepare/pallas_call | solution.py:49
  7.5 4.1 %collective-permute-done.refs_0_ = bf16[32,5120]{1,0:T(8,128)(2,1)S(1)} collective-permute-done((bf16[32,5120]{1,0:T(8,128)(2,1)}, bf16[32,5120]{1,0:T(8,128)(2,1)S(1)}, u32[]{:S(2)}, u32[]{:S(2)}) %collective-permute-start) | collective-permute-done | bytes 327712 | tf_op jit(solution)/shard_map/ppermute | solution.py:320
  11.6 0.7 collective-permute-start.1
  12.3 0.0 collective-permute-done.3.refs_1_
  12.3 4.6 %collective-permute-start.4 = (bf16[32,5120]{1,0:T(8,128)(2,1)S(1)}, bf16[32,5120]{1,0:T(8,128)(2,1)S(1)}, u32[]{:S(2)}, u32[]{:S(2)}) collective-permute-start(bf16[32,5120]{1,0:T(8,128)(2,1)S(1)} %collective-permute-done.3.refs_1_), channel_id=1, source_target_pairs={{0,1},{1,0},{2,3},{3,2},{4,5},{5,4},{6,7},{7,6},{8,9},{9,8},{10,11... | collective-permute-start | bytes 983048 | tf_op jit(solution)/shard_map/ppermute | solution.py:324
  17.0 1.8 %rows.3 = (bf16[256,5120]{1,0:T(8,128)(2,1)S(1)}, bf16[128,512]{1,0:T(8,128)(2,1)S(1)}, f32[64,5120]{1,0:T(8,128)S(1)}) custom-call(bf16[32,5120]{1,0:T(8,128)(2,1)S(1)} %collective-permute-done.refs_0_, bf16[5120,512]{1,0:T(8,128)(2,1)S(1)} %get-tuple-element.57.refs_1_.refs_2_.w, ...), custom_call_target="tpu_custom_call", output_to_operand_aliasing={{0}: (5, {}), {1}: (6, {})} | custom-call | flops 167772160 | bytes 1000000 | tf_op jit(solution)/shard_map/rows/pallas_call | solution.py:49
  18.8 5.1 %collective-permute-start.5 = (bf16[32,3840]{1,0:T(8,128)(2,1)S(1)}, bf16[32,3840]{1,0:T(8,128)(2,1)S(1)}, u32[]{:S(2)}, u32[]{:S(2)}) collective-permute-start(bf16[32,3840]{1,0:T(8,128)(2,1)S(1)} %slice.7), channel_id=1, source_target_pairs={{0,1},{1,0},{2,3},{3,2},{4,5},{5,4},{6,7},{7,6},{8,9},{9,8},{10,11... | collective-permute-start | bytes 737288 | tf_op jit(solution)/shard_map/ppermute | solution.py:328
  23.9 0.1 collective-permute-start.2
  24.0 0.1 collective-permute-done.4.refs_0_
  24.1 1.7 %rows.4 = (bf16[256,5120]{1,0:T(8,128)(2,1)S(1)}, bf16[128,512]{1,0:T(8,128)(2,1)S(1)}, f32[64,5120]{1,0:T(8,128)S(1)}) custom-call(bf16[32,5120]{1,0:T(8,128)(2,1)S(1)} %collective-permute-done.4.refs_0_, bf16[32,5120]{1,0:T(8,128)(2,1)S(1)} %collective-permute-done.3.refs_1_, ...), custom_call_target="tpu_custom_call", output_to_operand_aliasing={{0}: (6, {}), {1}: (7, {})} | custom-call | flops 167772160 | bytes 1000000 | tf_op jit(solution)/shard_map/rows/pallas_call | solution.py:49
  25.8 3.9 %collective-permute-done.5.end = bf16[32,3840]{1,0:T(8,128)(2,1)S(1)} collective-permute-done((bf16[32,3840]{1,0:T(8,128)(2,1)S(1)}, bf16[32,3840]{1,0:T(8,128)(2,1)S(1)}, u32[]{:S(2)}, u32[]{:S(2)}) %collective-permute-start.5) | collective-permute-done | bytes 245792 | tf_op jit(solution)/shard_map/ppermute | solution.py:328
  29.6 0.8 %begin.1 = (bf16[256,5120]{1,0:T(8,128)(2,1)S(1)}, f32[32,512]{1,0:T(8,128)S(1)}) custom-call(bf16[5120,512]{1,0:T(8,128)(2,1)S(1)} %get-tuple-element.57.refs_1_.refs_2_.w, bf16[32,3840]{1,0:T(8,128)(2,1)S(1)} %collective-permute-done.5.end, bf16[32,5120]{1,0:T(8,128)(2,1)S(1)} %collective-permute-done.1.between.refs_1_, ...), custom_call_target="tpu_custom_call", output_to_operand_aliasing={{0}: (3, {})} | custom-call | flops 1000000 | bytes 1000000 | tf_op jit(solution)/shard_map/begin/pallas_call | solution.py:49
  30.4 0.1 collective-permute-done.2.refs_0_
  30.5 1.0 %rows.5 = (bf16[256,5120]{1,0:T(8,128)(2,1)S(1)}, bf16[128,512]{1,0:T(8,128)(2,1)S(1)}, f32[8,5120]{1,0:T(8,128)S(1)}, f32[8,5120]{1,0:T(8,128)S(1)}, f32[8,5120...) custom-call(bf16[32,1280]{1,0:T(8,128)(2,1)S(1)} %collective-permute, ...), custom_call_target="tpu_custom_call", output_to_operand_aliasing={{0}: (7, {}), {1}: (8, {})} | custom-call | flops 167772160 | bytes 1000000 | tf_op jit(solution)/shard_map/rows/pallas_call | solution.py:49
  31.5 0.1 collective-permute-start.7
  31.6 0.5 collective-permute-start.9
  32.1 0.1 collective-permute-start.11
  32.2 0.8 %collective-permute-done.7 = f32[8,5120]{1,0:T(8,128)S(1)} collective-permute-done((f32[8,5120]{1,0:T(8,128)S(1)}, f32[8,5120]{1,0:T(8,128)S(1)}, u32[]{:S(2)}, u32[]{:S(2)}) %collective-permute-start.7) | collective-permute-done | bytes 163872 | tf_op jit(solution)/shard_map/ppermute | solution.py:333
  33.0 1.6 %collective-permute-start.8 = (f32[8,5120]{1,0:T(8,128)S(1)}, f32[8,5120]{1,0:T(8,128)S(1)}, u32[]{:S(2)}, u32[]{:S(2)}) collective-permute-start(f32[8,5120]{1,0:T(8,128)S(1)} %add.34), channel_id=1, source_target_pairs={{0,8},{4,12},{8,0},{12,4},{16,24},{20,28},{24,16},{28,20},{1,9},{5... | collective-permute-start | bytes 491528 | tf_op jit(solution)/shard_map/ppermute | solution.py:333
  34.6 1.6 %collective-permute-start.10 = (f32[8,5120]{1,0:T(8,128)S(1)}, f32[8,5120]{1,0:T(8,128)S(1)}, u32[]{:S(2)}, u32[]{:S(2)}) collective-permute-start(f32[8,5120]{1,0:T(8,128)S(1)} %add.35), channel_id=1, source_target_pairs={{0,16},{4,20},{8,24},{12,28},{16,0},{20,4},{24,8},{28,12},{1,17},{... | collective-permute-start | bytes 491528 | tf_op jit(solution)/shard_map/ppermute | solution.py:333
  36.2 0.5 collective-permute-start.12
  36.7 0.4 merged.1.refs_4_
  37.1 3.0 %collective-permute-done.8 = f32[8,5120]{1,0:T(8,128)S(1)} collective-permute-done((f32[8,5120]{1,0:T(8,128)S(1)}, f32[8,5120]{1,0:T(8,128)S(1)}, u32[]{:S(2)}, u32[]{:S(2)}) %collective-permute-start.8) | collective-permute-done | bytes 163872 | tf_op jit(solution)/shard_map/ppermute | solution.py:333
  40.1 4.0 %collective-permute-done.10 = f32[8,5120]{1,0:T(8,128)S(1)} collective-permute-done((f32[8,5120]{1,0:T(8,128)S(1)}, f32[8,5120]{1,0:T(8,128)S(1)}, u32[]{:S(2)}, u32[]{:S(2)}) %collective-permute-start.10) | collective-permute-done | bytes 163872 | tf_op jit(solution)/shard_map/ppermute | solution.py:333
  44.1 0.1 add_add_fusion.refs_0_
  44.2 1.6 %collective-permute-start.18 = (f32[8,5120]{1,0:T(8,128)S(1)}, f32[8,5120]{1,0:T(8,128)S(1)}, u32[]{:S(2)}, u32[]{:S(2)}) collective-permute-start(f32[8,5120]{1,0:T(8,128)S(1)} %add_add_fusion.refs_0_), channel_id=1, source_target_pairs={{0,24},{4,28},{8,16},{12,20},{16,8},{20,12},{24,0},{28,4},{1,25},{... | collective-permute-start | bytes 491528 | tf_op jit(solution)/shard_map/ppermute | solution.py:333
  45.8 1.1 %collective-permute-start.16 = (f32[8,5120]{1,0:T(8,128)S(1)}, f32[8,5120]{1,0:T(8,128)S(1)}, u32[]{:S(2)}, u32[]{:S(2)}) collective-permute-start(f32[8,5120]{1,0:T(8,128)S(1)} %add_add_fusion.refs_0_), channel_id=1, source_target_pairs={{0,16},{4,20},{8,24},{12,28},{16,0},{20,4},{24,8},{28,12},{1,17},{... | collective-permute-start | bytes 491528 | tf_op jit(solution)/shard_map/ppermute | solution.py:333
  46.9 0.9 %collective-permute-start.14 = (f32[8,5120]{1,0:T(8,128)S(1)}, f32[8,5120]{1,0:T(8,128)S(1)}, u32[]{:S(2)}, u32[]{:S(2)}) collective-permute-start(f32[8,5120]{1,0:T(8,128)S(1)} %add_add_fusion.refs_0_), channel_id=1, source_target_pairs={{0,8},{4,12},{8,0},{12,4},{16,24},{20,28},{24,16},{28,20},{1,9},{5... | collective-permute-start | bytes 491528 | tf_op jit(solution)/shard_map/ppermute | solution.py:333
  47.8 4.3 %collective-permute-done.18.refs_6_ = f32[8,5120]{1,0:T(8,128)S(1)} collective-permute-done((f32[8,5120]{1,0:T(8,128)S(1)}, f32[8,5120]{1,0:T(8,128)S(1)}, u32[]{:S(2)}, u32[]{:S(2)}) %collective-permute-start.18) | collective-permute-done | bytes 163872 | tf_op jit(solution)/shard_map/ppermute | solution.py:333
  52.1 1.7 %collective-permute-done.16.refs_4_ = f32[8,5120]{1,0:T(8,128)S(1)} collective-permute-done((f32[8,5120]{1,0:T(8,128)S(1)}, f32[8,5120]{1,0:T(8,128)S(1)}, u32[]{:S(2)}, u32[]{:S(2)}) %collective-permute-start.16) | collective-permute-done | bytes 163872 | tf_op jit(solution)/shard_map/ppermute | solution.py:333
  53.8 0.0 collective-permute-done.14.refs_2_
  53.8 0.5 collective-permute-start.15
  54.3 0.9 %collective-permute-done.17.refs_5_ = f32[8,5120]{1,0:T(8,128)S(1)} collective-permute-done((f32[8,5120]{1,0:T(8,128)S(1)}, f32[8,5120]{1,0:T(8,128)S(1)}, u32[]{:S(2)}, u32[]{:S(2)}) %collective-permute-start.17) | collective-permute-done | bytes 163872 | tf_op jit(solution)/shard_map/ppermute | solution.py:333
  55.2 0.2 collective-permute-done.15.refs_3_
  55.4 2.0 %second.1 = (bf16[256,5120]{1,0:T(8,128)(2,1)S(1)}, f32[64,64]{1,0:T(8,128)S(1)}, f32[32,512]{1,0:T(8,128)S(1)}, f32[32,512]{1,0:T(8,128)S(1)}) custom-call(s32[1,4]{1,0:T(1,128)S(1)} %get-tuple-element.54.ids, f32[8,5120]{1,0:T(8,128)S(1)} %add_add_fusion.refs_0_, f32[8,5120]{1,0:T(8,128)S(1)} %collective-permute-done.13.refs_1_, ...), custom_call_target="tpu_custom_call", output_to_operand_aliasing={{0}: (11, {})} | custom-call | flops 1000000 | bytes 1000000 | tf_op jit(solution)/shard_map/second/pallas_call | solution.py:49
  57.4 0.3 collective-permute-start.20
  57.7 1.0 %collective-permute-done.20 = f32[32,512]{1,0:T(8,128)S(1)} collective-permute-done((f32[32,512]{1,0:T(8,128)S(1)}, f32[32,512]{1,0:T(8,128)S(1)}, u32[]{:S(2)}, u32[]{:S(2)}) %collective-permute-start.20) | collective-permute-done | bytes 65568 | tf_op jit(solution)/shard_map/ppermute | solution.py:333
  58.7 1.5 %collective-permute-start.23 = (f32[32,512]{1,0:T(8,128)S(1)}, f32[32,512]{1,0:T(8,128)S(1)}, u32[]{:S(2)}, u32[]{:S(2)}) collective-permute-start(f32[32,512]{1,0:T(8,128)S(1)} %add.40), channel_id=1, source_target_pairs={{0,24},{4,28},{8,16},{12,20},{16,8},{20,12},{24,0},{28,4},{1,25},{... | collective-permute-start | bytes 196616 | tf_op jit(solution)/shard_map/ppermute | solution.py:333
  60.2 1.5 %collective-permute-start.22 = (f32[32,512]{1,0:T(8,128)S(1)}, f32[32,512]{1,0:T(8,128)S(1)}, u32[]{:S(2)}, u32[]{:S(2)}) collective-permute-start(f32[32,512]{1,0:T(8,128)S(1)} %add.40), channel_id=1, source_target_pairs={{0,16},{4,20},{8,24},{12,28},{16,0},{20,4},{24,8},{28,12},{1,17},{... | collective-permute-start | bytes 196616 | tf_op jit(solution)/shard_map/ppermute | solution.py:333
  61.7 0.6 collective-permute-start.21
  62.3 2.3 %factor.1.linv.refs_2_ = f32[64,64]{1,0:T(8,128)S(1)} custom-call(f32[64,64]{1,0:T(8,128)S(1)} %get-tuple-element.90.gram), custom_call_target="tpu_custom_call" | custom-call | flops 1000000 | bytes 1000000 | tf_op jit(solution)/shard_map/factor/pallas_call | solution.py:49
  64.6 0.8 %collective-permute-done.22 = f32[32,512]{1,0:T(8,128)S(1)} collective-permute-done((f32[32,512]{1,0:T(8,128)S(1)}, f32[32,512]{1,0:T(8,128)S(1)}, u32[]{:S(2)}, u32[]{:S(2)}) %collective-permute-start.22) | collective-permute-done | bytes 65568 | tf_op jit(solution)/shard_map/ppermute | solution.py:333
  65.4 0.6 collective-permute-done.21
  66.0 0.1 collective-permute-start.24
  66.1 1.4 %left.1 = (f32[64,5120]{1,0:T(8,128)}, bf16[512,192]{1,0:T(8,128)(2,1)S(1)}) custom-call(s32[1,4]{1,0:T(1,128)S(1)} %get-tuple-element.54.ids, f32[64,64]{1,0:T(8,128)S(1)} %factor.1.linv.refs_2_, bf16[256,5120]{1,0:T(8,128)(2,1)S(1)} %get-tuple-element.96.bx), custom_call_target="tpu_custom_call" | custom-call | flops 1000000 | bytes 1000000 | tf_op jit(solution)/shard_map/left/pallas_call | solution.py:49
  67.5 1.5 %last.1 = (f32[64,512]{1,0:T(8,128)}, f32[4,128,512]{2,1,0:T(8,128)}) custom-call(f32[32,512]{1,0:T(8,128)S(1)} %add_add_fusion.1.refs_0_, f32[32,512]{1,0:T(8,128)S(1)} %collective-permute-done.24.refs_1_, f32[64,64]{1,0:T(8,128)S(1)} %factor.1.linv.refs_2_, bf16[512,192]{1,0:T(8,128)(2,1)S(1)} %get-tuple-element.101.refs_3_, f32[4,128,512]{2,1,0:T(8,128)S(1)} %merged.1.refs_4_), custom_call_target="tpu_custom_call" | custom-call | flops 1000000 | bytes 1000000 | tf_op jit(solution)/shard_map/last/pallas_call | solution.py:49
  (21 shorter events, 0.2 us)
Async XLA Ops:
  0.6 11.0 %collective-permute-start = (bf16[32,5120]{1,0:T(8,128)(2,1)}, bf16[32,5120]{1,0:T(8,128)(2,1)S(1)}, u32[]{:S(2)}, u32[]{:S(2)}) collective-permute-start(bf16[32,5120]{1,0:T(8,128)(2,1)} %refs_8_.1), channel_id=1, source_target_pairs={{0,1},{1,0},{2,3},{3,2},{4,5},{5,4},{6,7},{7,6},{8,9},{9,8},{10,11... | collective-permute-start | bytes 983048 | tf_op jit(solution)/shard_map/ppermute | solution.py:320
  3.7 8.6 %collective-permute-start.3 = (bf16[32,5120]{1,0:T(8,128)(2,1)}, bf16[32,5120]{1,0:T(8,128)(2,1)S(1)}, u32[]{:S(2)}, u32[]{:S(2)}) collective-permute-start(bf16[32,5120]{1,0:T(8,128)(2,1)} %refs_8_.1), channel_id=1, source_target_pairs={{1,2},{2,1},{5,6},{6,5},{9,10},{10,9},{13,14},{14,13},{17,18},{18,... | collective-permute-start | bytes 983048 | tf_op jit(solution)/shard_map/ppermute | solution.py:321
  11.6 7.1 %collective-permute-start.1 = (bf16[32,5120]{1,0:T(8,128)(2,1)S(1)}, bf16[32,5120]{1,0:T(8,128)(2,1)S(1)}, u32[]{:S(2)}, u32[]{:S(2)}) collective-permute-start(bf16[32,5120]{1,0:T(8,128)(2,1)S(1)} %collective-permute-done.refs_0_), channel_id=1, source_target_pairs={{1,2},{2,1},{5,6},{6,5},{9,10},{10,9},{13,14},{14,13},{17,18},{18,... | collective-permute-start | bytes 983048 | tf_op jit(solution)/shard_map/ppermute | solution.py:323
  12.3 11.8 %collective-permute-start.4 = (bf16[32,5120]{1,0:T(8,128)(2,1)S(1)}, bf16[32,5120]{1,0:T(8,128)(2,1)S(1)}, u32[]{:S(2)}, u32[]{:S(2)}) collective-permute-start(bf16[32,5120]{1,0:T(8,128)(2,1)S(1)} %collective-permute-done.3.refs_1_), channel_id=1, source_target_pairs={{0,1},{1,0},{2,3},{3,2},{4,5},{5,4},{6,7},{7,6},{8,9},{9,8},{10,11... | collective-permute-start | bytes 983048 | tf_op jit(solution)/shard_map/ppermute | solution.py:324
  18.8 10.8 %collective-permute-start.5 = (bf16[32,3840]{1,0:T(8,128)(2,1)S(1)}, bf16[32,3840]{1,0:T(8,128)(2,1)S(1)}, u32[]{:S(2)}, u32[]{:S(2)}) collective-permute-start(bf16[32,3840]{1,0:T(8,128)(2,1)S(1)} %slice.7), channel_id=1, source_target_pairs={{0,1},{1,0},{2,3},{3,2},{4,5},{5,4},{6,7},{7,6},{8,9},{9,8},{10,11... | collective-permute-start | bytes 737288 | tf_op jit(solution)/shard_map/ppermute | solution.py:328
  23.9 6.6 %collective-permute-start.2 = (bf16[32,1280]{1,0:T(8,128)(2,1)S(1)}, bf16[32,1280]{1,0:T(8,128)(2,1)S(1)}, u32[]{:S(2)}, u32[]{:S(2)}) collective-permute-start(bf16[32,1280]{1,0:T(8,128)(2,1)S(1)} %slice.6), channel_id=1, source_target_pairs={{0,1},{1,0},{2,3},{3,2},{4,5},{5,4},{6,7},{7,6},{8,9},{9,8},{10,11... | collective-permute-start | bytes 245768 | tf_op jit(solution)/shard_map/ppermute | solution.py:328
  31.5 1.5 %collective-permute-start.7 = (f32[8,5120]{1,0:T(8,128)S(1)}, f32[8,5120]{1,0:T(8,128)S(1)}, u32[]{:S(2)}, u32[]{:S(2)}) collective-permute-start(f32[8,5120]{1,0:T(8,128)S(1)} %get-tuple-element.76), channel_id=1, source_target_pairs={{0,4},{4,0},{8,12},{12,8},{16,20},{20,16},{24,28},{28,24},{1,5},{5... | collective-permute-start | bytes 491528 | tf_op jit(solution)/shard_map/ppermute | solution.py:333
  31.6 3.0 %collective-permute-start.9 = (f32[8,5120]{1,0:T(8,128)S(1)}, f32[8,5120]{1,0:T(8,128)S(1)}, u32[]{:S(2)}, u32[]{:S(2)}) collective-permute-start(f32[8,5120]{1,0:T(8,128)S(1)} %get-tuple-element.78), channel_id=1, source_target_pairs={{0,4},{4,0},{8,12},{12,8},{16,20},{20,16},{24,28},{28,24},{1,5},{5... | collective-permute-start | bytes 491528 | tf_op jit(solution)/shard_map/ppermute | solution.py:333
  32.1 4.1 %collective-permute-start.11 = (f32[8,5120]{1,0:T(8,128)S(1)}, f32[8,5120]{1,0:T(8,128)S(1)}, u32[]{:S(2)}, u32[]{:S(2)}) collective-permute-start(f32[8,5120]{1,0:T(8,128)S(1)} %get-tuple-element.80), channel_id=1, source_target_pairs={{0,4},{4,0},{8,12},{12,8},{16,20},{20,16},{24,28},{28,24},{1,5},{5... | collective-permute-start | bytes 491528 | tf_op jit(solution)/shard_map/ppermute | solution.py:333
  33.0 7.1 %collective-permute-start.8 = (f32[8,5120]{1,0:T(8,128)S(1)}, f32[8,5120]{1,0:T(8,128)S(1)}, u32[]{:S(2)}, u32[]{:S(2)}) collective-permute-start(f32[8,5120]{1,0:T(8,128)S(1)} %add.34), channel_id=1, source_target_pairs={{0,8},{4,12},{8,0},{12,4},{16,24},{20,28},{24,16},{28,20},{1,9},{5... | collective-permute-start | bytes 491528 | tf_op jit(solution)/shard_map/ppermute | solution.py:333
  34.6 9.5 %collective-permute-start.10 = (f32[8,5120]{1,0:T(8,128)S(1)}, f32[8,5120]{1,0:T(8,128)S(1)}, u32[]{:S(2)}, u32[]{:S(2)}) collective-permute-start(f32[8,5120]{1,0:T(8,128)S(1)} %add.35), channel_id=1, source_target_pairs={{0,16},{4,20},{8,24},{12,28},{16,0},{20,4},{24,8},{28,12},{1,17},{... | collective-permute-start | bytes 491528 | tf_op jit(solution)/shard_map/ppermute | solution.py:333
  36.2 7.9 %collective-permute-start.12 = (f32[8,5120]{1,0:T(8,128)S(1)}, f32[8,5120]{1,0:T(8,128)S(1)}, u32[]{:S(2)}, u32[]{:S(2)}) collective-permute-start(f32[8,5120]{1,0:T(8,128)S(1)} %add.36), channel_id=1, source_target_pairs={{0,24},{4,28},{8,16},{12,20},{16,8},{20,12},{24,0},{28,4},{1,25},{... | collective-permute-start | bytes 491528 | tf_op jit(solution)/shard_map/ppermute | solution.py:333
  36.7 7.4 %collective-permute-start.6 = (f32[8,5120]{1,0:T(8,128)S(1)}, f32[8,5120]{1,0:T(8,128)S(1)}, u32[]{:S(2)}, u32[]{:S(2)}) collective-permute-start(f32[8,5120]{1,0:T(8,128)S(1)} %get-tuple-element.74), channel_id=1, source_target_pairs={{0,4},{4,0},{8,12},{12,8},{16,20},{20,16},{24,28},{28,24},{1,5},{5... | collective-permute-start | bytes 491528 | tf_op jit(solution)/shard_map/ppermute | solution.py:333
  44.2 7.9 %collective-permute-start.18 = (f32[8,5120]{1,0:T(8,128)S(1)}, f32[8,5120]{1,0:T(8,128)S(1)}, u32[]{:S(2)}, u32[]{:S(2)}) collective-permute-start(f32[8,5120]{1,0:T(8,128)S(1)} %add_add_fusion.refs_0_), channel_id=1, source_target_pairs={{0,24},{4,28},{8,16},{12,20},{16,8},{20,12},{24,0},{28,4},{1,25},{... | collective-permute-start | bytes 491528 | tf_op jit(solution)/shard_map/ppermute | solution.py:333
  45.8 8.0 %collective-permute-start.16 = (f32[8,5120]{1,0:T(8,128)S(1)}, f32[8,5120]{1,0:T(8,128)S(1)}, u32[]{:S(2)}, u32[]{:S(2)}) collective-permute-start(f32[8,5120]{1,0:T(8,128)S(1)} %add_add_fusion.refs_0_), channel_id=1, source_target_pairs={{0,16},{4,20},{8,24},{12,28},{16,0},{20,4},{24,8},{28,12},{1,17},{... | collective-permute-start | bytes 491528 | tf_op jit(solution)/shard_map/ppermute | solution.py:333
  46.9 7.0 %collective-permute-start.14 = (f32[8,5120]{1,0:T(8,128)S(1)}, f32[8,5120]{1,0:T(8,128)S(1)}, u32[]{:S(2)}, u32[]{:S(2)}) collective-permute-start(f32[8,5120]{1,0:T(8,128)S(1)} %add_add_fusion.refs_0_), channel_id=1, source_target_pairs={{0,8},{4,12},{8,0},{12,4},{16,24},{20,28},{24,16},{28,20},{1,9},{5... | collective-permute-start | bytes 491528 | tf_op jit(solution)/shard_map/ppermute | solution.py:333
  47.8 6.5 %collective-permute-start.13 = (f32[8,5120]{1,0:T(8,128)S(1)}, f32[8,5120]{1,0:T(8,128)S(1)}, u32[]{:S(2)}, u32[]{:S(2)}) collective-permute-start(f32[8,5120]{1,0:T(8,128)S(1)} %add_add_fusion.refs_0_), channel_id=1, source_target_pairs={{0,4},{4,0},{8,12},{12,8},{16,20},{20,16},{24,28},{28,24},{1,5},{5... | collective-permute-start | bytes 491528 | tf_op jit(solution)/shard_map/ppermute | solution.py:333
  52.1 2.2 %collective-permute-start.19 = (f32[8,5120]{1,0:T(8,128)S(1)}, f32[8,5120]{1,0:T(8,128)S(1)}, u32[]{:S(2)}, u32[]{:S(2)}) collective-permute-start(f32[8,5120]{1,0:T(8,128)S(1)} %collective-permute-done.18.refs_6_), channel_id=1, source_target_pairs={{0,4},{4,0},{8,12},{12,8},{16,20},{20,16},{24,28},{28,24},{1,5},{5... | collective-permute-start | bytes 491528 | tf_op jit(solution)/shard_map/ppermute | solution.py:333
  53.8 1.4 %collective-permute-start.17 = (f32[8,5120]{1,0:T(8,128)S(1)}, f32[8,5120]{1,0:T(8,128)S(1)}, u32[]{:S(2)}, u32[]{:S(2)}) collective-permute-start(f32[8,5120]{1,0:T(8,128)S(1)} %collective-permute-done.16.refs_4_), channel_id=1, source_target_pairs={{0,4},{4,0},{8,12},{12,8},{16,20},{20,16},{24,28},{28,24},{1,5},{5... | collective-permute-start | bytes 491528 | tf_op jit(solution)/shard_map/ppermute | solution.py:333
  53.8 1.6 %collective-permute-start.15 = (f32[8,5120]{1,0:T(8,128)S(1)}, f32[8,5120]{1,0:T(8,128)S(1)}, u32[]{:S(2)}, u32[]{:S(2)}) collective-permute-start(f32[8,5120]{1,0:T(8,128)S(1)} %collective-permute-done.14.refs_2_), channel_id=1, source_target_pairs={{0,4},{4,0},{8,12},{12,8},{16,20},{20,16},{24,28},{28,24},{1,5},{5... | collective-permute-start | bytes 491528 | tf_op jit(solution)/shard_map/ppermute | solution.py:333
  57.4 1.3 %collective-permute-start.20 = (f32[32,512]{1,0:T(8,128)S(1)}, f32[32,512]{1,0:T(8,128)S(1)}, u32[]{:S(2)}, u32[]{:S(2)}) collective-permute-start(f32[32,512]{1,0:T(8,128)S(1)} %get-tuple-element.89), channel_id=1, source_target_pairs={{0,4},{4,0},{8,12},{12,8},{16,20},{20,16},{24,28},{28,24},{1,5},{5... | collective-permute-start | bytes 196616 | tf_op jit(solution)/shard_map/ppermute | solution.py:333
  58.7 5.9 %collective-permute-start.23 = (f32[32,512]{1,0:T(8,128)S(1)}, f32[32,512]{1,0:T(8,128)S(1)}, u32[]{:S(2)}, u32[]{:S(2)}) collective-permute-start(f32[32,512]{1,0:T(8,128)S(1)} %add.40), channel_id=1, source_target_pairs={{0,24},{4,28},{8,16},{12,20},{16,8},{20,12},{24,0},{28,4},{1,25},{... | collective-permute-start | bytes 196616 | tf_op jit(solution)/shard_map/ppermute | solution.py:333
  60.2 5.1 %collective-permute-start.22 = (f32[32,512]{1,0:T(8,128)S(1)}, f32[32,512]{1,0:T(8,128)S(1)}, u32[]{:S(2)}, u32[]{:S(2)}) collective-permute-start(f32[32,512]{1,0:T(8,128)S(1)} %add.40), channel_id=1, source_target_pairs={{0,16},{4,20},{8,24},{12,28},{16,0},{20,4},{24,8},{28,12},{1,17},{... | collective-permute-start | bytes 196616 | tf_op jit(solution)/shard_map/ppermute | solution.py:333
  61.7 4.3 %collective-permute-start.21 = (f32[32,512]{1,0:T(8,128)S(1)}, f32[32,512]{1,0:T(8,128)S(1)}, u32[]{:S(2)}, u32[]{:S(2)}) collective-permute-start(f32[32,512]{1,0:T(8,128)S(1)} %add.40), channel_id=1, source_target_pairs={{0,8},{4,12},{8,0},{12,4},{16,24},{20,28},{24,16},{28,20},{1,9},{5... | collective-permute-start | bytes 196616 | tf_op jit(solution)/shard_map/ppermute | solution.py:333
  66.0 1.5 %collective-permute-start.24 = (f32[32,512]{1,0:T(8,128)S(1)}, f32[32,512]{1,0:T(8,128)S(1)}, u32[]{:S(2)}, u32[]{:S(2)}) collective-permute-start(f32[32,512]{1,0:T(8,128)S(1)} %add_add_fusion.1.refs_0_), channel_id=1, source_target_pairs={{0,4},{4,0},{8,12},{12,8},{16,20},{20,16},{24,28},{28,24},{1,5},{5... | collective-permute-start | bytes 196616 | tf_op jit(solution)/shard_map/ppermute | solution.py:333
